TPU v7x, 32 devices: a whole 2x2x4 slice. The times are simulated.
32 devices in a mesh: groups: 2 (over y), ctx: 4 (over z), head: 2 (over x), pair: 2 (over core).
Axes of the slice: x: 2, y: 2, z: 4, core: 2. Of those that a mesh axis runs over, the one named last changes fastest.
Arguments:
- student_query: bfloat16 [1024, 4096], P(('groups', 'ctx'), ('head', 'pair')), parts along dimension 0, may hold values from -25 to 25
- teacher_keys: bfloat16 [1024, 1024], P(('groups', 'ctx'), ('head', 'pair')), parts along dimension 0, may hold values from -9 to 9
- teacher_values: bfloat16 [1024, 1024], P(('groups', 'ctx'), ('head', 'pair')), parts along dimension 0, may hold values from -6 to 6
- band_span: int32 [1024], P(('groups', 'ctx')), parts along dimension 0, may hold values from 256 to 1024, as said below
- residual_in: bfloat16 [1024, 4096], P(('groups', 'ctx'), ('head', 'pair')), parts along dimension 0, may hold values from -3 to 3
- norm_gain: float32 [4096], replicated, may hold values from 0.25 to 1.75
- w_gate: bfloat16 [4096, 7168], P('ctx', ('head', 'pair')), may hold values from -0.09375 to 0.09375
- w_up: bfloat16 [4096, 7168], P('ctx', ('head', 'pair')), may hold values from -0.09375 to 0.09375
- w_down: bfloat16 [7168, 4096], P(('head', 'pair'), 'ctx'), may hold values from -0.0625 to 0.0625
- teacher_feats: bfloat16 [1024, 7168], P(('groups', 'ctx'), ('head', 'pair')), parts along dimension 0, may hold values from -31 to 31
- keep_tiles: int32 [1024, 56], P(('groups', 'ctx'), ('head', 'pair')), parts along dimension 0, may hold values from 0 to 1, as said below
Outputs:
- layer_out: bfloat16 [1024, 4096], P(('groups', 'ctx'), ('head', 'pair')), parts along dimension 0
- loss_value: float32 [2], P('groups'), parts along dimension 0
- grad_resid: float32 [1024, 4096], P(('groups', 'ctx'), ('head', 'pair')), parts along dimension 0
There are 2 independent parts, one for each index of `groups`. A program takes and returns all parts, laid end to end along the dimension named above; an argument that names none is the same for every part. Nothing has to cross between parts.
Inputs may be any that keep to these rules, and one draw needn't show every extreme that they name: `band_span`: some token's span equals 1024. `keep_tiles`: the first token keeps every tile.
All inputs are finite; a program needn't handle non-finite values.
Results may differ from a plain program's by a relative error of at most 0.014.
Values may be sent and summed in bfloat16 or wider, within the bound.
No kernel may reach another device: no remote copies, remote signals or barrier semaphores. Data moves between devices by JAX's collectives and lax.ppermute only.
A program may use at most 128 MiB of HBM per device.

v0:
```python
import math

import jax
import jax.numpy as jnp
from jax import lax
from jax.sharding import PartitionSpec as P

D = 4096
HEADS = 32
KV_HEADS = 8
HEAD_DIM = 128
TILE = 128
BAND = 8


def passed_along(block, axis, distance):
    devices = range(lax.axis_size(axis))
    route = [(i - distance, i) for i in devices if i - distance in devices]
    return lax.ppermute(block, axis, route)


def attend_heads(query_part, key_rows, value_rows, allowed):
    scores = jnp.einsum("thd,sd->hts", query_part, key_rows, preferred_element_type=jnp.float32) * (
        1.0 / math.sqrt(HEAD_DIM)
    )
    masked = jnp.where(allowed[None], scores, -jnp.inf)
    highest = jnp.max(masked, axis=-1, keepdims=True)
    weights = jnp.exp(masked - highest)
    normalized = (weights / jnp.sum(weights, axis=-1, keepdims=True)).astype(jnp.bfloat16)
    return jnp.einsum("hts,sd->thd", normalized, value_rows, preferred_element_type=jnp.float32)


def local(
    student_query,
    teacher_keys,
    teacher_values,
    band_span,
    residual_in,
    norm_gain,
    w_gate,
    w_up,
    w_down,
    teacher_feats,
    keep_tiles,
):
    tok_rows = student_query.shape[0]
    kv_local = teacher_keys.shape[1] // HEAD_DIM
    group_size = HEADS // KV_HEADS
    ctx_index = lax.axis_index("ctx")
    paired = jnp.stack([teacher_keys, teacher_values])

    def pass_block(carried, unused_step):
        moved = passed_along(carried, "ctx", 1)
        return (moved, moved)

    unused_last, earlier = lax.scan(pass_block, paired, None, length=BAND)
    all_blocks = jnp.concatenate([paired[None], earlier], axis=0)
    rounds_count = BAND + 1
    round_ids = jnp.arange(rounds_count, dtype=jnp.int32)
    key_pos = (
        (ctx_index - round_ids)[:, None] * tok_rows + jnp.arange(tok_rows, dtype=jnp.int32)[None, :]
    ).reshape(-1)
    query_pos = ctx_index * tok_rows + jnp.arange(tok_rows, dtype=jnp.int32)
    distance = query_pos[:, None] - key_pos[None, :]
    allowed = (distance >= 0) & (distance < band_span[:, None]) & (key_pos[None, :] >= 0)
    keys_flat = all_blocks[:, 0].reshape(rounds_count * tok_rows, kv_local, HEAD_DIM)
    values_flat = all_blocks[:, 1].reshape(rounds_count * tok_rows, kv_local, HEAD_DIM)
    query_heads = student_query.reshape(tok_rows, kv_local, group_size, HEAD_DIM)
    outputs = []
    for kv_head in range(kv_local):
        for first_head in range(0, group_size, 2):
            outputs.append(
                attend_heads(
                    query_heads[:, kv_head, first_head : first_head + 2],
                    keys_flat[:, kv_head],
                    values_flat[:, kv_head],
                    allowed,
                )
            )
    attended = jnp.concatenate(outputs, axis=1).reshape(tok_rows, -1)
    residual = (residual_in.astype(jnp.float32) + attended).astype(jnp.bfloat16)
    gathered = lax.all_gather(residual, ("head", "pair"), axis=1, tiled=True)
    full_float = gathered.astype(jnp.float32)
    rms_value = jnp.sqrt(jnp.mean(full_float * full_float, axis=1, keepdims=True) + 1e-05)
    normed = (full_float / rms_value * norm_gain).astype(jnp.bfloat16)
    gate_full, up_full = (
        lax.all_gather(w_gate, "ctx", axis=0, tiled=True),
        lax.all_gather(w_up, "ctx", axis=0, tiled=True),
    )
    gate_proj = jnp.dot(normed, gate_full, preferred_element_type=jnp.float32)
    up_proj = jnp.dot(normed, up_full, preferred_element_type=jnp.float32)
    lifted = jnp.maximum(gate_proj, 0.0)
    squared = lifted * lifted
    act_value = squared * up_proj
    hidden = act_value.astype(jnp.bfloat16)
    all_hidden = lax.all_gather(hidden, "ctx", axis=0, tiled=True)
    local_part = jnp.dot(all_hidden, w_down, preferred_element_type=jnp.float32).astype(
        jnp.bfloat16
    )
    routed = lax.all_to_all(local_part, "ctx", split_axis=0, concat_axis=1, tiled=True)
    down_sum = lax.psum_scatter(
        routed.astype(jnp.float32).astype(jnp.bfloat16),
        ("head", "pair"),
        scatter_dimension=1,
        tiled=True,
    ).astype(jnp.float32)
    resid_own = residual.astype(jnp.float32)
    layer_out = (resid_own + down_sum).astype(jnp.bfloat16)
    tile_count = keep_tiles.shape[1]
    keep_float = keep_tiles.astype(jnp.float32)
    keep_wide = jnp.broadcast_to(keep_float[:, :, None], (tok_rows, tile_count, TILE)).reshape(
        tok_rows, tile_count * TILE
    )
    differ = act_value - teacher_feats.astype(jnp.float32)
    loss_part = jnp.sum(keep_wide * differ * differ)
    count_part = jnp.sum(keep_float) * TILE
    loss_total, count_total = lax.psum((loss_part, count_part), ("ctx", "head", "pair"))
    loss_value = (loss_total / count_total).reshape(1)
    grad_act = keep_wide * differ
    grad_gate = (grad_act * up_proj * 2.0 * lifted).astype(jnp.bfloat16)
    grad_up = (grad_act * squared).astype(jnp.bfloat16)
    contract = (((1,), (1,)), ((), ()))
    grad_part = lax.dot_general(grad_gate, gate_full, contract, preferred_element_type=jnp.float32)
    grad_part = grad_part + lax.dot_general(
        grad_up, up_full, contract, preferred_element_type=jnp.float32
    )
    own_cols = residual.shape[1]
    own_start = lax.axis_index(("head", "pair")) * own_cols
    gain_own = lax.dynamic_slice_in_dim(norm_gain, own_start, own_cols, 0)
    rms_cubed = rms_value * rms_value * rms_value
    grad_norm = lax.psum_scatter(
        grad_part.astype(jnp.bfloat16), ("head", "pair"), scatter_dimension=1, tiled=True
    ).astype(jnp.float32)
    inner_sum = lax.psum(
        jnp.sum(gain_own * grad_norm * resid_own, axis=1, keepdims=True), ("head", "pair")
    )
    grad_resid = gain_own * grad_norm / rms_value - resid_own * inner_sum / (D * rms_cubed)
    return (layer_out, loss_value, grad_resid)


def solution(mesh):
    in_specs = (
        P(("groups", "ctx"), ("head", "pair")),
        P(("groups", "ctx"), ("head", "pair")),
        P(("groups", "ctx"), ("head", "pair")),
        P(("groups", "ctx")),
        P(("groups", "ctx"), ("head", "pair")),
        P(),
        P("ctx", ("head", "pair")),
        P("ctx", ("head", "pair")),
        P(("head", "pair"), "ctx"),
        P(("groups", "ctx"), ("head", "pair")),
        P(("groups", "ctx"), ("head", "pair")),
    )
    out_specs = (
        P(("groups", "ctx"), ("head", "pair")),
        P("groups"),
        P(("groups", "ctx"), ("head", "pair")),
    )
    return jax.shard_map(local, mesh=mesh, in_specs=in_specs, out_specs=out_specs, check_vma=False)
```

profile of v0, /device:TPU:2, one launch (start us, length us, event | category | flops | bytes accessed | tf_op | source)
XLA Modules:
  0.0 734.4 jit_solution(9024494652574293018)
XLA Ops:
  7.4 0.9 fusion.71
  8.3 56.4 %while.12 = (s32[]{:T(128)}, bf16[2,128,256]{2,1,0:T(8,128)(2,1)S(1)}, bf16[8,2,128,256]{3,2,1,0:T(8,128)(2,1)S(1)}, s32[]{:T(128)}) while((s32[]{:T(128)}, bf16[2,128,256]{2,1,0:T(8,128)(2,1)S(1)}, bf16[8,2,128,256]{3,2,1,0:T(8,128)(2,1)S(1)}, s32[]{:T(128)}) %tuple.30), condition=%wide.region_1.2_spmd, body=%wide.region_0.1_spmd.sunk | while | flops 2 | bytes 1048681 | solution.py:56
  8.3 3.5 collective-permute-start
  11.8 2.7 collective-permute-done
  14.6 4.4 collective-permute-start
  19.0 2.5 collective-permute-done
  21.5 4.4 collective-permute-start
  25.9 2.5 collective-permute-done
  28.4 4.4 collective-permute-start
  32.8 2.5 collective-permute-done
  35.3 4.4 collective-permute-start
  39.7 3.5 collective-permute-done
  43.3 4.4 collective-permute-start
  47.7 3.0 collective-permute-done
  50.8 4.4 collective-permute-start
  55.2 2.5 collective-permute-done
  57.7 4.4 collective-permute-start
  62.1 2.5 collective-permute-done
  64.9 0.9 fusion.76
  66.0 0.9 fusion.27
  68.1 0.6 fusion.78
  69.5 0.9 fusion.75
  70.4 0.6 copy.42
  71.0 0.8 convolution_bitcast_fusion.3
  71.8 0.8 convolution_bitcast_fusion.2
  72.6 0.6 copy.46
  73.2 0.8 convolution_bitcast_fusion.1
  74.1 0.8 convolution_bitcast_fusion
  75.1 0.7 copy-done.5
  75.8 0.8 add_convert_fusion
  76.7 0.7 all-gather.7.cloned.1.call-update
  77.4 0.7 all-gather.9.cloned.1.call-update
  78.7 15.7 %all-gather.5.cloned.1.call-done = bf16[128,4096]{1,0:T(8,128)(2,1)} async-done(((bf16[128,1024]{1,0:T(8,128)(2,1)}), bf16[128,4096]{1,0:T(8,128)(2,1)}) %all-gather.5.cloned.1.call-update) | async-done | bytes 1048592 | tf_op jit(solution)/shard_map/all_gather | solution.py:82
  94.4 1.5 fusion.21
  96.0 253.7 %all-gather.7.cloned.1.call-done = bf16[4096,1792]{1,0:T(8,128)(2,1)} async-done(((bf16[1024,1792]{1,0:T(8,128)(2,1)}), bf16[4096,1792]{1,0:T(8,128)(2,1)}) %all-gather.7.cloned.1.call-update) | async-done | bytes 14680080 | tf_op jit(solution)/shard_map/all_gather | solution.py:87
  349.6 7.7 %convolution_maximum_fusion = f32[128,1792]{1,0:T(8,128)S(1)} fusion(bf16[4096,1792]{1,0:T(8,128)(2,1)} %all-gather.7.cloned.1.call-done, bf16[128,4096]{1,0:T(8,128)(2,1)} %all-gather.5.cloned.1.call-done, f32[4096]{0:T(1024)S(1)} %copy-done.7, f32[128]{0:T(128)S(1)} %get-tuple-element.42), kind=kOutput, calls=%fused_computation.29 | convolution fusion | flops 1881374720 | bytes 16663040 | tf_op jit(solution)/shard_map/dot_general | solution.py:90
  357.4 244.5 %all-gather.9.cloned.1.call-done = bf16[4096,1792]{1,0:T(8,128)(2,1)} async-done(((bf16[1024,1792]{1,0:T(8,128)(2,1)}), bf16[4096,1792]{1,0:T(8,128)(2,1)}) %all-gather.9.cloned.1.call-update) | async-done | bytes 14680080 | tf_op jit(solution)/shard_map/all_gather | solution.py:88
  601.9 9.0 %multiply_reduce_fusion = (f32[]{:T(128)}, bf16[128,1792]{1,0:T(8,128)(2,1)}, f32[128,1792]{1,0:T(8,128)}) fusion(bf16[128,1792]{1,0:T(8,128)(2,1)S(1)} %copy-done.2, f32[128,1792]{1,0:T(8,128)S(1)} %copy.37, f32[128,1792]{1,0:T(8,128)S(1)} %convolution_maximum_fusion, bf16[4096,1792]{1,0:T(8,128)(2,1)} %all-gather.9.cloned.1.call-done, ...), kind=kOutput, calls=%fused_computation.46 | convolution fusion | flops 1882980352 | bytes 19415556 | tf_op jit(solution)/shard_map/dot_general | solution.py:91
  611.0 10.7 %fusion.32 = f32[128,4096]{1,0:T(8,128)S(1)} fusion(bf16[4096,1792]{1,0:T(8,128)(2,1)} %all-gather.7.cloned.1.call-done, f32[128,1792]{1,0:T(8,128)} %copy-done.1, f32[128,1792]{1,0:T(8,128)} %get-tuple-element.43, f32[128,1792]{1,0:T(8,128)S(1)} %copy.37, bf16[128,1792]{1,0:T(8,128)(2,1)S(1)} %copy-done.2), kind=kOutput, calls=%fused_computation.66 | convolution fusion | flops 1881112576 | bytes 19988480 | tf_op jit(solution)/shard_map/dot_general | solution.py:123
  621.7 11.6 %fusion.4 = bf16[128,4096]{1,0:T(8,128)(2,1)} fusion(f32[128,4096]{1,0:T(8,128)S(1)} %fusion.32, bf16[4096,1792]{1,0:T(8,128)(2,1)} %all-gather.9.cloned.1.call-done, f32[128,1792]{1,0:T(8,128)} %copy-done.1, f32[128,1792]{1,0:T(8,128)S(1)} %copy.37, bf16[128,1792]{1,0:T(8,128)(2,1)S(1)} %copy-done.2, f32[128,1792]{1,0:T(8,128)} %get-tuple-element.43), kind=kOutput, calls=%fused_computation.6 | convolution fusion | flops 1881702400 | bytes 21037056 | tf_op jit(solution)/shard_map/dot_general | solution.py:124
  633.4 17.2 %all-gather.11.cloned.1.call-done = bf16[512,1792]{1,0:T(8,128)(2,1)} async-done(((bf16[128,1792]{1,0:T(8,128)(2,1)}), bf16[512,1792]{1,0:T(8,128)(2,1)}) %all-gather.11.cloned.1.call-update) | async-done | bytes 1835024 | tf_op jit(solution)/shard_map/all_gather | solution.py:96
  650.6 4.7 convolution_convert_fusion
  655.3 28.1 %all_to_all.19 = bf16[4,128,1024]{2,1,0:T(8,128)(2,1)S(1)} all-to-all(bf16[4,128,1024]{2,1,0:T(8,128)(2,1)S(1)} %bitcast.216), channel_id=1, replica_groups=mesh['groups'=2,'ctx'=4,'head'=2,'pair'=2] {'ctx'}, dimensions={0} | all-to-all | bytes 2097152 | tf_op jit(solution)/shard_map/all_to_all | solution.py:100
  683.4 1.1 copy.50
  685.8 27.3 %all-reduce = (f32[]{:T(128)}, f32[]{:T(128)}) all-reduce(f32[]{:T(128)} %get-tuple-element.29, f32[]{:T(128)S(6)} %mul.149), channel_id=1, replica_groups=mesh['groups'=2,'ctx'=4,'head'=2,'pair'=2] {'ctx','head','pair'}, use_global_device_ids=true, to_apply=%region_13.14 | all-reduce | flops 2 | bytes 16 | tf_op jit(solution)/shard_map/psum | solution.py:117
  714.5 1.1 fusion.29
  715.6 8.7 %psum.23 = f32[128]{0:T(128)S(1)} all-reduce(f32[128]{0:T(128)S(1)} %fusion.29), channel_id=1, replica_groups=mesh['groups'=2,'ctx'=4,'head'=2,'pair'=2] {'head','pair'}, use_global_device_ids=true, to_apply=%region_18.19 | all-reduce | flops 128 | bytes 1024 | tf_op jit(solution)/shard_map/psum | solution.py:134
  724.3 2.1 fusion.31
  (65 shorter events, 4.5 us)
Async XLA Ops:
  7.2 87.3 %all-gather.5.cloned.1.call-start = ((), (), s32[]{:S(2)}) async-start(), calls=%async_computation.3 | async-start | bytes 1310720 | tf_op jit(solution)/shard_map/all_gather | solution.py:82
  8.3 6.2 collective-permute-start
  14.6 6.9 collective-permute-start
  21.5 6.9 collective-permute-start
  28.4 6.9 collective-permute-start
  35.3 7.9 %collective-permute-start = (bf16[2,128,256]{2,1,0:T(8,128)(2,1)S(1)}, bf16[2,128,256]{2,1,0:T(8,128)(2,1)S(1)}, u32[]{:S(2)}, u32[]{:S(2)}) collective-permute-start(bf16[2,128,256]{2,1,0:T(8,128)(2,1)S(1)} %get-tuple-element.68), channel_id=1, source_target_pairs={{0,4},{4,8},{8,12},{1,5},{5,9},{9,13},{2,6},{6,10},{10,14},{3,7},{... | collective-permute-start | bytes 393224 | tf_op jit(solution)/shard_map/while/body/eval_jaxpr/ppermute | solution.py:19
  43.3 7.4 %collective-permute-start = (bf16[2,128,256]{2,1,0:T(8,128)(2,1)S(1)}, bf16[2,128,256]{2,1,0:T(8,128)(2,1)S(1)}, u32[]{:S(2)}, u32[]{:S(2)}) collective-permute-start(bf16[2,128,256]{2,1,0:T(8,128)(2,1)S(1)} %get-tuple-element.68), channel_id=1, source_target_pairs={{0,4},{4,8},{8,12},{1,5},{5,9},{9,13},{2,6},{6,10},{10,14},{3,7},{... | collective-permute-start | bytes 393224 | tf_op jit(solution)/shard_map/while/body/eval_jaxpr/ppermute | solution.py:19
  50.8 6.9 collective-permute-start
  57.7 6.9 collective-permute-start
  64.9 1.0 copy-start.4
  64.9 1.1 copy-start.8
  74.9 1.0 copy-start.5
  76.6 273.0 %all-gather.7.cloned.1.call-start = ((), (), s32[]{:S(2)}) async-start(), calls=%async_computation.4 | async-start | bytes 18350080 | tf_op jit(solution)/shard_map/all_gather | solution.py:87
  77.4 1.0 copy-start.6
  77.4 524.5 %all-gather.9.cloned.1.call-start = ((), (), s32[]{:S(2)}) async-start(), calls=%async_computation.5 | async-start | bytes 18350080 | tf_op jit(solution)/shard_map/all_gather | solution.py:88
  78.1 572.5 %all-gather.11.cloned.1.call-start = ((), (), s32[]{:S(2)}) async-start(), calls=%async_computation.6 | async-start | bytes 2293760 | tf_op jit(solution)/shard_map/all_gather | solution.py:96
  78.4 271.2 %copy-start.7 = (f32[4096]{0:T(1024)S(1)}, f32[4096]{0:T(1024)}, u32[]{:S(2)}) copy-start(f32[4096]{0:T(1024)} %param.18) | copy-start | bytes 49156
  349.6 252.3 %copy-start.2 = (bf16[128,1792]{1,0:T(8,128)(2,1)S(1)}, bf16[128,1792]{1,0:T(8,128)(2,1)}, u32[]{:S(2)}) copy-start(bf16[128,1792]{1,0:T(8,128)(2,1)} %param.22) | copy-start | bytes 1376260
  349.6 252.3 %copy-start.3 = (bf16[128,4096]{1,0:T(8,128)(2,1)S(1)}, bf16[128,4096]{1,0:T(8,128)(2,1)}, u32[]{:S(2)}) copy-start(bf16[128,4096]{1,0:T(8,128)(2,1)} %all-gather.5.cloned.1.call-done) | copy-start | bytes 3145732
  357.4 253.5 %copy-start.1 = (f32[128,1792]{1,0:T(8,128)}, f32[128,1792]{1,0:T(8,128)S(1)}, u32[]{:S(2)}) copy-start(f32[128,1792]{1,0:T(8,128)S(1)} %convolution_maximum_fusion) | copy-start | bytes 2752516
  611.0 103.5 %reduce-scatter.5.cloned.1.call-start = ((), (), s32[]{:S(2)}) async-start(), calls=%async_computation.8 | async-start | bytes 1310720 | tf_op jit(solution)/shard_map/reduce_scatter | solution.py:131
  633.4 91.0 %reduce-scatter.3.cloned.1.call-start = ((), (), s32[]{:S(2)}) async-start(), calls=%async_computation.7 | async-start | bytes 1310720 | tf_op jit(solution)/shard_map/reduce_scatter | solution.py:101
  683.4 31.1 %copy-start = (bf16[128,1024]{1,0:T(8,128)(2,1)S(1)}, bf16[128,1024]{1,0:T(8,128)(2,1)}, u32[]{:S(2)}) copy-start(bf16[128,1024]{1,0:T(8,128)(2,1)} %add_convert_fusion) | copy-start | bytes 786436
Sparse Core Ops, SparseCore 0:
  76.7 17.6 all-gather.4
  96.0 253.5 all-gather.6
  351.2 250.6 all-gather.8
  611.1 39.5 all-gather.10
  653.0 22.4 reduce-scatter.4
  684.7 22.8 reduce-scatter.2
where the time goes:
time: 738 us; the launch traced here: 734 us
  waiting for transfers between devices  554 us (75%)
  blocking collectives  64.1 us (9%)
  matrix products  49.4 us (7%)
  starting transfers between devices  34.5 us (5%)
  between operations  17.5 us (2%)
  other arithmetic  8.21 us (1%)
    all_gather x1, waiting for transfers between devices, local(): lax.all_gather(w_gate, 'ctx', axis=0, tiled=True)  254 us
    all_gather x1, waiting for transfers between devices, local(): lax.all_gather(w_up, 'ctx', axis=0, tiled=True)  245 us
    ppermute x8, starting transfers between devices, passed_along(): return lax.ppermute(block, axis, route)  34.1 us
    all_to_all x1, blocking collectives, local(): lax.all_to_all(local_part, 'ctx', split_axis=0, concat_axis=1, tiled=True)  28.1 us
    psum x1, blocking collectives, local(): lax.psum((loss_part, count_part), ('ctx', 'head', 'pair'))  27.3 us
    ppermute x8, waiting for transfers between devices, passed_along(): return lax.ppermute(block, axis, route)  21.8 us
    all_gather x1, waiting for transfers between devices, local(): all_hidden = lax.all_gather(hidden, 'ctx', axis=0, tiled=True)  17.2 us
    all_gather x1, waiting for transfers between devices, local(): gathered = lax.all_gather(residual, ('head', 'pair'), axis=1, tiled=True)  15.7 us
  transfers between devices with their start and end apart: 14, of which 12 were waited for; matrix products, arithmetic and copies ran while one was open for 5% of the time, Pallas kernels for 0%

commit v1 on v0

v1 whole, which is shorter than its diff:
```python
import math

import jax
import jax.numpy as jnp
from jax import lax
from jax.sharding import PartitionSpec as P

D = 4096
HEADS = 32
KV_HEADS = 8
HEAD_DIM = 128
TILE = 128
WINDOW = 1024
HP = ("head", "pair")
F32 = jnp.float32
BF16 = jnp.bfloat16


def passed_along(block, axis, distance):
    devices = range(lax.axis_size(axis))
    route = [(i - distance, i) for i in devices if i - distance in devices]
    return lax.ppermute(block, axis, route)


def swapped(block, axis):
    return lax.ppermute(block, axis, [(0, 1), (1, 0)])


def transposed(block):
    n = lax.axis_size("ctx")
    route = [(c * n + h, h * n + c) for c in range(n) for h in range(n)]
    return lax.ppermute(block, ("ctx",) + HP, route)


def attend_heads(query_part, key_rows, value_rows, allowed):
    scores = jnp.einsum("thd,sd->hts", query_part, key_rows, preferred_element_type=F32) * (
        1.0 / math.sqrt(HEAD_DIM)
    )
    masked = jnp.where(allowed[None], scores, -jnp.inf)
    highest = jnp.max(masked, axis=-1, keepdims=True)
    weights = jnp.exp(masked - highest)
    normalized = (weights / jnp.sum(weights, axis=-1, keepdims=True)).astype(BF16)
    return jnp.einsum("hts,sd->thd", normalized, value_rows, preferred_element_type=F32)


def attention(student_query, teacher_keys, teacher_values, band_span):
    rows = student_query.shape[0]
    kv_local = teacher_keys.shape[1] // HEAD_DIM
    group_size = HEADS // KV_HEADS
    ctx_index = lax.axis_index("ctx")
    paired = jnp.stack([teacher_keys, teacher_values])
    back = min(-(-WINDOW // rows), lax.axis_size("ctx") - 1)
    blocks = [paired] + [passed_along(paired, "ctx", d) for d in range(1, back + 1)]
    round_ids = jnp.arange(back + 1, dtype=jnp.int32)
    key_pos = (
        (ctx_index - round_ids)[:, None] * rows + jnp.arange(rows, dtype=jnp.int32)[None, :]
    ).reshape(-1)
    query_pos = ctx_index * rows + jnp.arange(rows, dtype=jnp.int32)
    distance = query_pos[:, None] - key_pos[None, :]
    allowed = (distance >= 0) & (distance < band_span[:, None]) & (key_pos[None, :] >= 0)
    all_blocks = jnp.concatenate(blocks, axis=1)
    outputs = []
    for kv_head in range(kv_local):
        cols = slice(kv_head * HEAD_DIM, (kv_head + 1) * HEAD_DIM)
        first = kv_head * group_size * HEAD_DIM
        query_part = student_query[:, first : first + group_size * HEAD_DIM]
        outputs.append(
            attend_heads(
                query_part.reshape(rows, group_size, HEAD_DIM),
                all_blocks[0][:, cols],
                all_blocks[1][:, cols],
                allowed,
            ).reshape(rows, group_size * HEAD_DIM)
        )
    return jnp.concatenate(outputs, axis=1)


def shifted(block, distance):
    return passed_along(block, "ctx", distance)


def picked(blocks, index):
    return lax.dynamic_index_in_dim(blocks, index, 0, keepdims=False)


def summed_over_hp(small):
    small = small + swapped(small, "pair")
    return small + swapped(small, "head")


def split_bits(wide):
    high = lax.reduce_precision(wide, 8, 7)
    middle = lax.reduce_precision(wide - high, 8, 7)
    return [v.astype(BF16) for v in (high, middle, wide - high - middle)]


def block_terms(gate_proj, up_proj, feats, keep_cols, weights):
    w_gate, w_up, w_down = weights
    rows, ff = gate_proj.shape
    tiles = keep_cols.shape[1]
    keep = jnp.broadcast_to(keep_cols.astype(F32)[:, :, None], (rows, tiles, TILE)).reshape(rows, ff)
    lifted = jnp.maximum(gate_proj, 0.0)
    squared = lifted * lifted
    act = squared * up_proj
    differ = act - feats.astype(F32)
    grad_act = keep * differ
    grad_gate = (grad_act * up_proj * 2.0 * lifted).astype(BF16)
    grad_up = (grad_act * squared).astype(BF16)
    contract = (((1,), (1,)), ((), ()))
    down = jnp.dot(act.astype(BF16), w_down, preferred_element_type=F32)
    grad = lax.dot_general(grad_gate, w_gate, contract, preferred_element_type=F32)
    grad = grad + lax.dot_general(grad_up, w_up, contract, preferred_element_type=F32)
    return down, grad, jnp.sum(grad_act * act, axis=1), jnp.sum(grad_act * differ)


def on_square(residual, norm_gain, weights, teacher_feats, keep_tiles):
    w_gate, w_up, _ = weights
    rows, d_ctx = residual.shape
    ff = w_gate.shape[1]
    tiles = keep_tiles.shape[1]
    z = lax.axis_index("ctx")
    hp = lax.axis_index(HP)
    low = z < 2

    tile = transposed(residual)
    own_wide = residual.astype(F32)
    mean = summed_over_hp(jnp.sum(own_wide * own_wide, axis=1)) / D
    rms = jnp.sqrt(mean + 1e-05)
    extra = [keep_tiles.astype(BF16)] + [v[:, None] for v in split_bits(rms)]
    marked = jnp.concatenate([teacher_feats] + extra, axis=1)
    marked = jnp.pad(marked, ((0, 0), (0, -marked.shape[1] % 128)))
    across = swapped(tile, "head")
    both = swapped(jnp.stack([tile, across]), "pair")
    marked, _ = lax.optimization_barrier((marked, tile))
    mark_right, mark_left = [shifted(marked, 1)], [shifted(marked, -1)]

    gain = lax.dynamic_slice_in_dim(norm_gain, z * d_ctx, d_ctx, 0)
    resid = jnp.stack([tile, both[0], across, both[1]]).astype(F32)
    scaled = (resid * gain).astype(BF16).reshape(4 * rows, d_ctx)
    parts = [
        jnp.dot(scaled, w, preferred_element_type=F32).astype(BF16).reshape(4, rows, ff)
        for w in (w_gate, w_up)
    ]

    came = [[None, None], [None, None]]
    for s in range(3):
        if s == 1:
            held, _ = lax.optimization_barrier(((mark_right[0], mark_left[0]), came[0][0]))
            mark_right.append(shifted(held[0], 1))
            mark_left.append(shifted(held[1], -1))
        if s == 2:
            held, _ = lax.optimization_barrier(((mark_right[1], mark_left[1]), came[0][0]))
            mark_right.append(shifted(held[0], 1))
            mark_left.append(shifted(held[1], -1))
        for i in range(2):
            right = picked(parts[i], jnp.clip(3 - s + z, 0, 3) ^ hp)
            left = picked(parts[i], jnp.clip(s - 3 + z, 0, 3) ^ hp)
            if s > 0:
                right = (right.astype(F32) + came[i][0].astype(F32)).astype(BF16)
                left = (left.astype(F32) + came[i][1].astype(F32)).astype(BF16)
            came[i] = [shifted(right, 1), shifted(left, -1)]
    owned = jnp.concatenate(
        [
            (picked(parts[i], z ^ hp).astype(F32) + came[i][0].astype(F32) + came[i][1].astype(F32)).astype(BF16)
            for i in range(2)
        ],
        axis=1,
    )

    owned, mark_right[2], mark_left[2] = lax.optimization_barrier((owned, mark_right[2], mark_left[2]))
    right, left = [shifted(owned, 1)], [shifted(owned, -1)]
    for s in range(2):
        right.append(shifted(right[s], 1))
        left.append(shifted(left[s], -1))

    def slots_of(mine, right, left):
        first = jnp.where(low, left[0], right[0])
        second = jnp.where(low, left[1], right[1])
        inner = jnp.where(low, right[0], left[0])
        outer = jnp.where(low, left[2], right[2])
        third = jnp.where((z == 0) | (z == 3), outer, inner)
        return [mine, first, second, third]

    def slot(token):
        return jnp.where(low, token - z, z - token) & 3

    sums = slots_of(owned, right, left)
    marks = slots_of(marked, mark_right, mark_left)
    results, rms_slots = [], []
    for k in range(4):
        bits = marks[k][:, ff + tiles : ff + tiles + 3].astype(F32)
        rms_k = bits[:, 0] + bits[:, 1] + bits[:, 2]
        inv = (1.0 / rms_k)[:, None]
        rms_slots.append(rms_k)
        results.append(
            block_terms(
                sums[k][:, :ff].astype(F32) * inv,
                sums[k][:, ff:].astype(F32) * inv,
                marks[k][:, :ff],
                marks[k][:, ff : ff + tiles],
                weights,
            )
        )
    down, grad, inner, loss = [[r[i] for r in results] for i in range(4)]

    count = sum(jnp.sum(m[:, ff : ff + tiles].astype(F32)) for m in marks) * TILE
    inner = jnp.stack(inner)
    by_token = jnp.concatenate([picked(inner, slot(t)) for t in range(4)])
    small = jnp.concatenate([by_token, sum(loss)[None], count[None], jnp.zeros(126, F32)])
    small = summed_over_hp(small)
    loss_value = (small[4 * rows] / small[4 * rows + 1]).reshape(1)
    rms_own = picked(jnp.stack(rms_slots), slot(hp))[:, None]
    inner_own = 3.0 * rms_own * lax.dynamic_slice_in_dim(small, hp * rows, rows, 0)[:, None]

    def reduced(blocks):
        blocks = jnp.stack(blocks)
        j = [picked(blocks, slot(i ^ hp)) for i in range(4)]
        came = swapped(jnp.stack([j[1], j[3]]).astype(BF16), "pair").astype(F32)
        half = (j[2] + came[1]).astype(BF16)
        return j[0] + came[0] + swapped(half, "head").astype(F32)

    own = tile.astype(F32)
    layer_out = transposed((own + reduced(down)).astype(BF16))
    slope = gain * reduced(grad) / rms_own - own * inner_own / (D * rms_own * rms_own * rms_own)
    return layer_out, loss_value, transposed(slope.astype(BF16)).astype(F32)


def on_any(residual, norm_gain, weights, teacher_feats, keep_tiles):
    w_gate, w_up, _ = weights
    rows = residual.shape[0]
    d_ctx, ff = w_gate.shape
    tiles = keep_tiles.shape[1]
    n_ctx = lax.axis_size("ctx")
    z = lax.axis_index("ctx")
    hp = lax.axis_index(HP)
    keep_cols = jnp.pad(keep_tiles.astype(BF16), ((0, 0), (0, -tiles % 128)))
    marked = lax.all_gather(jnp.concatenate([teacher_feats, keep_cols], axis=1), "ctx", tiled=True)
    wide = lax.all_gather(residual, HP, axis=1, tiled=True)
    resid = lax.all_to_all(wide, "ctx", split_axis=1, concat_axis=0, tiled=True).astype(F32)
    gain = lax.dynamic_slice_in_dim(norm_gain, z * d_ctx, d_ctx, 0)
    rms = jnp.sqrt(lax.psum(jnp.sum(resid * resid, axis=1), "ctx") / D + 1e-05)
    scaled = (resid * gain).astype(BF16)
    inv = (1.0 / rms)[:, None]
    sums = [
        lax.psum(jnp.dot(scaled, w, preferred_element_type=F32).astype(BF16), "ctx").astype(F32) * inv
        for w in (w_gate, w_up)
    ]
    keep_cols = marked[:, ff : ff + tiles]
    down, grad, inner, loss = block_terms(sums[0], sums[1], marked[:, :ff], keep_cols, weights)
    count = jnp.sum(keep_cols.astype(F32)) * TILE
    small = lax.psum(jnp.concatenate([inner, loss[None], count[None]]), HP)
    loss_value = (small[-2] / small[-1]).reshape(1)

    def home(whole):
        routed = lax.all_to_all(whole.astype(BF16), "ctx", 0, 1, tiled=True)
        return lax.psum_scatter(routed, HP, scatter_dimension=1, tiled=True).astype(F32)

    own = residual.astype(F32)
    layer_out = (own + home(down)).astype(BF16)
    rms_own = lax.dynamic_slice_in_dim(rms, z * rows, rows, 0)[:, None]
    inner_own = 3.0 * rms_own * lax.dynamic_slice_in_dim(small, z * rows, rows, 0)[:, None]
    gain_own = lax.dynamic_slice_in_dim(norm_gain, hp * own.shape[1], own.shape[1], 0)
    slope = gain_own * home(grad) / rms_own - own * inner_own / (D * rms_own * rms_own * rms_own)
    return layer_out, loss_value, slope


def local(
    student_query,
    teacher_keys,
    teacher_values,
    band_span,
    residual_in,
    norm_gain,
    w_gate,
    w_up,
    w_down,
    teacher_feats,
    keep_tiles,
):
    attended = attention(student_query, teacher_keys, teacher_values, band_span)
    residual = (residual_in.astype(F32) + attended).astype(BF16)
    sizes = tuple(lax.axis_size(a) for a in ("ctx", "head", "pair"))
    finish = on_square if sizes == (4, 2, 2) else on_any
    return finish(residual, norm_gain, (w_gate, w_up, w_down), teacher_feats, keep_tiles)


def solution(mesh):
    rows = P(("groups", "ctx"), HP)
    in_specs = (
        rows, rows, rows, P(("groups", "ctx")), rows, P(),
        P("ctx", HP), P("ctx", HP), P(HP, "ctx"), rows, rows,
    )
    out_specs = (rows, P("groups"), rows)
    return jax.shard_map(local, mesh=mesh, in_specs=in_specs, out_specs=out_specs, check_vma=False)
```

time: 738 us -> 302 us (0.41)
  waiting for transfers between devices: 554 us -> 116 us
  starting transfers between devices: 34.5 us -> 100 us
  blocking collectives: 64.1 us -> 0 us
  matrix products: 49.4 us -> 22.7 us
  local copies, waits for them, and re-layouts: 6.06 us -> 27.2 us
  other arithmetic: 8.21 us -> 24.6 us
  between operations: 17.5 us -> 9.15 us
    all_gather x4 -> x0, waiting for transfers between devices: 531 us -> none  [the longest x1 254 us: local(): lax.all_gather(w_gate, 'ctx', axis=0, tiled=True)]
    ppermute x0 -> x13, waiting for transfers between devices: none -> 48.7 us  [the longest x3 30.1 us: transposed(): return lax.ppermute(block, ('ctx',) + HP, route)]
    ppermute x8 -> x27, starting transfers between devices: 34.1 us -> 80 us  [passed_along(): return lax.ppermute(block, axis, route)]
    ppermute x8 -> x27, waiting for transfers between devices: 21.8 us -> 67.5 us  [passed_along(): return lax.ppermute(block, axis, route)]
    psum x2 -> x0, blocking collectives: 36 us -> none  [the longest x1 27.3 us: local(): lax.psum((loss_part, count_part), ('ctx', 'head', 'pair'))]
    all_to_all x1 -> x0, blocking collectives: 28.1 us -> none  [local(): lax.all_to_all(local_part, 'ctx', split_axis=0, concat_axis=1, tiled=True)]
    dot_general x5 -> x16, matrix products: 43.7 us -> 21 us  [the longest x4 7.65 us: block_terms(): lax.dot_general(grad_gate, w_gate, contract, preferred_element_type=F32)]
    ppermute x0 -> x13, starting transfers between devices: none -> 20.4 us  [the longest x3 15.7 us: transposed(): return lax.ppermute(block, ('ctx',) + HP, route)]
  transfers between devices with their start and end apart: 14 -> 40, of which waited for: 12 -> 24; matrix products, arithmetic and copies ran while one was open for 5% -> 17% of each run, Pallas kernels for 0% -> 0%
where the time goes in v1:
time: 302 us; the launch traced here: 300 us
  waiting for transfers between devices  116 us (38%)
  starting transfers between devices  100 us (33%)
  local copies, waits for them, and re-layouts  27.2 us (9%)
  other arithmetic  24.6 us (8%)
  matrix products  22.7 us (8%)
  between operations  9.15 us (3%)
    ppermute x27, starting transfers between devices, passed_along(): return lax.ppermute(block, axis, route)  80 us
    ppermute x27, waiting for transfers between devices, passed_along(): return lax.ppermute(block, axis, route)  67.5 us
    ppermute x3, waiting for transfers between devices, transposed(): return lax.ppermute(block, ('ctx',) + HP, route)  30.1 us
    ppermute x10, waiting for transfers between devices, swapped(): return lax.ppermute(block, axis, [(0, 1), (1, 0)])  18.6 us
    ppermute x3, starting transfers between devices, transposed(): return lax.ppermute(block, ('ctx',) + HP, route)  15.7 us
    unnamed x40, local copies, waits for them, and re-layouts  14.1 us
    dynamic_slice x5, local copies, waits for them, and re-layouts, picked(): return lax.dynamic_index_in_dim(blocks, index, 0, keepdims=False)  9.99 us
    dot_general x4, matrix products, block_terms(): lax.dot_general(grad_gate, w_gate, contract, preferred_element_type=F32)  7.65 us
  transfers between devices with their start and end apart: 40, of which 24 were waited for; matrix products, arithmetic and copies ran while one was open for 17% of the time, Pallas kernels for 0%

profile of v1, /device:TPU:2, one launch (start us, length us, event | category | flops | bytes accessed | tf_op | source)
XLA Modules:
  0.0 300.4 jit_solution(13252534180419540515)
XLA Ops:
  1.5 5.5 %collective-permute-start.2 = (bf16[2,128,256]{2,1,0:T(8,128)(2,1)S(1)}, bf16[2,128,256]{2,1,0:T(8,128)(2,1)S(1)}, u32[]{:S(2)}, u32[]{:S(2)}) collective-permute-start(bf16[2,128,256]{2,1,0:T(8,128)(2,1)S(1)} %pad_maximum_fusion.8), channel_id=1, source_target_pairs={{0,12},{1,13},{2,14},{3,15},{16,28},{17,29},{18,30},{19,31}} | collective-permute-start | bytes 393224 | tf_op jit(solution)/shard_map/ppermute | solution.py:22
  8.3 2.5 collective-permute-start
  13.8 1.7 collective-permute-done
  19.5 8.0 %collective-permute-start.3 = (bf16[128,1024]{1,0:T(8,128)(2,1)S(1)}, bf16[128,1024]{1,0:T(8,128)(2,1)S(1)}, u32[]{:S(2)}, u32[]{:S(2)}) collective-permute-start(bf16[128,1024]{1,0:T(8,128)(2,1)S(1)} %get-tuple-element.40), channel_id=1, source_target_pairs={{0,0},{1,4},{2,8},{3,12},{4,1},{5,5},{6,9},{7,13},{8,2},{9,6},{10,... | collective-permute-start | bytes 786440 | tf_op jit(solution)/shard_map/ppermute | solution.py:32
  27.5 11.0 %collective-permute-done.3 = bf16[128,1024]{1,0:T(8,128)(2,1)S(1)} collective-permute-done((bf16[128,1024]{1,0:T(8,128)(2,1)S(1)}, bf16[128,1024]{1,0:T(8,128)(2,1)S(1)}, u32[]{:S(2)}, u32[]{:S(2)}) %collective-permute-start.3) | collective-permute-done | bytes 262176 | tf_op jit(solution)/shard_map/ppermute | solution.py:32
  40.6 2.0 collective-permute-start.19
  42.6 2.2 collective-permute-done.4
  45.3 1.6 collective-permute-start.21
  46.9 5.4 %collective-permute-start.20 = (bf16[128,1920]{0,1:T(8,128)(2,1)S(1)}, bf16[128,1920]{0,1:T(8,128)(2,1)}, u32[]{:S(2)}, u32[]{:S(2)}) collective-permute-start(bf16[128,1920]{0,1:T(8,128)(2,1)S(1)} %pad.4), channel_id=1, source_target_pairs={{0,4},{4,8},{8,12},{1,5},{5,9},{9,13},{2,6},{6,10},{10,14},{3,7},{... | collective-permute-start | bytes 1474568 | tf_op jit(solution)/shard_map/ppermute | solution.py:22
  52.7 2.1 convolution_convert_fusion
  54.8 2.1 convolution_convert_fusion.1
  56.9 2.0 constant_dynamic-slice_fusion.11
  59.0 2.0 copy.47
  65.1 2.0 copy.44
  67.1 5.3 %collective-permute-start.12 = (bf16[128,1792]{0,1:T(8,128)(2,1)}, bf16[128,1792]{0,1:T(8,128)(2,1)}, u32[]{:S(2)}, u32[]{:S(2)}) collective-permute-start(bf16[128,1792]{0,1:T(8,128)(2,1)} %bitcast.295), channel_id=1, source_target_pairs={{0,4},{4,8},{8,12},{1,5},{5,9},{9,13},{2,6},{6,10},{10,14},{3,7},{... | collective-permute-start | bytes 1376264 | tf_op jit(solution)/shard_map/ppermute | solution.py:22
  74.9 2.0 copy.40
  78.2 2.0 copy.63
  80.2 2.0 copy.62
  82.2 2.0 copy.37
  86.8 4.7 %collective-permute-start.6 = (bf16[128,1792]{0,1:T(8,128)(2,1)}, bf16[128,1792]{0,1:T(8,128)(2,1)S(1)}, u32[]{:S(2)}, u32[]{:S(2)}) collective-permute-start(bf16[128,1792]{0,1:T(8,128)(2,1)} %bitcast.296), channel_id=1, source_target_pairs={{0,4},{4,8},{8,12},{1,5},{5,9},{9,13},{2,6},{6,10},{10,14},{3,7},{... | collective-permute-start | bytes 1376264 | tf_op jit(solution)/shard_map/ppermute | solution.py:22
  95.5 4.6 %collective-permute-start.13 = (bf16[128,1792]{0,1:T(8,128)(2,1)S(1)}, bf16[128,1792]{0,1:T(8,128)(2,1)S(1)}, u32[]{:S(2)}, u32[]{:S(2)}) collective-permute-start(bf16[128,1792]{0,1:T(8,128)(2,1)S(1)} %fusion.17), channel_id=1, source_target_pairs={{0,4},{4,8},{8,12},{1,5},{5,9},{9,13},{2,6},{6,10},{10,14},{3,7},{... | collective-permute-start | bytes 1376264 | tf_op jit(solution)/shard_map/ppermute | solution.py:22
  104.3 4.9 %collective-permute-start.7 = (bf16[128,1792]{0,1:T(8,128)(2,1)S(1)}, bf16[128,1792]{0,1:T(8,128)(2,1)S(1)}, u32[]{:S(2)}, u32[]{:S(2)}) collective-permute-start(bf16[128,1792]{0,1:T(8,128)(2,1)S(1)} %fusion.23), channel_id=1, source_target_pairs={{0,4},{4,8},{8,12},{1,5},{5,9},{9,13},{2,6},{6,10},{10,14},{3,7},{... | collective-permute-start | bytes 1376264 | tf_op jit(solution)/shard_map/ppermute | solution.py:22
  109.2 3.9 %collective-permute-start.22 = (bf16[128,1920]{0,1:T(8,128)(2,1)}, bf16[128,1920]{0,1:T(8,128)(2,1)S(1)}, u32[]{:S(2)}, u32[]{:S(2)}) collective-permute-start(bf16[128,1920]{0,1:T(8,128)(2,1)} %collective-permute-done.20), channel_id=1, source_target_pairs={{0,4},{4,8},{8,12},{1,5},{5,9},{9,13},{2,6},{6,10},{10,14},{3,7},{... | collective-permute-start | bytes 1474568 | tf_op jit(solution)/shard_map/ppermute | solution.py:22
  116.0 2.2 collective-permute-done.10
  118.3 3.0 collective-permute-start.14
  123.6 9.2 %collective-permute-done.22 = bf16[128,1920]{0,1:T(8,128)(2,1)S(1)} collective-permute-done((bf16[128,1920]{0,1:T(8,128)(2,1)}, bf16[128,1920]{0,1:T(8,128)(2,1)S(1)}, u32[]{:S(2)}, u32[]{:S(2)}) %collective-permute-start.22) | collective-permute-done | bytes 491552 | tf_op jit(solution)/shard_map/ppermute | solution.py:22
  132.8 4.3 %collective-permute-start.8 = (bf16[128,1792]{0,1:T(8,128)(2,1)S(1)}, bf16[128,1792]{0,1:T(8,128)(2,1)S(1)}, u32[]{:S(2)}, u32[]{:S(2)}) collective-permute-start(bf16[128,1792]{0,1:T(8,128)(2,1)S(1)} %fusion.24), channel_id=1, source_target_pairs={{0,4},{4,8},{8,12},{1,5},{5,9},{9,13},{2,6},{6,10},{10,14},{3,7},{... | collective-permute-start | bytes 1376264 | tf_op jit(solution)/shard_map/ppermute | solution.py:22
  137.9 1.9 collective-permute-start.24
  142.8 6.3 %collective-permute-done.11 = bf16[128,1792]{0,1:T(8,128)(2,1)S(1)} collective-permute-done((bf16[128,1792]{0,1:T(8,128)(2,1)S(1)}, bf16[128,1792]{0,1:T(8,128)(2,1)S(1)}, u32[]{:S(2)}, u32[]{:S(2)}) %collective-permute-start.11) | collective-permute-done | bytes 458784 | tf_op jit(solution)/shard_map/ppermute | solution.py:22
  149.0 3.4 %collective-permute-done.8 = bf16[128,1792]{0,1:T(8,128)(2,1)S(1)} collective-permute-done((bf16[128,1792]{0,1:T(8,128)(2,1)S(1)}, bf16[128,1792]{0,1:T(8,128)(2,1)S(1)}, u32[]{:S(2)}, u32[]{:S(2)}) %collective-permute-start.8) | collective-permute-done | bytes 458784 | tf_op jit(solution)/shard_map/ppermute | solution.py:22
  152.7 8.4 %collective-permute-done.24 = bf16[128,1920]{0,1:T(8,128)(2,1)S(1)} collective-permute-done((bf16[128,1920]{0,1:T(8,128)(2,1)S(1)}, bf16[128,1920]{0,1:T(8,128)(2,1)S(1)}, u32[]{:S(2)}, u32[]{:S(2)}) %collective-permute-start.24) | collective-permute-done | bytes 491552 | tf_op jit(solution)/shard_map/ppermute | solution.py:22
  162.3 6.0 %collective-permute-start.27 = (bf16[128,3584]{0,1:T(8,128)(2,1)S(1)}, bf16[128,3584]{0,1:T(8,128)(2,1)}, u32[]{:S(2)}, u32[]{:S(2)}) collective-permute-start(bf16[128,3584]{0,1:T(8,128)(2,1)S(1)} %pad_maximum_fusion.3), channel_id=1, source_target_pairs={{0,4},{4,8},{8,12},{1,5},{5,9},{9,13},{2,6},{6,10},{10,14},{3,7},{... | collective-permute-start | bytes 2752520 | tf_op jit(solution)/shard_map/ppermute | solution.py:22
  171.1 13.2 %collective-permute-done.26 = bf16[128,3584]{0,1:T(8,128)(2,1)} collective-permute-done((bf16[128,3584]{0,1:T(8,128)(2,1)S(1)}, bf16[128,3584]{0,1:T(8,128)(2,1)}, u32[]{:S(2)}, u32[]{:S(2)}) %collective-permute-start.26) | collective-permute-done | bytes 917536 | tf_op jit(solution)/shard_map/ppermute | solution.py:22
  185.6 5.5 %collective-permute-start.29 = (bf16[128,3584]{0,1:T(8,128)(2,1)}, bf16[128,3584]{0,1:T(8,128)(2,1)}, u32[]{:S(2)}, u32[]{:S(2)}) collective-permute-start(bf16[128,3584]{0,1:T(8,128)(2,1)} %collective-permute-done.27), channel_id=1, source_target_pairs={{0,4},{4,8},{8,12},{1,5},{5,9},{9,13},{2,6},{6,10},{10,14},{3,7},{... | collective-permute-start | bytes 2752520 | tf_op jit(solution)/shard_map/ppermute | solution.py:22
  191.7 2.0 fusion.62
  196.3 3.7 %fusion.148 = f32[128,1024]{1,0:T(8,128)S(1)} fusion(bf16[128,1792]{0,1:T(8,128)(2,1)} %get-tuple-element.62, bf16[1024,1792]{1,0:T(8,128)(2,1)} %param.17), kind=kOutput, calls=%fused_computation.266 | convolution fusion | flops 469762048 | bytes 4653056 | tf_op jit(solution)/shard_map/dot_general | solution.py:111
  201.4 5.0 %collective-permute-done.28 = bf16[128,3584]{0,1:T(8,128)(2,1)} collective-permute-done((bf16[128,3584]{0,1:T(8,128)(2,1)}, bf16[128,3584]{0,1:T(8,128)(2,1)}, u32[]{:S(2)}, u32[]{:S(2)}) %collective-permute-start.28) | collective-permute-done | bytes 917536 | tf_op jit(solution)/shard_map/ppermute | solution.py:22
  211.3 5.3 %collective-permute-start.31 = (bf16[128,3584]{0,1:T(8,128)(2,1)}, bf16[128,3584]{0,1:T(8,128)(2,1)S(1)}, u32[]{:S(2)}, u32[]{:S(2)}) collective-permute-start(bf16[128,3584]{0,1:T(8,128)(2,1)} %collective-permute-done.29), channel_id=1, source_target_pairs={{0,4},{4,8},{8,12},{1,5},{5,9},{9,13},{2,6},{6,10},{10,14},{3,7},{... | collective-permute-start | bytes 2752520 | tf_op jit(solution)/shard_map/ppermute | solution.py:22
  220.2 11.5 %collective-permute-done.30 = bf16[128,3584]{0,1:T(8,128)(2,1)S(1)} collective-permute-done((bf16[128,3584]{0,1:T(8,128)(2,1)}, bf16[128,3584]{0,1:T(8,128)(2,1)S(1)}, u32[]{:S(2)}, u32[]{:S(2)}) %collective-permute-start.30) | collective-permute-done | bytes 917536 | tf_op jit(solution)/shard_map/ppermute | solution.py:22
  232.9 1.8 broadcast_select_fusion.1
  251.9 3.6 %collective-permute-done.36 = f32[640]{0:T(1024)S(1)} collective-permute-done((f32[640]{0:T(1024)S(1)}, f32[640]{0:T(1024)S(1)}, u32[]{:S(2)}, u32[]{:S(2)}) %collective-permute-start.36) | collective-permute-done | bytes 2592 | tf_op jit(solution)/shard_map/ppermute | solution.py:26
  256.0 2.1 collective-permute-start.33
  258.2 6.8 %collective-permute-done.38 = bf16[128,1024]{1,0:T(8,128)(2,1)S(1)} collective-permute-done((bf16[128,1024]{1,0:T(8,128)(2,1)S(1)}, bf16[128,1024]{1,0:T(8,128)(2,1)S(1)}, u32[]{:S(2)}, u32[]{:S(2)}) %collective-permute-start.38) | collective-permute-done | bytes 262176 | tf_op jit(solution)/shard_map/ppermute | solution.py:26
  265.0 3.7 %collective-permute-done.33 = bf16[128,1024]{1,0:T(8,128)(2,1)S(1)} collective-permute-done((bf16[128,1024]{1,0:T(8,128)(2,1)S(1)}, bf16[128,1024]{1,0:T(8,128)(2,1)S(1)}, u32[]{:S(2)}, u32[]{:S(2)}) %collective-permute-start.33) | collective-permute-done | bytes 262176 | tf_op jit(solution)/shard_map/ppermute | solution.py:26
  269.0 5.4 %collective-permute-start.34 = (bf16[128,1024]{1,0:T(8,128)(2,1)S(1)}, bf16[128,1024]{1,0:T(8,128)(2,1)S(1)}, u32[]{:S(2)}, u32[]{:S(2)}) collective-permute-start(bf16[128,1024]{1,0:T(8,128)(2,1)S(1)} %get-tuple-element.76), channel_id=1, source_target_pairs={{0,0},{1,4},{2,8},{3,12},{4,1},{5,5},{6,9},{7,13},{8,2},{9,6},{10,... | collective-permute-start | bytes 786440 | tf_op jit(solution)/shard_map/ppermute | solution.py:32
  274.4 2.2 collective-permute-start.39
  278.5 13.5 %collective-permute-done.34 = bf16[128,1024]{1,0:T(8,128)(2,1)S(1)} collective-permute-done((bf16[128,1024]{1,0:T(8,128)(2,1)S(1)}, bf16[128,1024]{1,0:T(8,128)(2,1)S(1)}, u32[]{:S(2)}, u32[]{:S(2)}) %collective-permute-start.34) | collective-permute-done | bytes 262176 | tf_op jit(solution)/shard_map/ppermute | solution.py:32
  292.1 5.6 %collective-permute-done.39 = bf16[128,1024]{1,0:T(8,128)(2,1)S(1)} collective-permute-done((bf16[128,1024]{1,0:T(8,128)(2,1)S(1)}, bf16[128,1024]{1,0:T(8,128)(2,1)S(1)}, u32[]{:S(2)}, u32[]{:S(2)}) %collective-permute-start.39) | collective-permute-done | bytes 262176 | tf_op jit(solution)/shard_map/ppermute | solution.py:32
  (177 shorter events, 74.3 us)
Async XLA Ops:
  1.5 11.6 %collective-permute-start.2 = (bf16[2,128,256]{2,1,0:T(8,128)(2,1)S(1)}, bf16[2,128,256]{2,1,0:T(8,128)(2,1)S(1)}, u32[]{:S(2)}, u32[]{:S(2)}) collective-permute-start(bf16[2,128,256]{2,1,0:T(8,128)(2,1)S(1)} %pad_maximum_fusion.8), channel_id=1, source_target_pairs={{0,12},{1,13},{2,14},{3,15},{16,28},{17,29},{18,30},{19,31}} | collective-permute-start | bytes 393224 | tf_op jit(solution)/shard_map/ppermute | solution.py:22
  7.0 6.7 %collective-permute-start.1 = (bf16[2,128,256]{2,1,0:T(8,128)(2,1)S(1)}, bf16[2,128,256]{2,1,0:T(8,128)(2,1)S(1)}, u32[]{:S(2)}, u32[]{:S(2)}) collective-permute-start(bf16[2,128,256]{2,1,0:T(8,128)(2,1)S(1)} %pad_maximum_fusion.8), channel_id=1, source_target_pairs={{0,8},{4,12},{1,9},{5,13},{2,10},{6,14},{3,11},{7,15},{16,24},{20,... | collective-permute-start | bytes 393224 | tf_op jit(solution)/shard_map/ppermute | solution.py:22
  8.3 7.1 %collective-permute-start = (bf16[2,128,256]{2,1,0:T(8,128)(2,1)S(1)}, bf16[2,128,256]{2,1,0:T(8,128)(2,1)S(1)}, u32[]{:S(2)}, u32[]{:S(2)}) collective-permute-start(bf16[2,128,256]{2,1,0:T(8,128)(2,1)S(1)} %pad_maximum_fusion.8), channel_id=1, source_target_pairs={{0,4},{4,8},{8,12},{1,5},{5,9},{9,13},{2,6},{6,10},{10,14},{3,7},{... | collective-permute-start | bytes 393224 | tf_op jit(solution)/shard_map/ppermute | solution.py:22
  18.4 20.1 %copy-start.10 = (bf16[128,1792]{1,0:T(8,128)(2,1)S(1)}, bf16[128,1792]{1,0:T(8,128)(2,1)}, u32[]{:S(2)}) copy-start(bf16[128,1792]{1,0:T(8,128)(2,1)} %param.20) | copy-start | bytes 1376260
  18.5 20.2 %copy-start.12 = (s32[128,14]{0,1:T(8,128)S(1)}, s32[128,14]{0,1:T(8,128)}, u32[]{:S(2)}) copy-start(s32[128,14]{0,1:T(8,128)} %param.21) | copy-start | bytes 21508
  19.5 19.0 %collective-permute-start.3 = (bf16[128,1024]{1,0:T(8,128)(2,1)S(1)}, bf16[128,1024]{1,0:T(8,128)(2,1)S(1)}, u32[]{:S(2)}, u32[]{:S(2)}) collective-permute-start(bf16[128,1024]{1,0:T(8,128)(2,1)S(1)} %get-tuple-element.40), channel_id=1, source_target_pairs={{0,0},{1,4},{2,8},{3,12},{4,1},{5,5},{6,9},{7,13},{8,2},{9,6},{10,... | collective-permute-start | bytes 786440 | tf_op jit(solution)/shard_map/ppermute | solution.py:32
  38.5 6.4 %collective-permute-start.4 = (bf16[128,1024]{1,0:T(8,128)(2,1)S(1)}, bf16[128,1024]{1,0:T(8,128)(2,1)S(1)}, u32[]{:S(2)}, u32[]{:S(2)}) collective-permute-start(bf16[128,1024]{1,0:T(8,128)(2,1)S(1)} %collective-permute-done.3), channel_id=1, source_target_pairs={{0,2},{2,0},{1,3},{3,1},{4,6},{6,4},{5,7},{7,5},{8,10},{10,8},{9,1... | collective-permute-start | bytes 786440 | tf_op jit(solution)/shard_map/ppermute | solution.py:26
  39.4 1.2 collective-permute-start.18
  40.6 4.4 %collective-permute-start.19 = (f32[128]{0:T(128)S(1)}, f32[128]{0:T(128)S(1)}, u32[]{:S(2)}, u32[]{:S(2)}) collective-permute-start(f32[128]{0:T(128)S(1)} %add.386), channel_id=1, source_target_pairs={{0,2},{2,0},{1,3},{3,1},{4,6},{6,4},{5,7},{7,5},{8,10},{10,8},{9,1... | collective-permute-start | bytes 1544 | tf_op jit(solution)/shard_map/ppermute | solution.py:26
  44.9 7.3 %collective-permute-start.5 = (bf16[2,128,1024]{2,1,0:T(8,128)(2,1)S(1)}, bf16[2,128,1024]{2,1,0:T(8,128)(2,1)S(1)}, u32[]{:S(2)}, u32[]{:S(2)}) collective-permute-start(bf16[2,128,1024]{2,1,0:T(8,128)(2,1)S(1)} %pad_maximum_fusion.5), channel_id=1, source_target_pairs={{0,1},{1,0},{2,3},{3,2},{4,5},{5,4},{6,7},{7,6},{8,9},{9,8},{10,11... | collective-permute-start | bytes 1572872 | tf_op jit(solution)/shard_map/ppermute | solution.py:26
  45.3 7.5 %copy-start = (bf16[1024,1792]{1,0:T(8,128)(2,1)S(1)}, bf16[1024,1792]{1,0:T(8,128)(2,1)}, u32[]{:S(2)}) copy-start(bf16[1024,1792]{1,0:T(8,128)(2,1)} %param.18) | copy-start | bytes 11010052
  45.3 59.0 %collective-permute-start.21 = (bf16[128,1920]{0,1:T(8,128)(2,1)S(1)}, bf16[128,1920]{0,1:T(8,128)(2,1)}, u32[]{:S(2)}, u32[]{:S(2)}) collective-permute-start(bf16[128,1920]{0,1:T(8,128)(2,1)S(1)} %pad.4), channel_id=1, source_target_pairs={{4,0},{8,4},{12,8},{5,1},{9,5},{13,9},{6,2},{10,6},{14,10},{7,3},{... | collective-permute-start | bytes 1474568 | tf_op jit(solution)/shard_map/ppermute | solution.py:22
  46.9 62.4 %collective-permute-start.20 = (bf16[128,1920]{0,1:T(8,128)(2,1)S(1)}, bf16[128,1920]{0,1:T(8,128)(2,1)}, u32[]{:S(2)}, u32[]{:S(2)}) collective-permute-start(bf16[128,1920]{0,1:T(8,128)(2,1)S(1)} %pad.4), channel_id=1, source_target_pairs={{0,4},{4,8},{8,12},{1,5},{5,9},{9,13},{2,6},{6,10},{10,14},{3,7},{... | collective-permute-start | bytes 1474568 | tf_op jit(solution)/shard_map/ppermute | solution.py:22
  61.0 25.8 %collective-permute-start.15 = (bf16[128,1792]{0,1:T(8,128)(2,1)}, bf16[128,1792]{0,1:T(8,128)(2,1)}, u32[]{:S(2)}, u32[]{:S(2)}) collective-permute-start(bf16[128,1792]{0,1:T(8,128)(2,1)} %bitcast.294), channel_id=1, source_target_pairs={{4,0},{8,4},{12,8},{5,1},{9,5},{13,9},{6,2},{10,6},{14,10},{7,3},{... | collective-permute-start | bytes 1376264 | tf_op jit(solution)/shard_map/ppermute | solution.py:22
  67.1 25.7 %collective-permute-start.12 = (bf16[128,1792]{0,1:T(8,128)(2,1)}, bf16[128,1792]{0,1:T(8,128)(2,1)}, u32[]{:S(2)}, u32[]{:S(2)}) collective-permute-start(bf16[128,1792]{0,1:T(8,128)(2,1)} %bitcast.295), channel_id=1, source_target_pairs={{0,4},{4,8},{8,12},{1,5},{5,9},{9,13},{2,6},{6,10},{10,14},{3,7},{... | collective-permute-start | bytes 1376264 | tf_op jit(solution)/shard_map/ppermute | solution.py:22
  76.9 18.5 %collective-permute-start.9 = (bf16[128,1792]{0,1:T(8,128)(2,1)}, bf16[128,1792]{0,1:T(8,128)(2,1)}, u32[]{:S(2)}, u32[]{:S(2)}) collective-permute-start(bf16[128,1792]{0,1:T(8,128)(2,1)} %bitcast.297), channel_id=1, source_target_pairs={{4,0},{8,4},{12,8},{5,1},{9,5},{13,9},{6,2},{10,6},{14,10},{7,3},{... | collective-permute-start | bytes 1376264 | tf_op jit(solution)/shard_map/ppermute | solution.py:22
  86.7 17.4 %copy-start.9 = (bf16[1,128,1792]{1,2,0:T(8,128)(2,1)S(1)}, bf16[1,128,1792]{1,2,0:T(8,128)(2,1)}, u32[]{:S(2)}) copy-start(bf16[1,128,1792]{1,2,0:T(8,128)(2,1)} %copy.61) | copy-start | bytes 1376260
  86.8 15.9 %collective-permute-start.6 = (bf16[128,1792]{0,1:T(8,128)(2,1)}, bf16[128,1792]{0,1:T(8,128)(2,1)S(1)}, u32[]{:S(2)}, u32[]{:S(2)}) collective-permute-start(bf16[128,1792]{0,1:T(8,128)(2,1)} %bitcast.296), channel_id=1, source_target_pairs={{0,4},{4,8},{8,12},{1,5},{5,9},{9,13},{2,6},{6,10},{10,14},{3,7},{... | collective-permute-start | bytes 1376264 | tf_op jit(solution)/shard_map/ppermute | solution.py:22
  92.8 28.5 %copy-start.8 = (bf16[1,128,1792]{1,2,0:T(8,128)(2,1)S(1)}, bf16[1,128,1792]{1,2,0:T(8,128)(2,1)}, u32[]{:S(2)}) copy-start(bf16[1,128,1792]{1,2,0:T(8,128)(2,1)} %copy.62) | copy-start | bytes 1376260
  92.8 20.4 %collective-permute-start.16 = (bf16[128,1792]{0,1:T(8,128)(2,1)S(1)}, bf16[128,1792]{0,1:T(8,128)(2,1)S(1)}, u32[]{:S(2)}, u32[]{:S(2)}) collective-permute-start(bf16[128,1792]{0,1:T(8,128)(2,1)S(1)} %fusion.15), channel_id=1, source_target_pairs={{4,0},{8,4},{12,8},{5,1},{9,5},{13,9},{6,2},{10,6},{14,10},{7,3},{... | collective-permute-start | bytes 1376264 | tf_op jit(solution)/shard_map/ppermute | solution.py:22
  95.5 19.1 %collective-permute-start.13 = (bf16[128,1792]{0,1:T(8,128)(2,1)S(1)}, bf16[128,1792]{0,1:T(8,128)(2,1)S(1)}, u32[]{:S(2)}, u32[]{:S(2)}) collective-permute-start(bf16[128,1792]{0,1:T(8,128)(2,1)S(1)} %fusion.17), channel_id=1, source_target_pairs={{0,4},{4,8},{8,12},{1,5},{5,9},{9,13},{2,6},{6,10},{10,14},{3,7},{... | collective-permute-start | bytes 1376264 | tf_op jit(solution)/shard_map/ppermute | solution.py:22
  102.7 15.6 %collective-permute-start.10 = (bf16[128,1792]{0,1:T(8,128)(2,1)S(1)}, bf16[128,1792]{0,1:T(8,128)(2,1)S(1)}, u32[]{:S(2)}, u32[]{:S(2)}) collective-permute-start(bf16[128,1792]{0,1:T(8,128)(2,1)S(1)} %fusion.21), channel_id=1, source_target_pairs={{4,0},{8,4},{12,8},{5,1},{9,5},{13,9},{6,2},{10,6},{14,10},{7,3},{... | collective-permute-start | bytes 1376264 | tf_op jit(solution)/shard_map/ppermute | solution.py:22
  104.3 17.9 %collective-permute-start.7 = (bf16[128,1792]{0,1:T(8,128)(2,1)S(1)}, bf16[128,1792]{0,1:T(8,128)(2,1)S(1)}, u32[]{:S(2)}, u32[]{:S(2)}) collective-permute-start(bf16[128,1792]{0,1:T(8,128)(2,1)S(1)} %fusion.23), channel_id=1, source_target_pairs={{0,4},{4,8},{8,12},{1,5},{5,9},{9,13},{2,6},{6,10},{10,14},{3,7},{... | collective-permute-start | bytes 1376264 | tf_op jit(solution)/shard_map/ppermute | solution.py:22
  109.2 23.6 %collective-permute-start.22 = (bf16[128,1920]{0,1:T(8,128)(2,1)}, bf16[128,1920]{0,1:T(8,128)(2,1)S(1)}, u32[]{:S(2)}, u32[]{:S(2)}) collective-permute-start(bf16[128,1920]{0,1:T(8,128)(2,1)} %collective-permute-done.20), channel_id=1, source_target_pairs={{0,4},{4,8},{8,12},{1,5},{5,9},{9,13},{2,6},{6,10},{10,14},{3,7},{... | collective-permute-start | bytes 1474568 | tf_op jit(solution)/shard_map/ppermute | solution.py:22
  113.2 24.0 %collective-permute-start.23 = (bf16[128,1920]{0,1:T(8,128)(2,1)}, bf16[128,1920]{0,1:T(8,128)(2,1)S(1)}, u32[]{:S(2)}, u32[]{:S(2)}) collective-permute-start(bf16[128,1920]{0,1:T(8,128)(2,1)} %collective-permute-done.21), channel_id=1, source_target_pairs={{4,0},{8,4},{12,8},{5,1},{9,5},{13,9},{6,2},{10,6},{14,10},{7,3},{... | collective-permute-start | bytes 1474568 | tf_op jit(solution)/shard_map/ppermute | solution.py:22
  114.6 25.2 %collective-permute-start.17 = (bf16[128,1792]{0,1:T(8,128)(2,1)S(1)}, bf16[128,1792]{0,1:T(8,128)(2,1)S(1)}, u32[]{:S(2)}, u32[]{:S(2)}) collective-permute-start(bf16[128,1792]{0,1:T(8,128)(2,1)S(1)} %fusion.16), channel_id=1, source_target_pairs={{4,0},{8,4},{12,8},{5,1},{9,5},{13,9},{6,2},{10,6},{14,10},{7,3},{... | collective-permute-start | bytes 1376264 | tf_op jit(solution)/shard_map/ppermute | solution.py:22
  118.3 24.3 %collective-permute-start.14 = (bf16[128,1792]{0,1:T(8,128)(2,1)S(1)}, bf16[128,1792]{0,1:T(8,128)(2,1)S(1)}, u32[]{:S(2)}, u32[]{:S(2)}) collective-permute-start(bf16[128,1792]{0,1:T(8,128)(2,1)S(1)} %fusion.18), channel_id=1, source_target_pairs={{0,4},{4,8},{8,12},{1,5},{5,9},{9,13},{2,6},{6,10},{10,14},{3,7},{... | collective-permute-start | bytes 1376264 | tf_op jit(solution)/shard_map/ppermute | solution.py:22
  122.2 26.8 %collective-permute-start.11 = (bf16[128,1792]{0,1:T(8,128)(2,1)S(1)}, bf16[128,1792]{0,1:T(8,128)(2,1)S(1)}, u32[]{:S(2)}, u32[]{:S(2)}) collective-permute-start(bf16[128,1792]{0,1:T(8,128)(2,1)S(1)} %fusion.22), channel_id=1, source_target_pairs={{4,0},{8,4},{12,8},{5,1},{9,5},{13,9},{6,2},{10,6},{14,10},{7,3},{... | collective-permute-start | bytes 1376264 | tf_op jit(solution)/shard_map/ppermute | solution.py:22
  132.8 19.6 %collective-permute-start.8 = (bf16[128,1792]{0,1:T(8,128)(2,1)S(1)}, bf16[128,1792]{0,1:T(8,128)(2,1)S(1)}, u32[]{:S(2)}, u32[]{:S(2)}) collective-permute-start(bf16[128,1792]{0,1:T(8,128)(2,1)S(1)} %fusion.24), channel_id=1, source_target_pairs={{0,4},{4,8},{8,12},{1,5},{5,9},{9,13},{2,6},{6,10},{10,14},{3,7},{... | collective-permute-start | bytes 1376264 | tf_op jit(solution)/shard_map/ppermute | solution.py:22
  137.9 23.2 %collective-permute-start.24 = (bf16[128,1920]{0,1:T(8,128)(2,1)S(1)}, bf16[128,1920]{0,1:T(8,128)(2,1)S(1)}, u32[]{:S(2)}, u32[]{:S(2)}) collective-permute-start(bf16[128,1920]{0,1:T(8,128)(2,1)S(1)} %collective-permute-done.22), channel_id=1, source_target_pairs={{0,4},{4,8},{8,12},{1,5},{5,9},{9,13},{2,6},{6,10},{10,14},{3,7},{... | collective-permute-start | bytes 1474568 | tf_op jit(solution)/shard_map/ppermute | solution.py:22
  139.8 21.2 %collective-permute-start.25 = (bf16[128,1920]{0,1:T(8,128)(2,1)S(1)}, bf16[128,1920]{0,1:T(8,128)(2,1)S(1)}, u32[]{:S(2)}, u32[]{:S(2)}) collective-permute-start(bf16[128,1920]{0,1:T(8,128)(2,1)S(1)} %collective-permute-done.23), channel_id=1, source_target_pairs={{4,0},{8,4},{12,8},{5,1},{9,5},{13,9},{6,2},{10,6},{14,10},{7,3},{... | collective-permute-start | bytes 1474568 | tf_op jit(solution)/shard_map/ppermute | solution.py:22
  142.8 27.5 %copy-start.2 = (bf16[1792,1024]{1,0:T(8,128)(2,1)S(1)}, bf16[1792,1024]{1,0:T(8,128)(2,1)}, u32[]{:S(2)}) copy-start(bf16[1792,1024]{1,0:T(8,128)(2,1)} %param.19) | copy-start | bytes 11010052
  161.1 23.2 %collective-permute-start.26 = (bf16[128,3584]{0,1:T(8,128)(2,1)S(1)}, bf16[128,3584]{0,1:T(8,128)(2,1)}, u32[]{:S(2)}, u32[]{:S(2)}) collective-permute-start(bf16[128,3584]{0,1:T(8,128)(2,1)S(1)} %pad_maximum_fusion.3), channel_id=1, source_target_pairs={{4,0},{8,4},{12,8},{5,1},{9,5},{13,9},{6,2},{10,6},{14,10},{7,3},{... | collective-permute-start | bytes 2752520 | tf_op jit(solution)/shard_map/ppermute | solution.py:22
  162.3 23.2 %collective-permute-start.27 = (bf16[128,3584]{0,1:T(8,128)(2,1)S(1)}, bf16[128,3584]{0,1:T(8,128)(2,1)}, u32[]{:S(2)}, u32[]{:S(2)}) collective-permute-start(bf16[128,3584]{0,1:T(8,128)(2,1)S(1)} %pad_maximum_fusion.3), channel_id=1, source_target_pairs={{0,4},{4,8},{8,12},{1,5},{5,9},{9,13},{2,6},{6,10},{10,14},{3,7},{... | collective-permute-start | bytes 2752520 | tf_op jit(solution)/shard_map/ppermute | solution.py:22
  184.3 22.1 %collective-permute-start.28 = (bf16[128,3584]{0,1:T(8,128)(2,1)}, bf16[128,3584]{0,1:T(8,128)(2,1)}, u32[]{:S(2)}, u32[]{:S(2)}) collective-permute-start(bf16[128,3584]{0,1:T(8,128)(2,1)} %collective-permute-done.26), channel_id=1, source_target_pairs={{4,0},{8,4},{12,8},{5,1},{9,5},{13,9},{6,2},{10,6},{14,10},{7,3},{... | collective-permute-start | bytes 2752520 | tf_op jit(solution)/shard_map/ppermute | solution.py:22
  185.6 22.0 %collective-permute-start.29 = (bf16[128,3584]{0,1:T(8,128)(2,1)}, bf16[128,3584]{0,1:T(8,128)(2,1)}, u32[]{:S(2)}, u32[]{:S(2)}) collective-permute-start(bf16[128,3584]{0,1:T(8,128)(2,1)} %collective-permute-done.27), channel_id=1, source_target_pairs={{0,4},{4,8},{8,12},{1,5},{5,9},{9,13},{2,6},{6,10},{10,14},{3,7},{... | collective-permute-start | bytes 2752520 | tf_op jit(solution)/shard_map/ppermute | solution.py:22
  201.3 15.3 %copy-start.3 = (bf16[1792,1024]{1,0:T(8,128)(2,1)S(1)}, bf16[1792,1024]{1,0:T(8,128)(2,1)}, u32[]{:S(2)}) copy-start(bf16[1792,1024]{1,0:T(8,128)(2,1)} %param.19) | copy-start | bytes 11010052
  208.8 8.6 %copy-start.5 = (bf16[1024,1792]{1,0:T(8,128)(2,1)S(1)}, bf16[1024,1792]{1,0:T(8,128)(2,1)}, u32[]{:S(2)}) copy-start(bf16[1024,1792]{1,0:T(8,128)(2,1)} %param.17) | copy-start | bytes 11010052
  210.1 21.6 %collective-permute-start.30 = (bf16[128,3584]{0,1:T(8,128)(2,1)}, bf16[128,3584]{0,1:T(8,128)(2,1)S(1)}, u32[]{:S(2)}, u32[]{:S(2)}) collective-permute-start(bf16[128,3584]{0,1:T(8,128)(2,1)} %collective-permute-done.28), channel_id=1, source_target_pairs={{4,0},{8,4},{12,8},{5,1},{9,5},{13,9},{6,2},{10,6},{14,10},{7,3},{... | collective-permute-start | bytes 2752520 | tf_op jit(solution)/shard_map/ppermute | solution.py:22
  211.3 21.6 %collective-permute-start.31 = (bf16[128,3584]{0,1:T(8,128)(2,1)}, bf16[128,3584]{0,1:T(8,128)(2,1)S(1)}, u32[]{:S(2)}, u32[]{:S(2)}) collective-permute-start(bf16[128,3584]{0,1:T(8,128)(2,1)} %collective-permute-done.29), channel_id=1, source_target_pairs={{0,4},{4,8},{8,12},{1,5},{5,9},{9,13},{2,6},{6,10},{10,14},{3,7},{... | collective-permute-start | bytes 2752520 | tf_op jit(solution)/shard_map/ppermute | solution.py:22
  245.2 10.3 %collective-permute-start.37 = (bf16[2,128,1024]{2,1,0:T(8,128)(2,1)}, bf16[2,128,1024]{2,1,0:T(8,128)(2,1)S(1)}, u32[]{:S(2)}, u32[]{:S(2)}) collective-permute-start(bf16[2,128,1024]{2,1,0:T(8,128)(2,1)} %pad_maximum_fusion.7), channel_id=1, source_target_pairs={{0,1},{1,0},{2,3},{3,2},{4,5},{5,4},{6,7},{7,6},{8,9},{9,8},{10,11... | collective-permute-start | bytes 1572872 | tf_op jit(solution)/shard_map/ppermute | solution.py:26
  247.7 8.1 %collective-permute-start.32 = (bf16[2,128,1024]{2,1,0:T(8,128)(2,1)}, bf16[2,128,1024]{2,1,0:T(8,128)(2,1)S(1)}, u32[]{:S(2)}, u32[]{:S(2)}) collective-permute-start(bf16[2,128,1024]{2,1,0:T(8,128)(2,1)} %pad_maximum_fusion.6), channel_id=1, source_target_pairs={{0,1},{1,0},{2,3},{3,2},{4,5},{5,4},{6,7},{7,6},{8,9},{9,8},{10,11... | collective-permute-start | bytes 1572872 | tf_op jit(solution)/shard_map/ppermute | solution.py:26
  250.7 1.2 collective-permute-start.35
  251.9 3.6 %collective-permute-start.36 = (f32[640]{0:T(1024)S(1)}, f32[640]{0:T(1024)S(1)}, u32[]{:S(2)}, u32[]{:S(2)}) collective-permute-start(f32[640]{0:T(1024)S(1)} %add.417), channel_id=1, source_target_pairs={{0,2},{2,0},{1,3},{3,1},{4,6},{6,4},{5,7},{7,5},{8,10},{10,8},{9,1... | collective-permute-start | bytes 7688 | tf_op jit(solution)/shard_map/ppermute | solution.py:26
  255.7 9.2 %collective-permute-start.38 = (bf16[128,1024]{1,0:T(8,128)(2,1)S(1)}, bf16[128,1024]{1,0:T(8,128)(2,1)S(1)}, u32[]{:S(2)}, u32[]{:S(2)}) collective-permute-start(bf16[128,1024]{1,0:T(8,128)(2,1)S(1)} %fusion.107), channel_id=1, source_target_pairs={{0,2},{2,0},{1,3},{3,1},{4,6},{6,4},{5,7},{7,5},{8,10},{10,8},{9,1... | collective-permute-start | bytes 786440 | tf_op jit(solution)/shard_map/ppermute | solution.py:26
  256.0 12.6 %collective-permute-start.33 = (bf16[128,1024]{1,0:T(8,128)(2,1)S(1)}, bf16[128,1024]{1,0:T(8,128)(2,1)S(1)}, u32[]{:S(2)}, u32[]{:S(2)}) collective-permute-start(bf16[128,1024]{1,0:T(8,128)(2,1)S(1)} %fusion.106), channel_id=1, source_target_pairs={{0,2},{2,0},{1,3},{3,1},{4,6},{6,4},{5,7},{7,5},{8,10},{10,8},{9,1... | collective-permute-start | bytes 786440 | tf_op jit(solution)/shard_map/ppermute | solution.py:26
  269.0 23.1 %collective-permute-start.34 = (bf16[128,1024]{1,0:T(8,128)(2,1)S(1)}, bf16[128,1024]{1,0:T(8,128)(2,1)S(1)}, u32[]{:S(2)}, u32[]{:S(2)}) collective-permute-start(bf16[128,1024]{1,0:T(8,128)(2,1)S(1)} %get-tuple-element.76), channel_id=1, source_target_pairs={{0,0},{1,4},{2,8},{3,12},{4,1},{5,5},{6,9},{7,13},{8,2},{9,6},{10,... | collective-permute-start | bytes 786440 | tf_op jit(solution)/shard_map/ppermute | solution.py:32
  274.4 23.3 %collective-permute-start.39 = (bf16[128,1024]{1,0:T(8,128)(2,1)S(1)}, bf16[128,1024]{1,0:T(8,128)(2,1)S(1)}, u32[]{:S(2)}, u32[]{:S(2)}) collective-permute-start(bf16[128,1024]{1,0:T(8,128)(2,1)S(1)} %get-tuple-element.75), channel_id=1, source_target_pairs={{0,0},{1,4},{2,8},{3,12},{4,1},{5,5},{6,9},{7,13},{8,2},{9,6},{10,... | collective-permute-start | bytes 786440 | tf_op jit(solution)/shard_map/ppermute | solution.py:32
  (5 other events, 13.3 us)

commit v2 on v1

--- a/solution.py
+++ b/solution.py
@@ -3,6 +3,7 @@
 import jax
 import jax.numpy as jnp
 from jax import lax
+from jax.experimental.layout import Layout, with_layout_constraint
 from jax.sharding import PartitionSpec as P
 
 D = 4096
@@ -75,8 +76,12 @@
     return jnp.concatenate(outputs, axis=1)
 
 
+def row_major(block):
+    return with_layout_constraint(block, Layout(major_to_minor=tuple(range(block.ndim))))
+
+
 def shifted(block, distance):
-    return passed_along(block, "ctx", distance)
+    return row_major(passed_along(row_major(block), "ctx", distance))
 
 
 def picked(blocks, index):

time: 302 us -> 294 us (0.974)
  local copies, waits for them, and re-layouts: 27.2 us -> 17.2 us
  other arithmetic: 24.6 us -> 31.1 us
  waiting for transfers between devices: 116 us -> 112 us
    unnamed x40 -> x57, local copies, waits for them, and re-layouts: 14.1 us -> 3.63 us
    dynamic_slice x5 -> x0, local copies, waits for them, and re-layouts: 9.99 us -> none  [picked(): return lax.dynamic_index_in_dim(blocks, index, 0, keepdims=False)]
    reshape x0 -> x4, local copies, waits for them, and re-layouts: none -> 6.42 us  [block_terms(): jnp.broadcast_to(keep_cols.astype(F32)[:, :, None], (rows, tiles, TILE))]
  transfers between devices with their start and end apart: 40 -> 40, of which waited for: 24 -> 20; matrix products, arithmetic and copies ran while one was open for 17% -> 17% of each run, Pallas kernels for 0% -> 0%
where the time goes in v2:
time: 294 us; the launch traced here: 292 us
  waiting for transfers between devices  112 us (38%)
  starting transfers between devices  99 us (34%)
  other arithmetic  31.1 us (11%)
  matrix products  23.4 us (8%)
  local copies, waits for them, and re-layouts  17.2 us (6%)
  between operations  9.28 us (3%)
    ppermute x27, starting transfers between devices, passed_along(): return lax.ppermute(block, axis, route)  80.6 us
    ppermute x27, waiting for transfers between devices, passed_along(): return lax.ppermute(block, axis, route)  67.9 us
    ppermute x3, waiting for transfers between devices, transposed(): return lax.ppermute(block, ('ctx',) + HP, route)  28.6 us
    ppermute x3, starting transfers between devices, transposed(): return lax.ppermute(block, ('ctx',) + HP, route)  15.7 us
    ppermute x10, waiting for transfers between devices, swapped(): return lax.ppermute(block, axis, [(0, 1), (1, 0)])  15.6 us
    dot_general x4, matrix products, block_terms(): lax.dot_general(grad_gate, w_gate, contract, preferred_element_type=F32)  7.38 us
    reshape x4, local copies, waits for them, and re-layouts, block_terms(): jnp.broadcast_to(keep_cols.astype(F32)[:, :, None], (rows, tiles, TILE))  6.42 us
  transfers between devices with their start and end apart: 40, of which 20 were waited for; matrix products, arithmetic and copies ran while one was open for 17% of the time, Pallas kernels for 0%

profile of v2, /device:TPU:2, one launch (start us, length us, event | category | flops | bytes accessed | tf_op | source)
XLA Modules:
  0.0 292.1 jit_solution(2594821361359248123)
XLA Ops:
  1.5 5.5 %collective-permute-start.2 = (bf16[2,128,256]{2,1,0:T(8,128)(2,1)S(1)}, bf16[2,128,256]{2,1,0:T(8,128)(2,1)S(1)}, u32[]{:S(2)}, u32[]{:S(2)}) collective-permute-start(bf16[2,128,256]{2,1,0:T(8,128)(2,1)S(1)} %pad_maximum_fusion.8), channel_id=1, source_target_pairs={{0,12},{1,13},{2,14},{3,15},{16,28},{17,29},{18,30},{19,31}} | collective-permute-start | bytes 393224 | tf_op jit(solution)/shard_map/ppermute | solution.py:23
  8.3 2.5 collective-permute-start
  13.8 1.7 collective-permute-done
  19.5 8.0 %collective-permute-start.3 = (bf16[128,1024]{1,0:T(8,128)(2,1)S(1)}, bf16[128,1024]{1,0:T(8,128)(2,1)S(1)}, u32[]{:S(2)}, u32[]{:S(2)}) collective-permute-start(bf16[128,1024]{1,0:T(8,128)(2,1)S(1)} %get-tuple-element.44), channel_id=1, source_target_pairs={{0,0},{1,4},{2,8},{3,12},{4,1},{5,5},{6,9},{7,13},{8,2},{9,6},{10,... | collective-permute-start | bytes 786440 | tf_op jit(solution)/shard_map/ppermute | solution.py:33
  29.0 9.5 %collective-permute-done.3 = bf16[128,1024]{1,0:T(8,128)(2,1)S(1)} collective-permute-done((bf16[128,1024]{1,0:T(8,128)(2,1)S(1)}, bf16[128,1024]{1,0:T(8,128)(2,1)S(1)}, u32[]{:S(2)}, u32[]{:S(2)}) %collective-permute-start.3) | collective-permute-done | bytes 262176 | tf_op jit(solution)/shard_map/ppermute | solution.py:33
  40.6 5.4 %collective-permute-start.20 = (bf16[128,1920]{1,0:T(8,128)(2,1)S(1)}, bf16[128,1920]{1,0:T(8,128)(2,1)}, u32[]{:S(2)}, u32[]{:S(2)}) collective-permute-start(bf16[128,1920]{1,0:T(8,128)(2,1)S(1)} %pad.4), channel_id=1, source_target_pairs={{0,4},{4,8},{8,12},{1,5},{5,9},{9,13},{2,6},{6,10},{10,14},{3,7},{... | collective-permute-start | bytes 1474568 | tf_op jit(solution)/shard_map/ppermute | solution.py:23
  49.5 2.1 convolution_convert_fusion
  51.7 1.7 collective-permute-start.12
  54.7 2.1 convolution_convert_fusion.1
  56.9 4.7 %collective-permute-start.6 = (bf16[128,1792]{1,0:T(8,128)(2,1)S(1)}, bf16[128,1792]{1,0:T(8,128)(2,1)S(1)}, u32[]{:S(2)}, u32[]{:S(2)}) collective-permute-start(bf16[128,1792]{1,0:T(8,128)(2,1)S(1)} %get-tuple-element.53), channel_id=1, source_target_pairs={{0,4},{4,8},{8,12},{1,5},{5,9},{9,13},{2,6},{6,10},{10,14},{3,7},{... | collective-permute-start | bytes 1376264 | tf_op jit(solution)/shard_map/ppermute | solution.py:23
  61.6 2.7 collective-permute-done.12
  65.7 7.9 %collective-permute-done.6 = bf16[128,1792]{1,0:T(8,128)(2,1)S(1)} collective-permute-done((bf16[128,1792]{1,0:T(8,128)(2,1)S(1)}, bf16[128,1792]{1,0:T(8,128)(2,1)S(1)}, u32[]{:S(2)}, u32[]{:S(2)}) %collective-permute-start.6) | collective-permute-done | bytes 458784 | tf_op jit(solution)/shard_map/ppermute | solution.py:23
  73.6 4.4 %collective-permute-start.13 = (bf16[128,1792]{1,0:T(8,128)(2,1)S(1)}, bf16[128,1792]{1,0:T(8,128)(2,1)S(1)}, u32[]{:S(2)}, u32[]{:S(2)}) collective-permute-start(bf16[128,1792]{1,0:T(8,128)(2,1)S(1)} %fusion.17), channel_id=1, source_target_pairs={{0,4},{4,8},{8,12},{1,5},{5,9},{9,13},{2,6},{6,10},{10,14},{3,7},{... | collective-permute-start | bytes 1376264 | tf_op jit(solution)/shard_map/ppermute | solution.py:23
  78.1 4.2 %collective-permute-start.7 = (bf16[128,1792]{1,0:T(8,128)(2,1)S(1)}, bf16[128,1792]{1,0:T(8,128)(2,1)S(1)}, u32[]{:S(2)}, u32[]{:S(2)}) collective-permute-start(bf16[128,1792]{1,0:T(8,128)(2,1)S(1)} %fusion.23), channel_id=1, source_target_pairs={{0,4},{4,8},{8,12},{1,5},{5,9},{9,13},{2,6},{6,10},{10,14},{3,7},{... | collective-permute-start | bytes 1376264 | tf_op jit(solution)/shard_map/ppermute | solution.py:23
  82.4 4.0 %collective-permute-start.22 = (bf16[128,1920]{1,0:T(8,128)(2,1)}, bf16[128,1920]{1,0:T(8,128)(2,1)}, u32[]{:S(2)}, u32[]{:S(2)}) collective-permute-start(bf16[128,1920]{1,0:T(8,128)(2,1)} %collective-permute-done.20), channel_id=1, source_target_pairs={{0,4},{4,8},{8,12},{1,5},{5,9},{9,13},{2,6},{6,10},{10,14},{3,7},{... | collective-permute-start | bytes 1474568 | tf_op jit(solution)/shard_map/ppermute | solution.py:23
  91.4 5.8 %collective-permute-start.14 = (bf16[128,1792]{1,0:T(8,128)(2,1)}, bf16[128,1792]{1,0:T(8,128)(2,1)}, u32[]{:S(2)}, u32[]{:S(2)}) collective-permute-start(bf16[128,1792]{1,0:T(8,128)(2,1)} %get-tuple-element.55), channel_id=1, source_target_pairs={{0,4},{4,8},{8,12},{1,5},{5,9},{9,13},{2,6},{6,10},{10,14},{3,7},{... | collective-permute-start | bytes 1376264 | tf_op jit(solution)/shard_map/ppermute | solution.py:23
  97.2 1.5 collective-permute-done.7
  101.2 8.2 %collective-permute-done.22 = bf16[128,1920]{1,0:T(8,128)(2,1)} collective-permute-done((bf16[128,1920]{1,0:T(8,128)(2,1)}, bf16[128,1920]{1,0:T(8,128)(2,1)}, u32[]{:S(2)}, u32[]{:S(2)}) %collective-permute-start.22) | collective-permute-done | bytes 491552 | tf_op jit(solution)/shard_map/ppermute | solution.py:23
  109.3 5.2 %collective-permute-start.8 = (bf16[128,1792]{1,0:T(8,128)(2,1)}, bf16[128,1792]{1,0:T(8,128)(2,1)}, u32[]{:S(2)}, u32[]{:S(2)}) collective-permute-start(bf16[128,1792]{1,0:T(8,128)(2,1)} %get-tuple-element.51), channel_id=1, source_target_pairs={{0,4},{4,8},{8,12},{1,5},{5,9},{9,13},{2,6},{6,10},{10,14},{3,7},{... | collective-permute-start | bytes 1376264 | tf_op jit(solution)/shard_map/ppermute | solution.py:23
  114.5 4.2 %collective-permute-start.24 = (bf16[128,1920]{1,0:T(8,128)(2,1)}, bf16[128,1920]{1,0:T(8,128)(2,1)}, u32[]{:S(2)}, u32[]{:S(2)}) collective-permute-start(bf16[128,1920]{1,0:T(8,128)(2,1)} %collective-permute-done.22), channel_id=1, source_target_pairs={{0,4},{4,8},{8,12},{1,5},{5,9},{9,13},{2,6},{6,10},{10,14},{3,7},{... | collective-permute-start | bytes 1474568 | tf_op jit(solution)/shard_map/ppermute | solution.py:23
  126.2 1.5 collective-permute-start.11
  127.7 19.5 %collective-permute-done.17 = bf16[128,1792]{1,0:T(8,128)(2,1)S(1)} collective-permute-done((bf16[128,1792]{1,0:T(8,128)(2,1)S(1)}, bf16[128,1792]{1,0:T(8,128)(2,1)S(1)}, u32[]{:S(2)}, u32[]{:S(2)}) %collective-permute-start.17) | collective-permute-done | bytes 458784 | tf_op jit(solution)/shard_map/ppermute | solution.py:23
  148.4 4.9 %collective-permute-done.11 = bf16[128,1792]{1,0:T(8,128)(2,1)S(1)} collective-permute-done((bf16[128,1792]{1,0:T(8,128)(2,1)S(1)}, bf16[128,1792]{1,0:T(8,128)(2,1)S(1)}, u32[]{:S(2)}, u32[]{:S(2)}) %collective-permute-start.11) | collective-permute-done | bytes 458784 | tf_op jit(solution)/shard_map/ppermute | solution.py:23
  154.8 1.6 collective-permute-start.26
  156.3 5.5 %collective-permute-start.27 = (bf16[128,3584]{1,0:T(8,128)(2,1)S(1)}, bf16[128,3584]{1,0:T(8,128)(2,1)}, u32[]{:S(2)}, u32[]{:S(2)}) collective-permute-start(bf16[128,3584]{1,0:T(8,128)(2,1)S(1)} %pad_maximum_fusion.3), channel_id=1, source_target_pairs={{0,4},{4,8},{8,12},{1,5},{5,9},{9,13},{2,6},{6,10},{10,14},{3,7},{... | collective-permute-start | bytes 2752520 | tf_op jit(solution)/shard_map/ppermute | solution.py:23
  166.0 1.4 multiply_reduce_fusion.3
  167.4 1.7 convolution_bitcast_fusion.3
  169.1 7.8 %collective-permute-done.26 = bf16[128,3584]{1,0:T(8,128)(2,1)} collective-permute-done((bf16[128,3584]{1,0:T(8,128)(2,1)S(1)}, bf16[128,3584]{1,0:T(8,128)(2,1)}, u32[]{:S(2)}, u32[]{:S(2)}) %collective-permute-start.26) | collective-permute-done | bytes 917536 | tf_op jit(solution)/shard_map/ppermute | solution.py:23
  178.2 5.5 %collective-permute-start.29 = (bf16[128,3584]{1,0:T(8,128)(2,1)}, bf16[128,3584]{1,0:T(8,128)(2,1)}, u32[]{:S(2)}, u32[]{:S(2)}) collective-permute-start(bf16[128,3584]{1,0:T(8,128)(2,1)} %collective-permute-done.27), channel_id=1, source_target_pairs={{0,4},{4,8},{8,12},{1,5},{5,9},{9,13},{2,6},{6,10},{10,14},{3,7},{... | collective-permute-start | bytes 2752520 | tf_op jit(solution)/shard_map/ppermute | solution.py:23
  185.4 1.5 copy.45
  188.8 2.5 copy.41
  193.7 1.8 fusion.130
  195.5 3.4 %fusion.54 = f32[128,1024]{1,0:T(8,128)S(1)} fusion(bf16[1024,1792]{1,0:T(8,128)(2,1)} %param.17, f32[128,1792]{1,0:T(8,128)S(1)} %get-tuple-element.37, f32[128]{0:T(128)S(1)} %get-tuple-element.28, bf16[128,3584]{1,0:T(8,128)(2,1)S(1)} %pad_maximum_fusion.3), kind=kOutput, calls=%fused_computation.133 | convolution fusion | flops 471826432 | bytes 6029824 | tf_op jit(solution)/shard_map/dot_general | solution.py:116
  200.3 1.4 broadcast_select_fusion
  202.5 1.4 collective-permute-start.30
  203.9 4.6 %collective-permute-start.31 = (bf16[128,3584]{1,0:T(8,128)(2,1)}, bf16[128,3584]{1,0:T(8,128)(2,1)S(1)}, u32[]{:S(2)}, u32[]{:S(2)}) collective-permute-start(bf16[128,3584]{1,0:T(8,128)(2,1)} %collective-permute-done.29), channel_id=1, source_target_pairs={{0,4},{4,8},{8,12},{1,5},{5,9},{9,13},{2,6},{6,10},{10,14},{3,7},{... | collective-permute-start | bytes 2752520 | tf_op jit(solution)/shard_map/ppermute | solution.py:23
  209.9 1.3 fusion.56
  212.6 10.6 %collective-permute-done.30 = bf16[128,3584]{1,0:T(8,128)(2,1)S(1)} collective-permute-done((bf16[128,3584]{1,0:T(8,128)(2,1)}, bf16[128,3584]{1,0:T(8,128)(2,1)S(1)}, u32[]{:S(2)}, u32[]{:S(2)}) %collective-permute-start.30) | collective-permute-done | bytes 917536 | tf_op jit(solution)/shard_map/ppermute | solution.py:23
  224.5 1.8 broadcast_select_fusion.1
  228.4 1.9 multiply_reduce_fusion
  243.8 3.6 %collective-permute-done.36 = f32[640]{0:T(1024)S(1)} collective-permute-done((f32[640]{0:T(1024)S(1)}, f32[640]{0:T(1024)S(1)}, u32[]{:S(2)}, u32[]{:S(2)}) %collective-permute-start.36) | collective-permute-done | bytes 2592 | tf_op jit(solution)/shard_map/ppermute | solution.py:27
  247.8 2.1 collective-permute-start.33
  250.0 6.8 %collective-permute-done.38 = bf16[128,1024]{1,0:T(8,128)(2,1)S(1)} collective-permute-done((bf16[128,1024]{1,0:T(8,128)(2,1)S(1)}, bf16[128,1024]{1,0:T(8,128)(2,1)S(1)}, u32[]{:S(2)}, u32[]{:S(2)}) %collective-permute-start.38) | collective-permute-done | bytes 262176 | tf_op jit(solution)/shard_map/ppermute | solution.py:27
  256.8 3.7 %collective-permute-done.33 = bf16[128,1024]{1,0:T(8,128)(2,1)S(1)} collective-permute-done((bf16[128,1024]{1,0:T(8,128)(2,1)S(1)}, bf16[128,1024]{1,0:T(8,128)(2,1)S(1)}, u32[]{:S(2)}, u32[]{:S(2)}) %collective-permute-start.33) | collective-permute-done | bytes 262176 | tf_op jit(solution)/shard_map/ppermute | solution.py:27
  260.7 5.3 %collective-permute-start.34 = (bf16[128,1024]{1,0:T(8,128)(2,1)S(1)}, bf16[128,1024]{1,0:T(8,128)(2,1)S(1)}, u32[]{:S(2)}, u32[]{:S(2)}) collective-permute-start(bf16[128,1024]{1,0:T(8,128)(2,1)S(1)} %get-tuple-element.66), channel_id=1, source_target_pairs={{0,0},{1,4},{2,8},{3,12},{4,1},{5,5},{6,9},{7,13},{8,2},{9,6},{10,... | collective-permute-start | bytes 786440 | tf_op jit(solution)/shard_map/ppermute | solution.py:33
  266.1 2.3 collective-permute-start.39
  270.3 13.5 %collective-permute-done.34 = bf16[128,1024]{1,0:T(8,128)(2,1)S(1)} collective-permute-done((bf16[128,1024]{1,0:T(8,128)(2,1)S(1)}, bf16[128,1024]{1,0:T(8,128)(2,1)S(1)}, u32[]{:S(2)}, u32[]{:S(2)}) %collective-permute-start.34) | collective-permute-done | bytes 262176 | tf_op jit(solution)/shard_map/ppermute | solution.py:33
  283.8 5.6 %collective-permute-done.39 = bf16[128,1024]{1,0:T(8,128)(2,1)S(1)} collective-permute-done((bf16[128,1024]{1,0:T(8,128)(2,1)S(1)}, bf16[128,1024]{1,0:T(8,128)(2,1)S(1)}, u32[]{:S(2)}, u32[]{:S(2)}) %collective-permute-start.39) | collective-permute-done | bytes 262176 | tf_op jit(solution)/shard_map/ppermute | solution.py:33
  (203 shorter events, 67.3 us)
Async XLA Ops:
  1.5 11.6 %collective-permute-start.2 = (bf16[2,128,256]{2,1,0:T(8,128)(2,1)S(1)}, bf16[2,128,256]{2,1,0:T(8,128)(2,1)S(1)}, u32[]{:S(2)}, u32[]{:S(2)}) collective-permute-start(bf16[2,128,256]{2,1,0:T(8,128)(2,1)S(1)} %pad_maximum_fusion.8), channel_id=1, source_target_pairs={{0,12},{1,13},{2,14},{3,15},{16,28},{17,29},{18,30},{19,31}} | collective-permute-start | bytes 393224 | tf_op jit(solution)/shard_map/ppermute | solution.py:23
  7.0 6.7 %collective-permute-start.1 = (bf16[2,128,256]{2,1,0:T(8,128)(2,1)S(1)}, bf16[2,128,256]{2,1,0:T(8,128)(2,1)S(1)}, u32[]{:S(2)}, u32[]{:S(2)}) collective-permute-start(bf16[2,128,256]{2,1,0:T(8,128)(2,1)S(1)} %pad_maximum_fusion.8), channel_id=1, source_target_pairs={{0,8},{4,12},{1,9},{5,13},{2,10},{6,14},{3,11},{7,15},{16,24},{20,... | collective-permute-start | bytes 393224 | tf_op jit(solution)/shard_map/ppermute | solution.py:23
  8.3 7.1 %collective-permute-start = (bf16[2,128,256]{2,1,0:T(8,128)(2,1)S(1)}, bf16[2,128,256]{2,1,0:T(8,128)(2,1)S(1)}, u32[]{:S(2)}, u32[]{:S(2)}) collective-permute-start(bf16[2,128,256]{2,1,0:T(8,128)(2,1)S(1)} %pad_maximum_fusion.8), channel_id=1, source_target_pairs={{0,4},{4,8},{8,12},{1,5},{5,9},{9,13},{2,6},{6,10},{10,14},{3,7},{... | collective-permute-start | bytes 393224 | tf_op jit(solution)/shard_map/ppermute | solution.py:23
  18.4 20.5 %copy-start.18 = (bf16[128,1792]{1,0:T(8,128)(2,1)S(1)}, bf16[128,1792]{1,0:T(8,128)(2,1)}, u32[]{:S(2)}) copy-start(bf16[128,1792]{1,0:T(8,128)(2,1)} %param.20) | copy-start | bytes 1376260
  19.5 19.0 %collective-permute-start.3 = (bf16[128,1024]{1,0:T(8,128)(2,1)S(1)}, bf16[128,1024]{1,0:T(8,128)(2,1)S(1)}, u32[]{:S(2)}, u32[]{:S(2)}) collective-permute-start(bf16[128,1024]{1,0:T(8,128)(2,1)S(1)} %get-tuple-element.44), channel_id=1, source_target_pairs={{0,0},{1,4},{2,8},{3,12},{4,1},{5,5},{6,9},{7,13},{8,2},{9,6},{10,... | collective-permute-start | bytes 786440 | tf_op jit(solution)/shard_map/ppermute | solution.py:33
  27.7 1.2 collective-permute-start.18
  29.0 9.5 %collective-permute-start.19 = (f32[128]{0:T(128)S(1)}, f32[128]{0:T(128)S(1)}, u32[]{:S(2)}, u32[]{:S(2)}) collective-permute-start(f32[128]{0:T(128)S(1)} %add.386), channel_id=1, source_target_pairs={{0,2},{2,0},{1,3},{3,1},{4,6},{6,4},{5,7},{7,5},{8,10},{10,8},{9,1... | collective-permute-start | bytes 1544 | tf_op jit(solution)/shard_map/ppermute | solution.py:27
  38.5 7.5 %collective-permute-start.4 = (bf16[128,1024]{1,0:T(8,128)(2,1)S(1)}, bf16[128,1024]{1,0:T(8,128)(2,1)S(1)}, u32[]{:S(2)}, u32[]{:S(2)}) collective-permute-start(bf16[128,1024]{1,0:T(8,128)(2,1)S(1)} %collective-permute-done.3), channel_id=1, source_target_pairs={{0,2},{2,0},{1,3},{3,1},{4,6},{6,4},{5,7},{7,5},{8,10},{10,8},{9,1... | collective-permute-start | bytes 786440 | tf_op jit(solution)/shard_map/ppermute | solution.py:27
  39.3 38.9 %collective-permute-start.21 = (bf16[128,1920]{1,0:T(8,128)(2,1)S(1)}, bf16[128,1920]{1,0:T(8,128)(2,1)}, u32[]{:S(2)}, u32[]{:S(2)}) collective-permute-start(bf16[128,1920]{1,0:T(8,128)(2,1)S(1)} %pad.4), channel_id=1, source_target_pairs={{4,0},{8,4},{12,8},{5,1},{9,5},{13,9},{6,2},{10,6},{14,10},{7,3},{... | collective-permute-start | bytes 1474568 | tf_op jit(solution)/shard_map/ppermute | solution.py:23
  40.6 41.8 %collective-permute-start.20 = (bf16[128,1920]{1,0:T(8,128)(2,1)S(1)}, bf16[128,1920]{1,0:T(8,128)(2,1)}, u32[]{:S(2)}, u32[]{:S(2)}) collective-permute-start(bf16[128,1920]{1,0:T(8,128)(2,1)S(1)} %pad.4), channel_id=1, source_target_pairs={{0,4},{4,8},{8,12},{1,5},{5,9},{9,13},{2,6},{6,10},{10,14},{3,7},{... | collective-permute-start | bytes 1474568 | tf_op jit(solution)/shard_map/ppermute | solution.py:23
  46.0 2.4 collective-permute-start.5
  51.7 12.6 %collective-permute-start.12 = (bf16[128,1792]{1,0:T(8,128)(2,1)S(1)}, bf16[128,1792]{1,0:T(8,128)(2,1)S(1)}, u32[]{:S(2)}, u32[]{:S(2)}) collective-permute-start(bf16[128,1792]{1,0:T(8,128)(2,1)S(1)} %get-tuple-element.57), channel_id=1, source_target_pairs={{0,4},{4,8},{8,12},{1,5},{5,9},{9,13},{2,6},{6,10},{10,14},{3,7},{... | collective-permute-start | bytes 1376264 | tf_op jit(solution)/shard_map/ppermute | solution.py:23
  53.4 33.0 %collective-permute-start.15 = (bf16[128,1792]{1,0:T(8,128)(2,1)S(1)}, bf16[128,1792]{1,0:T(8,128)(2,1)S(1)}, u32[]{:S(2)}, u32[]{:S(2)}) collective-permute-start(bf16[128,1792]{1,0:T(8,128)(2,1)S(1)} %get-tuple-element.58), channel_id=1, source_target_pairs={{4,0},{8,4},{12,8},{5,1},{9,5},{13,9},{6,2},{10,6},{14,10},{7,3},{... | collective-permute-start | bytes 1376264 | tf_op jit(solution)/shard_map/ppermute | solution.py:23
  56.8 41.9 %copy-start.6 = (bf16[512,1792]{1,0:T(8,128)(2,1)}, bf16[512,1792]{1,0:T(8,128)(2,1)S(1)}, u32[]{:S(2)}) copy-start(bf16[512,1792]{1,0:T(8,128)(2,1)S(1)} %convolution_convert_fusion.1) | copy-start | bytes 5505028
  56.9 16.7 %collective-permute-start.6 = (bf16[128,1792]{1,0:T(8,128)(2,1)S(1)}, bf16[128,1792]{1,0:T(8,128)(2,1)S(1)}, u32[]{:S(2)}, u32[]{:S(2)}) collective-permute-start(bf16[128,1792]{1,0:T(8,128)(2,1)S(1)} %get-tuple-element.53), channel_id=1, source_target_pairs={{0,4},{4,8},{8,12},{1,5},{5,9},{9,13},{2,6},{6,10},{10,14},{3,7},{... | collective-permute-start | bytes 1376264 | tf_op jit(solution)/shard_map/ppermute | solution.py:23
  64.2 27.1 %collective-permute-start.9 = (bf16[128,1792]{1,0:T(8,128)(2,1)S(1)}, bf16[128,1792]{1,0:T(8,128)(2,1)S(1)}, u32[]{:S(2)}, u32[]{:S(2)}) collective-permute-start(bf16[128,1792]{1,0:T(8,128)(2,1)S(1)} %get-tuple-element.54), channel_id=1, source_target_pairs={{4,0},{8,4},{12,8},{5,1},{9,5},{13,9},{6,2},{10,6},{14,10},{7,3},{... | collective-permute-start | bytes 1376264 | tf_op jit(solution)/shard_map/ppermute | solution.py:23
  73.6 15.3 %collective-permute-start.13 = (bf16[128,1792]{1,0:T(8,128)(2,1)S(1)}, bf16[128,1792]{1,0:T(8,128)(2,1)S(1)}, u32[]{:S(2)}, u32[]{:S(2)}) collective-permute-start(bf16[128,1792]{1,0:T(8,128)(2,1)S(1)} %fusion.17), channel_id=1, source_target_pairs={{0,4},{4,8},{8,12},{1,5},{5,9},{9,13},{2,6},{6,10},{10,14},{3,7},{... | collective-permute-start | bytes 1376264 | tf_op jit(solution)/shard_map/ppermute | solution.py:23
  78.1 20.6 %collective-permute-start.7 = (bf16[128,1792]{1,0:T(8,128)(2,1)S(1)}, bf16[128,1792]{1,0:T(8,128)(2,1)S(1)}, u32[]{:S(2)}, u32[]{:S(2)}) collective-permute-start(bf16[128,1792]{1,0:T(8,128)(2,1)S(1)} %fusion.23), channel_id=1, source_target_pairs={{0,4},{4,8},{8,12},{1,5},{5,9},{9,13},{2,6},{6,10},{10,14},{3,7},{... | collective-permute-start | bytes 1376264 | tf_op jit(solution)/shard_map/ppermute | solution.py:23
  82.4 27.0 %collective-permute-start.22 = (bf16[128,1920]{1,0:T(8,128)(2,1)}, bf16[128,1920]{1,0:T(8,128)(2,1)}, u32[]{:S(2)}, u32[]{:S(2)}) collective-permute-start(bf16[128,1920]{1,0:T(8,128)(2,1)} %collective-permute-done.20), channel_id=1, source_target_pairs={{0,4},{4,8},{8,12},{1,5},{5,9},{9,13},{2,6},{6,10},{10,14},{3,7},{... | collective-permute-start | bytes 1474568 | tf_op jit(solution)/shard_map/ppermute | solution.py:23
  86.4 28.1 %collective-permute-start.23 = (bf16[128,1920]{1,0:T(8,128)(2,1)}, bf16[128,1920]{1,0:T(8,128)(2,1)S(1)}, u32[]{:S(2)}, u32[]{:S(2)}) collective-permute-start(bf16[128,1920]{1,0:T(8,128)(2,1)} %collective-permute-done.21), channel_id=1, source_target_pairs={{4,0},{8,4},{12,8},{5,1},{9,5},{13,9},{6,2},{10,6},{14,10},{7,3},{... | collective-permute-start | bytes 1474568 | tf_op jit(solution)/shard_map/ppermute | solution.py:23
  90.1 31.1 %collective-permute-start.16 = (bf16[128,1792]{1,0:T(8,128)(2,1)}, bf16[128,1792]{1,0:T(8,128)(2,1)}, u32[]{:S(2)}, u32[]{:S(2)}) collective-permute-start(bf16[128,1792]{1,0:T(8,128)(2,1)} %get-tuple-element.56), channel_id=1, source_target_pairs={{4,0},{8,4},{12,8},{5,1},{9,5},{13,9},{6,2},{10,6},{14,10},{7,3},{... | collective-permute-start | bytes 1376264 | tf_op jit(solution)/shard_map/ppermute | solution.py:23
  91.4 34.8 %collective-permute-start.14 = (bf16[128,1792]{1,0:T(8,128)(2,1)}, bf16[128,1792]{1,0:T(8,128)(2,1)}, u32[]{:S(2)}, u32[]{:S(2)}) collective-permute-start(bf16[128,1792]{1,0:T(8,128)(2,1)} %get-tuple-element.55), channel_id=1, source_target_pairs={{0,4},{4,8},{8,12},{1,5},{5,9},{9,13},{2,6},{6,10},{10,14},{3,7},{... | collective-permute-start | bytes 1376264 | tf_op jit(solution)/shard_map/ppermute | solution.py:23
  99.9 23.7 %collective-permute-start.10 = (bf16[128,1792]{1,0:T(8,128)(2,1)}, bf16[128,1792]{1,0:T(8,128)(2,1)}, u32[]{:S(2)}, u32[]{:S(2)}) collective-permute-start(bf16[128,1792]{1,0:T(8,128)(2,1)} %get-tuple-element.52), channel_id=1, source_target_pairs={{4,0},{8,4},{12,8},{5,1},{9,5},{13,9},{6,2},{10,6},{14,10},{7,3},{... | collective-permute-start | bytes 1376264 | tf_op jit(solution)/shard_map/ppermute | solution.py:23
  109.3 39.1 %collective-permute-start.8 = (bf16[128,1792]{1,0:T(8,128)(2,1)}, bf16[128,1792]{1,0:T(8,128)(2,1)}, u32[]{:S(2)}, u32[]{:S(2)}) collective-permute-start(bf16[128,1792]{1,0:T(8,128)(2,1)} %get-tuple-element.51), channel_id=1, source_target_pairs={{0,4},{4,8},{8,12},{1,5},{5,9},{9,13},{2,6},{6,10},{10,14},{3,7},{... | collective-permute-start | bytes 1376264 | tf_op jit(solution)/shard_map/ppermute | solution.py:23
  114.5 40.2 %collective-permute-start.24 = (bf16[128,1920]{1,0:T(8,128)(2,1)}, bf16[128,1920]{1,0:T(8,128)(2,1)}, u32[]{:S(2)}, u32[]{:S(2)}) collective-permute-start(bf16[128,1920]{1,0:T(8,128)(2,1)} %collective-permute-done.22), channel_id=1, source_target_pairs={{0,4},{4,8},{8,12},{1,5},{5,9},{9,13},{2,6},{6,10},{10,14},{3,7},{... | collective-permute-start | bytes 1474568 | tf_op jit(solution)/shard_map/ppermute | solution.py:23
  118.8 29.6 %copy-start.14 = (bf16[128,1920]{1,0:T(8,128)(2,1)}, bf16[128,1920]{1,0:T(8,128)(2,1)S(1)}, u32[]{:S(2)}) copy-start(bf16[128,1920]{1,0:T(8,128)(2,1)S(1)} %broadcast_select_fusion.2) | copy-start | bytes 1474564
  121.2 33.6 %collective-permute-start.25 = (bf16[128,1920]{1,0:T(8,128)(2,1)}, bf16[128,1920]{1,0:T(8,128)(2,1)S(1)}, u32[]{:S(2)}, u32[]{:S(2)}) collective-permute-start(bf16[128,1920]{1,0:T(8,128)(2,1)} %copy-done.17), channel_id=1, source_target_pairs={{4,0},{8,4},{12,8},{5,1},{9,5},{13,9},{6,2},{10,6},{14,10},{7,3},{... | collective-permute-start | bytes 1474568 | tf_op jit(solution)/shard_map/ppermute | solution.py:23
  123.6 23.6 %collective-permute-start.17 = (bf16[128,1792]{1,0:T(8,128)(2,1)S(1)}, bf16[128,1792]{1,0:T(8,128)(2,1)S(1)}, u32[]{:S(2)}, u32[]{:S(2)}) collective-permute-start(bf16[128,1792]{1,0:T(8,128)(2,1)S(1)} %fusion.16), channel_id=1, source_target_pairs={{4,0},{8,4},{12,8},{5,1},{9,5},{13,9},{6,2},{10,6},{14,10},{7,3},{... | collective-permute-start | bytes 1376264 | tf_op jit(solution)/shard_map/ppermute | solution.py:23
  126.2 27.2 %collective-permute-start.11 = (bf16[128,1792]{1,0:T(8,128)(2,1)S(1)}, bf16[128,1792]{1,0:T(8,128)(2,1)S(1)}, u32[]{:S(2)}, u32[]{:S(2)}) collective-permute-start(bf16[128,1792]{1,0:T(8,128)(2,1)S(1)} %fusion.22), channel_id=1, source_target_pairs={{4,0},{8,4},{12,8},{5,1},{9,5},{13,9},{6,2},{10,6},{14,10},{7,3},{... | collective-permute-start | bytes 1376264 | tf_op jit(solution)/shard_map/ppermute | solution.py:23
  148.4 17.6 %copy-start.8 = (f32[128,1792]{1,0:T(8,128)S(1)}, f32[128,1792]{1,0:T(8,128)}, u32[]{:S(2)}) copy-start(f32[128,1792]{1,0:T(8,128)} %copy.39) | copy-start | bytes 2752516
  148.4 17.6 %copy-start.13 = (bf16[128,1920]{1,0:T(8,128)(2,1)S(1)}, bf16[128,1920]{1,0:T(8,128)(2,1)}, u32[]{:S(2)}) copy-start(bf16[128,1920]{1,0:T(8,128)(2,1)} %copy-done.12) | copy-start | bytes 1474564
  154.7 12.7 %copy-start.25 = (bf16[1792,1024]{1,0:T(8,128)(2,1)S(1)}, bf16[1792,1024]{1,0:T(8,128)(2,1)}, u32[]{:S(2)}) copy-start(bf16[1792,1024]{1,0:T(8,128)(2,1)} %param.19) | copy-start | bytes 11010052
  154.8 22.1 %collective-permute-start.26 = (bf16[128,3584]{1,0:T(8,128)(2,1)S(1)}, bf16[128,3584]{1,0:T(8,128)(2,1)}, u32[]{:S(2)}, u32[]{:S(2)}) collective-permute-start(bf16[128,3584]{1,0:T(8,128)(2,1)S(1)} %pad_maximum_fusion.3), channel_id=1, source_target_pairs={{4,0},{8,4},{12,8},{5,1},{9,5},{13,9},{6,2},{10,6},{14,10},{7,3},{... | collective-permute-start | bytes 2752520 | tf_op jit(solution)/shard_map/ppermute | solution.py:23
  156.3 21.8 %collective-permute-start.27 = (bf16[128,3584]{1,0:T(8,128)(2,1)S(1)}, bf16[128,3584]{1,0:T(8,128)(2,1)}, u32[]{:S(2)}, u32[]{:S(2)}) collective-permute-start(bf16[128,3584]{1,0:T(8,128)(2,1)S(1)} %pad_maximum_fusion.3), channel_id=1, source_target_pairs={{0,4},{4,8},{8,12},{1,5},{5,9},{9,13},{2,6},{6,10},{10,14},{3,7},{... | collective-permute-start | bytes 2752520 | tf_op jit(solution)/shard_map/ppermute | solution.py:23
  163.2 20.5 %copy-start.10 = (bf16[128,1920]{1,0:T(8,128)(2,1)}, bf16[128,1920]{1,0:T(8,128)(2,1)S(1)}, u32[]{:S(2)}) copy-start(bf16[128,1920]{1,0:T(8,128)(2,1)S(1)} %get-tuple-element.60) | copy-start | bytes 1474564
  167.4 16.9 %copy-start.19 = (f32[128,14]{1,0:T(8,128)S(1)}, f32[128,14]{1,0:T(8,128)}, u32[]{:S(2)}) copy-start(f32[128,14]{1,0:T(8,128)} %slice_convert_fusion) | copy-start | bytes 21508
  176.9 23.4 %collective-permute-start.28 = (bf16[128,3584]{1,0:T(8,128)(2,1)}, bf16[128,3584]{1,0:T(8,128)(2,1)}, u32[]{:S(2)}, u32[]{:S(2)}) collective-permute-start(bf16[128,3584]{1,0:T(8,128)(2,1)} %collective-permute-done.26), channel_id=1, source_target_pairs={{4,0},{8,4},{12,8},{5,1},{9,5},{13,9},{6,2},{10,6},{14,10},{7,3},{... | collective-permute-start | bytes 2752520 | tf_op jit(solution)/shard_map/ppermute | solution.py:23
  178.2 22.1 %collective-permute-start.29 = (bf16[128,3584]{1,0:T(8,128)(2,1)}, bf16[128,3584]{1,0:T(8,128)(2,1)}, u32[]{:S(2)}, u32[]{:S(2)}) collective-permute-start(bf16[128,3584]{1,0:T(8,128)(2,1)} %collective-permute-done.27), channel_id=1, source_target_pairs={{0,4},{4,8},{8,12},{1,5},{5,9},{9,13},{2,6},{6,10},{10,14},{3,7},{... | collective-permute-start | bytes 2752520 | tf_op jit(solution)/shard_map/ppermute | solution.py:23
  202.5 20.7 %collective-permute-start.30 = (bf16[128,3584]{1,0:T(8,128)(2,1)}, bf16[128,3584]{1,0:T(8,128)(2,1)S(1)}, u32[]{:S(2)}, u32[]{:S(2)}) collective-permute-start(bf16[128,3584]{1,0:T(8,128)(2,1)} %collective-permute-done.28), channel_id=1, source_target_pairs={{4,0},{8,4},{12,8},{5,1},{9,5},{13,9},{6,2},{10,6},{14,10},{7,3},{... | collective-permute-start | bytes 2752520 | tf_op jit(solution)/shard_map/ppermute | solution.py:23
  203.9 20.5 %collective-permute-start.31 = (bf16[128,3584]{1,0:T(8,128)(2,1)}, bf16[128,3584]{1,0:T(8,128)(2,1)S(1)}, u32[]{:S(2)}, u32[]{:S(2)}) collective-permute-start(bf16[128,3584]{1,0:T(8,128)(2,1)} %collective-permute-done.29), channel_id=1, source_target_pairs={{0,4},{4,8},{8,12},{1,5},{5,9},{9,13},{2,6},{6,10},{10,14},{3,7},{... | collective-permute-start | bytes 2752520 | tf_op jit(solution)/shard_map/ppermute | solution.py:23
  236.9 10.4 %collective-permute-start.37 = (bf16[2,128,1024]{2,1,0:T(8,128)(2,1)}, bf16[2,128,1024]{2,1,0:T(8,128)(2,1)S(1)}, u32[]{:S(2)}, u32[]{:S(2)}) collective-permute-start(bf16[2,128,1024]{2,1,0:T(8,128)(2,1)} %pad_maximum_fusion.7), channel_id=1, source_target_pairs={{0,1},{1,0},{2,3},{3,2},{4,5},{5,4},{6,7},{7,6},{8,9},{9,8},{10,11... | collective-permute-start | bytes 1572872 | tf_op jit(solution)/shard_map/ppermute | solution.py:27
  239.3 8.3 %collective-permute-start.32 = (bf16[2,128,1024]{2,1,0:T(8,128)(2,1)}, bf16[2,128,1024]{2,1,0:T(8,128)(2,1)S(1)}, u32[]{:S(2)}, u32[]{:S(2)}) collective-permute-start(bf16[2,128,1024]{2,1,0:T(8,128)(2,1)} %pad_maximum_fusion.6), channel_id=1, source_target_pairs={{0,1},{1,0},{2,3},{3,2},{4,5},{5,4},{6,7},{7,6},{8,9},{9,8},{10,11... | collective-permute-start | bytes 1572872 | tf_op jit(solution)/shard_map/ppermute | solution.py:27
  242.5 1.2 collective-permute-start.35
  243.7 3.6 %collective-permute-start.36 = (f32[640]{0:T(1024)S(1)}, f32[640]{0:T(1024)S(1)}, u32[]{:S(2)}, u32[]{:S(2)}) collective-permute-start(f32[640]{0:T(1024)S(1)} %add.417), channel_id=1, source_target_pairs={{0,2},{2,0},{1,3},{3,1},{4,6},{6,4},{5,7},{7,5},{8,10},{10,8},{9,1... | collective-permute-start | bytes 7688 | tf_op jit(solution)/shard_map/ppermute | solution.py:27
  247.5 9.2 %collective-permute-start.38 = (bf16[128,1024]{1,0:T(8,128)(2,1)S(1)}, bf16[128,1024]{1,0:T(8,128)(2,1)S(1)}, u32[]{:S(2)}, u32[]{:S(2)}) collective-permute-start(bf16[128,1024]{1,0:T(8,128)(2,1)S(1)} %fusion.95), channel_id=1, source_target_pairs={{0,2},{2,0},{1,3},{3,1},{4,6},{6,4},{5,7},{7,5},{8,10},{10,8},{9,1... | collective-permute-start | bytes 786440 | tf_op jit(solution)/shard_map/ppermute | solution.py:27
  247.8 12.6 %collective-permute-start.33 = (bf16[128,1024]{1,0:T(8,128)(2,1)S(1)}, bf16[128,1024]{1,0:T(8,128)(2,1)S(1)}, u32[]{:S(2)}, u32[]{:S(2)}) collective-permute-start(bf16[128,1024]{1,0:T(8,128)(2,1)S(1)} %fusion.94), channel_id=1, source_target_pairs={{0,2},{2,0},{1,3},{3,1},{4,6},{6,4},{5,7},{7,5},{8,10},{10,8},{9,1... | collective-permute-start | bytes 786440 | tf_op jit(solution)/shard_map/ppermute | solution.py:27
  260.7 23.1 %collective-permute-start.34 = (bf16[128,1024]{1,0:T(8,128)(2,1)S(1)}, bf16[128,1024]{1,0:T(8,128)(2,1)S(1)}, u32[]{:S(2)}, u32[]{:S(2)}) collective-permute-start(bf16[128,1024]{1,0:T(8,128)(2,1)S(1)} %get-tuple-element.66), channel_id=1, source_target_pairs={{0,0},{1,4},{2,8},{3,12},{4,1},{5,5},{6,9},{7,13},{8,2},{9,6},{10,... | collective-permute-start | bytes 786440 | tf_op jit(solution)/shard_map/ppermute | solution.py:33
  266.1 23.4 %collective-permute-start.39 = (bf16[128,1024]{1,0:T(8,128)(2,1)S(1)}, bf16[128,1024]{1,0:T(8,128)(2,1)S(1)}, u32[]{:S(2)}, u32[]{:S(2)}) collective-permute-start(bf16[128,1024]{1,0:T(8,128)(2,1)S(1)} %get-tuple-element.65), channel_id=1, source_target_pairs={{0,0},{1,4},{2,8},{3,12},{4,1},{5,5},{6,9},{7,13},{8,2},{9,6},{10,... | collective-permute-start | bytes 786440 | tf_op jit(solution)/shard_map/ppermute | solution.py:33
  (19 other events, 93.2 us)

commit v3 on v2

--- a/solution.py
+++ b/solution.py
@@ -93,14 +93,7 @@
     return small + swapped(small, "head")
 
 
-def split_bits(wide):
-    high = lax.reduce_precision(wide, 8, 7)
-    middle = lax.reduce_precision(wide - high, 8, 7)
-    return [v.astype(BF16) for v in (high, middle, wide - high - middle)]
-
-
-def block_terms(gate_proj, up_proj, feats, keep_cols, weights):
-    w_gate, w_up, w_down = weights
+def elementwise(gate_proj, up_proj, feats, keep_cols):
     rows, ff = gate_proj.shape
     tiles = keep_cols.shape[1]
     keep = jnp.broadcast_to(keep_cols.astype(F32)[:, :, None], (rows, tiles, TILE)).reshape(rows, ff)
@@ -111,34 +104,36 @@
     grad_act = keep * differ
     grad_gate = (grad_act * up_proj * 2.0 * lifted).astype(BF16)
     grad_up = (grad_act * squared).astype(BF16)
+    inner = 3.0 * jnp.sum(grad_act * act, axis=1)
+    return act.astype(BF16), grad_gate, grad_up, inner, jnp.sum(grad_act * differ)
+
+
+def products(hidden, grad_gate, grad_up, weights):
+    w_gate, w_up, w_down = weights
     contract = (((1,), (1,)), ((), ()))
-    down = jnp.dot(act.astype(BF16), w_down, preferred_element_type=F32)
+    down = jnp.dot(hidden, w_down, preferred_element_type=F32)
     grad = lax.dot_general(grad_gate, w_gate, contract, preferred_element_type=F32)
-    grad = grad + lax.dot_general(grad_up, w_up, contract, preferred_element_type=F32)
-    return down, grad, jnp.sum(grad_act * act, axis=1), jnp.sum(grad_act * differ)
+    return down, grad + lax.dot_general(grad_up, w_up, contract, preferred_element_type=F32)
+
+
+TURNS = ((0, 1, 2, 3), (1, 2, 3, 0), (2, 1, 0, 3), (3, 2, 1, 0))
 
 
 def on_square(residual, norm_gain, weights, teacher_feats, keep_tiles):
     w_gate, w_up, _ = weights
     rows, d_ctx = residual.shape
     ff = w_gate.shape[1]
-    tiles = keep_tiles.shape[1]
     z = lax.axis_index("ctx")
     hp = lax.axis_index(HP)
+    pair = lax.axis_index("pair")
     low = z < 2
 
     tile = transposed(residual)
     own_wide = residual.astype(F32)
     mean = summed_over_hp(jnp.sum(own_wide * own_wide, axis=1)) / D
-    rms = jnp.sqrt(mean + 1e-05)
-    extra = [keep_tiles.astype(BF16)] + [v[:, None] for v in split_bits(rms)]
-    marked = jnp.concatenate([teacher_feats] + extra, axis=1)
-    marked = jnp.pad(marked, ((0, 0), (0, -marked.shape[1] % 128)))
+    rms = jnp.sqrt(mean + 1e-05)[:, None]
     across = swapped(tile, "head")
     both = swapped(jnp.stack([tile, across]), "pair")
-    marked, _ = lax.optimization_barrier((marked, tile))
-    mark_right, mark_left = [shifted(marked, 1)], [shifted(marked, -1)]
-
     gain = lax.dynamic_slice_in_dim(norm_gain, z * d_ctx, d_ctx, 0)
     resid = jnp.stack([tile, both[0], across, both[1]]).astype(F32)
     scaled = (resid * gain).astype(BF16).reshape(4 * rows, d_ctx)
@@ -149,14 +144,6 @@
 
     came = [[None, None], [None, None]]
     for s in range(3):
-        if s == 1:
-            held, _ = lax.optimization_barrier(((mark_right[0], mark_left[0]), came[0][0]))
-            mark_right.append(shifted(held[0], 1))
-            mark_left.append(shifted(held[1], -1))
-        if s == 2:
-            held, _ = lax.optimization_barrier(((mark_right[1], mark_left[1]), came[0][0]))
-            mark_right.append(shifted(held[0], 1))
-            mark_left.append(shifted(held[1], -1))
         for i in range(2):
             right = picked(parts[i], jnp.clip(3 - s + z, 0, 3) ^ hp)
             left = picked(parts[i], jnp.clip(s - 3 + z, 0, 3) ^ hp)
@@ -164,70 +151,56 @@
                 right = (right.astype(F32) + came[i][0].astype(F32)).astype(BF16)
                 left = (left.astype(F32) + came[i][1].astype(F32)).astype(BF16)
             came[i] = [shifted(right, 1), shifted(left, -1)]
-    owned = jnp.concatenate(
-        [
-            (picked(parts[i], z ^ hp).astype(F32) + came[i][0].astype(F32) + came[i][1].astype(F32)).astype(BF16)
-            for i in range(2)
-        ],
-        axis=1,
-    )
-
-    owned, mark_right[2], mark_left[2] = lax.optimization_barrier((owned, mark_right[2], mark_left[2]))
+    gate_proj, up_proj = [
+        (picked(parts[i], z ^ hp).astype(F32) + came[i][0].astype(F32) + came[i][1].astype(F32)) / rms
+        for i in range(2)
+    ]
+    hidden, grad_gate, grad_up, inner, loss = elementwise(gate_proj, up_proj, teacher_feats, keep_tiles)
+    owned = jnp.concatenate([hidden, grad_gate, grad_up], axis=1)
+
     right, left = [shifted(owned, 1)], [shifted(owned, -1)]
     for s in range(2):
         right.append(shifted(right[s], 1))
         left.append(shifted(left[s], -1))
-
-    def slots_of(mine, right, left):
-        first = jnp.where(low, left[0], right[0])
-        second = jnp.where(low, left[1], right[1])
-        inner = jnp.where(low, right[0], left[0])
-        outer = jnp.where(low, left[2], right[2])
-        third = jnp.where((z == 0) | (z == 3), outer, inner)
-        return [mine, first, second, third]
-
-    def slot(token):
-        return jnp.where(low, token - z, z - token) & 3
-
-    sums = slots_of(owned, right, left)
-    marks = slots_of(marked, mark_right, mark_left)
-    results, rms_slots = [], []
+    turns = [owned, jnp.where(low, left[0], right[0])]
+    first, second = lax.optimization_barrier((turns[1], (left[1], right[1])))
+    turns = [owned, first, jnp.where(low, *second)]
+    second, third = lax.optimization_barrier((turns[2], (left[2], right[2])))
+    outer = jnp.where(low, *third)
+    inward = jnp.where(low, right[0], left[0])
+    turns = [owned, first, second, jnp.where((z == 0) | (z == 3), outer, inward)]
+
+    def brought_home(k, down, grad):
+        keeps_down = pair == (k & 1)
+        sent = jnp.where(keeps_down, grad, down).astype(BF16)
+        half = jnp.where(keeps_down, down, grad) + swapped(sent, "pair").astype(F32)
+        route = [(k ^ 2, k), (k ^ 1, k ^ 3)]
+        whole = (half + lax.ppermute(half.astype(BF16), HP, route).astype(F32)).astype(BF16)
+        return [
+            lax.ppermute(whole, ("ctx",) + HP, [(4 * c + h, 4 * TURNS[c][k] + c) for c in range(4)])
+            for h in (k, k ^ 3)
+        ]
+
+    home = []
     for k in range(4):
-        bits = marks[k][:, ff + tiles : ff + tiles + 3].astype(F32)
-        rms_k = bits[:, 0] + bits[:, 1] + bits[:, 2]
-        inv = (1.0 / rms_k)[:, None]
-        rms_slots.append(rms_k)
-        results.append(
-            block_terms(
-                sums[k][:, :ff].astype(F32) * inv,
-                sums[k][:, ff:].astype(F32) * inv,
-                marks[k][:, :ff],
-                marks[k][:, ff : ff + tiles],
-                weights,
-            )
-        )
-    down, grad, inner, loss = [[r[i] for r in results] for i in range(4)]
-
-    count = sum(jnp.sum(m[:, ff : ff + tiles].astype(F32)) for m in marks) * TILE
-    inner = jnp.stack(inner)
-    by_token = jnp.concatenate([picked(inner, slot(t)) for t in range(4)])
-    small = jnp.concatenate([by_token, sum(loss)[None], count[None], jnp.zeros(126, F32)])
+        block = turns[k]
+        down, grad = products(block[:, :ff], block[:, ff : 2 * ff], block[:, 2 * ff :], weights)
+        home.append(brought_home(k, down, grad))
+
+    count = jnp.sum(keep_tiles.astype(F32)) * TILE
+    small = jnp.concatenate([inner, loss[None], count[None], jnp.zeros(126, F32)])
     small = summed_over_hp(small)
-    loss_value = (small[4 * rows] / small[4 * rows + 1]).reshape(1)
-    rms_own = picked(jnp.stack(rms_slots), slot(hp))[:, None]
-    inner_own = 3.0 * rms_own * lax.dynamic_slice_in_dim(small, hp * rows, rows, 0)[:, None]
-
-    def reduced(blocks):
-        blocks = jnp.stack(blocks)
-        j = [picked(blocks, slot(i ^ hp)) for i in range(4)]
-        came = swapped(jnp.stack([j[1], j[3]]).astype(BF16), "pair").astype(F32)
-        half = (j[2] + came[1]).astype(BF16)
-        return j[0] + came[0] + swapped(half, "head").astype(F32)
-
-    own = tile.astype(F32)
-    layer_out = transposed((own + reduced(down)).astype(BF16))
-    slope = gain * reduced(grad) / rms_own - own * inner_own / (D * rms_own * rms_own * rms_own)
-    return layer_out, loss_value, transposed(slope.astype(BF16)).astype(F32)
+    totals = small[rows:]
+    for d in (1, 2):
+        totals = totals + lax.ppermute(totals, "ctx", [(c, c ^ d) for c in range(4)])
+    loss_value = (totals[0] / totals[1]).reshape(1)
+
+    down, grad = [sum(h[i].astype(F32) for h in home) for i in range(2)]
+    gain_own = lax.dynamic_slice_in_dim(norm_gain, hp * d_ctx, d_ctx, 0)
+    layer_out = (own_wide + down).astype(BF16)
+    inner_own = small[:rows][:, None] * rms
+    slope = gain_own * grad / rms - own_wide * inner_own / (D * rms * rms * rms)
+    return layer_out, loss_value, slope
 
 
 def on_any(residual, norm_gain, weights, teacher_feats, keep_tiles):
@@ -251,7 +224,8 @@
         for w in (w_gate, w_up)
     ]
     keep_cols = marked[:, ff : ff + tiles]
-    down, grad, inner, loss = block_terms(sums[0], sums[1], marked[:, :ff], keep_cols, weights)
+    *values, inner, loss = elementwise(sums[0], sums[1], marked[:, :ff], keep_cols)
+    down, grad = products(*values, weights)
     count = jnp.sum(keep_cols.astype(F32)) * TILE
     small = lax.psum(jnp.concatenate([inner, loss[None], count[None]]), HP)
     loss_value = (small[-2] / small[-1]).reshape(1)
@@ -263,7 +237,7 @@
     own = residual.astype(F32)
     layer_out = (own + home(down)).astype(BF16)
     rms_own = lax.dynamic_slice_in_dim(rms, z * rows, rows, 0)[:, None]
-    inner_own = 3.0 * rms_own * lax.dynamic_slice_in_dim(small, z * rows, rows, 0)[:, None]
+    inner_own = rms_own * lax.dynamic_slice_in_dim(small, z * rows, rows, 0)[:, None]
     gain_own = lax.dynamic_slice_in_dim(norm_gain, hp * own.shape[1], own.shape[1], 0)
     slope = gain_own * home(grad) / rms_own - own * inner_own / (D * rms_own * rms_own * rms_own)
     return layer_out, loss_value, slope

time: 294 us -> 300 us (1.020)
  waiting for transfers between devices: 112 us -> 148 us
  other arithmetic: 31.1 us -> 19.5 us
  starting transfers between devices: 99 us -> 91.3 us
  local copies, waits for them, and re-layouts: 17.2 us -> 11.7 us
  between operations: 9.28 us -> 4.68 us
    ppermute x0 -> x14, waiting for transfers between devices: none -> 45.5 us  [the longest x4 21.6 us: brought_home(): lax.ppermute(half.astype(BF16), HP, route).astype(F32)]
    ppermute x0 -> x14, starting transfers between devices: none -> 21.7 us  [the longest x8 10.4 us: brought_home(): lax.ppermute(whole, ('ctx',) + HP, [(4 * c + h, 4 * TURNS[c][k] + c) for...]
    ppermute x27 -> x21, starting transfers between devices: 80.6 us -> 64.5 us  [passed_along(): return lax.ppermute(block, axis, route)]
    ppermute x3 -> x1, waiting for transfers between devices: 28.6 us -> 13.8 us  [transposed(): return lax.ppermute(block, ('ctx',) + HP, route)]
    ppermute x3 -> x1, starting transfers between devices: 15.7 us -> 3.87 us  [transposed(): return lax.ppermute(block, ('ctx',) + HP, route)]
    ppermute x27 -> x21, waiting for transfers between devices: 67.9 us -> 75.3 us  [passed_along(): return lax.ppermute(block, axis, route)]
    reshape x4 -> x1, local copies, waits for them, and re-layouts: 6.42 us -> 1.47 us  [elementwise(): jnp.broadcast_to(keep_cols.astype(F32)[:, :, None], (rows, tiles, TILE))]
    select_n x4 -> x3, other arithmetic: 4.56 us -> 0.54 us  [the longest x1 0.25 us: on_square(): jnp.where((z == 0) | (z == 3), outer, inward)]
  transfers between devices with their start and end apart: 40 -> 46, of which waited for: 20 -> 26; matrix products, arithmetic and copies ran while one was open for 17% -> 10% of each run, Pallas kernels for 0% -> 0%
where the time goes in v3:
time: 300 us; the launch traced here: 296 us
  waiting for transfers between devices  148 us (49%)
  starting transfers between devices  91.3 us (30%)
  matrix products  20.5 us (7%)
  other arithmetic  19.5 us (6%)
  local copies, waits for them, and re-layouts  11.7 us (4%)
  between operations  4.68 us (2%)
    ppermute x21, waiting for transfers between devices, passed_along(): return lax.ppermute(block, axis, route)  75.3 us
    ppermute x21, starting transfers between devices, passed_along(): return lax.ppermute(block, axis, route)  64.5 us
    ppermute x4, waiting for transfers between devices, brought_home(): lax.ppermute(half.astype(BF16), HP, route).astype(F32)  21.6 us
    ppermute x2, waiting for transfers between devices, on_square(): lax.ppermute(totals, 'ctx', [(c, c ^ d) for c in range(4)])  16 us
    ppermute x1, waiting for transfers between devices, transposed(): return lax.ppermute(block, ('ctx',) + HP, route)  13.8 us
    ppermute x10, waiting for transfers between devices, swapped(): return lax.ppermute(block, axis, [(0, 1), (1, 0)])  13.4 us
    ppermute x8, starting transfers between devices, brought_home(): lax.ppermute(whole, ('ctx',) + HP, [(4 * c + h, 4 * TURNS[c][k] + c) for...  10.4 us
    ppermute x8, waiting for transfers between devices, brought_home(): lax.ppermute(whole, ('ctx',) + HP, [(4 * c + h, 4 * TURNS[c][k] + c) for...  7.93 us
  transfers between devices with their start and end apart: 46, of which 26 were waited for; matrix products, arithmetic and copies ran while one was open for 10% of the time, Pallas kernels for 0%

profile of v3, /device:TPU:2, one launch (start us, length us, event | category | flops | bytes accessed | tf_op | source)
XLA Modules:
  0.0 295.6 jit_solution(6650040524653746260)
XLA Ops:
  1.5 3.5 %collective-permute-start = (bf16[2,128,256]{2,1,0:T(8,128)(2,1)S(1)}, bf16[2,128,256]{2,1,0:T(8,128)(2,1)S(1)}, u32[]{:S(2)}, u32[]{:S(2)}) collective-permute-start(bf16[2,128,256]{2,1,0:T(8,128)(2,1)S(1)} %pad_maximum_fusion.4), channel_id=1, source_target_pairs={{0,4},{4,8},{8,12},{1,5},{5,9},{9,13},{2,6},{6,10},{10,14},{3,7},{... | collective-permute-start | bytes 393224 | tf_op jit(solution)/shard_map/ppermute | solution.py:23
  5.0 4.5 %collective-permute-start.1 = (bf16[2,128,256]{2,1,0:T(8,128)(2,1)S(1)}, bf16[2,128,256]{2,1,0:T(8,128)(2,1)S(1)}, u32[]{:S(2)}, u32[]{:S(2)}) collective-permute-start(bf16[2,128,256]{2,1,0:T(8,128)(2,1)S(1)} %pad_maximum_fusion.4), channel_id=1, source_target_pairs={{0,8},{4,12},{1,9},{5,13},{2,10},{6,14},{3,11},{7,15},{16,24},{20,... | collective-permute-start | bytes 393224 | tf_op jit(solution)/shard_map/ppermute | solution.py:23
  13.4 1.4 collective-permute-done.2
  19.0 3.9 %collective-permute-start.3 = (bf16[128,1024]{1,0:T(8,128)(2,1)S(1)}, bf16[128,1024]{1,0:T(8,128)(2,1)S(1)}, u32[]{:S(2)}, u32[]{:S(2)}) collective-permute-start(bf16[128,1024]{1,0:T(8,128)(2,1)S(1)} %get-tuple-element.22), channel_id=1, source_target_pairs={{0,0},{1,4},{2,8},{3,12},{4,1},{5,5},{6,9},{7,13},{8,2},{9,6},{10,... | collective-permute-start | bytes 786440 | tf_op jit(solution)/shard_map/ppermute | solution.py:33
  22.9 13.8 %collective-permute-done.3 = bf16[128,1024]{1,0:T(8,128)(2,1)S(1)} collective-permute-done((bf16[128,1024]{1,0:T(8,128)(2,1)S(1)}, bf16[128,1024]{1,0:T(8,128)(2,1)S(1)}, u32[]{:S(2)}, u32[]{:S(2)}) %collective-permute-start.3) | collective-permute-done | bytes 262176 | tf_op jit(solution)/shard_map/ppermute | solution.py:33
  36.6 6.4 %collective-permute-done.4 = bf16[128,1024]{1,0:T(8,128)(2,1)S(1)} collective-permute-done((bf16[128,1024]{1,0:T(8,128)(2,1)S(1)}, bf16[128,1024]{1,0:T(8,128)(2,1)S(1)}, u32[]{:S(2)}, u32[]{:S(2)}) %collective-permute-start.4) | collective-permute-done | bytes 262176 | tf_op jit(solution)/shard_map/ppermute | solution.py:27
  43.2 1.8 collective-permute-done.5
  45.5 1.6 copy-done.5
  47.1 2.1 convolution_convert_fusion.1
  49.3 3.4 %collective-permute-start.6 = (bf16[128,1792]{1,0:T(8,128)(2,1)S(1)}, bf16[128,1792]{1,0:T(8,128)(2,1)S(1)}, u32[]{:S(2)}, u32[]{:S(2)}) collective-permute-start(bf16[128,1792]{1,0:T(8,128)(2,1)S(1)} %get-tuple-element.28), channel_id=1, source_target_pairs={{0,4},{4,8},{8,12},{1,5},{5,9},{9,13},{2,6},{6,10},{10,14},{3,7},{... | collective-permute-start | bytes 1376264 | tf_op jit(solution)/shard_map/ppermute | solution.py:23
  54.0 2.1 convolution_convert_fusion
  56.2 4.6 %collective-permute-start.14 = (bf16[128,1792]{1,0:T(8,128)(2,1)S(1)}, bf16[128,1792]{1,0:T(8,128)(2,1)S(1)}, u32[]{:S(2)}, u32[]{:S(2)}) collective-permute-start(bf16[128,1792]{1,0:T(8,128)(2,1)S(1)} %get-tuple-element.32), channel_id=1, source_target_pairs={{0,4},{4,8},{8,12},{1,5},{5,9},{9,13},{2,6},{6,10},{10,14},{3,7},{... | collective-permute-start | bytes 1376264 | tf_op jit(solution)/shard_map/ppermute | solution.py:23
  62.1 1.5 collective-permute-done.6
  63.7 4.4 %collective-permute-start.7 = (bf16[128,1792]{1,0:T(8,128)(2,1)S(1)}, bf16[128,1792]{1,0:T(8,128)(2,1)S(1)}, u32[]{:S(2)}, u32[]{:S(2)}) collective-permute-start(bf16[128,1792]{1,0:T(8,128)(2,1)S(1)} %fusion.19), channel_id=1, source_target_pairs={{0,4},{4,8},{8,12},{1,5},{5,9},{9,13},{2,6},{6,10},{10,14},{3,7},{... | collective-permute-start | bytes 1376264 | tf_op jit(solution)/shard_map/ppermute | solution.py:23
  68.1 5.3 %collective-permute-done.14 = bf16[128,1792]{1,0:T(8,128)(2,1)S(1)} collective-permute-done((bf16[128,1792]{1,0:T(8,128)(2,1)S(1)}, bf16[128,1792]{1,0:T(8,128)(2,1)S(1)}, u32[]{:S(2)}, u32[]{:S(2)}) %collective-permute-start.14) | collective-permute-done | bytes 458784 | tf_op jit(solution)/shard_map/ppermute | solution.py:23
  73.5 4.4 %collective-permute-start.15 = (bf16[128,1792]{1,0:T(8,128)(2,1)S(1)}, bf16[128,1792]{1,0:T(8,128)(2,1)S(1)}, u32[]{:S(2)}, u32[]{:S(2)}) collective-permute-start(bf16[128,1792]{1,0:T(8,128)(2,1)S(1)} %fusion.13), channel_id=1, source_target_pairs={{0,4},{4,8},{8,12},{1,5},{5,9},{9,13},{2,6},{6,10},{10,14},{3,7},{... | collective-permute-start | bytes 1376264 | tf_op jit(solution)/shard_map/ppermute | solution.py:23
  78.0 5.3 %collective-permute-done.7 = bf16[128,1792]{1,0:T(8,128)(2,1)S(1)} collective-permute-done((bf16[128,1792]{1,0:T(8,128)(2,1)S(1)}, bf16[128,1792]{1,0:T(8,128)(2,1)S(1)}, u32[]{:S(2)}, u32[]{:S(2)}) %collective-permute-start.7) | collective-permute-done | bytes 458784 | tf_op jit(solution)/shard_map/ppermute | solution.py:23
  85.5 5.8 %collective-permute-start.8 = (bf16[128,1792]{1,0:T(8,128)(2,1)}, bf16[128,1792]{1,0:T(8,128)(2,1)}, u32[]{:S(2)}, u32[]{:S(2)}) collective-permute-start(bf16[128,1792]{1,0:T(8,128)(2,1)} %get-tuple-element.26), channel_id=1, source_target_pairs={{0,4},{4,8},{8,12},{1,5},{5,9},{9,13},{2,6},{6,10},{10,14},{3,7},{... | collective-permute-start | bytes 1376264 | tf_op jit(solution)/shard_map/ppermute | solution.py:23
  91.4 1.7 collective-permute-done.15
  94.1 1.4 collective-permute-start.18
  95.5 5.8 %collective-permute-start.16 = (bf16[128,1792]{1,0:T(8,128)(2,1)}, bf16[128,1792]{1,0:T(8,128)(2,1)}, u32[]{:S(2)}, u32[]{:S(2)}) collective-permute-start(bf16[128,1792]{1,0:T(8,128)(2,1)} %get-tuple-element.30), channel_id=1, source_target_pairs={{0,4},{4,8},{8,12},{1,5},{5,9},{9,13},{2,6},{6,10},{10,14},{3,7},{... | collective-permute-start | bytes 1376264 | tf_op jit(solution)/shard_map/ppermute | solution.py:23
  102.2 1.4 collective-permute-start.11
  103.6 6.3 %collective-permute-done.18 = bf16[128,1792]{1,0:T(8,128)(2,1)S(1)} collective-permute-done((bf16[128,1792]{1,0:T(8,128)(2,1)S(1)}, bf16[128,1792]{1,0:T(8,128)(2,1)S(1)}, u32[]{:S(2)}, u32[]{:S(2)}) %collective-permute-start.18) | collective-permute-done | bytes 458784 | tf_op jit(solution)/shard_map/ppermute | solution.py:23
  114.7 1.5 copy.31
  117.0 2.9 collective-permute-done.11
  119.9 7.6 %collective-permute-done.19 = bf16[128,1792]{1,0:T(8,128)(2,1)} collective-permute-done((bf16[128,1792]{1,0:T(8,128)(2,1)}, bf16[128,1792]{1,0:T(8,128)(2,1)}, u32[]{:S(2)}, u32[]{:S(2)}) %collective-permute-start.19) | collective-permute-done | bytes 458784 | tf_op jit(solution)/shard_map/ppermute | solution.py:23
  127.5 3.0 %multiply_reduce_fusion.1 = (f32[128]{0:T(128)S(1)}, f32[]{:T(128)}, f32[128,1792]{1,0:T(8,128)S(1)}, f32[128,1792]{1,0:T(8,128)S(1)}) fusion(f32[128,1792]{1,0:T(8,128)S(1)} %copy.31, bf16[128,1792]{1,0:T(8,128)(2,1)S(1)} %copy-done.10, f32[128]{0:T(128)S(1)} %get-tuple-element.18, bf16[128,1792]{1,0:T(8,128)(2,1)} %collective-permute-done.19, ...), kind=kLoop, calls=%fused_computation.51 | loop fusion | flops 5046143 | bytes 5964808 | tf_op jit(solution)/shard_map/reduce_sum | solution.py:107
  130.8 1.7 copy-done.6
  135.1 1.5 collective-permute-start.23
  136.5 4.6 %collective-permute-start.24 = (bf16[128,5376]{1,0:T(8,128)(2,1)}, bf16[128,5376]{1,0:T(8,128)(2,1)S(1)}, u32[]{:S(2)}, u32[]{:S(2)}) collective-permute-start(bf16[128,5376]{1,0:T(8,128)(2,1)} %pad_maximum_fusion), channel_id=1, source_target_pairs={{0,4},{4,8},{8,12},{1,5},{5,9},{9,13},{2,6},{6,10},{10,14},{3,7},{... | collective-permute-start | bytes 4128776 | tf_op jit(solution)/shard_map/ppermute | solution.py:23
  144.0 2.2 select_convert_fusion.3
  147.2 3.3 %collective-permute-done.39 = f32[256]{0:T(256)S(1)} collective-permute-done((f32[256]{0:T(256)S(1)}, f32[256]{0:T(256)S(1)}, u32[]{:S(2)}, u32[]{:S(2)}) %collective-permute-start.39) | collective-permute-done | bytes 1056 | tf_op jit(solution)/shard_map/ppermute | solution.py:27
  151.0 1.6 collective-permute-start.40
  152.6 16.0 %collective-permute-done.40 = f32[128]{0:T(128)} collective-permute-done((f32[128]{0:T(128)}, f32[128]{0:T(128)}, u32[]{:S(2)}, u32[]{:S(2)}) %collective-permute-start.40) | collective-permute-done | bytes 544 | tf_op jit(solution)/shard_map/ppermute | solution.py:195
  169.3 2.1 collective-permute-start.41
  172.4 3.5 %collective-permute-start.21 = (bf16[128,1024]{1,0:T(8,128)(2,1)S(1)}, bf16[128,1024]{1,0:T(8,128)(2,1)S(1)}, u32[]{:S(2)}, u32[]{:S(2)}) collective-permute-start(bf16[128,1024]{1,0:T(8,128)(2,1)S(1)} %fusion.49), channel_id=1, source_target_pairs={{2,0},{1,3},{6,4},{5,7},{10,8},{9,11},{14,12},{13,15},{18,16},{17,... | collective-permute-start | bytes 786440 | tf_op jit(solution)/shard_map/ppermute | solution.py:178
  177.2 5.0 %collective-permute-start.26 = (bf16[128,5376]{1,0:T(8,128)(2,1)S(1)}, bf16[128,5376]{1,0:T(8,128)(2,1)S(1)}, u32[]{:S(2)}, u32[]{:S(2)}) collective-permute-start(bf16[128,5376]{1,0:T(8,128)(2,1)S(1)} %collective-permute-done.24), channel_id=1, source_target_pairs={{0,4},{4,8},{8,12},{1,5},{5,9},{9,13},{2,6},{6,10},{10,14},{3,7},{... | collective-permute-start | bytes 4128776 | tf_op jit(solution)/shard_map/ppermute | solution.py:23
  182.4 23.1 %collective-permute-done.25 = bf16[128,5376]{1,0:T(8,128)(2,1)S(1)} collective-permute-done((bf16[128,5376]{1,0:T(8,128)(2,1)S(1)}, bf16[128,5376]{1,0:T(8,128)(2,1)S(1)}, u32[]{:S(2)}, u32[]{:S(2)}) %collective-permute-start.25) | collective-permute-done | bytes 1376288 | tf_op jit(solution)/shard_map/ppermute | solution.py:23
  208.7 1.3 copy-done.7
  214.6 5.1 %collective-permute-start.31 = (bf16[128,5376]{1,0:T(8,128)(2,1)S(1)}, bf16[128,5376]{1,0:T(8,128)(2,1)S(1)}, u32[]{:S(2)}, u32[]{:S(2)}) collective-permute-start(bf16[128,5376]{1,0:T(8,128)(2,1)S(1)} %collective-permute-done.26), channel_id=1, source_target_pairs={{0,4},{4,8},{8,12},{1,5},{5,9},{9,13},{2,6},{6,10},{10,14},{3,7},{... | collective-permute-start | bytes 4128776 | tf_op jit(solution)/shard_map/ppermute | solution.py:23
  221.3 8.3 %collective-permute-done.28 = bf16[128,1024]{1,0:T(8,128)(2,1)S(1)} collective-permute-done((bf16[128,1024]{1,0:T(8,128)(2,1)S(1)}, bf16[128,1024]{1,0:T(8,128)(2,1)S(1)}, u32[]{:S(2)}, u32[]{:S(2)}) %collective-permute-start.28) | collective-permute-done | bytes 262176 | tf_op jit(solution)/shard_map/ppermute | solution.py:178
  230.4 18.1 %collective-permute-done.30 = bf16[128,5376]{1,0:T(8,128)(2,1)S(1)} collective-permute-done((bf16[128,5376]{1,0:T(8,128)(2,1)S(1)}, bf16[128,5376]{1,0:T(8,128)(2,1)S(1)}, u32[]{:S(2)}, u32[]{:S(2)}) %collective-permute-start.30) | collective-permute-done | bytes 1376288 | tf_op jit(solution)/shard_map/ppermute | solution.py:23
  259.7 9.6 %collective-permute-done.33 = bf16[128,1024]{1,0:T(8,128)(2,1)S(1)} collective-permute-done((bf16[128,1024]{1,0:T(8,128)(2,1)S(1)}, bf16[128,1024]{1,0:T(8,128)(2,1)S(1)}, u32[]{:S(2)}, u32[]{:S(2)}) %collective-permute-start.33) | collective-permute-done | bytes 262176 | tf_op jit(solution)/shard_map/ppermute | solution.py:178
  269.4 1.5 collective-permute-start.36
  271.0 3.7 %collective-permute-done.36 = bf16[128,1024]{1,0:T(8,128)(2,1)S(1)} collective-permute-done((bf16[128,1024]{1,0:T(8,128)(2,1)S(1)}, bf16[128,1024]{1,0:T(8,128)(2,1)S(1)}, u32[]{:S(2)}, u32[]{:S(2)}) %collective-permute-start.36) | collective-permute-done | bytes 262176 | tf_op jit(solution)/shard_map/ppermute | solution.py:178
  274.7 3.8 %collective-permute-start.43 = (bf16[128,1024]{1,0:T(8,128)(2,1)S(1)}, bf16[128,1024]{1,0:T(8,128)(2,1)S(1)}, u32[]{:S(2)}, u32[]{:S(2)}) collective-permute-start(bf16[128,1024]{1,0:T(8,128)(2,1)S(1)} %add_convert_fusion.2), channel_id=1, source_target_pairs={{2,4},{6,9},{10,6},{14,11},{18,20},{22,25},{26,22},{30,27}} | collective-permute-start | bytes 786440 | tf_op jit(solution)/shard_map/ppermute | solution.py:180
  278.7 1.9 collective-permute-start.34
  285.3 7.9 %collective-permute-done.34 = bf16[128,1024]{1,0:T(8,128)(2,1)S(1)} collective-permute-done((bf16[128,1024]{1,0:T(8,128)(2,1)S(1)}, bf16[128,1024]{1,0:T(8,128)(2,1)S(1)}, u32[]{:S(2)}, u32[]{:S(2)}) %collective-permute-start.34) | collective-permute-done | bytes 262176 | tf_op jit(solution)/shard_map/ppermute | solution.py:180
  (149 shorter events, 57.6 us)
Async XLA Ops:
  1.5 11.6 %collective-permute-start = (bf16[2,128,256]{2,1,0:T(8,128)(2,1)S(1)}, bf16[2,128,256]{2,1,0:T(8,128)(2,1)S(1)}, u32[]{:S(2)}, u32[]{:S(2)}) collective-permute-start(bf16[2,128,256]{2,1,0:T(8,128)(2,1)S(1)} %pad_maximum_fusion.4), channel_id=1, source_target_pairs={{0,4},{4,8},{8,12},{1,5},{5,9},{9,13},{2,6},{6,10},{10,14},{3,7},{... | collective-permute-start | bytes 393224 | tf_op jit(solution)/shard_map/ppermute | solution.py:23
  5.0 8.4 %collective-permute-start.1 = (bf16[2,128,256]{2,1,0:T(8,128)(2,1)S(1)}, bf16[2,128,256]{2,1,0:T(8,128)(2,1)S(1)}, u32[]{:S(2)}, u32[]{:S(2)}) collective-permute-start(bf16[2,128,256]{2,1,0:T(8,128)(2,1)S(1)} %pad_maximum_fusion.4), channel_id=1, source_target_pairs={{0,8},{4,12},{1,9},{5,13},{2,10},{6,14},{3,11},{7,15},{16,24},{20,... | collective-permute-start | bytes 393224 | tf_op jit(solution)/shard_map/ppermute | solution.py:23
  9.5 5.3 %collective-permute-start.2 = (bf16[2,128,256]{2,1,0:T(8,128)(2,1)S(1)}, bf16[2,128,256]{2,1,0:T(8,128)(2,1)S(1)}, u32[]{:S(2)}, u32[]{:S(2)}) collective-permute-start(bf16[2,128,256]{2,1,0:T(8,128)(2,1)S(1)} %pad_maximum_fusion.4), channel_id=1, source_target_pairs={{0,12},{1,13},{2,14},{3,15},{16,28},{17,29},{18,30},{19,31}} | collective-permute-start | bytes 393224 | tf_op jit(solution)/shard_map/ppermute | solution.py:23
  19.0 17.7 %collective-permute-start.3 = (bf16[128,1024]{1,0:T(8,128)(2,1)S(1)}, bf16[128,1024]{1,0:T(8,128)(2,1)S(1)}, u32[]{:S(2)}, u32[]{:S(2)}) collective-permute-start(bf16[128,1024]{1,0:T(8,128)(2,1)S(1)} %get-tuple-element.22), channel_id=1, source_target_pairs={{0,0},{1,4},{2,8},{3,12},{4,1},{5,5},{6,9},{7,13},{8,2},{9,6},{10,... | collective-permute-start | bytes 786440 | tf_op jit(solution)/shard_map/ppermute | solution.py:33
  36.6 6.4 %collective-permute-start.4 = (bf16[128,1024]{1,0:T(8,128)(2,1)S(1)}, bf16[128,1024]{1,0:T(8,128)(2,1)S(1)}, u32[]{:S(2)}, u32[]{:S(2)}) collective-permute-start(bf16[128,1024]{1,0:T(8,128)(2,1)S(1)} %collective-permute-done.3), channel_id=1, source_target_pairs={{0,2},{2,0},{1,3},{3,1},{4,6},{6,4},{5,7},{7,5},{8,10},{10,8},{9,1... | collective-permute-start | bytes 786440 | tf_op jit(solution)/shard_map/ppermute | solution.py:27
  43.1 2.0 collective-permute-start.5
  49.3 14.3 %collective-permute-start.6 = (bf16[128,1792]{1,0:T(8,128)(2,1)S(1)}, bf16[128,1792]{1,0:T(8,128)(2,1)S(1)}, u32[]{:S(2)}, u32[]{:S(2)}) collective-permute-start(bf16[128,1792]{1,0:T(8,128)(2,1)S(1)} %get-tuple-element.28), channel_id=1, source_target_pairs={{0,4},{4,8},{8,12},{1,5},{5,9},{9,13},{2,6},{6,10},{10,14},{3,7},{... | collective-permute-start | bytes 1376264 | tf_op jit(solution)/shard_map/ppermute | solution.py:23
  52.7 25.2 %collective-permute-start.9 = (bf16[128,1792]{1,0:T(8,128)(2,1)S(1)}, bf16[128,1792]{1,0:T(8,128)(2,1)S(1)}, u32[]{:S(2)}, u32[]{:S(2)}) collective-permute-start(bf16[128,1792]{1,0:T(8,128)(2,1)S(1)} %get-tuple-element.29), channel_id=1, source_target_pairs={{4,0},{8,4},{12,8},{5,1},{9,5},{13,9},{6,2},{10,6},{14,10},{7,3},{... | collective-permute-start | bytes 1376264 | tf_op jit(solution)/shard_map/ppermute | solution.py:23
  56.1 53.8 %copy-start.8 = (bf16[512,1792]{1,0:T(8,128)(2,1)}, bf16[512,1792]{1,0:T(8,128)(2,1)S(1)}, u32[]{:S(2)}) copy-start(bf16[512,1792]{1,0:T(8,128)(2,1)S(1)} %convolution_convert_fusion) | copy-start | bytes 5505028
  56.2 17.2 %collective-permute-start.14 = (bf16[128,1792]{1,0:T(8,128)(2,1)S(1)}, bf16[128,1792]{1,0:T(8,128)(2,1)S(1)}, u32[]{:S(2)}, u32[]{:S(2)}) collective-permute-start(bf16[128,1792]{1,0:T(8,128)(2,1)S(1)} %get-tuple-element.32), channel_id=1, source_target_pairs={{0,4},{4,8},{8,12},{1,5},{5,9},{9,13},{2,6},{6,10},{10,14},{3,7},{... | collective-permute-start | bytes 1376264 | tf_op jit(solution)/shard_map/ppermute | solution.py:23
  60.8 30.6 %collective-permute-start.17 = (bf16[128,1792]{1,0:T(8,128)(2,1)S(1)}, bf16[128,1792]{1,0:T(8,128)(2,1)S(1)}, u32[]{:S(2)}, u32[]{:S(2)}) collective-permute-start(bf16[128,1792]{1,0:T(8,128)(2,1)S(1)} %get-tuple-element.33), channel_id=1, source_target_pairs={{4,0},{8,4},{12,8},{5,1},{9,5},{13,9},{6,2},{10,6},{14,10},{7,3},{... | collective-permute-start | bytes 1376264 | tf_op jit(solution)/shard_map/ppermute | solution.py:23
  63.7 19.5 %collective-permute-start.7 = (bf16[128,1792]{1,0:T(8,128)(2,1)S(1)}, bf16[128,1792]{1,0:T(8,128)(2,1)S(1)}, u32[]{:S(2)}, u32[]{:S(2)}) collective-permute-start(bf16[128,1792]{1,0:T(8,128)(2,1)S(1)} %fusion.19), channel_id=1, source_target_pairs={{0,4},{4,8},{8,12},{1,5},{5,9},{9,13},{2,6},{6,10},{10,14},{3,7},{... | collective-permute-start | bytes 1376264 | tf_op jit(solution)/shard_map/ppermute | solution.py:23
  73.5 19.5 %collective-permute-start.15 = (bf16[128,1792]{1,0:T(8,128)(2,1)S(1)}, bf16[128,1792]{1,0:T(8,128)(2,1)S(1)}, u32[]{:S(2)}, u32[]{:S(2)}) collective-permute-start(bf16[128,1792]{1,0:T(8,128)(2,1)S(1)} %fusion.13), channel_id=1, source_target_pairs={{0,4},{4,8},{8,12},{1,5},{5,9},{9,13},{2,6},{6,10},{10,14},{3,7},{... | collective-permute-start | bytes 1376264 | tf_op jit(solution)/shard_map/ppermute | solution.py:23
  84.3 17.0 %collective-permute-start.10 = (bf16[128,1792]{1,0:T(8,128)(2,1)S(1)}, bf16[128,1792]{1,0:T(8,128)(2,1)S(1)}, u32[]{:S(2)}, u32[]{:S(2)}) collective-permute-start(bf16[128,1792]{1,0:T(8,128)(2,1)S(1)} %get-tuple-element.27), channel_id=1, source_target_pairs={{4,0},{8,4},{12,8},{5,1},{9,5},{13,9},{6,2},{10,6},{14,10},{7,3},{... | collective-permute-start | bytes 1376264 | tf_op jit(solution)/shard_map/ppermute | solution.py:23
  85.5 31.4 %collective-permute-start.8 = (bf16[128,1792]{1,0:T(8,128)(2,1)}, bf16[128,1792]{1,0:T(8,128)(2,1)}, u32[]{:S(2)}, u32[]{:S(2)}) collective-permute-start(bf16[128,1792]{1,0:T(8,128)(2,1)} %get-tuple-element.26), channel_id=1, source_target_pairs={{0,4},{4,8},{8,12},{1,5},{5,9},{9,13},{2,6},{6,10},{10,14},{3,7},{... | collective-permute-start | bytes 1376264 | tf_op jit(solution)/shard_map/ppermute | solution.py:23
  94.1 15.9 %collective-permute-start.18 = (bf16[128,1792]{1,0:T(8,128)(2,1)S(1)}, bf16[128,1792]{1,0:T(8,128)(2,1)S(1)}, u32[]{:S(2)}, u32[]{:S(2)}) collective-permute-start(bf16[128,1792]{1,0:T(8,128)(2,1)S(1)} %get-tuple-element.31), channel_id=1, source_target_pairs={{4,0},{8,4},{12,8},{5,1},{9,5},{13,9},{6,2},{10,6},{14,10},{7,3},{... | collective-permute-start | bytes 1376264 | tf_op jit(solution)/shard_map/ppermute | solution.py:23
  95.5 21.5 %collective-permute-start.16 = (bf16[128,1792]{1,0:T(8,128)(2,1)}, bf16[128,1792]{1,0:T(8,128)(2,1)}, u32[]{:S(2)}, u32[]{:S(2)}) collective-permute-start(bf16[128,1792]{1,0:T(8,128)(2,1)} %get-tuple-element.30), channel_id=1, source_target_pairs={{0,4},{4,8},{8,12},{1,5},{5,9},{9,13},{2,6},{6,10},{10,14},{3,7},{... | collective-permute-start | bytes 1376264 | tf_op jit(solution)/shard_map/ppermute | solution.py:23
  102.2 17.7 %collective-permute-start.11 = (bf16[128,1792]{1,0:T(8,128)(2,1)}, bf16[128,1792]{1,0:T(8,128)(2,1)}, u32[]{:S(2)}, u32[]{:S(2)}) collective-permute-start(bf16[128,1792]{1,0:T(8,128)(2,1)} %fusion.18), channel_id=1, source_target_pairs={{4,0},{8,4},{12,8},{5,1},{9,5},{13,9},{6,2},{10,6},{14,10},{7,3},{... | collective-permute-start | bytes 1376264 | tf_op jit(solution)/shard_map/ppermute | solution.py:23
  110.8 16.6 %collective-permute-start.19 = (bf16[128,1792]{1,0:T(8,128)(2,1)}, bf16[128,1792]{1,0:T(8,128)(2,1)}, u32[]{:S(2)}, u32[]{:S(2)}) collective-permute-start(bf16[128,1792]{1,0:T(8,128)(2,1)} %fusion.12), channel_id=1, source_target_pairs={{4,0},{8,4},{12,8},{5,1},{9,5},{13,9},{6,2},{10,6},{14,10},{7,3},{... | collective-permute-start | bytes 1376264 | tf_op jit(solution)/shard_map/ppermute | solution.py:23
  112.1 1.2 collective-permute-start.12
  113.4 3.6 %collective-permute-start.13 = (f32[128]{0:T(128)S(1)}, f32[128]{0:T(128)S(1)}, u32[]{:S(2)}, u32[]{:S(2)}) collective-permute-start(f32[128]{0:T(128)S(1)} %add.244), channel_id=1, source_target_pairs={{0,2},{2,0},{1,3},{3,1},{4,6},{6,4},{5,7},{7,5},{8,10},{10,8},{9,1... | collective-permute-start | bytes 1544 | tf_op jit(solution)/shard_map/ppermute | solution.py:27
  135.1 40.8 %collective-permute-start.23 = (bf16[128,5376]{1,0:T(8,128)(2,1)}, bf16[128,5376]{1,0:T(8,128)(2,1)S(1)}, u32[]{:S(2)}, u32[]{:S(2)}) collective-permute-start(bf16[128,5376]{1,0:T(8,128)(2,1)} %pad_maximum_fusion), channel_id=1, source_target_pairs={{4,0},{8,4},{12,8},{5,1},{9,5},{13,9},{6,2},{10,6},{14,10},{7,3},{... | collective-permute-start | bytes 4128776 | tf_op jit(solution)/shard_map/ppermute | solution.py:23
  136.5 40.7 %collective-permute-start.24 = (bf16[128,5376]{1,0:T(8,128)(2,1)}, bf16[128,5376]{1,0:T(8,128)(2,1)S(1)}, u32[]{:S(2)}, u32[]{:S(2)}) collective-permute-start(bf16[128,5376]{1,0:T(8,128)(2,1)} %pad_maximum_fusion), channel_id=1, source_target_pairs={{0,4},{4,8},{8,12},{1,5},{5,9},{9,13},{2,6},{6,10},{10,14},{3,7},{... | collective-permute-start | bytes 4128776 | tf_op jit(solution)/shard_map/ppermute | solution.py:23
  141.9 4.2 %collective-permute-start.38 = (f32[256]{0:T(256)S(1)}, f32[256]{0:T(256)S(1)}, u32[]{:S(2)}, u32[]{:S(2)}) collective-permute-start(f32[256]{0:T(256)S(1)} %pad_maximum_fusion.5), channel_id=1, source_target_pairs={{0,1},{1,0},{2,3},{3,2},{4,5},{5,4},{6,7},{7,6},{8,9},{9,8},{10,11... | collective-permute-start | bytes 3080 | tf_op jit(solution)/shard_map/ppermute | solution.py:27
  146.2 25.2 %collective-permute-start.20 = (bf16[128,1024]{1,0:T(8,128)(2,1)}, bf16[128,1024]{1,0:T(8,128)(2,1)}, u32[]{:S(2)}, u32[]{:S(2)}) collective-permute-start(bf16[128,1024]{1,0:T(8,128)(2,1)} %get-tuple-element.54), channel_id=1, source_target_pairs={{0,1},{1,0},{2,3},{3,2},{4,5},{5,4},{6,7},{7,6},{8,9},{9,8},{10,11... | collective-permute-start | bytes 786440 | tf_op jit(solution)/shard_map/ppermute | solution.py:27
  146.9 3.6 %collective-permute-start.39 = (f32[256]{0:T(256)S(1)}, f32[256]{0:T(256)S(1)}, u32[]{:S(2)}, u32[]{:S(2)}) collective-permute-start(f32[256]{0:T(256)S(1)} %fusion.96), channel_id=1, source_target_pairs={{0,2},{2,0},{1,3},{3,1},{4,6},{6,4},{5,7},{7,5},{8,10},{10,8},{9,1... | collective-permute-start | bytes 3080 | tf_op jit(solution)/shard_map/ppermute | solution.py:27
  151.0 17.6 %collective-permute-start.40 = (f32[128]{0:T(128)}, f32[128]{0:T(128)}, u32[]{:S(2)}, u32[]{:S(2)}) collective-permute-start(f32[128]{0:T(128)} %slice.90), channel_id=1, source_target_pairs={{0,4},{4,0},{8,12},{12,8},{1,5},{5,1},{9,13},{13,9},{2,6},{6,2},{1... | collective-permute-start | bytes 1544 | tf_op jit(solution)/shard_map/ppermute | solution.py:195
  169.3 109.4 %collective-permute-start.41 = (f32[128]{0:T(128)S(1)}, f32[128]{0:T(128)S(1)}, u32[]{:S(2)}, u32[]{:S(2)}) collective-permute-start(f32[128]{0:T(128)S(1)} %get-tuple-element.45), channel_id=1, source_target_pairs={{0,8},{4,12},{8,0},{12,4},{1,9},{5,13},{9,1},{13,5},{2,10},{6,14},... | collective-permute-start | bytes 1544 | tf_op jit(solution)/shard_map/ppermute | solution.py:195
  172.4 34.3 %copy-start.2 = (bf16[1024,1792]{1,0:T(8,128)(2,1)S(1)}, bf16[1024,1792]{1,0:T(8,128)(2,1)}, u32[]{:S(2)}) copy-start(bf16[1024,1792]{1,0:T(8,128)(2,1)} %param.18) | copy-start | bytes 11010052
  172.4 39.1 %collective-permute-start.21 = (bf16[128,1024]{1,0:T(8,128)(2,1)S(1)}, bf16[128,1024]{1,0:T(8,128)(2,1)S(1)}, u32[]{:S(2)}, u32[]{:S(2)}) collective-permute-start(bf16[128,1024]{1,0:T(8,128)(2,1)S(1)} %fusion.49), channel_id=1, source_target_pairs={{2,0},{1,3},{6,4},{5,7},{10,8},{9,11},{14,12},{13,15},{18,16},{17,... | collective-permute-start | bytes 786440 | tf_op jit(solution)/shard_map/ppermute | solution.py:178
  175.9 29.6 %collective-permute-start.25 = (bf16[128,5376]{1,0:T(8,128)(2,1)S(1)}, bf16[128,5376]{1,0:T(8,128)(2,1)S(1)}, u32[]{:S(2)}, u32[]{:S(2)}) collective-permute-start(bf16[128,5376]{1,0:T(8,128)(2,1)S(1)} %collective-permute-done.23), channel_id=1, source_target_pairs={{4,0},{8,4},{12,8},{5,1},{9,5},{13,9},{6,2},{10,6},{14,10},{7,3},{... | collective-permute-start | bytes 4128776 | tf_op jit(solution)/shard_map/ppermute | solution.py:23
  177.2 29.5 %collective-permute-start.26 = (bf16[128,5376]{1,0:T(8,128)(2,1)S(1)}, bf16[128,5376]{1,0:T(8,128)(2,1)S(1)}, u32[]{:S(2)}, u32[]{:S(2)}) collective-permute-start(bf16[128,5376]{1,0:T(8,128)(2,1)S(1)} %collective-permute-done.24), channel_id=1, source_target_pairs={{0,4},{4,8},{8,12},{1,5},{5,9},{9,13},{2,6},{6,10},{10,14},{3,7},{... | collective-permute-start | bytes 4128776 | tf_op jit(solution)/shard_map/ppermute | solution.py:23
  211.4 8.3 %collective-permute-start.27 = (bf16[128,1024]{1,0:T(8,128)(2,1)S(1)}, bf16[128,1024]{1,0:T(8,128)(2,1)S(1)}, u32[]{:S(2)}, u32[]{:S(2)}) collective-permute-start(bf16[128,1024]{1,0:T(8,128)(2,1)S(1)} %get-tuple-element.52), channel_id=1, source_target_pairs={{0,1},{1,0},{2,3},{3,2},{4,5},{5,4},{6,7},{7,6},{8,9},{9,8},{10,11... | collective-permute-start | bytes 786440 | tf_op jit(solution)/shard_map/ppermute | solution.py:27
  212.6 68.0 %collective-permute-start.22 = (bf16[128,1024]{1,0:T(8,128)(2,1)S(1)}, bf16[128,1024]{1,0:T(8,128)(2,1)S(1)}, u32[]{:S(2)}, u32[]{:S(2)}) collective-permute-start(bf16[128,1024]{1,0:T(8,128)(2,1)S(1)} %add_convert_fusion.3), channel_id=1, source_target_pairs={{0,0},{4,5},{8,10},{12,15},{16,16},{20,21},{24,26},{28,31}} | collective-permute-start | bytes 786440 | tf_op jit(solution)/shard_map/ppermute | solution.py:180
  213.3 35.2 %collective-permute-start.30 = (bf16[128,5376]{1,0:T(8,128)(2,1)S(1)}, bf16[128,5376]{1,0:T(8,128)(2,1)S(1)}, u32[]{:S(2)}, u32[]{:S(2)}) collective-permute-start(bf16[128,5376]{1,0:T(8,128)(2,1)S(1)} %collective-permute-done.25), channel_id=1, source_target_pairs={{4,0},{8,4},{12,8},{5,1},{9,5},{13,9},{6,2},{10,6},{14,10},{7,3},{... | collective-permute-start | bytes 4128776 | tf_op jit(solution)/shard_map/ppermute | solution.py:23
  214.6 35.1 %collective-permute-start.31 = (bf16[128,5376]{1,0:T(8,128)(2,1)S(1)}, bf16[128,5376]{1,0:T(8,128)(2,1)S(1)}, u32[]{:S(2)}, u32[]{:S(2)}) collective-permute-start(bf16[128,5376]{1,0:T(8,128)(2,1)S(1)} %collective-permute-done.26), channel_id=1, source_target_pairs={{0,4},{4,8},{8,12},{1,5},{5,9},{9,13},{2,6},{6,10},{10,14},{3,7},{... | collective-permute-start | bytes 4128776 | tf_op jit(solution)/shard_map/ppermute | solution.py:23
  219.8 9.7 %collective-permute-start.28 = (bf16[128,1024]{1,0:T(8,128)(2,1)S(1)}, bf16[128,1024]{1,0:T(8,128)(2,1)S(1)}, u32[]{:S(2)}, u32[]{:S(2)}) collective-permute-start(bf16[128,1024]{1,0:T(8,128)(2,1)S(1)} %fusion.50), channel_id=1, source_target_pairs={{3,1},{0,2},{7,5},{4,6},{11,9},{8,10},{15,13},{12,14},{19,17},{16,... | collective-permute-start | bytes 786440 | tf_op jit(solution)/shard_map/ppermute | solution.py:178
  229.6 52.4 %collective-permute-start.42 = (bf16[128,1024]{1,0:T(8,128)(2,1)S(1)}, bf16[128,1024]{1,0:T(8,128)(2,1)S(1)}, u32[]{:S(2)}, u32[]{:S(2)}) collective-permute-start(bf16[128,1024]{1,0:T(8,128)(2,1)S(1)} %add_convert_fusion.3), channel_id=1, source_target_pairs={{3,0},{7,5},{11,10},{15,15},{19,16},{23,21},{27,26},{31,31}} | collective-permute-start | bytes 786440 | tf_op jit(solution)/shard_map/ppermute | solution.py:180
  248.5 34.1 %collective-permute-start.29 = (bf16[128,1024]{1,0:T(8,128)(2,1)S(1)}, bf16[128,1024]{1,0:T(8,128)(2,1)S(1)}, u32[]{:S(2)}, u32[]{:S(2)}) collective-permute-start(bf16[128,1024]{1,0:T(8,128)(2,1)S(1)} %add_convert_fusion.2), channel_id=1, source_target_pairs={{1,4},{5,9},{9,6},{13,11},{17,20},{21,25},{25,22},{29,27}} | collective-permute-start | bytes 786440 | tf_op jit(solution)/shard_map/ppermute | solution.py:180
  255.2 1.6 collective-permute-start.32
  256.8 1.5 collective-permute-start.35
  258.3 11.0 %collective-permute-start.33 = (bf16[128,1024]{1,0:T(8,128)(2,1)S(1)}, bf16[128,1024]{1,0:T(8,128)(2,1)S(1)}, u32[]{:S(2)}, u32[]{:S(2)}) collective-permute-start(bf16[128,1024]{1,0:T(8,128)(2,1)S(1)} %fusion.51), channel_id=1, source_target_pairs={{0,2},{3,1},{4,6},{7,5},{8,10},{11,9},{12,14},{15,13},{16,18},{19,... | collective-permute-start | bytes 786440 | tf_op jit(solution)/shard_map/ppermute | solution.py:178
  269.4 5.3 %collective-permute-start.36 = (bf16[128,1024]{1,0:T(8,128)(2,1)S(1)}, bf16[128,1024]{1,0:T(8,128)(2,1)S(1)}, u32[]{:S(2)}, u32[]{:S(2)}) collective-permute-start(bf16[128,1024]{1,0:T(8,128)(2,1)S(1)} %fusion.52), channel_id=1, source_target_pairs={{1,3},{2,0},{5,7},{6,4},{9,11},{10,8},{13,15},{14,12},{17,19},{18,... | collective-permute-start | bytes 786440 | tf_op jit(solution)/shard_map/ppermute | solution.py:178
  274.7 10.6 %collective-permute-start.43 = (bf16[128,1024]{1,0:T(8,128)(2,1)S(1)}, bf16[128,1024]{1,0:T(8,128)(2,1)S(1)}, u32[]{:S(2)}, u32[]{:S(2)}) collective-permute-start(bf16[128,1024]{1,0:T(8,128)(2,1)S(1)} %add_convert_fusion.2), channel_id=1, source_target_pairs={{2,4},{6,9},{10,6},{14,11},{18,20},{22,25},{26,22},{30,27}} | collective-permute-start | bytes 786440 | tf_op jit(solution)/shard_map/ppermute | solution.py:180
  278.7 14.5 %collective-permute-start.34 = (bf16[128,1024]{1,0:T(8,128)(2,1)S(1)}, bf16[128,1024]{1,0:T(8,128)(2,1)S(1)}, u32[]{:S(2)}, u32[]{:S(2)}) collective-permute-start(bf16[128,1024]{1,0:T(8,128)(2,1)S(1)} %add_convert_fusion.1), channel_id=1, source_target_pairs={{2,8},{6,13},{10,2},{14,7},{18,24},{22,29},{26,18},{30,23}} | collective-permute-start | bytes 786440 | tf_op jit(solution)/shard_map/ppermute | solution.py:180
  280.6 12.6 %collective-permute-start.44 = (bf16[128,1024]{1,0:T(8,128)(2,1)S(1)}, bf16[128,1024]{1,0:T(8,128)(2,1)S(1)}, u32[]{:S(2)}, u32[]{:S(2)}) collective-permute-start(bf16[128,1024]{1,0:T(8,128)(2,1)S(1)} %add_convert_fusion.1), channel_id=1, source_target_pairs={{1,8},{5,13},{9,2},{13,7},{17,24},{21,29},{25,18},{29,23}} | collective-permute-start | bytes 786440 | tf_op jit(solution)/shard_map/ppermute | solution.py:180
  281.9 11.2 %collective-permute-start.37 = (bf16[128,1024]{1,0:T(8,128)(2,1)S(1)}, bf16[128,1024]{1,0:T(8,128)(2,1)S(1)}, u32[]{:S(2)}, u32[]{:S(2)}) collective-permute-start(bf16[128,1024]{1,0:T(8,128)(2,1)S(1)} %add_convert_fusion), channel_id=1, source_target_pairs={{3,12},{7,1},{11,14},{15,3},{19,28},{23,17},{27,30},{31,19}} | collective-permute-start | bytes 786440 | tf_op jit(solution)/shard_map/ppermute | solution.py:180
  282.6 10.6 %collective-permute-start.45 = (bf16[128,1024]{1,0:T(8,128)(2,1)S(1)}, bf16[128,1024]{1,0:T(8,128)(2,1)S(1)}, u32[]{:S(2)}, u32[]{:S(2)}) collective-permute-start(bf16[128,1024]{1,0:T(8,128)(2,1)S(1)} %add_convert_fusion), channel_id=1, source_target_pairs={{0,12},{4,1},{8,14},{12,3},{16,28},{20,17},{24,30},{28,19}} | collective-permute-start | bytes 786440 | tf_op jit(solution)/shard_map/ppermute | solution.py:180
  (12 other events, 120.8 us)

commit v4 on v3

--- a/solution.py
+++ b/solution.py
@@ -131,6 +131,7 @@
     tile = transposed(residual)
     own_wide = residual.astype(F32)
     mean = summed_over_hp(jnp.sum(own_wide * own_wide, axis=1)) / D
+    tile, mean = lax.optimization_barrier((tile, mean))
     rms = jnp.sqrt(mean + 1e-05)[:, None]
     across = swapped(tile, "head")
     both = swapped(jnp.stack([tile, across]), "pair")
@@ -150,6 +151,7 @@
             if s > 0:
                 right = (right.astype(F32) + came[i][0].astype(F32)).astype(BF16)
                 left = (left.astype(F32) + came[i][1].astype(F32)).astype(BF16)
+            right, left = lax.optimization_barrier((right, left))
             came[i] = [shifted(right, 1), shifted(left, -1)]
     gate_proj, up_proj = [
         (picked(parts[i], z ^ hp).astype(F32) + came[i][0].astype(F32) + came[i][1].astype(F32)) / rms
@@ -163,12 +165,12 @@
         right.append(shifted(right[s], 1))
         left.append(shifted(left[s], -1))
     turns = [owned, jnp.where(low, left[0], right[0])]
-    first, second = lax.optimization_barrier((turns[1], (left[1], right[1])))
-    turns = [owned, first, jnp.where(low, *second)]
-    second, third = lax.optimization_barrier((turns[2], (left[2], right[2])))
-    outer = jnp.where(low, *third)
+    _, arrived = lax.optimization_barrier((turns[1], (left[1], right[1])))
+    turns.append(jnp.where(low, *arrived))
+    _, arrived = lax.optimization_barrier((turns[2], (left[2], right[2])))
+    outer = jnp.where(low, *arrived)
     inward = jnp.where(low, right[0], left[0])
-    turns = [owned, first, second, jnp.where((z == 0) | (z == 3), outer, inward)]
+    turns.append(jnp.where((z == 0) | (z == 3), outer, inward))
 
     def brought_home(k, down, grad):
         keeps_down = pair == (k & 1)
@@ -190,7 +192,7 @@
     count = jnp.sum(keep_tiles.astype(F32)) * TILE
     small = jnp.concatenate([inner, loss[None], count[None], jnp.zeros(126, F32)])
     small = summed_over_hp(small)
-    totals = small[rows:]
+    totals, _ = lax.optimization_barrier((small[rows:], turns[3]))
     for d in (1, 2):
         totals = totals + lax.ppermute(totals, "ctx", [(c, c ^ d) for c in range(4)])
     loss_value = (totals[0] / totals[1]).reshape(1)

time: 300 us -> 271 us (0.903)
  waiting for transfers between devices: 148 us -> 128 us
  other arithmetic: 19.5 us -> 16.1 us
    ppermute x2, waiting for transfers between devices: 16 us -> 0.01 us  [on_square(): lax.ppermute(totals, 'ctx', [(c, c ^ d) for c in range(4)])]
    ppermute x21, waiting for transfers between devices: 75.3 us -> 87.4 us  [passed_along(): return lax.ppermute(block, axis, route)]
    ppermute x21, starting transfers between devices: 64.5 us -> 54 us  [passed_along(): return lax.ppermute(block, axis, route)]
    ppermute x4, waiting for transfers between devices: 21.6 us -> 12.7 us  [brought_home(): lax.ppermute(half.astype(BF16), HP, route).astype(F32)]
    ppermute x1, waiting for transfers between devices: 13.8 us -> 6.18 us  [transposed(): return lax.ppermute(block, ('ctx',) + HP, route)]
    ppermute x1, starting transfers between devices: 3.87 us -> 8.02 us  [transposed(): return lax.ppermute(block, ('ctx',) + HP, route)]
    unnamed x30 -> x24, local copies, waits for them, and re-layouts: 6.61 us -> 3.41 us
  transfers between devices with their start and end apart: 46 -> 46, of which waited for: 26 -> 31; matrix products, arithmetic and copies ran while one was open for 10% -> 10% of each run, Pallas kernels for 0% -> 0%
where the time goes in v4:
time: 271 us; the launch traced here: 267 us
  waiting for transfers between devices  128 us (47%)
  starting transfers between devices  89.2 us (33%)
  matrix products  19.6 us (7%)
  other arithmetic  16.1 us (6%)
  local copies, waits for them, and re-layouts  9 us (3%)
  between operations  4.71 us (2%)
    ppermute x21, waiting for transfers between devices, passed_along(): return lax.ppermute(block, axis, route)  87.4 us
    ppermute x21, starting transfers between devices, passed_along(): return lax.ppermute(block, axis, route)  54 us
    ppermute x10, waiting for transfers between devices, swapped(): return lax.ppermute(block, axis, [(0, 1), (1, 0)])  14.3 us
    ppermute x4, waiting for transfers between devices, brought_home(): lax.ppermute(half.astype(BF16), HP, route).astype(F32)  12.7 us
    ppermute x8, starting transfers between devices, brought_home(): lax.ppermute(whole, ('ctx',) + HP, [(4 * c + h, 4 * TURNS[c][k] + c) for...  12.6 us
    ppermute x1, starting transfers between devices, transposed(): return lax.ppermute(block, ('ctx',) + HP, route)  8.02 us
    ppermute x8, waiting for transfers between devices, brought_home(): lax.ppermute(whole, ('ctx',) + HP, [(4 * c + h, 4 * TURNS[c][k] + c) for...  7.72 us
    ppermute x4, starting transfers between devices, brought_home(): lax.ppermute(half.astype(BF16), HP, route).astype(F32)  7.2 us
  transfers between devices with their start and end apart: 46, of which 31 were waited for; matrix products, arithmetic and copies ran while one was open for 10% of the time, Pallas kernels for 0%

profile of v4, /device:TPU:2, one launch (start us, length us, event | category | flops | bytes accessed | tf_op | source)
XLA Modules:
  0.0 267.0 jit_solution(10713483981621688991)
XLA Ops:
  1.5 5.5 %collective-permute-start.2 = (bf16[2,128,256]{2,1,0:T(8,128)(2,1)S(1)}, bf16[2,128,256]{2,1,0:T(8,128)(2,1)S(1)}, u32[]{:S(2)}, u32[]{:S(2)}) collective-permute-start(bf16[2,128,256]{2,1,0:T(8,128)(2,1)S(1)} %pad_maximum_fusion.4), channel_id=1, source_target_pairs={{0,12},{1,13},{2,14},{3,15},{16,28},{17,29},{18,30},{19,31}} | collective-permute-start | bytes 393224 | tf_op jit(solution)/shard_map/ppermute | solution.py:23
  8.3 2.5 collective-permute-start
  13.8 1.7 collective-permute-done
  19.6 8.0 %collective-permute-start.3 = (bf16[128,1024]{1,0:T(8,128)(2,1)S(1)}, bf16[128,1024]{1,0:T(8,128)(2,1)S(1)}, u32[]{:S(2)}, u32[]{:S(2)}) collective-permute-start(bf16[128,1024]{1,0:T(8,128)(2,1)S(1)} %get-tuple-element.46), channel_id=1, source_target_pairs={{0,0},{1,4},{2,8},{3,12},{4,1},{5,5},{6,9},{7,13},{8,2},{9,6},{10,... | collective-permute-start | bytes 786440 | tf_op jit(solution)/shard_map/ppermute | solution.py:33
  28.9 3.6 %collective-permute-done.5 = f32[128]{0:T(128)S(1)} collective-permute-done((f32[128]{0:T(128)S(1)}, f32[128]{0:T(128)S(1)}, u32[]{:S(2)}, u32[]{:S(2)}) %collective-permute-start.5) | collective-permute-done | bytes 544 | tf_op jit(solution)/shard_map/ppermute | solution.py:27
  32.4 6.2 %collective-permute-done.3 = bf16[128,1024]{1,0:T(8,128)(2,1)S(1)} collective-permute-done((bf16[128,1024]{1,0:T(8,128)(2,1)S(1)}, bf16[128,1024]{1,0:T(8,128)(2,1)S(1)}, u32[]{:S(2)}, u32[]{:S(2)}) %collective-permute-start.3) | collective-permute-done | bytes 262176 | tf_op jit(solution)/shard_map/ppermute | solution.py:33
  38.6 6.4 %collective-permute-done.6 = bf16[128,1024]{1,0:T(8,128)(2,1)S(1)} collective-permute-done((bf16[128,1024]{1,0:T(8,128)(2,1)S(1)}, bf16[128,1024]{1,0:T(8,128)(2,1)S(1)}, u32[]{:S(2)}, u32[]{:S(2)}) %collective-permute-start.6) | collective-permute-done | bytes 262176 | tf_op jit(solution)/shard_map/ppermute | solution.py:27
  45.2 1.8 collective-permute-done.7
  47.5 1.6 copy-done.1
  49.1 2.1 convolution_convert_fusion
  51.2 2.1 convolution_convert_fusion.1
  55.0 2.5 collective-permute-start.8
  58.8 4.6 %collective-permute-start.14 = (bf16[128,1792]{1,0:T(8,128)(2,1)}, bf16[128,1792]{1,0:T(8,128)(2,1)S(1)}, u32[]{:S(2)}, u32[]{:S(2)}) collective-permute-start(bf16[128,1792]{1,0:T(8,128)(2,1)} %get-tuple-element.30), channel_id=1, source_target_pairs={{0,4},{4,8},{8,12},{1,5},{5,9},{9,13},{2,6},{6,10},{10,14},{3,7},{... | collective-permute-start | bytes 1376264 | tf_op jit(solution)/shard_map/ppermute | solution.py:23
  64.7 4.0 %collective-permute-done.8 = bf16[128,1792]{1,0:T(8,128)(2,1)S(1)} collective-permute-done((bf16[128,1792]{1,0:T(8,128)(2,1)}, bf16[128,1792]{1,0:T(8,128)(2,1)S(1)}, u32[]{:S(2)}, u32[]{:S(2)}) %collective-permute-start.8) | collective-permute-done | bytes 458784 | tf_op jit(solution)/shard_map/ppermute | solution.py:23
  68.6 4.3 %collective-permute-done.9 = bf16[128,1792]{1,0:T(8,128)(2,1)S(1)} collective-permute-done((bf16[128,1792]{1,0:T(8,128)(2,1)}, bf16[128,1792]{1,0:T(8,128)(2,1)S(1)}, u32[]{:S(2)}, u32[]{:S(2)}) %collective-permute-start.9) | collective-permute-done | bytes 458784 | tf_op jit(solution)/shard_map/ppermute | solution.py:23
  73.0 1.4 fusion.18
  74.3 2.4 collective-permute-start.10
  78.5 4.3 %collective-permute-done.15 = bf16[128,1792]{1,0:T(8,128)(2,1)S(1)} collective-permute-done((bf16[128,1792]{1,0:T(8,128)(2,1)S(1)}, bf16[128,1792]{1,0:T(8,128)(2,1)S(1)}, u32[]{:S(2)}, u32[]{:S(2)}) %collective-permute-start.15) | collective-permute-done | bytes 458784 | tf_op jit(solution)/shard_map/ppermute | solution.py:23
  83.0 2.3 collective-permute-start.16
  86.6 1.6 collective-permute-done.10
  88.2 4.4 %collective-permute-done.11 = bf16[128,1792]{1,0:T(8,128)(2,1)S(1)} collective-permute-done((bf16[128,1792]{1,0:T(8,128)(2,1)S(1)}, bf16[128,1792]{1,0:T(8,128)(2,1)S(1)}, u32[]{:S(2)}, u32[]{:S(2)}) %collective-permute-start.11) | collective-permute-done | bytes 458784 | tf_op jit(solution)/shard_map/ppermute | solution.py:23
  93.8 3.1 %collective-permute-start.12 = (bf16[128,1792]{1,0:T(8,128)(2,1)}, bf16[128,1792]{1,0:T(8,128)(2,1)}, u32[]{:S(2)}, u32[]{:S(2)}) collective-permute-start(bf16[128,1792]{1,0:T(8,128)(2,1)} %get-tuple-element.27), channel_id=1, source_target_pairs={{0,4},{4,8},{8,12},{1,5},{5,9},{9,13},{2,6},{6,10},{10,14},{3,7},{... | collective-permute-start | bytes 1376264 | tf_op jit(solution)/shard_map/ppermute | solution.py:23
  98.2 4.2 %collective-permute-done.17 = bf16[128,1792]{1,0:T(8,128)(2,1)S(1)} collective-permute-done((bf16[128,1792]{1,0:T(8,128)(2,1)S(1)}, bf16[128,1792]{1,0:T(8,128)(2,1)S(1)}, u32[]{:S(2)}, u32[]{:S(2)}) %collective-permute-start.17) | collective-permute-done | bytes 458784 | tf_op jit(solution)/shard_map/ppermute | solution.py:23
  103.6 3.1 %collective-permute-start.18 = (bf16[128,1792]{1,0:T(8,128)(2,1)}, bf16[128,1792]{1,0:T(8,128)(2,1)}, u32[]{:S(2)}, u32[]{:S(2)}) collective-permute-start(bf16[128,1792]{1,0:T(8,128)(2,1)} %get-tuple-element.34), channel_id=1, source_target_pairs={{0,4},{4,8},{8,12},{1,5},{5,9},{9,13},{2,6},{6,10},{10,14},{3,7},{... | collective-permute-start | bytes 1376264 | tf_op jit(solution)/shard_map/ppermute | solution.py:23
  109.1 1.5 copy.31
  112.5 4.4 %collective-permute-done.18 = bf16[128,1792]{1,0:T(8,128)(2,1)} collective-permute-done((bf16[128,1792]{1,0:T(8,128)(2,1)}, bf16[128,1792]{1,0:T(8,128)(2,1)}, u32[]{:S(2)}, u32[]{:S(2)}) %collective-permute-start.18) | collective-permute-done | bytes 458784 | tf_op jit(solution)/shard_map/ppermute | solution.py:23
  117.0 4.1 %collective-permute-done.19 = bf16[128,1792]{1,0:T(8,128)(2,1)} collective-permute-done((bf16[128,1792]{1,0:T(8,128)(2,1)}, bf16[128,1792]{1,0:T(8,128)(2,1)}, u32[]{:S(2)}, u32[]{:S(2)}) %collective-permute-start.19) | collective-permute-done | bytes 458784 | tf_op jit(solution)/shard_map/ppermute | solution.py:23
  121.1 3.0 %multiply_reduce_fusion.1 = (f32[128]{0:T(128)S(1)}, f32[]{:T(128)}, f32[128,1792]{1,0:T(8,128)S(1)}, f32[128,1792]{1,0:T(8,128)S(1)}) fusion(f32[128,1792]{1,0:T(8,128)S(1)} %copy.31, bf16[128,1792]{1,0:T(8,128)(2,1)S(1)} %copy-done.7, f32[128]{0:T(128)S(1)} %add_sqrt_fusion, bf16[128,1792]{1,0:T(8,128)(2,1)} %collective-permute-done.19, ...), kind=kLoop, calls=%fused_computation.51 | loop fusion | flops 5046143 | bytes 5964808 | tf_op jit(solution)/shard_map/reduce_sum | solution.py:107
  124.6 1.4 collective-permute-start.23
  126.0 4.8 %collective-permute-start.24 = (bf16[128,5376]{1,0:T(8,128)(2,1)S(1)}, bf16[128,5376]{1,0:T(8,128)(2,1)S(1)}, u32[]{:S(2)}, u32[]{:S(2)}) collective-permute-start(bf16[128,5376]{1,0:T(8,128)(2,1)S(1)} %pad_maximum_fusion), channel_id=1, source_target_pairs={{0,4},{4,8},{8,12},{1,5},{5,9},{9,13},{2,6},{6,10},{10,14},{3,7},{... | collective-permute-start | bytes 4128776 | tf_op jit(solution)/shard_map/ppermute | solution.py:23
  136.3 1.3 select_convert_fusion.3
  139.0 18.6 %collective-permute-done.23 = bf16[128,5376]{1,0:T(8,128)(2,1)S(1)} collective-permute-done((bf16[128,5376]{1,0:T(8,128)(2,1)S(1)}, bf16[128,5376]{1,0:T(8,128)(2,1)S(1)}, u32[]{:S(2)}, u32[]{:S(2)}) %collective-permute-start.23) | collective-permute-done | bytes 1376288 | tf_op jit(solution)/shard_map/ppermute | solution.py:23
  162.2 5.1 %collective-permute-start.29 = (bf16[128,5376]{1,0:T(8,128)(2,1)S(1)}, bf16[128,5376]{1,0:T(8,128)(2,1)S(1)}, u32[]{:S(2)}, u32[]{:S(2)}) collective-permute-start(bf16[128,5376]{1,0:T(8,128)(2,1)S(1)} %collective-permute-done.24), channel_id=1, source_target_pairs={{0,4},{4,8},{8,12},{1,5},{5,9},{9,13},{2,6},{6,10},{10,14},{3,7},{... | collective-permute-start | bytes 4128776 | tf_op jit(solution)/shard_map/ppermute | solution.py:23
  168.8 3.2 %collective-permute-start.21 = (bf16[128,1024]{1,0:T(8,128)(2,1)S(1)}, bf16[128,1024]{1,0:T(8,128)(2,1)S(1)}, u32[]{:S(2)}, u32[]{:S(2)}) collective-permute-start(bf16[128,1024]{1,0:T(8,128)(2,1)S(1)} %fusion.49), channel_id=1, source_target_pairs={{2,0},{1,3},{6,4},{5,7},{10,8},{9,11},{14,12},{13,15},{18,16},{17,... | collective-permute-start | bytes 786440 | tf_op jit(solution)/shard_map/ppermute | solution.py:180
  173.4 3.2 %collective-permute-done.21 = bf16[128,1024]{1,0:T(8,128)(2,1)S(1)} collective-permute-done((bf16[128,1024]{1,0:T(8,128)(2,1)S(1)}, bf16[128,1024]{1,0:T(8,128)(2,1)S(1)}, u32[]{:S(2)}, u32[]{:S(2)}) %collective-permute-start.21) | collective-permute-done | bytes 262176 | tf_op jit(solution)/shard_map/ppermute | solution.py:180
  178.1 2.3 collective-permute-done.26
  180.5 4.1 %collective-permute-start.43 = (bf16[128,1024]{1,0:T(8,128)(2,1)S(1)}, bf16[128,1024]{1,0:T(8,128)(2,1)S(1)}, u32[]{:S(2)}, u32[]{:S(2)}) collective-permute-start(bf16[128,1024]{1,0:T(8,128)(2,1)S(1)} %add_convert_fusion.2), channel_id=1, source_target_pairs={{2,4},{6,9},{10,6},{14,11},{18,20},{22,25},{26,22},{30,27}} | collective-permute-start | bytes 786440 | tf_op jit(solution)/shard_map/ppermute | solution.py:182
  184.6 8.7 %collective-permute-done.28 = bf16[128,5376]{1,0:T(8,128)(2,1)S(1)} collective-permute-done((bf16[128,5376]{1,0:T(8,128)(2,1)S(1)}, bf16[128,5376]{1,0:T(8,128)(2,1)S(1)}, u32[]{:S(2)}, u32[]{:S(2)}) %collective-permute-start.28) | collective-permute-done | bytes 1376288 | tf_op jit(solution)/shard_map/ppermute | solution.py:23
  195.8 5.1 %collective-permute-start.34 = (bf16[128,5376]{1,0:T(8,128)(2,1)S(1)}, bf16[128,5376]{1,0:T(8,128)(2,1)S(1)}, u32[]{:S(2)}, u32[]{:S(2)}) collective-permute-start(bf16[128,5376]{1,0:T(8,128)(2,1)S(1)} %collective-permute-done.29), channel_id=1, source_target_pairs={{0,4},{4,8},{8,12},{1,5},{5,9},{9,13},{2,6},{6,10},{10,14},{3,7},{... | collective-permute-start | bytes 4128776 | tf_op jit(solution)/shard_map/ppermute | solution.py:23
  204.4 21.7 %collective-permute-done.33 = bf16[128,5376]{1,0:T(8,128)(2,1)S(1)} collective-permute-done((bf16[128,5376]{1,0:T(8,128)(2,1)S(1)}, bf16[128,5376]{1,0:T(8,128)(2,1)S(1)}, u32[]{:S(2)}, u32[]{:S(2)}) %collective-permute-start.33) | collective-permute-done | bytes 1376288 | tf_op jit(solution)/shard_map/ppermute | solution.py:23
  232.4 2.5 collective-permute-start.40
  235.0 4.3 %collective-permute-done.31 = bf16[128,1024]{1,0:T(8,128)(2,1)S(1)} collective-permute-done((bf16[128,1024]{1,0:T(8,128)(2,1)S(1)}, bf16[128,1024]{1,0:T(8,128)(2,1)S(1)}, u32[]{:S(2)}, u32[]{:S(2)}) %collective-permute-start.31) | collective-permute-done | bytes 262176 | tf_op jit(solution)/shard_map/ppermute | solution.py:180
  239.2 1.5 collective-permute-start.36
  241.5 3.0 %collective-permute-done.36 = bf16[128,1024]{1,0:T(8,128)(2,1)S(1)} collective-permute-done((bf16[128,1024]{1,0:T(8,128)(2,1)S(1)}, bf16[128,1024]{1,0:T(8,128)(2,1)S(1)}, u32[]{:S(2)}, u32[]{:S(2)}) %collective-permute-start.36) | collective-permute-done | bytes 262176 | tf_op jit(solution)/shard_map/ppermute | solution.py:180
  244.6 3.7 %collective-permute-start.41 = (f32[128]{0:T(128)S(1)}, f32[128]{0:T(128)S(1)}, u32[]{:S(2)}, u32[]{:S(2)}) collective-permute-start(f32[128]{0:T(128)S(1)} %add.272), channel_id=1, source_target_pairs={{0,8},{4,12},{8,0},{12,4},{1,9},{5,13},{9,1},{13,5},{2,10},{6,14},... | collective-permute-start | bytes 1544 | tf_op jit(solution)/shard_map/ppermute | solution.py:197
  249.7 3.8 %collective-permute-start.32 = (bf16[128,1024]{1,0:T(8,128)(2,1)S(1)}, bf16[128,1024]{1,0:T(8,128)(2,1)S(1)}, u32[]{:S(2)}, u32[]{:S(2)}) collective-permute-start(bf16[128,1024]{1,0:T(8,128)(2,1)S(1)} %add_convert_fusion.1), channel_id=1, source_target_pairs={{2,8},{6,13},{10,2},{14,7},{18,24},{22,29},{26,18},{30,23}} | collective-permute-start | bytes 786440 | tf_op jit(solution)/shard_map/ppermute | solution.py:182
  256.9 3.9 %collective-permute-done.44 = bf16[128,1024]{1,0:T(8,128)(2,1)S(1)} collective-permute-done((bf16[128,1024]{1,0:T(8,128)(2,1)S(1)}, bf16[128,1024]{1,0:T(8,128)(2,1)S(1)}, u32[]{:S(2)}, u32[]{:S(2)}) %collective-permute-start.44) | collective-permute-done | bytes 262176 | tf_op jit(solution)/shard_map/ppermute | solution.py:182
  260.8 3.8 %collective-permute-done.32 = bf16[128,1024]{1,0:T(8,128)(2,1)S(1)} collective-permute-done((bf16[128,1024]{1,0:T(8,128)(2,1)S(1)}, bf16[128,1024]{1,0:T(8,128)(2,1)S(1)}, u32[]{:S(2)}, u32[]{:S(2)}) %collective-permute-start.32) | collective-permute-done | bytes 262176 | tf_op jit(solution)/shard_map/ppermute | solution.py:182
  (141 shorter events, 59.7 us)
Async XLA Ops:
  1.5 11.6 %collective-permute-start.2 = (bf16[2,128,256]{2,1,0:T(8,128)(2,1)S(1)}, bf16[2,128,256]{2,1,0:T(8,128)(2,1)S(1)}, u32[]{:S(2)}, u32[]{:S(2)}) collective-permute-start(bf16[2,128,256]{2,1,0:T(8,128)(2,1)S(1)} %pad_maximum_fusion.4), channel_id=1, source_target_pairs={{0,12},{1,13},{2,14},{3,15},{16,28},{17,29},{18,30},{19,31}} | collective-permute-start | bytes 393224 | tf_op jit(solution)/shard_map/ppermute | solution.py:23
  7.0 6.7 %collective-permute-start.1 = (bf16[2,128,256]{2,1,0:T(8,128)(2,1)S(1)}, bf16[2,128,256]{2,1,0:T(8,128)(2,1)S(1)}, u32[]{:S(2)}, u32[]{:S(2)}) collective-permute-start(bf16[2,128,256]{2,1,0:T(8,128)(2,1)S(1)} %pad_maximum_fusion.4), channel_id=1, source_target_pairs={{0,8},{4,12},{1,9},{5,13},{2,10},{6,14},{3,11},{7,15},{16,24},{20,... | collective-permute-start | bytes 393224 | tf_op jit(solution)/shard_map/ppermute | solution.py:23
  8.3 7.1 %collective-permute-start = (bf16[2,128,256]{2,1,0:T(8,128)(2,1)S(1)}, bf16[2,128,256]{2,1,0:T(8,128)(2,1)S(1)}, u32[]{:S(2)}, u32[]{:S(2)}) collective-permute-start(bf16[2,128,256]{2,1,0:T(8,128)(2,1)S(1)} %pad_maximum_fusion.4), channel_id=1, source_target_pairs={{0,4},{4,8},{8,12},{1,5},{5,9},{9,13},{2,6},{6,10},{10,14},{3,7},{... | collective-permute-start | bytes 393224 | tf_op jit(solution)/shard_map/ppermute | solution.py:23
  18.9 26.2 %copy-start.10 = (f32[4096]{0:T(1024)S(1)}, f32[4096]{0:T(1024)}, u32[]{:S(2)}) copy-start(f32[4096]{0:T(1024)} %param.16) | copy-start | bytes 49156
  19.6 19.0 %collective-permute-start.3 = (bf16[128,1024]{1,0:T(8,128)(2,1)S(1)}, bf16[128,1024]{1,0:T(8,128)(2,1)S(1)}, u32[]{:S(2)}, u32[]{:S(2)}) collective-permute-start(bf16[128,1024]{1,0:T(8,128)(2,1)S(1)} %get-tuple-element.46), channel_id=1, source_target_pairs={{0,0},{1,4},{2,8},{3,12},{4,1},{5,5},{6,9},{7,13},{8,2},{9,6},{10,... | collective-permute-start | bytes 786440 | tf_op jit(solution)/shard_map/ppermute | solution.py:33
  27.6 1.2 collective-permute-start.4
  28.9 3.6 %collective-permute-start.5 = (f32[128]{0:T(128)S(1)}, f32[128]{0:T(128)S(1)}, u32[]{:S(2)}, u32[]{:S(2)}) collective-permute-start(f32[128]{0:T(128)S(1)} %add.223), channel_id=1, source_target_pairs={{0,2},{2,0},{1,3},{3,1},{4,6},{6,4},{5,7},{7,5},{8,10},{10,8},{9,1... | collective-permute-start | bytes 1544 | tf_op jit(solution)/shard_map/ppermute | solution.py:27
  38.6 6.4 %collective-permute-start.6 = (bf16[128,1024]{1,0:T(8,128)(2,1)S(1)}, bf16[128,1024]{1,0:T(8,128)(2,1)S(1)}, u32[]{:S(2)}, u32[]{:S(2)}) collective-permute-start(bf16[128,1024]{1,0:T(8,128)(2,1)S(1)} %collective-permute-done.3), channel_id=1, source_target_pairs={{0,2},{2,0},{1,3},{3,1},{4,6},{6,4},{5,7},{7,5},{8,10},{10,8},{9,1... | collective-permute-start | bytes 786440 | tf_op jit(solution)/shard_map/ppermute | solution.py:27
  45.0 2.0 collective-permute-start.7
  55.0 13.7 %collective-permute-start.8 = (bf16[128,1792]{1,0:T(8,128)(2,1)}, bf16[128,1792]{1,0:T(8,128)(2,1)S(1)}, u32[]{:S(2)}, u32[]{:S(2)}) collective-permute-start(bf16[128,1792]{1,0:T(8,128)(2,1)} %get-tuple-element.23), channel_id=1, source_target_pairs={{0,4},{4,8},{8,12},{1,5},{5,9},{9,13},{2,6},{6,10},{10,14},{3,7},{... | collective-permute-start | bytes 1376264 | tf_op jit(solution)/shard_map/ppermute | solution.py:23
  57.5 15.5 %collective-permute-start.9 = (bf16[128,1792]{1,0:T(8,128)(2,1)}, bf16[128,1792]{1,0:T(8,128)(2,1)S(1)}, u32[]{:S(2)}, u32[]{:S(2)}) collective-permute-start(bf16[128,1792]{1,0:T(8,128)(2,1)} %get-tuple-element.24), channel_id=1, source_target_pairs={{4,0},{8,4},{12,8},{5,1},{9,5},{13,9},{6,2},{10,6},{14,10},{7,3},{... | collective-permute-start | bytes 1376264 | tf_op jit(solution)/shard_map/ppermute | solution.py:23
  58.8 19.7 %collective-permute-start.14 = (bf16[128,1792]{1,0:T(8,128)(2,1)}, bf16[128,1792]{1,0:T(8,128)(2,1)S(1)}, u32[]{:S(2)}, u32[]{:S(2)}) collective-permute-start(bf16[128,1792]{1,0:T(8,128)(2,1)} %get-tuple-element.30), channel_id=1, source_target_pairs={{0,4},{4,8},{8,12},{1,5},{5,9},{9,13},{2,6},{6,10},{10,14},{3,7},{... | collective-permute-start | bytes 1376264 | tf_op jit(solution)/shard_map/ppermute | solution.py:23
  63.4 19.4 %collective-permute-start.15 = (bf16[128,1792]{1,0:T(8,128)(2,1)S(1)}, bf16[128,1792]{1,0:T(8,128)(2,1)S(1)}, u32[]{:S(2)}, u32[]{:S(2)}) collective-permute-start(bf16[128,1792]{1,0:T(8,128)(2,1)S(1)} %get-tuple-element.31), channel_id=1, source_target_pairs={{4,0},{8,4},{12,8},{5,1},{9,5},{13,9},{6,2},{10,6},{14,10},{7,3},{... | collective-permute-start | bytes 1376264 | tf_op jit(solution)/shard_map/ppermute | solution.py:23
  74.3 18.3 %copy-start.6 = (bf16[512,1792]{1,0:T(8,128)(2,1)S(1)}, bf16[512,1792]{1,0:T(8,128)(2,1)}, u32[]{:S(2)}) copy-start(bf16[512,1792]{1,0:T(8,128)(2,1)} %copy-done.5) | copy-start | bytes 5505028
  74.3 13.9 %collective-permute-start.10 = (bf16[128,1792]{1,0:T(8,128)(2,1)S(1)}, bf16[128,1792]{1,0:T(8,128)(2,1)S(1)}, u32[]{:S(2)}, u32[]{:S(2)}) collective-permute-start(bf16[128,1792]{1,0:T(8,128)(2,1)S(1)} %get-tuple-element.25), channel_id=1, source_target_pairs={{0,4},{4,8},{8,12},{1,5},{5,9},{9,13},{2,6},{6,10},{10,14},{3,7},{... | collective-permute-start | bytes 1376264 | tf_op jit(solution)/shard_map/ppermute | solution.py:23
  76.7 15.9 %collective-permute-start.11 = (bf16[128,1792]{1,0:T(8,128)(2,1)S(1)}, bf16[128,1792]{1,0:T(8,128)(2,1)S(1)}, u32[]{:S(2)}, u32[]{:S(2)}) collective-permute-start(bf16[128,1792]{1,0:T(8,128)(2,1)S(1)} %get-tuple-element.26), channel_id=1, source_target_pairs={{4,0},{8,4},{12,8},{5,1},{9,5},{13,9},{6,2},{10,6},{14,10},{7,3},{... | collective-permute-start | bytes 1376264 | tf_op jit(solution)/shard_map/ppermute | solution.py:23
  83.0 15.2 %collective-permute-start.16 = (bf16[128,1792]{1,0:T(8,128)(2,1)S(1)}, bf16[128,1792]{1,0:T(8,128)(2,1)S(1)}, u32[]{:S(2)}, u32[]{:S(2)}) collective-permute-start(bf16[128,1792]{1,0:T(8,128)(2,1)S(1)} %get-tuple-element.32), channel_id=1, source_target_pairs={{0,4},{4,8},{8,12},{1,5},{5,9},{9,13},{2,6},{6,10},{10,14},{3,7},{... | collective-permute-start | bytes 1376264 | tf_op jit(solution)/shard_map/ppermute | solution.py:23
  85.3 17.1 %collective-permute-start.17 = (bf16[128,1792]{1,0:T(8,128)(2,1)S(1)}, bf16[128,1792]{1,0:T(8,128)(2,1)S(1)}, u32[]{:S(2)}, u32[]{:S(2)}) collective-permute-start(bf16[128,1792]{1,0:T(8,128)(2,1)S(1)} %get-tuple-element.33), channel_id=1, source_target_pairs={{4,0},{8,4},{12,8},{5,1},{9,5},{13,9},{6,2},{10,6},{14,10},{7,3},{... | collective-permute-start | bytes 1376264 | tf_op jit(solution)/shard_map/ppermute | solution.py:23
  93.8 18.1 %collective-permute-start.12 = (bf16[128,1792]{1,0:T(8,128)(2,1)}, bf16[128,1792]{1,0:T(8,128)(2,1)}, u32[]{:S(2)}, u32[]{:S(2)}) collective-permute-start(bf16[128,1792]{1,0:T(8,128)(2,1)} %get-tuple-element.27), channel_id=1, source_target_pairs={{0,4},{4,8},{8,12},{1,5},{5,9},{9,13},{2,6},{6,10},{10,14},{3,7},{... | collective-permute-start | bytes 1376264 | tf_op jit(solution)/shard_map/ppermute | solution.py:23
  96.9 15.6 %collective-permute-start.13 = (bf16[128,1792]{1,0:T(8,128)(2,1)}, bf16[128,1792]{1,0:T(8,128)(2,1)}, u32[]{:S(2)}, u32[]{:S(2)}) collective-permute-start(bf16[128,1792]{1,0:T(8,128)(2,1)} %get-tuple-element.28), channel_id=1, source_target_pairs={{4,0},{8,4},{12,8},{5,1},{9,5},{13,9},{6,2},{10,6},{14,10},{7,3},{... | collective-permute-start | bytes 1376264 | tf_op jit(solution)/shard_map/ppermute | solution.py:23
  103.6 13.3 %collective-permute-start.18 = (bf16[128,1792]{1,0:T(8,128)(2,1)}, bf16[128,1792]{1,0:T(8,128)(2,1)}, u32[]{:S(2)}, u32[]{:S(2)}) collective-permute-start(bf16[128,1792]{1,0:T(8,128)(2,1)} %get-tuple-element.34), channel_id=1, source_target_pairs={{0,4},{4,8},{8,12},{1,5},{5,9},{9,13},{2,6},{6,10},{10,14},{3,7},{... | collective-permute-start | bytes 1376264 | tf_op jit(solution)/shard_map/ppermute | solution.py:23
  106.8 14.3 %collective-permute-start.19 = (bf16[128,1792]{1,0:T(8,128)(2,1)}, bf16[128,1792]{1,0:T(8,128)(2,1)}, u32[]{:S(2)}, u32[]{:S(2)}) collective-permute-start(bf16[128,1792]{1,0:T(8,128)(2,1)} %get-tuple-element.35), channel_id=1, source_target_pairs={{4,0},{8,4},{12,8},{5,1},{9,5},{13,9},{6,2},{10,6},{14,10},{7,3},{... | collective-permute-start | bytes 1376264 | tf_op jit(solution)/shard_map/ppermute | solution.py:23
  124.6 33.0 %collective-permute-start.23 = (bf16[128,5376]{1,0:T(8,128)(2,1)S(1)}, bf16[128,5376]{1,0:T(8,128)(2,1)S(1)}, u32[]{:S(2)}, u32[]{:S(2)}) collective-permute-start(bf16[128,5376]{1,0:T(8,128)(2,1)S(1)} %pad_maximum_fusion), channel_id=1, source_target_pairs={{4,0},{8,4},{12,8},{5,1},{9,5},{13,9},{6,2},{10,6},{14,10},{7,3},{... | collective-permute-start | bytes 4128776 | tf_op jit(solution)/shard_map/ppermute | solution.py:23
  126.0 32.7 %collective-permute-start.24 = (bf16[128,5376]{1,0:T(8,128)(2,1)S(1)}, bf16[128,5376]{1,0:T(8,128)(2,1)S(1)}, u32[]{:S(2)}, u32[]{:S(2)}) collective-permute-start(bf16[128,5376]{1,0:T(8,128)(2,1)S(1)} %pad_maximum_fusion), channel_id=1, source_target_pairs={{0,4},{4,8},{8,12},{1,5},{5,9},{9,13},{2,6},{6,10},{10,14},{3,7},{... | collective-permute-start | bytes 4128776 | tf_op jit(solution)/shard_map/ppermute | solution.py:23
  131.6 2.7 %collective-permute-start.38 = (f32[256]{0:T(256)S(1)}, f32[256]{0:T(256)S(1)}, u32[]{:S(2)}, u32[]{:S(2)}) collective-permute-start(f32[256]{0:T(256)S(1)} %pad_maximum_fusion.5), channel_id=1, source_target_pairs={{0,1},{1,0},{2,3},{3,2},{4,5},{5,4},{6,7},{7,6},{8,9},{9,8},{10,11... | collective-permute-start | bytes 3080 | tf_op jit(solution)/shard_map/ppermute | solution.py:27
  135.4 3.6 %collective-permute-start.39 = (f32[256]{0:T(256)S(1)}, f32[256]{0:T(256)S(1)}, u32[]{:S(2)}, u32[]{:S(2)}) collective-permute-start(f32[256]{0:T(256)S(1)} %fusion.96), channel_id=1, source_target_pairs={{0,2},{2,0},{1,3},{3,1},{4,6},{6,4},{5,7},{7,5},{8,10},{10,8},{9,1... | collective-permute-start | bytes 3080 | tf_op jit(solution)/shard_map/ppermute | solution.py:27
  137.6 31.1 %collective-permute-start.20 = (bf16[128,1024]{1,0:T(8,128)(2,1)S(1)}, bf16[128,1024]{1,0:T(8,128)(2,1)S(1)}, u32[]{:S(2)}, u32[]{:S(2)}) collective-permute-start(bf16[128,1024]{1,0:T(8,128)(2,1)S(1)} %get-tuple-element.83), channel_id=1, source_target_pairs={{0,1},{1,0},{2,3},{3,2},{4,5},{5,4},{6,7},{7,6},{8,9},{9,8},{10,11... | collective-permute-start | bytes 786440 | tf_op jit(solution)/shard_map/ppermute | solution.py:27
  160.9 32.5 %collective-permute-start.28 = (bf16[128,5376]{1,0:T(8,128)(2,1)S(1)}, bf16[128,5376]{1,0:T(8,128)(2,1)S(1)}, u32[]{:S(2)}, u32[]{:S(2)}) collective-permute-start(bf16[128,5376]{1,0:T(8,128)(2,1)S(1)} %collective-permute-done.23), channel_id=1, source_target_pairs={{4,0},{8,4},{12,8},{5,1},{9,5},{13,9},{6,2},{10,6},{14,10},{7,3},{... | collective-permute-start | bytes 4128776 | tf_op jit(solution)/shard_map/ppermute | solution.py:23
  162.2 32.3 %collective-permute-start.29 = (bf16[128,5376]{1,0:T(8,128)(2,1)S(1)}, bf16[128,5376]{1,0:T(8,128)(2,1)S(1)}, u32[]{:S(2)}, u32[]{:S(2)}) collective-permute-start(bf16[128,5376]{1,0:T(8,128)(2,1)S(1)} %collective-permute-done.24), channel_id=1, source_target_pairs={{0,4},{4,8},{8,12},{1,5},{5,9},{9,13},{2,6},{6,10},{10,14},{3,7},{... | collective-permute-start | bytes 4128776 | tf_op jit(solution)/shard_map/ppermute | solution.py:23
  168.6 3.4 %collective-permute-start.25 = (bf16[128,1024]{1,0:T(8,128)(2,1)S(1)}, bf16[128,1024]{1,0:T(8,128)(2,1)S(1)}, u32[]{:S(2)}, u32[]{:S(2)}) collective-permute-start(bf16[128,1024]{1,0:T(8,128)(2,1)S(1)} %get-tuple-element.81), channel_id=1, source_target_pairs={{0,1},{1,0},{2,3},{3,2},{4,5},{5,4},{6,7},{7,6},{8,9},{9,8},{10,11... | collective-permute-start | bytes 786440 | tf_op jit(solution)/shard_map/ppermute | solution.py:27
  168.8 7.8 %collective-permute-start.21 = (bf16[128,1024]{1,0:T(8,128)(2,1)S(1)}, bf16[128,1024]{1,0:T(8,128)(2,1)S(1)}, u32[]{:S(2)}, u32[]{:S(2)}) collective-permute-start(bf16[128,1024]{1,0:T(8,128)(2,1)S(1)} %fusion.49), channel_id=1, source_target_pairs={{2,0},{1,3},{6,4},{5,7},{10,8},{9,11},{14,12},{13,15},{18,16},{17,... | collective-permute-start | bytes 786440 | tf_op jit(solution)/shard_map/ppermute | solution.py:180
  172.1 8.3 %collective-permute-start.26 = (bf16[128,1024]{1,0:T(8,128)(2,1)S(1)}, bf16[128,1024]{1,0:T(8,128)(2,1)S(1)}, u32[]{:S(2)}, u32[]{:S(2)}) collective-permute-start(bf16[128,1024]{1,0:T(8,128)(2,1)S(1)} %fusion.50), channel_id=1, source_target_pairs={{3,1},{0,2},{7,5},{4,6},{11,9},{8,10},{15,13},{12,14},{19,17},{16,... | collective-permute-start | bytes 786440 | tf_op jit(solution)/shard_map/ppermute | solution.py:180
  176.7 71.7 %collective-permute-start.42 = (bf16[128,1024]{1,0:T(8,128)(2,1)S(1)}, bf16[128,1024]{1,0:T(8,128)(2,1)S(1)}, u32[]{:S(2)}, u32[]{:S(2)}) collective-permute-start(bf16[128,1024]{1,0:T(8,128)(2,1)S(1)} %add_convert_fusion.3), channel_id=1, source_target_pairs={{3,0},{7,5},{11,10},{15,15},{19,16},{23,21},{27,26},{31,31}} | collective-permute-start | bytes 786440 | tf_op jit(solution)/shard_map/ppermute | solution.py:182
  177.4 72.3 %collective-permute-start.22 = (bf16[128,1024]{1,0:T(8,128)(2,1)S(1)}, bf16[128,1024]{1,0:T(8,128)(2,1)S(1)}, u32[]{:S(2)}, u32[]{:S(2)}) collective-permute-start(bf16[128,1024]{1,0:T(8,128)(2,1)S(1)} %add_convert_fusion.3), channel_id=1, source_target_pairs={{0,0},{4,5},{8,10},{12,15},{16,16},{20,21},{24,26},{28,31}} | collective-permute-start | bytes 786440 | tf_op jit(solution)/shard_map/ppermute | solution.py:182
  180.5 73.0 %collective-permute-start.43 = (bf16[128,1024]{1,0:T(8,128)(2,1)S(1)}, bf16[128,1024]{1,0:T(8,128)(2,1)S(1)}, u32[]{:S(2)}, u32[]{:S(2)}) collective-permute-start(bf16[128,1024]{1,0:T(8,128)(2,1)S(1)} %add_convert_fusion.2), channel_id=1, source_target_pairs={{2,4},{6,9},{10,6},{14,11},{18,20},{22,25},{26,22},{30,27}} | collective-permute-start | bytes 786440 | tf_op jit(solution)/shard_map/ppermute | solution.py:182
  194.5 31.6 %collective-permute-start.33 = (bf16[128,5376]{1,0:T(8,128)(2,1)S(1)}, bf16[128,5376]{1,0:T(8,128)(2,1)S(1)}, u32[]{:S(2)}, u32[]{:S(2)}) collective-permute-start(bf16[128,5376]{1,0:T(8,128)(2,1)S(1)} %collective-permute-done.28), channel_id=1, source_target_pairs={{4,0},{8,4},{12,8},{5,1},{9,5},{13,9},{6,2},{10,6},{14,10},{7,3},{... | collective-permute-start | bytes 4128776 | tf_op jit(solution)/shard_map/ppermute | solution.py:23
  195.8 31.5 %collective-permute-start.34 = (bf16[128,5376]{1,0:T(8,128)(2,1)S(1)}, bf16[128,5376]{1,0:T(8,128)(2,1)S(1)}, u32[]{:S(2)}, u32[]{:S(2)}) collective-permute-start(bf16[128,5376]{1,0:T(8,128)(2,1)S(1)} %collective-permute-done.29), channel_id=1, source_target_pairs={{0,4},{4,8},{8,12},{1,5},{5,9},{9,13},{2,6},{6,10},{10,14},{3,7},{... | collective-permute-start | bytes 4128776 | tf_op jit(solution)/shard_map/ppermute | solution.py:23
  226.1 4.8 %collective-permute-start.30 = (bf16[128,1024]{1,0:T(8,128)(2,1)S(1)}, bf16[128,1024]{1,0:T(8,128)(2,1)S(1)}, u32[]{:S(2)}, u32[]{:S(2)}) collective-permute-start(bf16[128,1024]{1,0:T(8,128)(2,1)S(1)} %get-tuple-element.79), channel_id=1, source_target_pairs={{0,1},{1,0},{2,3},{3,2},{4,5},{5,4},{6,7},{7,6},{8,9},{9,8},{10,11... | collective-permute-start | bytes 786440 | tf_op jit(solution)/shard_map/ppermute | solution.py:27
  230.8 1.6 collective-permute-start.35
  231.0 8.3 %collective-permute-start.31 = (bf16[128,1024]{1,0:T(8,128)(2,1)S(1)}, bf16[128,1024]{1,0:T(8,128)(2,1)S(1)}, u32[]{:S(2)}, u32[]{:S(2)}) collective-permute-start(bf16[128,1024]{1,0:T(8,128)(2,1)S(1)} %fusion.51), channel_id=1, source_target_pairs={{0,2},{3,1},{4,6},{7,5},{8,10},{11,9},{12,14},{15,13},{16,18},{19,... | collective-permute-start | bytes 786440 | tf_op jit(solution)/shard_map/ppermute | solution.py:180
  232.4 8.5 %collective-permute-start.40 = (f32[128]{0:T(128)S(1)}, f32[128]{0:T(128)S(1)}, u32[]{:S(2)}, u32[]{:S(2)}) collective-permute-start(f32[128]{0:T(128)S(1)} %get-tuple-element.40), channel_id=1, source_target_pairs={{0,4},{4,0},{8,12},{12,8},{1,5},{5,1},{9,13},{13,9},{2,6},{6,2},{1... | collective-permute-start | bytes 1544 | tf_op jit(solution)/shard_map/ppermute | solution.py:197
  239.2 5.3 %collective-permute-start.36 = (bf16[128,1024]{1,0:T(8,128)(2,1)S(1)}, bf16[128,1024]{1,0:T(8,128)(2,1)S(1)}, u32[]{:S(2)}, u32[]{:S(2)}) collective-permute-start(bf16[128,1024]{1,0:T(8,128)(2,1)S(1)} %fusion.52), channel_id=1, source_target_pairs={{1,3},{2,0},{5,7},{6,4},{9,11},{10,8},{13,15},{14,12},{17,19},{18,... | collective-permute-start | bytes 786440 | tf_op jit(solution)/shard_map/ppermute | solution.py:180
  240.9 16.0 %collective-permute-start.27 = (bf16[128,1024]{1,0:T(8,128)(2,1)S(1)}, bf16[128,1024]{1,0:T(8,128)(2,1)S(1)}, u32[]{:S(2)}, u32[]{:S(2)}) collective-permute-start(bf16[128,1024]{1,0:T(8,128)(2,1)S(1)} %add_convert_fusion.2), channel_id=1, source_target_pairs={{1,4},{5,9},{9,6},{13,11},{17,20},{21,25},{25,22},{29,27}} | collective-permute-start | bytes 786440 | tf_op jit(solution)/shard_map/ppermute | solution.py:182
  244.6 9.7 %collective-permute-start.41 = (f32[128]{0:T(128)S(1)}, f32[128]{0:T(128)S(1)}, u32[]{:S(2)}, u32[]{:S(2)}) collective-permute-start(f32[128]{0:T(128)S(1)} %add.272), channel_id=1, source_target_pairs={{0,8},{4,12},{8,0},{12,4},{1,9},{5,13},{9,1},{13,5},{2,10},{6,14},... | collective-permute-start | bytes 1544 | tf_op jit(solution)/shard_map/ppermute | solution.py:197
  248.4 12.4 %collective-permute-start.44 = (bf16[128,1024]{1,0:T(8,128)(2,1)S(1)}, bf16[128,1024]{1,0:T(8,128)(2,1)S(1)}, u32[]{:S(2)}, u32[]{:S(2)}) collective-permute-start(bf16[128,1024]{1,0:T(8,128)(2,1)S(1)} %add_convert_fusion.1), channel_id=1, source_target_pairs={{1,8},{5,13},{9,2},{13,7},{17,24},{21,29},{25,18},{29,23}} | collective-permute-start | bytes 786440 | tf_op jit(solution)/shard_map/ppermute | solution.py:182
  249.7 14.9 %collective-permute-start.32 = (bf16[128,1024]{1,0:T(8,128)(2,1)S(1)}, bf16[128,1024]{1,0:T(8,128)(2,1)S(1)}, u32[]{:S(2)}, u32[]{:S(2)}) collective-permute-start(bf16[128,1024]{1,0:T(8,128)(2,1)S(1)} %add_convert_fusion.1), channel_id=1, source_target_pairs={{2,8},{6,13},{10,2},{14,7},{18,24},{22,29},{26,18},{30,23}} | collective-permute-start | bytes 786440 | tf_op jit(solution)/shard_map/ppermute | solution.py:182
  253.5 11.0 %collective-permute-start.45 = (bf16[128,1024]{1,0:T(8,128)(2,1)S(1)}, bf16[128,1024]{1,0:T(8,128)(2,1)S(1)}, u32[]{:S(2)}, u32[]{:S(2)}) collective-permute-start(bf16[128,1024]{1,0:T(8,128)(2,1)S(1)} %add_convert_fusion), channel_id=1, source_target_pairs={{0,12},{4,1},{8,14},{12,3},{16,28},{20,17},{24,30},{28,19}} | collective-permute-start | bytes 786440 | tf_op jit(solution)/shard_map/ppermute | solution.py:182
  254.2 10.3 %collective-permute-start.37 = (bf16[128,1024]{1,0:T(8,128)(2,1)S(1)}, bf16[128,1024]{1,0:T(8,128)(2,1)S(1)}, u32[]{:S(2)}, u32[]{:S(2)}) collective-permute-start(bf16[128,1024]{1,0:T(8,128)(2,1)S(1)} %add_convert_fusion), channel_id=1, source_target_pairs={{3,12},{7,1},{11,14},{15,3},{19,28},{23,17},{27,30},{31,19}} | collective-permute-start | bytes 786440 | tf_op jit(solution)/shard_map/ppermute | solution.py:182
  (9 other events, 50.7 us)

commit v5 on v4

--- a/solution.py
+++ b/solution.py
@@ -164,14 +164,6 @@
     for s in range(2):
         right.append(shifted(right[s], 1))
         left.append(shifted(left[s], -1))
-    turns = [owned, jnp.where(low, left[0], right[0])]
-    _, arrived = lax.optimization_barrier((turns[1], (left[1], right[1])))
-    turns.append(jnp.where(low, *arrived))
-    _, arrived = lax.optimization_barrier((turns[2], (left[2], right[2])))
-    outer = jnp.where(low, *arrived)
-    inward = jnp.where(low, right[0], left[0])
-    turns.append(jnp.where((z == 0) | (z == 3), outer, inward))
-
     def brought_home(k, down, grad):
         keeps_down = pair == (k & 1)
         sent = jnp.where(keeps_down, grad, down).astype(BF16)
@@ -183,18 +175,32 @@
             for h in (k, k ^ 3)
         ]
 
-    home = []
-    for k in range(4):
-        block = turns[k]
+    def turn(k, block):
         down, grad = products(block[:, :ff], block[:, ff : 2 * ff], block[:, 2 * ff :], weights)
-        home.append(brought_home(k, down, grad))
+        return brought_home(k, down, grad)
 
     count = jnp.sum(keep_tiles.astype(F32)) * TILE
     small = jnp.concatenate([inner, loss[None], count[None], jnp.zeros(126, F32)])
     small = summed_over_hp(small)
-    totals, _ = lax.optimization_barrier((small[rows:], turns[3]))
-    for d in (1, 2):
-        totals = totals + lax.ppermute(totals, "ctx", [(c, c ^ d) for c in range(4)])
+
+    def over_ctx(part, d, after):
+        met = lax.ppermute(part, "ctx", [(c, c ^ d) for c in range(4)])
+        return part + lax.optimization_barrier((met, after))[0]
+
+    home = [turn(0, owned)]
+    small, arrived = lax.optimization_barrier((small, (left[0], right[0])))
+    totals = small[rows:]
+    block = jnp.where(low, *arrived)
+    home.append(turn(1, block))
+    totals = over_ctx(totals, 1, block)
+    home, totals, arrived = lax.optimization_barrier((home, totals, (left[1], right[1])))
+    block = jnp.where(low, *arrived)
+    home.append(turn(2, block))
+    totals = over_ctx(totals, 2, block)
+    home[2], totals, arrived = lax.optimization_barrier((home[2], totals, (left[2], right[2])))
+    outer = jnp.where(low, *arrived)
+    inward = jnp.where(low, right[0], left[0])
+    home.append(turn(3, jnp.where((z == 0) | (z == 3), outer, inward)))
     loss_value = (totals[0] / totals[1]).reshape(1)
 
     down, grad = [sum(h[i].astype(F32) for h in home) for i in range(2)]

time: 271 us -> 288 us (1.063)
  the two profiles are of different devices: /device:TPU:2 before, /device:TPU:3 now
where the time goes in v5:
time: 288 us; the launch traced here: 286 us
  starting transfers between devices  123 us (43%)
  waiting for transfers between devices  106 us (37%)
  other arithmetic  20.6 us (7%)
  matrix products  19.5 us (7%)
  local copies, waits for them, and re-layouts  12.2 us (4%)
  between operations  4.65 us (2%)
    ppermute x21, starting transfers between devices, passed_along(): return lax.ppermute(block, axis, route)  54.4 us
    ppermute x21, waiting for transfers between devices, passed_along(): return lax.ppermute(block, axis, route)  53.6 us
    ppermute x10, starting transfers between devices, swapped(): return lax.ppermute(block, axis, [(0, 1), (1, 0)])  33.3 us
    ppermute x2, waiting for transfers between devices, over_ctx(): met = lax.ppermute(part, 'ctx', [(c, c ^ d) for c in range(4)])  18.5 us
    ppermute x8, starting transfers between devices, brought_home(): lax.ppermute(whole, ('ctx',) + HP, [(4 * c + h, 4 * TURNS[c][k] + c) for...  16 us
    ppermute x10, waiting for transfers between devices, swapped(): return lax.ppermute(block, axis, [(0, 1), (1, 0)])  14 us
    ppermute x4, waiting for transfers between devices, brought_home(): lax.ppermute(half.astype(BF16), HP, route).astype(F32)  11.3 us
    ppermute x4, starting transfers between devices, brought_home(): lax.ppermute(half.astype(BF16), HP, route).astype(F32)  10.2 us
  transfers between devices with their start and end apart: 46, of which 29 were waited for; matrix products, arithmetic and copies ran while one was open for 7% of the time, Pallas kernels for 0%

profile of v5, /device:TPU:3, one launch (start us, length us, event | category | flops | bytes accessed | tf_op | source)
XLA Modules:
  0.0 286.3 jit_solution(8974592222065617204)
XLA Ops:
  1.5 3.2 %collective-permute-start = (bf16[2,128,256]{2,1,0:T(8,128)(2,1)S(1)}, bf16[2,128,256]{2,1,0:T(8,128)(2,1)S(1)}, u32[]{:S(2)}, u32[]{:S(2)}) collective-permute-start(bf16[2,128,256]{2,1,0:T(8,128)(2,1)S(1)} %pad_maximum_fusion.4), channel_id=1, source_target_pairs={{0,4},{4,8},{8,12},{1,5},{5,9},{9,13},{2,6},{6,10},{10,14},{3,7},{... | collective-permute-start | bytes 393224 | tf_op jit(solution)/shard_map/ppermute | solution.py:23
  4.7 4.2 %collective-permute-start.1 = (bf16[2,128,256]{2,1,0:T(8,128)(2,1)S(1)}, bf16[2,128,256]{2,1,0:T(8,128)(2,1)S(1)}, u32[]{:S(2)}, u32[]{:S(2)}) collective-permute-start(bf16[2,128,256]{2,1,0:T(8,128)(2,1)S(1)} %pad_maximum_fusion.4), channel_id=1, source_target_pairs={{0,8},{4,12},{1,9},{5,13},{2,10},{6,14},{3,11},{7,15},{16,24},{20,... | collective-permute-start | bytes 393224 | tf_op jit(solution)/shard_map/ppermute | solution.py:23
  17.9 9.0 %collective-permute-start.3 = (bf16[128,1024]{1,0:T(8,128)(2,1)S(1)}, bf16[128,1024]{1,0:T(8,128)(2,1)S(1)}, u32[]{:S(2)}, u32[]{:S(2)}) collective-permute-start(bf16[128,1024]{1,0:T(8,128)(2,1)S(1)} %get-tuple-element.70), channel_id=1, source_target_pairs={{0,0},{1,4},{2,8},{3,12},{4,1},{5,5},{6,9},{7,13},{8,2},{9,6},{10,... | collective-permute-start | bytes 786440 | tf_op jit(solution)/shard_map/ppermute | solution.py:33
  28.1 2.7 collective-permute-done.5
  30.8 1.8 collective-permute-done.3
  32.7 6.0 %collective-permute-done.6 = bf16[128,1024]{1,0:T(8,128)(2,1)S(1)} collective-permute-done((bf16[128,1024]{1,0:T(8,128)(2,1)S(1)}, bf16[128,1024]{1,0:T(8,128)(2,1)S(1)}, u32[]{:S(2)}, u32[]{:S(2)}) %collective-permute-start.6) | collective-permute-done | bytes 262176 | tf_op jit(solution)/shard_map/ppermute | solution.py:27
  38.7 5.1 %collective-permute-start.7 = (bf16[2,128,1024]{2,1,0:T(8,128)(2,1)S(1)}, bf16[2,128,1024]{2,1,0:T(8,128)(2,1)S(1)}, u32[]{:S(2)}, u32[]{:S(2)}) collective-permute-start(bf16[2,128,1024]{2,1,0:T(8,128)(2,1)S(1)} %pad_maximum_fusion.3), channel_id=1, source_target_pairs={{0,1},{1,0},{2,3},{3,2},{4,5},{5,4},{6,7},{7,6},{8,9},{9,8},{10,11... | collective-permute-start | bytes 1572872 | tf_op jit(solution)/shard_map/ppermute | solution.py:27
  43.8 1.5 collective-permute-done.7
  45.8 1.6 copy-done.5
  47.4 2.1 convolution_convert_fusion.1
  49.5 2.1 convolution_convert_fusion
  53.3 3.1 %collective-permute-start.8 = (bf16[128,1792]{1,0:T(8,128)(2,1)}, bf16[128,1792]{1,0:T(8,128)(2,1)S(1)}, u32[]{:S(2)}, u32[]{:S(2)}) collective-permute-start(bf16[128,1792]{1,0:T(8,128)(2,1)} %get-tuple-element.35), channel_id=1, source_target_pairs={{0,4},{4,8},{8,12},{1,5},{5,9},{9,13},{2,6},{6,10},{10,14},{3,7},{... | collective-permute-start | bytes 1376264 | tf_op jit(solution)/shard_map/ppermute | solution.py:23
  57.8 4.1 %collective-permute-start.14 = (bf16[128,1792]{1,0:T(8,128)(2,1)}, bf16[128,1792]{1,0:T(8,128)(2,1)S(1)}, u32[]{:S(2)}, u32[]{:S(2)}) collective-permute-start(bf16[128,1792]{1,0:T(8,128)(2,1)} %get-tuple-element.42), channel_id=1, source_target_pairs={{0,4},{4,8},{8,12},{1,5},{5,9},{9,13},{2,6},{6,10},{10,14},{3,7},{... | collective-permute-start | bytes 1376264 | tf_op jit(solution)/shard_map/ppermute | solution.py:23
  63.3 3.0 %collective-permute-done.8 = bf16[128,1792]{1,0:T(8,128)(2,1)S(1)} collective-permute-done((bf16[128,1792]{1,0:T(8,128)(2,1)}, bf16[128,1792]{1,0:T(8,128)(2,1)S(1)}, u32[]{:S(2)}, u32[]{:S(2)}) %collective-permute-start.8) | collective-permute-done | bytes 458784 | tf_op jit(solution)/shard_map/ppermute | solution.py:23
  66.2 3.8 %collective-permute-done.9 = bf16[128,1792]{1,0:T(8,128)(2,1)S(1)} collective-permute-done((bf16[128,1792]{1,0:T(8,128)(2,1)}, bf16[128,1792]{1,0:T(8,128)(2,1)S(1)}, u32[]{:S(2)}, u32[]{:S(2)}) %collective-permute-start.9) | collective-permute-done | bytes 458784 | tf_op jit(solution)/shard_map/ppermute | solution.py:23
  70.2 2.2 collective-permute-start.10
  73.7 2.3 collective-permute-done.14
  76.1 3.8 %collective-permute-done.15 = bf16[128,1792]{1,0:T(8,128)(2,1)S(1)} collective-permute-done((bf16[128,1792]{1,0:T(8,128)(2,1)S(1)}, bf16[128,1792]{1,0:T(8,128)(2,1)S(1)}, u32[]{:S(2)}, u32[]{:S(2)}) %collective-permute-start.15) | collective-permute-done | bytes 458784 | tf_op jit(solution)/shard_map/ppermute | solution.py:23
  80.1 2.2 collective-permute-start.16
  83.6 2.2 collective-permute-done.10
  85.8 3.9 %collective-permute-done.11 = bf16[128,1792]{1,0:T(8,128)(2,1)S(1)} collective-permute-done((bf16[128,1792]{1,0:T(8,128)(2,1)S(1)}, bf16[128,1792]{1,0:T(8,128)(2,1)S(1)}, u32[]{:S(2)}, u32[]{:S(2)}) %collective-permute-start.11) | collective-permute-done | bytes 458784 | tf_op jit(solution)/shard_map/ppermute | solution.py:23
  90.9 3.1 %collective-permute-start.12 = (bf16[128,1792]{1,0:T(8,128)(2,1)}, bf16[128,1792]{1,0:T(8,128)(2,1)}, u32[]{:S(2)}, u32[]{:S(2)}) collective-permute-start(bf16[128,1792]{1,0:T(8,128)(2,1)} %get-tuple-element.39), channel_id=1, source_target_pairs={{0,4},{4,8},{8,12},{1,5},{5,9},{9,13},{2,6},{6,10},{10,14},{3,7},{... | collective-permute-start | bytes 1376264 | tf_op jit(solution)/shard_map/ppermute | solution.py:23
  95.6 3.9 %collective-permute-done.17 = bf16[128,1792]{1,0:T(8,128)(2,1)S(1)} collective-permute-done((bf16[128,1792]{1,0:T(8,128)(2,1)S(1)}, bf16[128,1792]{1,0:T(8,128)(2,1)S(1)}, u32[]{:S(2)}, u32[]{:S(2)}) %collective-permute-start.17) | collective-permute-done | bytes 458784 | tf_op jit(solution)/shard_map/ppermute | solution.py:23
  100.6 3.2 %collective-permute-start.18 = (bf16[128,1792]{1,0:T(8,128)(2,1)}, bf16[128,1792]{1,0:T(8,128)(2,1)}, u32[]{:S(2)}, u32[]{:S(2)}) collective-permute-start(bf16[128,1792]{1,0:T(8,128)(2,1)} %get-tuple-element.46), channel_id=1, source_target_pairs={{0,4},{4,8},{8,12},{1,5},{5,9},{9,13},{2,6},{6,10},{10,14},{3,7},{... | collective-permute-start | bytes 1376264 | tf_op jit(solution)/shard_map/ppermute | solution.py:23
  109.4 6.0 %collective-permute-done.18 = bf16[128,1792]{1,0:T(8,128)(2,1)} collective-permute-done((bf16[128,1792]{1,0:T(8,128)(2,1)}, bf16[128,1792]{1,0:T(8,128)(2,1)}, u32[]{:S(2)}, u32[]{:S(2)}) %collective-permute-start.18) | collective-permute-done | bytes 458784 | tf_op jit(solution)/shard_map/ppermute | solution.py:23
  115.4 3.9 %collective-permute-done.19 = bf16[128,1792]{1,0:T(8,128)(2,1)} collective-permute-done((bf16[128,1792]{1,0:T(8,128)(2,1)}, bf16[128,1792]{1,0:T(8,128)(2,1)}, u32[]{:S(2)}, u32[]{:S(2)}) %collective-permute-start.19) | collective-permute-done | bytes 458784 | tf_op jit(solution)/shard_map/ppermute | solution.py:23
  119.3 3.0 %multiply_reduce_fusion.1 = (f32[128]{0:T(128)S(1)}, f32[]{:T(128)}, f32[128,1792]{1,0:T(8,128)S(1)}, f32[128,1792]{1,0:T(8,128)S(1)}) fusion(f32[128,1792]{1,0:T(8,128)S(1)} %copy.31, bf16[128,1792]{1,0:T(8,128)(2,1)S(1)} %copy-done.10, f32[128]{0:T(128)S(1)} %add_sqrt_fusion, bf16[128,1792]{1,0:T(8,128)(2,1)} %collective-permute-done.19, ...), kind=kLoop, calls=%fused_computation.51 | loop fusion | flops 5046143 | bytes 5964808 | tf_op jit(solution)/shard_map/reduce_sum | solution.py:107
  124.2 4.3 %collective-permute-start.27 = (bf16[128,5376]{1,0:T(8,128)(2,1)S(1)}, bf16[128,5376]{1,0:T(8,128)(2,1)S(1)}, u32[]{:S(2)}, u32[]{:S(2)}) collective-permute-start(bf16[128,5376]{1,0:T(8,128)(2,1)S(1)} %pad_maximum_fusion), channel_id=1, source_target_pairs={{0,4},{4,8},{8,12},{1,5},{5,9},{9,13},{2,6},{6,10},{10,14},{3,7},{... | collective-permute-start | bytes 4128776 | tf_op jit(solution)/shard_map/ppermute | solution.py:23
  129.2 2.1 collective-permute-start.24
  137.0 18.0 %collective-permute-done.26 = bf16[128,5376]{1,0:T(8,128)(2,1)S(1)} collective-permute-done((bf16[128,5376]{1,0:T(8,128)(2,1)S(1)}, bf16[128,5376]{1,0:T(8,128)(2,1)S(1)}, u32[]{:S(2)}, u32[]{:S(2)}) %collective-permute-start.26) | collective-permute-done | bytes 1376288 | tf_op jit(solution)/shard_map/ppermute | solution.py:23
  159.3 5.8 %collective-permute-start.34 = (bf16[128,5376]{1,0:T(8,128)(2,1)S(1)}, bf16[128,5376]{1,0:T(8,128)(2,1)}, u32[]{:S(2)}, u32[]{:S(2)}) collective-permute-start(bf16[128,5376]{1,0:T(8,128)(2,1)S(1)} %collective-permute-done.27), channel_id=1, source_target_pairs={{0,4},{4,8},{8,12},{1,5},{5,9},{9,13},{2,6},{6,10},{10,14},{3,7},{... | collective-permute-start | bytes 4128776 | tf_op jit(solution)/shard_map/ppermute | solution.py:23
  166.4 3.0 %collective-permute-start.28 = (bf16[128,1024]{1,0:T(8,128)(2,1)S(1)}, bf16[128,1024]{1,0:T(8,128)(2,1)S(1)}, u32[]{:S(2)}, u32[]{:S(2)}) collective-permute-start(bf16[128,1024]{1,0:T(8,128)(2,1)S(1)} %get-tuple-element.103), channel_id=1, source_target_pairs={{0,1},{1,0},{2,3},{3,2},{4,5},{5,4},{6,7},{7,6},{8,9},{9,8},{10,11... | collective-permute-start | bytes 786440 | tf_op jit(solution)/shard_map/ppermute | solution.py:27
  171.0 4.0 %collective-permute-start.29 = (bf16[128,1024]{1,0:T(8,128)(2,1)S(1)}, bf16[128,1024]{1,0:T(8,128)(2,1)S(1)}, u32[]{:S(2)}, u32[]{:S(2)}) collective-permute-start(bf16[128,1024]{1,0:T(8,128)(2,1)S(1)} %fusion.50), channel_id=1, source_target_pairs={{3,1},{0,2},{7,5},{4,6},{11,9},{8,10},{15,13},{12,14},{19,17},{16,... | collective-permute-start | bytes 786440 | tf_op jit(solution)/shard_map/ppermute | solution.py:172
  175.0 2.2 collective-permute-done.21
  178.0 2.4 collective-permute-start.23
  181.3 9.7 %collective-permute-done.32 = f32[128]{0:T(128)S(1)} collective-permute-done((f32[128]{0:T(128)S(1)}, f32[128]{0:T(128)S(1)}, u32[]{:S(2)}, u32[]{:S(2)}) %collective-permute-start.32) | collective-permute-done | bytes 544 | tf_op jit(solution)/shard_map/ppermute | solution.py:187
  193.0 1.5 broadcast_select_fusion
  197.7 5.9 %collective-permute-start.41 = (bf16[128,5376]{1,0:T(8,128)(2,1)}, bf16[128,5376]{1,0:T(8,128)(2,1)}, u32[]{:S(2)}, u32[]{:S(2)}) collective-permute-start(bf16[128,5376]{1,0:T(8,128)(2,1)} %collective-permute-done.34), channel_id=1, source_target_pairs={{0,4},{4,8},{8,12},{1,5},{5,9},{9,13},{2,6},{6,10},{10,14},{3,7},{... | collective-permute-start | bytes 4128776 | tf_op jit(solution)/shard_map/ppermute | solution.py:23
  205.0 14.1 %collective-permute-start.35 = (bf16[128,1024]{1,0:T(8,128)(2,1)S(1)}, bf16[128,1024]{1,0:T(8,128)(2,1)S(1)}, u32[]{:S(2)}, u32[]{:S(2)}) collective-permute-start(bf16[128,1024]{1,0:T(8,128)(2,1)S(1)} %get-tuple-element.105), channel_id=1, source_target_pairs={{0,1},{1,0},{2,3},{3,2},{4,5},{5,4},{6,7},{7,6},{8,9},{9,8},{10,11... | collective-permute-start | bytes 786440 | tf_op jit(solution)/shard_map/ppermute | solution.py:27
  220.3 3.6 %collective-permute-start.36 = (bf16[128,1024]{1,0:T(8,128)(2,1)S(1)}, bf16[128,1024]{1,0:T(8,128)(2,1)S(1)}, u32[]{:S(2)}, u32[]{:S(2)}) collective-permute-start(bf16[128,1024]{1,0:T(8,128)(2,1)S(1)} %fusion.51), channel_id=1, source_target_pairs={{0,2},{3,1},{4,6},{7,5},{8,10},{11,9},{12,14},{15,13},{16,18},{19,... | collective-permute-start | bytes 786440 | tf_op jit(solution)/shard_map/ppermute | solution.py:172
  223.9 3.3 %collective-permute-done.36 = bf16[128,1024]{1,0:T(8,128)(2,1)S(1)} collective-permute-done((bf16[128,1024]{1,0:T(8,128)(2,1)S(1)}, bf16[128,1024]{1,0:T(8,128)(2,1)S(1)}, u32[]{:S(2)}, u32[]{:S(2)}) %collective-permute-start.36) | collective-permute-done | bytes 262176 | tf_op jit(solution)/shard_map/ppermute | solution.py:172
  230.8 8.8 %collective-permute-done.39 = f32[128]{0:T(128)} collective-permute-done((f32[128]{0:T(128)}, f32[128]{0:T(128)}, u32[]{:S(2)}, u32[]{:S(2)}) %collective-permute-start.39) | collective-permute-done | bytes 544 | tf_op jit(solution)/shard_map/ppermute | solution.py:187
  240.3 1.7 select_select_fusion
  248.1 8.2 %collective-permute-start.42 = (bf16[128,1024]{1,0:T(8,128)(2,1)S(1)}, bf16[128,1024]{1,0:T(8,128)(2,1)S(1)}, u32[]{:S(2)}, u32[]{:S(2)}) collective-permute-start(bf16[128,1024]{1,0:T(8,128)(2,1)S(1)} %get-tuple-element.107), channel_id=1, source_target_pairs={{0,1},{1,0},{2,3},{3,2},{4,5},{5,4},{6,7},{7,6},{8,9},{9,8},{10,11... | collective-permute-start | bytes 786440 | tf_op jit(solution)/shard_map/ppermute | solution.py:27
  258.9 5.8 %collective-permute-done.43 = bf16[128,1024]{1,0:T(8,128)(2,1)S(1)} collective-permute-done((bf16[128,1024]{1,0:T(8,128)(2,1)S(1)}, bf16[128,1024]{1,0:T(8,128)(2,1)S(1)}, u32[]{:S(2)}, u32[]{:S(2)}) %collective-permute-start.43) | collective-permute-done | bytes 262176 | tf_op jit(solution)/shard_map/ppermute | solution.py:172
  264.9 7.6 %collective-permute-start.44 = (bf16[128,1024]{1,0:T(8,128)(2,1)S(1)}, bf16[128,1024]{1,0:T(8,128)(2,1)S(1)}, u32[]{:S(2)}, u32[]{:S(2)}) collective-permute-start(bf16[128,1024]{1,0:T(8,128)(2,1)S(1)} %add_convert_fusion), channel_id=1, source_target_pairs={{3,12},{7,1},{11,14},{15,3},{19,28},{23,17},{27,30},{31,19}} | collective-permute-start | bytes 786440 | tf_op jit(solution)/shard_map/ppermute | solution.py:174
  275.8 7.1 %collective-permute-done.45 = bf16[128,1024]{1,0:T(8,128)(2,1)S(1)} collective-permute-done((bf16[128,1024]{1,0:T(8,128)(2,1)S(1)}, bf16[128,1024]{1,0:T(8,128)(2,1)S(1)}, u32[]{:S(2)}, u32[]{:S(2)}) %collective-permute-start.45) | collective-permute-done | bytes 262176 | tf_op jit(solution)/shard_map/ppermute | solution.py:174
  282.9 2.3 fusion.28
  (159 shorter events, 67.5 us)
Async XLA Ops:
  1.5 11.0 %collective-permute-start = (bf16[2,128,256]{2,1,0:T(8,128)(2,1)S(1)}, bf16[2,128,256]{2,1,0:T(8,128)(2,1)S(1)}, u32[]{:S(2)}, u32[]{:S(2)}) collective-permute-start(bf16[2,128,256]{2,1,0:T(8,128)(2,1)S(1)} %pad_maximum_fusion.4), channel_id=1, source_target_pairs={{0,4},{4,8},{8,12},{1,5},{5,9},{9,13},{2,6},{6,10},{10,14},{3,7},{... | collective-permute-start | bytes 393224 | tf_op jit(solution)/shard_map/ppermute | solution.py:23
  4.7 7.8 %collective-permute-start.1 = (bf16[2,128,256]{2,1,0:T(8,128)(2,1)S(1)}, bf16[2,128,256]{2,1,0:T(8,128)(2,1)S(1)}, u32[]{:S(2)}, u32[]{:S(2)}) collective-permute-start(bf16[2,128,256]{2,1,0:T(8,128)(2,1)S(1)} %pad_maximum_fusion.4), channel_id=1, source_target_pairs={{0,8},{4,12},{1,9},{5,13},{2,10},{6,14},{3,11},{7,15},{16,24},{20,... | collective-permute-start | bytes 393224 | tf_op jit(solution)/shard_map/ppermute | solution.py:23
  9.0 4.8 %collective-permute-start.2 = (bf16[2,128,256]{2,1,0:T(8,128)(2,1)S(1)}, bf16[2,128,256]{2,1,0:T(8,128)(2,1)S(1)}, u32[]{:S(2)}, u32[]{:S(2)}) collective-permute-start(bf16[2,128,256]{2,1,0:T(8,128)(2,1)S(1)} %pad_maximum_fusion.4), channel_id=1, source_target_pairs={{0,12},{1,13},{2,14},{3,15},{16,28},{17,29},{18,30},{19,31}} | collective-permute-start | bytes 393224 | tf_op jit(solution)/shard_map/ppermute | solution.py:23
  17.9 14.8 %collective-permute-start.3 = (bf16[128,1024]{1,0:T(8,128)(2,1)S(1)}, bf16[128,1024]{1,0:T(8,128)(2,1)S(1)}, u32[]{:S(2)}, u32[]{:S(2)}) collective-permute-start(bf16[128,1024]{1,0:T(8,128)(2,1)S(1)} %get-tuple-element.70), channel_id=1, source_target_pairs={{0,0},{1,4},{2,8},{3,12},{4,1},{5,5},{6,9},{7,13},{8,2},{9,6},{10,... | collective-permute-start | bytes 786440 | tf_op jit(solution)/shard_map/ppermute | solution.py:33
  26.9 1.2 collective-permute-start.4
  28.1 2.7 collective-permute-start.5
  30.8 78.1 %copy-start.18 = (f32[128]{0:T(128)}, f32[128]{0:T(128)S(1)}, u32[]{:S(2)}) copy-start(f32[128]{0:T(128)S(1)} %add_multiply_fusion) | copy-start | bytes 1540
  32.7 6.0 %collective-permute-start.6 = (bf16[128,1024]{1,0:T(8,128)(2,1)S(1)}, bf16[128,1024]{1,0:T(8,128)(2,1)S(1)}, u32[]{:S(2)}, u32[]{:S(2)}) collective-permute-start(bf16[128,1024]{1,0:T(8,128)(2,1)S(1)} %collective-permute-done.3), channel_id=1, source_target_pairs={{0,2},{2,0},{1,3},{3,1},{4,6},{6,4},{5,7},{7,5},{8,10},{10,8},{9,1... | collective-permute-start | bytes 786440 | tf_op jit(solution)/shard_map/ppermute | solution.py:27
  38.7 6.6 %collective-permute-start.7 = (bf16[2,128,1024]{2,1,0:T(8,128)(2,1)S(1)}, bf16[2,128,1024]{2,1,0:T(8,128)(2,1)S(1)}, u32[]{:S(2)}, u32[]{:S(2)}) collective-permute-start(bf16[2,128,1024]{2,1,0:T(8,128)(2,1)S(1)} %pad_maximum_fusion.3), channel_id=1, source_target_pairs={{0,1},{1,0},{2,3},{3,2},{4,5},{5,4},{6,7},{7,6},{8,9},{9,8},{10,11... | collective-permute-start | bytes 1572872 | tf_op jit(solution)/shard_map/ppermute | solution.py:27
  53.3 12.9 %collective-permute-start.8 = (bf16[128,1792]{1,0:T(8,128)(2,1)}, bf16[128,1792]{1,0:T(8,128)(2,1)S(1)}, u32[]{:S(2)}, u32[]{:S(2)}) collective-permute-start(bf16[128,1792]{1,0:T(8,128)(2,1)} %get-tuple-element.35), channel_id=1, source_target_pairs={{0,4},{4,8},{8,12},{1,5},{5,9},{9,13},{2,6},{6,10},{10,14},{3,7},{... | collective-permute-start | bytes 1376264 | tf_op jit(solution)/shard_map/ppermute | solution.py:23
  56.5 13.5 %collective-permute-start.9 = (bf16[128,1792]{1,0:T(8,128)(2,1)}, bf16[128,1792]{1,0:T(8,128)(2,1)S(1)}, u32[]{:S(2)}, u32[]{:S(2)}) collective-permute-start(bf16[128,1792]{1,0:T(8,128)(2,1)} %get-tuple-element.36), channel_id=1, source_target_pairs={{4,0},{8,4},{12,8},{5,1},{9,5},{13,9},{6,2},{10,6},{14,10},{7,3},{... | collective-permute-start | bytes 1376264 | tf_op jit(solution)/shard_map/ppermute | solution.py:23
  57.8 18.3 %collective-permute-start.14 = (bf16[128,1792]{1,0:T(8,128)(2,1)}, bf16[128,1792]{1,0:T(8,128)(2,1)S(1)}, u32[]{:S(2)}, u32[]{:S(2)}) collective-permute-start(bf16[128,1792]{1,0:T(8,128)(2,1)} %get-tuple-element.42), channel_id=1, source_target_pairs={{0,4},{4,8},{8,12},{1,5},{5,9},{9,13},{2,6},{6,10},{10,14},{3,7},{... | collective-permute-start | bytes 1376264 | tf_op jit(solution)/shard_map/ppermute | solution.py:23
  62.0 17.9 %collective-permute-start.15 = (bf16[128,1792]{1,0:T(8,128)(2,1)S(1)}, bf16[128,1792]{1,0:T(8,128)(2,1)S(1)}, u32[]{:S(2)}, u32[]{:S(2)}) collective-permute-start(bf16[128,1792]{1,0:T(8,128)(2,1)S(1)} %get-tuple-element.43), channel_id=1, source_target_pairs={{4,0},{8,4},{12,8},{5,1},{9,5},{13,9},{6,2},{10,6},{14,10},{7,3},{... | collective-permute-start | bytes 1376264 | tf_op jit(solution)/shard_map/ppermute | solution.py:23
  70.2 15.6 %collective-permute-start.10 = (bf16[128,1792]{1,0:T(8,128)(2,1)S(1)}, bf16[128,1792]{1,0:T(8,128)(2,1)S(1)}, u32[]{:S(2)}, u32[]{:S(2)}) collective-permute-start(bf16[128,1792]{1,0:T(8,128)(2,1)S(1)} %get-tuple-element.37), channel_id=1, source_target_pairs={{0,4},{4,8},{8,12},{1,5},{5,9},{9,13},{2,6},{6,10},{10,14},{3,7},{... | collective-permute-start | bytes 1376264 | tf_op jit(solution)/shard_map/ppermute | solution.py:23
  72.4 17.2 %collective-permute-start.11 = (bf16[128,1792]{1,0:T(8,128)(2,1)S(1)}, bf16[128,1792]{1,0:T(8,128)(2,1)S(1)}, u32[]{:S(2)}, u32[]{:S(2)}) collective-permute-start(bf16[128,1792]{1,0:T(8,128)(2,1)S(1)} %get-tuple-element.38), channel_id=1, source_target_pairs={{4,0},{8,4},{12,8},{5,1},{9,5},{13,9},{6,2},{10,6},{14,10},{7,3},{... | collective-permute-start | bytes 1376264 | tf_op jit(solution)/shard_map/ppermute | solution.py:23
  80.1 15.6 %collective-permute-start.16 = (bf16[128,1792]{1,0:T(8,128)(2,1)S(1)}, bf16[128,1792]{1,0:T(8,128)(2,1)S(1)}, u32[]{:S(2)}, u32[]{:S(2)}) collective-permute-start(bf16[128,1792]{1,0:T(8,128)(2,1)S(1)} %get-tuple-element.44), channel_id=1, source_target_pairs={{0,4},{4,8},{8,12},{1,5},{5,9},{9,13},{2,6},{6,10},{10,14},{3,7},{... | collective-permute-start | bytes 1376264 | tf_op jit(solution)/shard_map/ppermute | solution.py:23
  82.3 17.2 %collective-permute-start.17 = (bf16[128,1792]{1,0:T(8,128)(2,1)S(1)}, bf16[128,1792]{1,0:T(8,128)(2,1)S(1)}, u32[]{:S(2)}, u32[]{:S(2)}) collective-permute-start(bf16[128,1792]{1,0:T(8,128)(2,1)S(1)} %get-tuple-element.45), channel_id=1, source_target_pairs={{4,0},{8,4},{12,8},{5,1},{9,5},{13,9},{6,2},{10,6},{14,10},{7,3},{... | collective-permute-start | bytes 1376264 | tf_op jit(solution)/shard_map/ppermute | solution.py:23
  90.9 18.1 %collective-permute-start.12 = (bf16[128,1792]{1,0:T(8,128)(2,1)}, bf16[128,1792]{1,0:T(8,128)(2,1)}, u32[]{:S(2)}, u32[]{:S(2)}) collective-permute-start(bf16[128,1792]{1,0:T(8,128)(2,1)} %get-tuple-element.39), channel_id=1, source_target_pairs={{0,4},{4,8},{8,12},{1,5},{5,9},{9,13},{2,6},{6,10},{10,14},{3,7},{... | collective-permute-start | bytes 1376264 | tf_op jit(solution)/shard_map/ppermute | solution.py:23
  93.9 15.5 %collective-permute-start.13 = (bf16[128,1792]{1,0:T(8,128)(2,1)}, bf16[128,1792]{1,0:T(8,128)(2,1)}, u32[]{:S(2)}, u32[]{:S(2)}) collective-permute-start(bf16[128,1792]{1,0:T(8,128)(2,1)} %get-tuple-element.40), channel_id=1, source_target_pairs={{4,0},{8,4},{12,8},{5,1},{9,5},{13,9},{6,2},{10,6},{14,10},{7,3},{... | collective-permute-start | bytes 1376264 | tf_op jit(solution)/shard_map/ppermute | solution.py:23
  100.6 14.8 %collective-permute-start.18 = (bf16[128,1792]{1,0:T(8,128)(2,1)}, bf16[128,1792]{1,0:T(8,128)(2,1)}, u32[]{:S(2)}, u32[]{:S(2)}) collective-permute-start(bf16[128,1792]{1,0:T(8,128)(2,1)} %get-tuple-element.46), channel_id=1, source_target_pairs={{0,4},{4,8},{8,12},{1,5},{5,9},{9,13},{2,6},{6,10},{10,14},{3,7},{... | collective-permute-start | bytes 1376264 | tf_op jit(solution)/shard_map/ppermute | solution.py:23
  103.8 15.4 %collective-permute-start.19 = (bf16[128,1792]{1,0:T(8,128)(2,1)}, bf16[128,1792]{1,0:T(8,128)(2,1)}, u32[]{:S(2)}, u32[]{:S(2)}) collective-permute-start(bf16[128,1792]{1,0:T(8,128)(2,1)} %get-tuple-element.47), channel_id=1, source_target_pairs={{4,0},{8,4},{12,8},{5,1},{9,5},{13,9},{6,2},{10,6},{14,10},{7,3},{... | collective-permute-start | bytes 1376264 | tf_op jit(solution)/shard_map/ppermute | solution.py:23
  122.7 32.3 %collective-permute-start.26 = (bf16[128,5376]{1,0:T(8,128)(2,1)S(1)}, bf16[128,5376]{1,0:T(8,128)(2,1)S(1)}, u32[]{:S(2)}, u32[]{:S(2)}) collective-permute-start(bf16[128,5376]{1,0:T(8,128)(2,1)S(1)} %pad_maximum_fusion), channel_id=1, source_target_pairs={{4,0},{8,4},{12,8},{5,1},{9,5},{13,9},{6,2},{10,6},{14,10},{7,3},{... | collective-permute-start | bytes 4128776 | tf_op jit(solution)/shard_map/ppermute | solution.py:23
  124.2 31.7 %collective-permute-start.27 = (bf16[128,5376]{1,0:T(8,128)(2,1)S(1)}, bf16[128,5376]{1,0:T(8,128)(2,1)S(1)}, u32[]{:S(2)}, u32[]{:S(2)}) collective-permute-start(bf16[128,5376]{1,0:T(8,128)(2,1)S(1)} %pad_maximum_fusion), channel_id=1, source_target_pairs={{0,4},{4,8},{8,12},{1,5},{5,9},{9,13},{2,6},{6,10},{10,14},{3,7},{... | collective-permute-start | bytes 4128776 | tf_op jit(solution)/shard_map/ppermute | solution.py:23
  129.2 4.1 %collective-permute-start.24 = (f32[256]{0:T(256)S(1)}, f32[256]{0:T(256)S(1)}, u32[]{:S(2)}, u32[]{:S(2)}) collective-permute-start(f32[256]{0:T(256)S(1)} %pad_maximum_fusion.5), channel_id=1, source_target_pairs={{0,1},{1,0},{2,3},{3,2},{4,5},{5,4},{6,7},{7,6},{8,9},{9,8},{10,11... | collective-permute-start | bytes 3080 | tf_op jit(solution)/shard_map/ppermute | solution.py:27
  134.3 2.7 collective-permute-start.25
  135.9 33.5 %collective-permute-start.20 = (bf16[128,1024]{1,0:T(8,128)(2,1)S(1)}, bf16[128,1024]{1,0:T(8,128)(2,1)S(1)}, u32[]{:S(2)}, u32[]{:S(2)}) collective-permute-start(bf16[128,1024]{1,0:T(8,128)(2,1)S(1)} %get-tuple-element.101), channel_id=1, source_target_pairs={{0,1},{1,0},{2,3},{3,2},{4,5},{5,4},{6,7},{7,6},{8,9},{9,8},{10,11... | collective-permute-start | bytes 786440 | tf_op jit(solution)/shard_map/ppermute | solution.py:27
  158.0 34.2 %collective-permute-start.33 = (bf16[128,5376]{1,0:T(8,128)(2,1)S(1)}, bf16[128,5376]{1,0:T(8,128)(2,1)}, u32[]{:S(2)}, u32[]{:S(2)}) collective-permute-start(bf16[128,5376]{1,0:T(8,128)(2,1)S(1)} %collective-permute-done.26), channel_id=1, source_target_pairs={{4,0},{8,4},{12,8},{5,1},{9,5},{13,9},{6,2},{10,6},{14,10},{7,3},{... | collective-permute-start | bytes 4128776 | tf_op jit(solution)/shard_map/ppermute | solution.py:23
  159.3 32.9 %collective-permute-start.34 = (bf16[128,5376]{1,0:T(8,128)(2,1)S(1)}, bf16[128,5376]{1,0:T(8,128)(2,1)}, u32[]{:S(2)}, u32[]{:S(2)}) collective-permute-start(bf16[128,5376]{1,0:T(8,128)(2,1)S(1)} %collective-permute-done.27), channel_id=1, source_target_pairs={{0,4},{4,8},{8,12},{1,5},{5,9},{9,13},{2,6},{6,10},{10,14},{3,7},{... | collective-permute-start | bytes 4128776 | tf_op jit(solution)/shard_map/ppermute | solution.py:23
  166.4 4.4 %collective-permute-start.28 = (bf16[128,1024]{1,0:T(8,128)(2,1)S(1)}, bf16[128,1024]{1,0:T(8,128)(2,1)S(1)}, u32[]{:S(2)}, u32[]{:S(2)}) collective-permute-start(bf16[128,1024]{1,0:T(8,128)(2,1)S(1)} %get-tuple-element.103), channel_id=1, source_target_pairs={{0,1},{1,0},{2,3},{3,2},{4,5},{5,4},{6,7},{7,6},{8,9},{9,8},{10,11... | collective-permute-start | bytes 786440 | tf_op jit(solution)/shard_map/ppermute | solution.py:27
  169.5 7.6 %collective-permute-start.21 = (bf16[128,1024]{1,0:T(8,128)(2,1)S(1)}, bf16[128,1024]{1,0:T(8,128)(2,1)S(1)}, u32[]{:S(2)}, u32[]{:S(2)}) collective-permute-start(bf16[128,1024]{1,0:T(8,128)(2,1)S(1)} %fusion.49), channel_id=1, source_target_pairs={{2,0},{1,3},{6,4},{5,7},{10,8},{9,11},{14,12},{13,15},{18,16},{17,... | collective-permute-start | bytes 786440 | tf_op jit(solution)/shard_map/ppermute | solution.py:172
  171.0 9.4 %collective-permute-start.29 = (bf16[128,1024]{1,0:T(8,128)(2,1)S(1)}, bf16[128,1024]{1,0:T(8,128)(2,1)S(1)}, u32[]{:S(2)}, u32[]{:S(2)}) collective-permute-start(bf16[128,1024]{1,0:T(8,128)(2,1)S(1)} %fusion.50), channel_id=1, source_target_pairs={{3,1},{0,2},{7,5},{4,6},{11,9},{8,10},{15,13},{12,14},{19,17},{16,... | collective-permute-start | bytes 786440 | tf_op jit(solution)/shard_map/ppermute | solution.py:172
  177.3 3.3 %collective-permute-start.22 = (bf16[128,1024]{1,0:T(8,128)(2,1)S(1)}, bf16[128,1024]{1,0:T(8,128)(2,1)S(1)}, u32[]{:S(2)}, u32[]{:S(2)}) collective-permute-start(bf16[128,1024]{1,0:T(8,128)(2,1)S(1)} %add_convert_fusion.3), channel_id=1, source_target_pairs={{0,0},{4,5},{8,10},{12,15},{16,16},{20,21},{24,26},{28,31}} | collective-permute-start | bytes 786440 | tf_op jit(solution)/shard_map/ppermute | solution.py:174
  178.0 14.2 %collective-permute-start.23 = (bf16[128,1024]{1,0:T(8,128)(2,1)S(1)}, bf16[128,1024]{1,0:T(8,128)(2,1)S(1)}, u32[]{:S(2)}, u32[]{:S(2)}) collective-permute-start(bf16[128,1024]{1,0:T(8,128)(2,1)S(1)} %add_convert_fusion.3), channel_id=1, source_target_pairs={{3,0},{7,5},{11,10},{15,15},{19,16},{23,21},{27,26},{31,31}} | collective-permute-start | bytes 786440 | tf_op jit(solution)/shard_map/ppermute | solution.py:174
  180.4 10.6 %collective-permute-start.32 = (f32[128]{0:T(128)S(1)}, f32[128]{0:T(128)S(1)}, u32[]{:S(2)}, u32[]{:S(2)}) collective-permute-start(f32[128]{0:T(128)S(1)} %slice.84), channel_id=1, source_target_pairs={{0,4},{4,0},{8,12},{12,8},{1,5},{5,1},{9,13},{13,9},{2,6},{6,2},{1... | collective-permute-start | bytes 1544 | tf_op jit(solution)/shard_map/ppermute | solution.py:187
  180.6 11.6 %collective-permute-start.30 = (bf16[128,1024]{1,0:T(8,128)(2,1)S(1)}, bf16[128,1024]{1,0:T(8,128)(2,1)S(1)}, u32[]{:S(2)}, u32[]{:S(2)}) collective-permute-start(bf16[128,1024]{1,0:T(8,128)(2,1)S(1)} %add_convert_fusion.2), channel_id=1, source_target_pairs={{1,4},{5,9},{9,6},{13,11},{17,20},{21,25},{25,22},{29,27}} | collective-permute-start | bytes 786440 | tf_op jit(solution)/shard_map/ppermute | solution.py:174
  191.0 1.2 collective-permute-start.31
  196.4 43.9 %collective-permute-start.40 = (bf16[128,5376]{1,0:T(8,128)(2,1)}, bf16[128,5376]{1,0:T(8,128)(2,1)}, u32[]{:S(2)}, u32[]{:S(2)}) collective-permute-start(bf16[128,5376]{1,0:T(8,128)(2,1)} %collective-permute-done.33), channel_id=1, source_target_pairs={{4,0},{8,4},{12,8},{5,1},{9,5},{13,9},{6,2},{10,6},{14,10},{7,3},{... | collective-permute-start | bytes 4128776 | tf_op jit(solution)/shard_map/ppermute | solution.py:23
  197.7 42.6 %collective-permute-start.41 = (bf16[128,5376]{1,0:T(8,128)(2,1)}, bf16[128,5376]{1,0:T(8,128)(2,1)}, u32[]{:S(2)}, u32[]{:S(2)}) collective-permute-start(bf16[128,5376]{1,0:T(8,128)(2,1)} %collective-permute-done.34), channel_id=1, source_target_pairs={{0,4},{4,8},{8,12},{1,5},{5,9},{9,13},{2,6},{6,10},{10,14},{3,7},{... | collective-permute-start | bytes 4128776 | tf_op jit(solution)/shard_map/ppermute | solution.py:23
  205.0 15.2 %collective-permute-start.35 = (bf16[128,1024]{1,0:T(8,128)(2,1)S(1)}, bf16[128,1024]{1,0:T(8,128)(2,1)S(1)}, u32[]{:S(2)}, u32[]{:S(2)}) collective-permute-start(bf16[128,1024]{1,0:T(8,128)(2,1)S(1)} %get-tuple-element.105), channel_id=1, source_target_pairs={{0,1},{1,0},{2,3},{3,2},{4,5},{5,4},{6,7},{7,6},{8,9},{9,8},{10,11... | collective-permute-start | bytes 786440 | tf_op jit(solution)/shard_map/ppermute | solution.py:27
  220.3 6.9 %collective-permute-start.36 = (bf16[128,1024]{1,0:T(8,128)(2,1)S(1)}, bf16[128,1024]{1,0:T(8,128)(2,1)S(1)}, u32[]{:S(2)}, u32[]{:S(2)}) collective-permute-start(bf16[128,1024]{1,0:T(8,128)(2,1)S(1)} %fusion.51), channel_id=1, source_target_pairs={{0,2},{3,1},{4,6},{7,5},{8,10},{11,9},{12,14},{15,13},{16,18},{19,... | collective-permute-start | bytes 786440 | tf_op jit(solution)/shard_map/ppermute | solution.py:172
  228.0 12.3 %collective-permute-start.37 = (bf16[128,1024]{1,0:T(8,128)(2,1)}, bf16[128,1024]{1,0:T(8,128)(2,1)}, u32[]{:S(2)}, u32[]{:S(2)}) collective-permute-start(bf16[128,1024]{1,0:T(8,128)(2,1)} %add_convert_fusion.1), channel_id=1, source_target_pairs={{2,8},{6,13},{10,2},{14,7},{18,24},{22,29},{26,18},{30,23}} | collective-permute-start | bytes 786440 | tf_op jit(solution)/shard_map/ppermute | solution.py:174
  229.4 10.9 %collective-permute-start.38 = (bf16[128,1024]{1,0:T(8,128)(2,1)}, bf16[128,1024]{1,0:T(8,128)(2,1)}, u32[]{:S(2)}, u32[]{:S(2)}) collective-permute-start(bf16[128,1024]{1,0:T(8,128)(2,1)} %add_convert_fusion.1), channel_id=1, source_target_pairs={{1,8},{5,13},{9,2},{13,7},{17,24},{21,29},{25,18},{29,23}} | collective-permute-start | bytes 786440 | tf_op jit(solution)/shard_map/ppermute | solution.py:174
  230.7 8.9 %collective-permute-start.39 = (f32[128]{0:T(128)}, f32[128]{0:T(128)}, u32[]{:S(2)}, u32[]{:S(2)}) collective-permute-start(f32[128]{0:T(128)} %get-tuple-element.56), channel_id=1, source_target_pairs={{0,8},{4,12},{8,0},{12,4},{1,9},{5,13},{9,1},{13,5},{2,10},{6,14},... | collective-permute-start | bytes 1544 | tf_op jit(solution)/shard_map/ppermute | solution.py:187
  248.1 34.8 %copy-start.12 = (bf16[128,1024]{1,0:T(8,128)(2,1)S(1)}, bf16[128,1024]{1,0:T(8,128)(2,1)}, u32[]{:S(2)}) copy-start(bf16[128,1024]{1,0:T(8,128)(2,1)} %copy-done.11) | copy-start | bytes 786436
  248.1 9.4 %collective-permute-start.42 = (bf16[128,1024]{1,0:T(8,128)(2,1)S(1)}, bf16[128,1024]{1,0:T(8,128)(2,1)S(1)}, u32[]{:S(2)}, u32[]{:S(2)}) collective-permute-start(bf16[128,1024]{1,0:T(8,128)(2,1)S(1)} %get-tuple-element.107), channel_id=1, source_target_pairs={{0,1},{1,0},{2,3},{3,2},{4,5},{5,4},{6,7},{7,6},{8,9},{9,8},{10,11... | collective-permute-start | bytes 786440 | tf_op jit(solution)/shard_map/ppermute | solution.py:27
  257.6 7.1 %collective-permute-start.43 = (bf16[128,1024]{1,0:T(8,128)(2,1)S(1)}, bf16[128,1024]{1,0:T(8,128)(2,1)S(1)}, u32[]{:S(2)}, u32[]{:S(2)}) collective-permute-start(bf16[128,1024]{1,0:T(8,128)(2,1)S(1)} %fusion.52), channel_id=1, source_target_pairs={{1,3},{2,0},{5,7},{6,4},{9,11},{10,8},{13,15},{14,12},{17,19},{18,... | collective-permute-start | bytes 786440 | tf_op jit(solution)/shard_map/ppermute | solution.py:172
  264.9 10.9 %collective-permute-start.44 = (bf16[128,1024]{1,0:T(8,128)(2,1)S(1)}, bf16[128,1024]{1,0:T(8,128)(2,1)S(1)}, u32[]{:S(2)}, u32[]{:S(2)}) collective-permute-start(bf16[128,1024]{1,0:T(8,128)(2,1)S(1)} %add_convert_fusion), channel_id=1, source_target_pairs={{3,12},{7,1},{11,14},{15,3},{19,28},{23,17},{27,30},{31,19}} | collective-permute-start | bytes 786440 | tf_op jit(solution)/shard_map/ppermute | solution.py:174
  272.5 10.4 %collective-permute-start.45 = (bf16[128,1024]{1,0:T(8,128)(2,1)S(1)}, bf16[128,1024]{1,0:T(8,128)(2,1)S(1)}, u32[]{:S(2)}, u32[]{:S(2)}) collective-permute-start(bf16[128,1024]{1,0:T(8,128)(2,1)S(1)} %add_convert_fusion), channel_id=1, source_target_pairs={{0,12},{4,1},{8,14},{12,3},{16,28},{20,17},{24,30},{28,19}} | collective-permute-start | bytes 786440 | tf_op jit(solution)/shard_map/ppermute | solution.py:174
  (18 other events, 166.2 us)

commit v6 on v4

--- a/solution.py
+++ b/solution.py
@@ -5,6 +5,7 @@
 from jax import lax
 from jax.experimental.layout import Layout, with_layout_constraint
 from jax.sharding import PartitionSpec as P
+
 
 D = 4096
 HEADS = 32
@@ -158,43 +159,53 @@
         for i in range(2)
     ]
     hidden, grad_gate, grad_up, inner, loss = elementwise(gate_proj, up_proj, teacher_feats, keep_tiles)
-    owned = jnp.concatenate([hidden, grad_gate, grad_up], axis=1)
-
-    right, left = [shifted(owned, 1)], [shifted(owned, -1)]
-    for s in range(2):
-        right.append(shifted(right[s], 1))
-        left.append(shifted(left[s], -1))
-    turns = [owned, jnp.where(low, left[0], right[0])]
-    _, arrived = lax.optimization_barrier((turns[1], (left[1], right[1])))
-    turns.append(jnp.where(low, *arrived))
-    _, arrived = lax.optimization_barrier((turns[2], (left[2], right[2])))
-    outer = jnp.where(low, *arrived)
-    inward = jnp.where(low, right[0], left[0])
-    turns.append(jnp.where((z == 0) | (z == 3), outer, inward))
-
-    def brought_home(k, down, grad):
+
+    streams = [hidden, jnp.concatenate([grad_gate, grad_up], axis=1)]
+    right, left = [streams], [streams]
+    for s in range(3):
+        right.append([shifted(v, 1) for v in right[s]])
+        left.append([shifted(v, -1) for v in left[s]])
+    right, left = right[1:], left[1:]
+
+    def reduced(k, down, grad):
         keeps_down = pair == (k & 1)
         sent = jnp.where(keeps_down, grad, down).astype(BF16)
         half = jnp.where(keeps_down, down, grad) + swapped(sent, "pair").astype(F32)
         route = [(k ^ 2, k), (k ^ 1, k ^ 3)]
-        whole = (half + lax.ppermute(half.astype(BF16), HP, route).astype(F32)).astype(BF16)
+        return sent, (half + lax.ppermute(half.astype(BF16), HP, route).astype(F32)).astype(BF16)
+
+    def brought_home(k, whole):
         return [
             lax.ppermute(whole, ("ctx",) + HP, [(4 * c + h, 4 * TURNS[c][k] + c) for c in range(4)])
             for h in (k, k ^ 3)
         ]
 
-    home = []
-    for k in range(4):
-        block = turns[k]
-        down, grad = products(block[:, :ff], block[:, ff : 2 * ff], block[:, 2 * ff :], weights)
-        home.append(brought_home(k, down, grad))
+    def turn(k, values):
+        both = values[1]
+        return reduced(k, *products(values[0], both[:, :ff], both[:, ff:], weights))
+
+    def chosen(a, b):
+        return [jnp.where(low, v, w) for v, w in zip(a, b)]
 
     count = jnp.sum(keep_tiles.astype(F32)) * TILE
     small = jnp.concatenate([inner, loss[None], count[None], jnp.zeros(126, F32)])
     small = summed_over_hp(small)
-    totals, _ = lax.optimization_barrier((small[rows:], turns[3]))
-    for d in (1, 2):
-        totals = totals + lax.ppermute(totals, "ctx", [(c, c ^ d) for c in range(4)])
+
+    home, values = [], streams
+    ends = (z == 0) | (z == 3)
+    for k in range(4):
+        if k == 1:
+            values = chosen(left[0], right[0])
+        if k > 1:
+            _, arrived = lax.optimization_barrier((values, (left[k - 1], right[k - 1])))
+            values = chosen(*arrived)
+        if k == 3:
+            inward = chosen(right[0], left[0])
+            values = [jnp.where(ends, v, w) for v, w in zip(values, inward)]
+        sent, whole = turn(k, values)
+        home.append(brought_home(k, whole))
+    part, _ = lax.optimization_barrier((small[rows:], sent))
+    totals = part + sum(lax.ppermute(part, "ctx", [(c, c ^ d) for c in range(4)]) for d in (1, 2, 3))
     loss_value = (totals[0] / totals[1]).reshape(1)
 
     down, grad = [sum(h[i].astype(F32) for h in home) for i in range(2)]
@@ -210,7 +221,6 @@
     rows = residual.shape[0]
     d_ctx, ff = w_gate.shape
     tiles = keep_tiles.shape[1]
-    n_ctx = lax.axis_size("ctx")
     z = lax.axis_index("ctx")
     hp = lax.axis_index(HP)
     keep_cols = jnp.pad(keep_tiles.astype(BF16), ((0, 0), (0, -tiles % 128)))
@@ -261,8 +271,10 @@
     attended = attention(student_query, teacher_keys, teacher_values, band_span)
     residual = (residual_in.astype(F32) + attended).astype(BF16)
     sizes = tuple(lax.axis_size(a) for a in ("ctx", "head", "pair"))
-    finish = on_square if sizes == (4, 2, 2) else on_any
-    return finish(residual, norm_gain, (w_gate, w_up, w_down), teacher_feats, keep_tiles)
+    weights = (w_gate, w_up, w_down)
+    if sizes == (4, 2, 2):
+        return on_square(residual, norm_gain, weights, teacher_feats, keep_tiles)
+    return on_any(residual, norm_gain, weights, teacher_feats, keep_tiles)
 
 
 def solution(mesh):

time: 271 us -> 276 us (1.018)
  starting transfers between devices: 89.2 us -> 109 us
  waiting for transfers between devices: 128 us -> 117 us
    ppermute x21 -> x27, starting transfers between devices: 54 us -> 71.8 us  [passed_along(): return lax.ppermute(block, axis, route)]
    ppermute x6 -> x7, waiting for transfers between devices: 12.7 us -> 4.4 us  [the longest x4 4.39 us: reduced(): lax.ppermute(half.astype(BF16), HP, route).astype(F32)]
    ppermute x21 -> x27, waiting for transfers between devices: 87.4 us -> 81.2 us  [passed_along(): return lax.ppermute(block, axis, route)]
    ppermute x6 -> x7, starting transfers between devices: 13.4 us -> 14.7 us  [the longest x4 10.3 us: reduced(): lax.ppermute(half.astype(BF16), HP, route).astype(F32)]
  transfers between devices with their start and end apart: 46 -> 53, of which waited for: 31 -> 28; matrix products, arithmetic and copies ran while one was open for 10% -> 9% of each run, Pallas kernels for 0% -> 0%
where the time goes in v6:
time: 276 us; the launch traced here: 274 us
  waiting for transfers between devices  117 us (42%)
  starting transfers between devices  109 us (39%)
  matrix products  19.6 us (7%)
  other arithmetic  15.6 us (6%)
  local copies, waits for them, and re-layouts  7.28 us (3%)
  between operations  4.85 us (2%)
    ppermute x27, waiting for transfers between devices, passed_along(): return lax.ppermute(block, axis, route)  81.2 us
    ppermute x27, starting transfers between devices, passed_along(): return lax.ppermute(block, axis, route)  71.8 us
    ppermute x10, waiting for transfers between devices, swapped(): return lax.ppermute(block, axis, [(0, 1), (1, 0)])  14.8 us
    ppermute x8, starting transfers between devices, brought_home(): lax.ppermute(whole, ('ctx',) + HP, [(4 * c + h, 4 * TURNS[c][k] + c) for...  12.3 us
    ppermute x8, waiting for transfers between devices, brought_home(): lax.ppermute(whole, ('ctx',) + HP, [(4 * c + h, 4 * TURNS[c][k] + c) for...  10.4 us
    ppermute x4, starting transfers between devices, reduced(): lax.ppermute(half.astype(BF16), HP, route).astype(F32)  10.3 us
    ppermute x1, starting transfers between devices, transposed(): return lax.ppermute(block, ('ctx',) + HP, route)  8.02 us
    ppermute x1, waiting for transfers between devices, transposed(): return lax.ppermute(block, ('ctx',) + HP, route)  6.18 us
  transfers between devices with their start and end apart: 53, of which 28 were waited for; matrix products, arithmetic and copies ran while one was open for 9% of the time, Pallas kernels for 0%

profile of v6, /device:TPU:2, one launch (start us, length us, event | category | flops | bytes accessed | tf_op | source)
XLA Modules:
  0.0 273.7 jit_solution(10575172020679694686)
XLA Ops:
  1.5 5.5 %collective-permute-start.2 = (bf16[2,128,256]{2,1,0:T(8,128)(2,1)S(1)}, bf16[2,128,256]{2,1,0:T(8,128)(2,1)S(1)}, u32[]{:S(2)}, u32[]{:S(2)}) collective-permute-start(bf16[2,128,256]{2,1,0:T(8,128)(2,1)S(1)} %pad_maximum_fusion.4), channel_id=1, source_target_pairs={{0,12},{1,13},{2,14},{3,15},{16,28},{17,29},{18,30},{19,31}} | collective-permute-start | bytes 393224 | tf_op jit(solution)/shard_map/ppermute | solution.py:24
  8.3 2.5 collective-permute-start
  13.8 1.7 collective-permute-done
  19.5 8.0 %collective-permute-start.3 = (bf16[128,1024]{1,0:T(8,128)(2,1)S(1)}, bf16[128,1024]{1,0:T(8,128)(2,1)S(1)}, u32[]{:S(2)}, u32[]{:S(2)}) collective-permute-start(bf16[128,1024]{1,0:T(8,128)(2,1)S(1)} %get-tuple-element.54), channel_id=1, source_target_pairs={{0,0},{1,4},{2,8},{3,12},{4,1},{5,5},{6,9},{7,13},{8,2},{9,6},{10,... | collective-permute-start | bytes 786440 | tf_op jit(solution)/shard_map/ppermute | solution.py:34
  28.7 3.6 %collective-permute-done.5 = f32[128]{0:T(128)S(1)} collective-permute-done((f32[128]{0:T(128)S(1)}, f32[128]{0:T(128)S(1)}, u32[]{:S(2)}, u32[]{:S(2)}) %collective-permute-start.5) | collective-permute-done | bytes 544 | tf_op jit(solution)/shard_map/ppermute | solution.py:28
  32.3 6.2 %collective-permute-done.3 = bf16[128,1024]{1,0:T(8,128)(2,1)S(1)} collective-permute-done((bf16[128,1024]{1,0:T(8,128)(2,1)S(1)}, bf16[128,1024]{1,0:T(8,128)(2,1)S(1)}, u32[]{:S(2)}, u32[]{:S(2)}) %collective-permute-start.3) | collective-permute-done | bytes 262176 | tf_op jit(solution)/shard_map/ppermute | solution.py:34
  38.5 6.4 %collective-permute-done.6 = bf16[128,1024]{1,0:T(8,128)(2,1)S(1)} collective-permute-done((bf16[128,1024]{1,0:T(8,128)(2,1)S(1)}, bf16[128,1024]{1,0:T(8,128)(2,1)S(1)}, u32[]{:S(2)}, u32[]{:S(2)}) %collective-permute-start.6) | collective-permute-done | bytes 262176 | tf_op jit(solution)/shard_map/ppermute | solution.py:28
  45.0 1.8 collective-permute-done.7
  47.4 2.1 convolution_convert_fusion
  49.5 2.1 convolution_convert_fusion.1
  54.0 2.5 collective-permute-start.8
  57.8 4.7 %collective-permute-start.14 = (bf16[128,1792]{1,0:T(8,128)(2,1)}, bf16[128,1792]{1,0:T(8,128)(2,1)S(1)}, u32[]{:S(2)}, u32[]{:S(2)}) collective-permute-start(bf16[128,1792]{1,0:T(8,128)(2,1)} %get-tuple-element.34), channel_id=1, source_target_pairs={{0,4},{4,8},{8,12},{1,5},{5,9},{9,13},{2,6},{6,10},{10,14},{3,7},{... | collective-permute-start | bytes 1376264 | tf_op jit(solution)/shard_map/ppermute | solution.py:24
  63.8 3.8 %collective-permute-done.8 = bf16[128,1792]{1,0:T(8,128)(2,1)S(1)} collective-permute-done((bf16[128,1792]{1,0:T(8,128)(2,1)}, bf16[128,1792]{1,0:T(8,128)(2,1)S(1)}, u32[]{:S(2)}, u32[]{:S(2)}) %collective-permute-start.8) | collective-permute-done | bytes 458784 | tf_op jit(solution)/shard_map/ppermute | solution.py:24
  67.6 4.3 %collective-permute-done.9 = bf16[128,1792]{1,0:T(8,128)(2,1)S(1)} collective-permute-done((bf16[128,1792]{1,0:T(8,128)(2,1)}, bf16[128,1792]{1,0:T(8,128)(2,1)S(1)}, u32[]{:S(2)}, u32[]{:S(2)}) %collective-permute-start.9) | collective-permute-done | bytes 458784 | tf_op jit(solution)/shard_map/ppermute | solution.py:24
  71.9 1.4 fusion.18
  73.3 2.3 collective-permute-start.10
  77.4 4.3 %collective-permute-done.15 = bf16[128,1792]{1,0:T(8,128)(2,1)S(1)} collective-permute-done((bf16[128,1792]{1,0:T(8,128)(2,1)S(1)}, bf16[128,1792]{1,0:T(8,128)(2,1)S(1)}, u32[]{:S(2)}, u32[]{:S(2)}) %collective-permute-start.15) | collective-permute-done | bytes 458784 | tf_op jit(solution)/shard_map/ppermute | solution.py:24
  82.0 2.4 collective-permute-start.16
  85.7 1.4 collective-permute-done.10
  87.2 4.4 %collective-permute-done.11 = bf16[128,1792]{1,0:T(8,128)(2,1)S(1)} collective-permute-done((bf16[128,1792]{1,0:T(8,128)(2,1)S(1)}, bf16[128,1792]{1,0:T(8,128)(2,1)S(1)}, u32[]{:S(2)}, u32[]{:S(2)}) %collective-permute-start.11) | collective-permute-done | bytes 458784 | tf_op jit(solution)/shard_map/ppermute | solution.py:24
  92.8 3.0 %collective-permute-start.12 = (bf16[128,1792]{1,0:T(8,128)(2,1)}, bf16[128,1792]{1,0:T(8,128)(2,1)}, u32[]{:S(2)}, u32[]{:S(2)}) collective-permute-start(bf16[128,1792]{1,0:T(8,128)(2,1)} %get-tuple-element.31), channel_id=1, source_target_pairs={{0,4},{4,8},{8,12},{1,5},{5,9},{9,13},{2,6},{6,10},{10,14},{3,7},{... | collective-permute-start | bytes 1376264 | tf_op jit(solution)/shard_map/ppermute | solution.py:24
  97.1 4.3 %collective-permute-done.17 = bf16[128,1792]{1,0:T(8,128)(2,1)S(1)} collective-permute-done((bf16[128,1792]{1,0:T(8,128)(2,1)S(1)}, bf16[128,1792]{1,0:T(8,128)(2,1)S(1)}, u32[]{:S(2)}, u32[]{:S(2)}) %collective-permute-start.17) | collective-permute-done | bytes 458784 | tf_op jit(solution)/shard_map/ppermute | solution.py:24
  102.6 3.0 %collective-permute-start.18 = (bf16[128,1792]{1,0:T(8,128)(2,1)}, bf16[128,1792]{1,0:T(8,128)(2,1)}, u32[]{:S(2)}, u32[]{:S(2)}) collective-permute-start(bf16[128,1792]{1,0:T(8,128)(2,1)} %get-tuple-element.38), channel_id=1, source_target_pairs={{0,4},{4,8},{8,12},{1,5},{5,9},{9,13},{2,6},{6,10},{10,14},{3,7},{... | collective-permute-start | bytes 1376264 | tf_op jit(solution)/shard_map/ppermute | solution.py:24
  107.9 1.5 copy.31
  111.4 4.6 %collective-permute-done.18 = bf16[128,1792]{1,0:T(8,128)(2,1)} collective-permute-done((bf16[128,1792]{1,0:T(8,128)(2,1)}, bf16[128,1792]{1,0:T(8,128)(2,1)}, u32[]{:S(2)}, u32[]{:S(2)}) %collective-permute-start.18) | collective-permute-done | bytes 458784 | tf_op jit(solution)/shard_map/ppermute | solution.py:24
  115.9 4.1 %collective-permute-done.19 = bf16[128,1792]{1,0:T(8,128)(2,1)} collective-permute-done((bf16[128,1792]{1,0:T(8,128)(2,1)}, bf16[128,1792]{1,0:T(8,128)(2,1)}, u32[]{:S(2)}, u32[]{:S(2)}) %collective-permute-start.19) | collective-permute-done | bytes 458784 | tf_op jit(solution)/shard_map/ppermute | solution.py:24
  120.1 3.0 %multiply_reduce_fusion.1 = (f32[128]{0:T(128)S(1)}, f32[]{:T(128)}, f32[128,1792]{1,0:T(8,128)S(1)}, f32[128,1792]{1,0:T(8,128)S(1)}) fusion(f32[128,1792]{1,0:T(8,128)S(1)} %copy.31, bf16[128,1792]{1,0:T(8,128)(2,1)S(1)} %copy-done.7, f32[128]{0:T(128)S(1)} %add_sqrt_fusion, bf16[128,1792]{1,0:T(8,128)(2,1)} %collective-permute-done.19, ...), kind=kLoop, calls=%fused_computation.48 | loop fusion | flops 5046143 | bytes 5964808 | tf_op jit(solution)/shard_map/reduce_sum | solution.py:108
  123.5 1.6 collective-permute-start.23
  125.0 4.8 %collective-permute-start.24 = (bf16[128,1792]{1,0:T(8,128)(2,1)S(1)}, bf16[128,1792]{1,0:T(8,128)(2,1)S(1)}, u32[]{:S(2)}, u32[]{:S(2)}) collective-permute-start(bf16[128,1792]{1,0:T(8,128)(2,1)S(1)} %get-tuple-element.57), channel_id=1, source_target_pairs={{0,4},{4,8},{8,12},{1,5},{5,9},{9,13},{2,6},{6,10},{10,14},{3,7},{... | collective-permute-start | bytes 1376264 | tf_op jit(solution)/shard_map/ppermute | solution.py:24
  131.2 1.6 collective-permute-start.25
  132.8 4.6 %collective-permute-start.26 = (bf16[128,3584]{1,0:T(8,128)(2,1)S(1)}, bf16[128,3584]{1,0:T(8,128)(2,1)S(1)}, u32[]{:S(2)}, u32[]{:S(2)}) collective-permute-start(bf16[128,3584]{1,0:T(8,128)(2,1)S(1)} %pad_maximum_fusion.1), channel_id=1, source_target_pairs={{0,4},{4,8},{8,12},{1,5},{5,9},{9,13},{2,6},{6,10},{10,14},{3,7},{... | collective-permute-start | bytes 2752520 | tf_op jit(solution)/shard_map/ppermute | solution.py:24
  142.2 1.4 collective-permute-done.45
  144.3 12.4 %collective-permute-done.25 = bf16[128,3584]{1,0:T(8,128)(2,1)S(1)} collective-permute-done((bf16[128,3584]{1,0:T(8,128)(2,1)S(1)}, bf16[128,3584]{1,0:T(8,128)(2,1)S(1)}, u32[]{:S(2)}, u32[]{:S(2)}) %collective-permute-start.25) | collective-permute-done | bytes 917536 | tf_op jit(solution)/shard_map/ppermute | solution.py:24
  162.0 5.1 %collective-permute-start.33 = (bf16[128,3584]{1,0:T(8,128)(2,1)S(1)}, bf16[128,3584]{1,0:T(8,128)(2,1)S(1)}, u32[]{:S(2)}, u32[]{:S(2)}) collective-permute-start(bf16[128,3584]{1,0:T(8,128)(2,1)S(1)} %collective-permute-done.26), channel_id=1, source_target_pairs={{0,4},{4,8},{8,12},{1,5},{5,9},{9,13},{2,6},{6,10},{10,14},{3,7},{... | collective-permute-start | bytes 2752520 | tf_op jit(solution)/shard_map/ppermute | solution.py:24
  167.2 3.1 %collective-permute-start.21 = (bf16[128,1024]{1,0:T(8,128)(2,1)S(1)}, bf16[128,1024]{1,0:T(8,128)(2,1)S(1)}, u32[]{:S(2)}, u32[]{:S(2)}) collective-permute-start(bf16[128,1024]{1,0:T(8,128)(2,1)S(1)} %fusion.49), channel_id=1, source_target_pairs={{2,0},{1,3},{6,4},{5,7},{10,8},{9,11},{14,12},{13,15},{18,16},{17,... | collective-permute-start | bytes 786440 | tf_op jit(solution)/shard_map/ppermute | solution.py:175
  171.6 4.6 %collective-permute-start.32 = (bf16[128,1792]{1,0:T(8,128)(2,1)S(1)}, bf16[128,1792]{1,0:T(8,128)(2,1)S(1)}, u32[]{:S(2)}, u32[]{:S(2)}) collective-permute-start(bf16[128,1792]{1,0:T(8,128)(2,1)S(1)} %collective-permute-done.24), channel_id=1, source_target_pairs={{0,4},{4,8},{8,12},{1,5},{5,9},{9,13},{2,6},{6,10},{10,14},{3,7},{... | collective-permute-start | bytes 1376264 | tf_op jit(solution)/shard_map/ppermute | solution.py:24
  177.8 18.1 %collective-permute-done.30 = bf16[128,1792]{1,0:T(8,128)(2,1)S(1)} collective-permute-done((bf16[128,1792]{1,0:T(8,128)(2,1)S(1)}, bf16[128,1792]{1,0:T(8,128)(2,1)S(1)}, u32[]{:S(2)}, u32[]{:S(2)}) %collective-permute-start.30) | collective-permute-done | bytes 458784 | tf_op jit(solution)/shard_map/ppermute | solution.py:24
  198.4 5.0 %collective-permute-start.39 = (bf16[128,1792]{1,0:T(8,128)(2,1)S(1)}, bf16[128,1792]{1,0:T(8,128)(2,1)S(1)}, u32[]{:S(2)}, u32[]{:S(2)}) collective-permute-start(bf16[128,1792]{1,0:T(8,128)(2,1)S(1)} %collective-permute-done.32), channel_id=1, source_target_pairs={{0,4},{4,8},{8,12},{1,5},{5,9},{9,13},{2,6},{6,10},{10,14},{3,7},{... | collective-permute-start | bytes 1376264 | tf_op jit(solution)/shard_map/ppermute | solution.py:24
  205.1 4.6 %collective-permute-start.40 = (bf16[128,3584]{1,0:T(8,128)(2,1)S(1)}, bf16[128,3584]{1,0:T(8,128)(2,1)S(1)}, u32[]{:S(2)}, u32[]{:S(2)}) collective-permute-start(bf16[128,3584]{1,0:T(8,128)(2,1)S(1)} %collective-permute-done.33), channel_id=1, source_target_pairs={{0,4},{4,8},{8,12},{1,5},{5,9},{9,13},{2,6},{6,10},{10,14},{3,7},{... | collective-permute-start | bytes 2752520 | tf_op jit(solution)/shard_map/ppermute | solution.py:24
  213.9 5.4 %collective-permute-start.50 = (bf16[128,1024]{1,0:T(8,128)(2,1)S(1)}, bf16[128,1024]{1,0:T(8,128)(2,1)S(1)}, u32[]{:S(2)}, u32[]{:S(2)}) collective-permute-start(bf16[128,1024]{1,0:T(8,128)(2,1)S(1)} %add_convert_fusion.2), channel_id=1, source_target_pairs={{2,4},{6,9},{10,6},{14,11},{18,20},{22,25},{26,22},{30,27}} | collective-permute-start | bytes 786440 | tf_op jit(solution)/shard_map/ppermute | solution.py:179
  219.4 12.5 %collective-permute-done.38 = bf16[128,3584]{1,0:T(8,128)(2,1)S(1)} collective-permute-done((bf16[128,3584]{1,0:T(8,128)(2,1)S(1)}, bf16[128,3584]{1,0:T(8,128)(2,1)S(1)}, u32[]{:S(2)}, u32[]{:S(2)}) %collective-permute-start.38) | collective-permute-done | bytes 917536 | tf_op jit(solution)/shard_map/ppermute | solution.py:24
  235.8 1.3 select_convert_fusion
  239.5 4.6 %collective-permute-start.42 = (bf16[128,1024]{1,0:T(8,128)(2,1)S(1)}, bf16[128,1024]{1,0:T(8,128)(2,1)S(1)}, u32[]{:S(2)}, u32[]{:S(2)}) collective-permute-start(bf16[128,1024]{1,0:T(8,128)(2,1)S(1)} %fusion.52), channel_id=1, source_target_pairs={{1,3},{2,0},{5,7},{6,4},{9,11},{10,8},{13,15},{14,12},{17,19},{18,... | collective-permute-start | bytes 786440 | tf_op jit(solution)/shard_map/ppermute | solution.py:175
  244.1 4.4 %collective-permute-done.35 = bf16[128,1024]{1,0:T(8,128)(2,1)S(1)} collective-permute-done((bf16[128,1024]{1,0:T(8,128)(2,1)S(1)}, bf16[128,1024]{1,0:T(8,128)(2,1)S(1)}, u32[]{:S(2)}, u32[]{:S(2)}) %collective-permute-start.35) | collective-permute-done | bytes 262176 | tf_op jit(solution)/shard_map/ppermute | solution.py:175
  248.6 1.5 collective-permute-start.48
  250.1 2.5 collective-permute-start.47
  255.2 2.3 collective-permute-start.36
  260.9 10.4 %collective-permute-done.51 = bf16[128,1024]{1,0:T(8,128)(2,1)S(1)} collective-permute-done((bf16[128,1024]{1,0:T(8,128)(2,1)S(1)}, bf16[128,1024]{1,0:T(8,128)(2,1)S(1)}, u32[]{:S(2)}, u32[]{:S(2)}) %collective-permute-start.51) | collective-permute-done | bytes 262176 | tf_op jit(solution)/shard_map/ppermute | solution.py:179
  (156 shorter events, 62.2 us)
Async XLA Ops:
  1.5 11.6 %collective-permute-start.2 = (bf16[2,128,256]{2,1,0:T(8,128)(2,1)S(1)}, bf16[2,128,256]{2,1,0:T(8,128)(2,1)S(1)}, u32[]{:S(2)}, u32[]{:S(2)}) collective-permute-start(bf16[2,128,256]{2,1,0:T(8,128)(2,1)S(1)} %pad_maximum_fusion.4), channel_id=1, source_target_pairs={{0,12},{1,13},{2,14},{3,15},{16,28},{17,29},{18,30},{19,31}} | collective-permute-start | bytes 393224 | tf_op jit(solution)/shard_map/ppermute | solution.py:24
  7.0 6.7 %collective-permute-start.1 = (bf16[2,128,256]{2,1,0:T(8,128)(2,1)S(1)}, bf16[2,128,256]{2,1,0:T(8,128)(2,1)S(1)}, u32[]{:S(2)}, u32[]{:S(2)}) collective-permute-start(bf16[2,128,256]{2,1,0:T(8,128)(2,1)S(1)} %pad_maximum_fusion.4), channel_id=1, source_target_pairs={{0,8},{4,12},{1,9},{5,13},{2,10},{6,14},{3,11},{7,15},{16,24},{20,... | collective-permute-start | bytes 393224 | tf_op jit(solution)/shard_map/ppermute | solution.py:24
  8.3 7.1 %collective-permute-start = (bf16[2,128,256]{2,1,0:T(8,128)(2,1)S(1)}, bf16[2,128,256]{2,1,0:T(8,128)(2,1)S(1)}, u32[]{:S(2)}, u32[]{:S(2)}) collective-permute-start(bf16[2,128,256]{2,1,0:T(8,128)(2,1)S(1)} %pad_maximum_fusion.4), channel_id=1, source_target_pairs={{0,4},{4,8},{8,12},{1,5},{5,9},{9,13},{2,6},{6,10},{10,14},{3,7},{... | collective-permute-start | bytes 393224 | tf_op jit(solution)/shard_map/ppermute | solution.py:24
  19.5 19.0 %collective-permute-start.3 = (bf16[128,1024]{1,0:T(8,128)(2,1)S(1)}, bf16[128,1024]{1,0:T(8,128)(2,1)S(1)}, u32[]{:S(2)}, u32[]{:S(2)}) collective-permute-start(bf16[128,1024]{1,0:T(8,128)(2,1)S(1)} %get-tuple-element.54), channel_id=1, source_target_pairs={{0,0},{1,4},{2,8},{3,12},{4,1},{5,5},{6,9},{7,13},{8,2},{9,6},{10,... | collective-permute-start | bytes 786440 | tf_op jit(solution)/shard_map/ppermute | solution.py:34
  38.5 6.4 %collective-permute-start.6 = (bf16[128,1024]{1,0:T(8,128)(2,1)S(1)}, bf16[128,1024]{1,0:T(8,128)(2,1)S(1)}, u32[]{:S(2)}, u32[]{:S(2)}) collective-permute-start(bf16[128,1024]{1,0:T(8,128)(2,1)S(1)} %collective-permute-done.3), channel_id=1, source_target_pairs={{0,2},{2,0},{1,3},{3,1},{4,6},{6,4},{5,7},{7,5},{8,10},{10,8},{9,1... | collective-permute-start | bytes 786440 | tf_op jit(solution)/shard_map/ppermute | solution.py:28
  54.0 13.7 %collective-permute-start.8 = (bf16[128,1792]{1,0:T(8,128)(2,1)}, bf16[128,1792]{1,0:T(8,128)(2,1)S(1)}, u32[]{:S(2)}, u32[]{:S(2)}) collective-permute-start(bf16[128,1792]{1,0:T(8,128)(2,1)} %get-tuple-element.27), channel_id=1, source_target_pairs={{0,4},{4,8},{8,12},{1,5},{5,9},{9,13},{2,6},{6,10},{10,14},{3,7},{... | collective-permute-start | bytes 1376264 | tf_op jit(solution)/shard_map/ppermute | solution.py:24
  56.4 15.5 %collective-permute-start.9 = (bf16[128,1792]{1,0:T(8,128)(2,1)}, bf16[128,1792]{1,0:T(8,128)(2,1)S(1)}, u32[]{:S(2)}, u32[]{:S(2)}) collective-permute-start(bf16[128,1792]{1,0:T(8,128)(2,1)} %get-tuple-element.28), channel_id=1, source_target_pairs={{4,0},{8,4},{12,8},{5,1},{9,5},{13,9},{6,2},{10,6},{14,10},{7,3},{... | collective-permute-start | bytes 1376264 | tf_op jit(solution)/shard_map/ppermute | solution.py:24
  57.8 19.7 %collective-permute-start.14 = (bf16[128,1792]{1,0:T(8,128)(2,1)}, bf16[128,1792]{1,0:T(8,128)(2,1)S(1)}, u32[]{:S(2)}, u32[]{:S(2)}) collective-permute-start(bf16[128,1792]{1,0:T(8,128)(2,1)} %get-tuple-element.34), channel_id=1, source_target_pairs={{0,4},{4,8},{8,12},{1,5},{5,9},{9,13},{2,6},{6,10},{10,14},{3,7},{... | collective-permute-start | bytes 1376264 | tf_op jit(solution)/shard_map/ppermute | solution.py:24
  62.5 19.3 %collective-permute-start.15 = (bf16[128,1792]{1,0:T(8,128)(2,1)S(1)}, bf16[128,1792]{1,0:T(8,128)(2,1)S(1)}, u32[]{:S(2)}, u32[]{:S(2)}) collective-permute-start(bf16[128,1792]{1,0:T(8,128)(2,1)S(1)} %get-tuple-element.35), channel_id=1, source_target_pairs={{4,0},{8,4},{12,8},{5,1},{9,5},{13,9},{6,2},{10,6},{14,10},{7,3},{... | collective-permute-start | bytes 1376264 | tf_op jit(solution)/shard_map/ppermute | solution.py:24
  73.3 13.9 %collective-permute-start.10 = (bf16[128,1792]{1,0:T(8,128)(2,1)S(1)}, bf16[128,1792]{1,0:T(8,128)(2,1)S(1)}, u32[]{:S(2)}, u32[]{:S(2)}) collective-permute-start(bf16[128,1792]{1,0:T(8,128)(2,1)S(1)} %get-tuple-element.29), channel_id=1, source_target_pairs={{0,4},{4,8},{8,12},{1,5},{5,9},{9,13},{2,6},{6,10},{10,14},{3,7},{... | collective-permute-start | bytes 1376264 | tf_op jit(solution)/shard_map/ppermute | solution.py:24
  75.6 16.0 %collective-permute-start.11 = (bf16[128,1792]{1,0:T(8,128)(2,1)S(1)}, bf16[128,1792]{1,0:T(8,128)(2,1)S(1)}, u32[]{:S(2)}, u32[]{:S(2)}) collective-permute-start(bf16[128,1792]{1,0:T(8,128)(2,1)S(1)} %get-tuple-element.30), channel_id=1, source_target_pairs={{4,0},{8,4},{12,8},{5,1},{9,5},{13,9},{6,2},{10,6},{14,10},{7,3},{... | collective-permute-start | bytes 1376264 | tf_op jit(solution)/shard_map/ppermute | solution.py:24
  82.0 15.0 %collective-permute-start.16 = (bf16[128,1792]{1,0:T(8,128)(2,1)S(1)}, bf16[128,1792]{1,0:T(8,128)(2,1)S(1)}, u32[]{:S(2)}, u32[]{:S(2)}) collective-permute-start(bf16[128,1792]{1,0:T(8,128)(2,1)S(1)} %get-tuple-element.36), channel_id=1, source_target_pairs={{0,4},{4,8},{8,12},{1,5},{5,9},{9,13},{2,6},{6,10},{10,14},{3,7},{... | collective-permute-start | bytes 1376264 | tf_op jit(solution)/shard_map/ppermute | solution.py:24
  84.4 17.0 %collective-permute-start.17 = (bf16[128,1792]{1,0:T(8,128)(2,1)S(1)}, bf16[128,1792]{1,0:T(8,128)(2,1)S(1)}, u32[]{:S(2)}, u32[]{:S(2)}) collective-permute-start(bf16[128,1792]{1,0:T(8,128)(2,1)S(1)} %get-tuple-element.37), channel_id=1, source_target_pairs={{4,0},{8,4},{12,8},{5,1},{9,5},{13,9},{6,2},{10,6},{14,10},{7,3},{... | collective-permute-start | bytes 1376264 | tf_op jit(solution)/shard_map/ppermute | solution.py:24
  92.8 17.9 %collective-permute-start.12 = (bf16[128,1792]{1,0:T(8,128)(2,1)}, bf16[128,1792]{1,0:T(8,128)(2,1)}, u32[]{:S(2)}, u32[]{:S(2)}) collective-permute-start(bf16[128,1792]{1,0:T(8,128)(2,1)} %get-tuple-element.31), channel_id=1, source_target_pairs={{0,4},{4,8},{8,12},{1,5},{5,9},{9,13},{2,6},{6,10},{10,14},{3,7},{... | collective-permute-start | bytes 1376264 | tf_op jit(solution)/shard_map/ppermute | solution.py:24
  95.8 15.6 %collective-permute-start.13 = (bf16[128,1792]{1,0:T(8,128)(2,1)}, bf16[128,1792]{1,0:T(8,128)(2,1)}, u32[]{:S(2)}, u32[]{:S(2)}) collective-permute-start(bf16[128,1792]{1,0:T(8,128)(2,1)} %get-tuple-element.32), channel_id=1, source_target_pairs={{4,0},{8,4},{12,8},{5,1},{9,5},{13,9},{6,2},{10,6},{14,10},{7,3},{... | collective-permute-start | bytes 1376264 | tf_op jit(solution)/shard_map/ppermute | solution.py:24
  102.6 13.3 %collective-permute-start.18 = (bf16[128,1792]{1,0:T(8,128)(2,1)}, bf16[128,1792]{1,0:T(8,128)(2,1)}, u32[]{:S(2)}, u32[]{:S(2)}) collective-permute-start(bf16[128,1792]{1,0:T(8,128)(2,1)} %get-tuple-element.38), channel_id=1, source_target_pairs={{0,4},{4,8},{8,12},{1,5},{5,9},{9,13},{2,6},{6,10},{10,14},{3,7},{... | collective-permute-start | bytes 1376264 | tf_op jit(solution)/shard_map/ppermute | solution.py:24
  105.6 14.5 %collective-permute-start.19 = (bf16[128,1792]{1,0:T(8,128)(2,1)}, bf16[128,1792]{1,0:T(8,128)(2,1)}, u32[]{:S(2)}, u32[]{:S(2)}) collective-permute-start(bf16[128,1792]{1,0:T(8,128)(2,1)} %get-tuple-element.39), channel_id=1, source_target_pairs={{4,0},{8,4},{12,8},{5,1},{9,5},{13,9},{6,2},{10,6},{14,10},{7,3},{... | collective-permute-start | bytes 1376264 | tf_op jit(solution)/shard_map/ppermute | solution.py:24
  123.5 20.1 %collective-permute-start.23 = (bf16[128,1792]{1,0:T(8,128)(2,1)S(1)}, bf16[128,1792]{1,0:T(8,128)(2,1)S(1)}, u32[]{:S(2)}, u32[]{:S(2)}) collective-permute-start(bf16[128,1792]{1,0:T(8,128)(2,1)S(1)} %get-tuple-element.57), channel_id=1, source_target_pairs={{4,0},{8,4},{12,8},{5,1},{9,5},{13,9},{6,2},{10,6},{14,10},{7,3},{... | collective-permute-start | bytes 1376264 | tf_op jit(solution)/shard_map/ppermute | solution.py:24
  125.0 18.6 %collective-permute-start.24 = (bf16[128,1792]{1,0:T(8,128)(2,1)S(1)}, bf16[128,1792]{1,0:T(8,128)(2,1)S(1)}, u32[]{:S(2)}, u32[]{:S(2)}) collective-permute-start(bf16[128,1792]{1,0:T(8,128)(2,1)S(1)} %get-tuple-element.57), channel_id=1, source_target_pairs={{0,4},{4,8},{8,12},{1,5},{5,9},{9,13},{2,6},{6,10},{10,14},{3,7},{... | collective-permute-start | bytes 1376264 | tf_op jit(solution)/shard_map/ppermute | solution.py:24
  131.2 25.5 %collective-permute-start.25 = (bf16[128,3584]{1,0:T(8,128)(2,1)S(1)}, bf16[128,3584]{1,0:T(8,128)(2,1)S(1)}, u32[]{:S(2)}, u32[]{:S(2)}) collective-permute-start(bf16[128,3584]{1,0:T(8,128)(2,1)S(1)} %pad_maximum_fusion.1), channel_id=1, source_target_pairs={{4,0},{8,4},{12,8},{5,1},{9,5},{13,9},{6,2},{10,6},{14,10},{7,3},{... | collective-permute-start | bytes 2752520 | tf_op jit(solution)/shard_map/ppermute | solution.py:24
  132.8 25.1 %collective-permute-start.26 = (bf16[128,3584]{1,0:T(8,128)(2,1)S(1)}, bf16[128,3584]{1,0:T(8,128)(2,1)S(1)}, u32[]{:S(2)}, u32[]{:S(2)}) collective-permute-start(bf16[128,3584]{1,0:T(8,128)(2,1)S(1)} %pad_maximum_fusion.1), channel_id=1, source_target_pairs={{0,4},{4,8},{8,12},{1,5},{5,9},{9,13},{2,6},{6,10},{10,14},{3,7},{... | collective-permute-start | bytes 2752520 | tf_op jit(solution)/shard_map/ppermute | solution.py:24
  140.0 3.6 %collective-permute-start.45 = (f32[256]{0:T(256)S(1)}, f32[256]{0:T(256)S(1)}, u32[]{:S(2)}, u32[]{:S(2)}) collective-permute-start(f32[256]{0:T(256)S(1)} %fusion.100), channel_id=1, source_target_pairs={{0,2},{2,0},{1,3},{3,1},{4,6},{6,4},{5,7},{7,5},{8,10},{10,8},{9,1... | collective-permute-start | bytes 3080 | tf_op jit(solution)/shard_map/ppermute | solution.py:28
  143.6 23.5 %collective-permute-start.20 = (bf16[128,1024]{1,0:T(8,128)(2,1)S(1)}, bf16[128,1024]{1,0:T(8,128)(2,1)S(1)}, u32[]{:S(2)}, u32[]{:S(2)}) collective-permute-start(bf16[128,1024]{1,0:T(8,128)(2,1)S(1)} %get-tuple-element.91), channel_id=1, source_target_pairs={{0,1},{1,0},{2,3},{3,2},{4,5},{5,4},{6,7},{7,6},{8,9},{9,8},{10,11... | collective-permute-start | bytes 786440 | tf_op jit(solution)/shard_map/ppermute | solution.py:28
  160.6 11.0 %collective-permute-start.27 = (bf16[128,1024]{1,0:T(8,128)(2,1)S(1)}, bf16[128,1024]{1,0:T(8,128)(2,1)S(1)}, u32[]{:S(2)}, u32[]{:S(2)}) collective-permute-start(bf16[128,1024]{1,0:T(8,128)(2,1)S(1)} %get-tuple-element.89), channel_id=1, source_target_pairs={{0,1},{1,0},{2,3},{3,2},{4,5},{5,4},{6,7},{7,6},{8,9},{9,8},{10,11... | collective-permute-start | bytes 786440 | tf_op jit(solution)/shard_map/ppermute | solution.py:28
  160.7 42.9 %collective-permute-start.31 = (bf16[128,3584]{1,0:T(8,128)(2,1)S(1)}, bf16[128,3584]{1,0:T(8,128)(2,1)S(1)}, u32[]{:S(2)}, u32[]{:S(2)}) collective-permute-start(bf16[128,3584]{1,0:T(8,128)(2,1)S(1)} %collective-permute-done.25), channel_id=1, source_target_pairs={{4,0},{8,4},{12,8},{5,1},{9,5},{13,9},{6,2},{10,6},{14,10},{7,3},{... | collective-permute-start | bytes 2752520 | tf_op jit(solution)/shard_map/ppermute | solution.py:24
  162.0 41.6 %collective-permute-start.33 = (bf16[128,3584]{1,0:T(8,128)(2,1)S(1)}, bf16[128,3584]{1,0:T(8,128)(2,1)S(1)}, u32[]{:S(2)}, u32[]{:S(2)}) collective-permute-start(bf16[128,3584]{1,0:T(8,128)(2,1)S(1)} %collective-permute-done.26), channel_id=1, source_target_pairs={{0,4},{4,8},{8,12},{1,5},{5,9},{9,13},{2,6},{6,10},{10,14},{3,7},{... | collective-permute-start | bytes 2752520 | tf_op jit(solution)/shard_map/ppermute | solution.py:24
  167.2 9.1 %collective-permute-start.21 = (bf16[128,1024]{1,0:T(8,128)(2,1)S(1)}, bf16[128,1024]{1,0:T(8,128)(2,1)S(1)}, u32[]{:S(2)}, u32[]{:S(2)}) collective-permute-start(bf16[128,1024]{1,0:T(8,128)(2,1)S(1)} %fusion.49), channel_id=1, source_target_pairs={{2,0},{1,3},{6,4},{5,7},{10,8},{9,11},{14,12},{13,15},{18,16},{17,... | collective-permute-start | bytes 786440 | tf_op jit(solution)/shard_map/ppermute | solution.py:175
  170.3 25.6 %collective-permute-start.30 = (bf16[128,1792]{1,0:T(8,128)(2,1)S(1)}, bf16[128,1792]{1,0:T(8,128)(2,1)S(1)}, u32[]{:S(2)}, u32[]{:S(2)}) collective-permute-start(bf16[128,1792]{1,0:T(8,128)(2,1)S(1)} %collective-permute-done.23), channel_id=1, source_target_pairs={{4,0},{8,4},{12,8},{5,1},{9,5},{13,9},{6,2},{10,6},{14,10},{7,3},{... | collective-permute-start | bytes 1376264 | tf_op jit(solution)/shard_map/ppermute | solution.py:24
  171.6 25.5 %collective-permute-start.32 = (bf16[128,1792]{1,0:T(8,128)(2,1)S(1)}, bf16[128,1792]{1,0:T(8,128)(2,1)S(1)}, u32[]{:S(2)}, u32[]{:S(2)}) collective-permute-start(bf16[128,1792]{1,0:T(8,128)(2,1)S(1)} %collective-permute-done.24), channel_id=1, source_target_pairs={{0,4},{4,8},{8,12},{1,5},{5,9},{9,13},{2,6},{6,10},{10,14},{3,7},{... | collective-permute-start | bytes 1376264 | tf_op jit(solution)/shard_map/ppermute | solution.py:24
  176.3 22.0 %collective-permute-start.28 = (bf16[128,1024]{1,0:T(8,128)(2,1)S(1)}, bf16[128,1024]{1,0:T(8,128)(2,1)S(1)}, u32[]{:S(2)}, u32[]{:S(2)}) collective-permute-start(bf16[128,1024]{1,0:T(8,128)(2,1)S(1)} %fusion.50), channel_id=1, source_target_pairs={{3,1},{0,2},{7,5},{4,6},{11,9},{8,10},{15,13},{12,14},{19,17},{16,... | collective-permute-start | bytes 786440 | tf_op jit(solution)/shard_map/ppermute | solution.py:175
  195.9 54.2 %collective-permute-start.49 = (bf16[128,1024]{1,0:T(8,128)(2,1)S(1)}, bf16[128,1024]{1,0:T(8,128)(2,1)S(1)}, u32[]{:S(2)}, u32[]{:S(2)}) collective-permute-start(bf16[128,1024]{1,0:T(8,128)(2,1)S(1)} %add_convert_fusion.3), channel_id=1, source_target_pairs={{3,0},{7,5},{11,10},{15,15},{19,16},{23,21},{27,26},{31,31}} | collective-permute-start | bytes 786440 | tf_op jit(solution)/shard_map/ppermute | solution.py:179
  197.1 15.9 %collective-permute-start.37 = (bf16[128,1792]{1,0:T(8,128)(2,1)S(1)}, bf16[128,1792]{1,0:T(8,128)(2,1)S(1)}, u32[]{:S(2)}, u32[]{:S(2)}) collective-permute-start(bf16[128,1792]{1,0:T(8,128)(2,1)S(1)} %collective-permute-done.30), channel_id=1, source_target_pairs={{4,0},{8,4},{12,8},{5,1},{9,5},{13,9},{6,2},{10,6},{14,10},{7,3},{... | collective-permute-start | bytes 1376264 | tf_op jit(solution)/shard_map/ppermute | solution.py:24
  198.4 15.5 %collective-permute-start.39 = (bf16[128,1792]{1,0:T(8,128)(2,1)S(1)}, bf16[128,1792]{1,0:T(8,128)(2,1)S(1)}, u32[]{:S(2)}, u32[]{:S(2)}) collective-permute-start(bf16[128,1792]{1,0:T(8,128)(2,1)S(1)} %collective-permute-done.32), channel_id=1, source_target_pairs={{0,4},{4,8},{8,12},{1,5},{5,9},{9,13},{2,6},{6,10},{10,14},{3,7},{... | collective-permute-start | bytes 1376264 | tf_op jit(solution)/shard_map/ppermute | solution.py:24
  203.8 28.1 %collective-permute-start.38 = (bf16[128,3584]{1,0:T(8,128)(2,1)S(1)}, bf16[128,3584]{1,0:T(8,128)(2,1)S(1)}, u32[]{:S(2)}, u32[]{:S(2)}) collective-permute-start(bf16[128,3584]{1,0:T(8,128)(2,1)S(1)} %collective-permute-done.31), channel_id=1, source_target_pairs={{4,0},{8,4},{12,8},{5,1},{9,5},{13,9},{6,2},{10,6},{14,10},{7,3},{... | collective-permute-start | bytes 2752520 | tf_op jit(solution)/shard_map/ppermute | solution.py:24
  205.1 28.5 %collective-permute-start.40 = (bf16[128,3584]{1,0:T(8,128)(2,1)S(1)}, bf16[128,3584]{1,0:T(8,128)(2,1)S(1)}, u32[]{:S(2)}, u32[]{:S(2)}) collective-permute-start(bf16[128,3584]{1,0:T(8,128)(2,1)S(1)} %collective-permute-done.33), channel_id=1, source_target_pairs={{0,4},{4,8},{8,12},{1,5},{5,9},{9,13},{2,6},{6,10},{10,14},{3,7},{... | collective-permute-start | bytes 2752520 | tf_op jit(solution)/shard_map/ppermute | solution.py:24
  213.0 40.2 %collective-permute-start.22 = (bf16[128,1024]{1,0:T(8,128)(2,1)S(1)}, bf16[128,1024]{1,0:T(8,128)(2,1)S(1)}, u32[]{:S(2)}, u32[]{:S(2)}) collective-permute-start(bf16[128,1024]{1,0:T(8,128)(2,1)S(1)} %add_convert_fusion.3), channel_id=1, source_target_pairs={{0,0},{4,5},{8,10},{12,15},{16,16},{20,21},{24,26},{28,31}} | collective-permute-start | bytes 786440 | tf_op jit(solution)/shard_map/ppermute | solution.py:179
  213.9 40.0 %collective-permute-start.50 = (bf16[128,1024]{1,0:T(8,128)(2,1)S(1)}, bf16[128,1024]{1,0:T(8,128)(2,1)S(1)}, u32[]{:S(2)}, u32[]{:S(2)}) collective-permute-start(bf16[128,1024]{1,0:T(8,128)(2,1)S(1)} %add_convert_fusion.2), channel_id=1, source_target_pairs={{2,4},{6,9},{10,6},{14,11},{18,20},{22,25},{26,22},{30,27}} | collective-permute-start | bytes 786440 | tf_op jit(solution)/shard_map/ppermute | solution.py:179
  231.9 6.1 %collective-permute-start.34 = (bf16[128,1024]{1,0:T(8,128)(2,1)S(1)}, bf16[128,1024]{1,0:T(8,128)(2,1)S(1)}, u32[]{:S(2)}, u32[]{:S(2)}) collective-permute-start(bf16[128,1024]{1,0:T(8,128)(2,1)S(1)} %get-tuple-element.87), channel_id=1, source_target_pairs={{0,1},{1,0},{2,3},{3,2},{4,5},{5,4},{6,7},{7,6},{8,9},{9,8},{10,11... | collective-permute-start | bytes 786440 | tf_op jit(solution)/shard_map/ppermute | solution.py:28
  238.1 10.4 %collective-permute-start.35 = (bf16[128,1024]{1,0:T(8,128)(2,1)S(1)}, bf16[128,1024]{1,0:T(8,128)(2,1)S(1)}, u32[]{:S(2)}, u32[]{:S(2)}) collective-permute-start(bf16[128,1024]{1,0:T(8,128)(2,1)S(1)} %fusion.51), channel_id=1, source_target_pairs={{0,2},{3,1},{4,6},{7,5},{8,10},{11,9},{12,14},{15,13},{16,18},{19,... | collective-permute-start | bytes 786440 | tf_op jit(solution)/shard_map/ppermute | solution.py:175
  239.5 13.1 %collective-permute-start.42 = (bf16[128,1024]{1,0:T(8,128)(2,1)S(1)}, bf16[128,1024]{1,0:T(8,128)(2,1)S(1)}, u32[]{:S(2)}, u32[]{:S(2)}) collective-permute-start(bf16[128,1024]{1,0:T(8,128)(2,1)S(1)} %fusion.52), channel_id=1, source_target_pairs={{1,3},{2,0},{5,7},{6,4},{9,11},{10,8},{13,15},{14,12},{17,19},{18,... | collective-permute-start | bytes 786440 | tf_op jit(solution)/shard_map/ppermute | solution.py:175
  248.6 6.6 %collective-permute-start.48 = (f32[128]{0:T(128)S(1)}, f32[128]{0:T(128)S(1)}, u32[]{:S(2)}, u32[]{:S(2)}) collective-permute-start(f32[128]{0:T(128)S(1)} %get-tuple-element.48), channel_id=1, source_target_pairs={{0,12},{4,8},{8,4},{12,0},{1,13},{5,9},{9,5},{13,1},{2,14},{6,10},... | collective-permute-start | bytes 1544 | tf_op jit(solution)/shard_map/ppermute | solution.py:208
  250.1 7.4 %collective-permute-start.47 = (f32[128]{0:T(128)S(1)}, f32[128]{0:T(128)S(1)}, u32[]{:S(2)}, u32[]{:S(2)}) collective-permute-start(f32[128]{0:T(128)S(1)} %get-tuple-element.48), channel_id=1, source_target_pairs={{0,8},{4,12},{8,0},{12,4},{1,9},{5,13},{9,1},{13,5},{2,10},{6,14},... | collective-permute-start | bytes 1544 | tf_op jit(solution)/shard_map/ppermute | solution.py:208
  252.7 5.6 %collective-permute-start.46 = (f32[128]{0:T(128)S(1)}, f32[128]{0:T(128)S(1)}, u32[]{:S(2)}, u32[]{:S(2)}) collective-permute-start(f32[128]{0:T(128)S(1)} %get-tuple-element.48), channel_id=1, source_target_pairs={{0,4},{4,0},{8,12},{12,8},{1,5},{5,1},{9,13},{13,9},{2,6},{6,2},{1... | collective-permute-start | bytes 1544 | tf_op jit(solution)/shard_map/ppermute | solution.py:208
  253.2 7.6 %collective-permute-start.29 = (bf16[128,1024]{1,0:T(8,128)(2,1)S(1)}, bf16[128,1024]{1,0:T(8,128)(2,1)S(1)}, u32[]{:S(2)}, u32[]{:S(2)}) collective-permute-start(bf16[128,1024]{1,0:T(8,128)(2,1)S(1)} %add_convert_fusion.2), channel_id=1, source_target_pairs={{1,4},{5,9},{9,6},{13,11},{17,20},{21,25},{25,22},{29,27}} | collective-permute-start | bytes 786440 | tf_op jit(solution)/shard_map/ppermute | solution.py:179
  253.9 17.4 %collective-permute-start.51 = (bf16[128,1024]{1,0:T(8,128)(2,1)S(1)}, bf16[128,1024]{1,0:T(8,128)(2,1)S(1)}, u32[]{:S(2)}, u32[]{:S(2)}) collective-permute-start(bf16[128,1024]{1,0:T(8,128)(2,1)S(1)} %add_convert_fusion.1), channel_id=1, source_target_pairs={{1,8},{5,13},{9,2},{13,7},{17,24},{21,29},{25,18},{29,23}} | collective-permute-start | bytes 786440 | tf_op jit(solution)/shard_map/ppermute | solution.py:179
  255.2 16.0 %collective-permute-start.36 = (bf16[128,1024]{1,0:T(8,128)(2,1)S(1)}, bf16[128,1024]{1,0:T(8,128)(2,1)S(1)}, u32[]{:S(2)}, u32[]{:S(2)}) collective-permute-start(bf16[128,1024]{1,0:T(8,128)(2,1)S(1)} %add_convert_fusion.1), channel_id=1, source_target_pairs={{2,8},{6,13},{10,2},{14,7},{18,24},{22,29},{26,18},{30,23}} | collective-permute-start | bytes 786440 | tf_op jit(solution)/shard_map/ppermute | solution.py:179
  257.5 13.8 %collective-permute-start.52 = (bf16[128,1024]{1,0:T(8,128)(2,1)S(1)}, bf16[128,1024]{1,0:T(8,128)(2,1)S(1)}, u32[]{:S(2)}, u32[]{:S(2)}) collective-permute-start(bf16[128,1024]{1,0:T(8,128)(2,1)S(1)} %add_convert_fusion), channel_id=1, source_target_pairs={{0,12},{4,1},{8,14},{12,3},{16,28},{20,17},{24,30},{28,19}} | collective-permute-start | bytes 786440 | tf_op jit(solution)/shard_map/ppermute | solution.py:179
  258.2 13.1 %collective-permute-start.43 = (bf16[128,1024]{1,0:T(8,128)(2,1)S(1)}, bf16[128,1024]{1,0:T(8,128)(2,1)S(1)}, u32[]{:S(2)}, u32[]{:S(2)}) collective-permute-start(bf16[128,1024]{1,0:T(8,128)(2,1)S(1)} %add_convert_fusion), channel_id=1, source_target_pairs={{3,12},{7,1},{11,14},{15,3},{19,28},{23,17},{27,30},{31,19}} | collective-permute-start | bytes 786440 | tf_op jit(solution)/shard_map/ppermute | solution.py:179
  (16 other events, 180.1 us)

commit v7 on v6

--- a/solution.py
+++ b/solution.py
@@ -94,19 +94,24 @@
     return small + swapped(small, "head")
 
 
-def elementwise(gate_proj, up_proj, feats, keep_cols):
+def elementwise(gate_proj, up_proj, feats, keep_cols, first_hidden=False):
     rows, ff = gate_proj.shape
     tiles = keep_cols.shape[1]
     keep = jnp.broadcast_to(keep_cols.astype(F32)[:, :, None], (rows, tiles, TILE)).reshape(rows, ff)
     lifted = jnp.maximum(gate_proj, 0.0)
     squared = lifted * lifted
     act = squared * up_proj
+    hidden = act.astype(BF16)
+    if first_hidden:
+        hidden, lifted, squared, up_proj, act = lax.optimization_barrier(
+            (hidden, lifted, squared, up_proj, act)
+        )
     differ = act - feats.astype(F32)
     grad_act = keep * differ
     grad_gate = (grad_act * up_proj * 2.0 * lifted).astype(BF16)
     grad_up = (grad_act * squared).astype(BF16)
     inner = 3.0 * jnp.sum(grad_act * act, axis=1)
-    return act.astype(BF16), grad_gate, grad_up, inner, jnp.sum(grad_act * differ)
+    return hidden, grad_gate, grad_up, inner, jnp.sum(grad_act * differ)
 
 
 def products(hidden, grad_gate, grad_up, weights):
@@ -139,14 +144,19 @@
     gain = lax.dynamic_slice_in_dim(norm_gain, z * d_ctx, d_ctx, 0)
     resid = jnp.stack([tile, both[0], across, both[1]]).astype(F32)
     scaled = (resid * gain).astype(BF16).reshape(4 * rows, d_ctx)
-    parts = [
-        jnp.dot(scaled, w, preferred_element_type=F32).astype(BF16).reshape(4, rows, ff)
-        for w in (w_gate, w_up)
-    ]
-
-    came = [[None, None], [None, None]]
+
+    def projected(w):
+        return jnp.dot(scaled, w, preferred_element_type=F32).astype(BF16).reshape(4, rows, ff)
+
+    parts = [projected(w_gate)]
+    came = [None, None]
     for s in range(3):
         for i in range(2):
+            if s == 0 and i == 1:
+                scaled, _ = lax.optimization_barrier((scaled, right))
+                parts.append(projected(w_up))
+            if s > 0:
+                came[i], _ = lax.optimization_barrier((came[i], right))
             right = picked(parts[i], jnp.clip(3 - s + z, 0, 3) ^ hp)
             left = picked(parts[i], jnp.clip(s - 3 + z, 0, 3) ^ hp)
             if s > 0:
@@ -158,7 +168,9 @@
         (picked(parts[i], z ^ hp).astype(F32) + came[i][0].astype(F32) + came[i][1].astype(F32)) / rms
         for i in range(2)
     ]
-    hidden, grad_gate, grad_up, inner, loss = elementwise(gate_proj, up_proj, teacher_feats, keep_tiles)
+    hidden, grad_gate, grad_up, inner, loss = elementwise(
+        gate_proj, up_proj, teacher_feats, keep_tiles, True
+    )
 
     streams = [hidden, jnp.concatenate([grad_gate, grad_up], axis=1)]
     right, left = [streams], [streams]

time: 276 us -> 270 us (0.978)
  other arithmetic: 15.6 us -> 11.7 us
  local copies, waits for them, and re-layouts: 7.28 us -> 4.03 us
  starting transfers between devices: 109 us -> 112 us
    ppermute x27, starting transfers between devices: 71.8 us -> 77.6 us  [passed_along(): return lax.ppermute(block, axis, route)]
    convert_element_type x4, other arithmetic: 3.97 us -> 1 us  [on_square(): left = (left.astype(F32) + came[i][1].astype(F32)).astype(BF16)]
  transfers between devices with their start and end apart: 53 -> 53, of which waited for: 28 -> 26; matrix products, arithmetic and copies ran while one was open for 9% -> 9% of each run, Pallas kernels for 0% -> 0%
where the time goes in v7:
time: 270 us; the launch traced here: 267 us
  waiting for transfers between devices  115 us (43%)
  starting transfers between devices  112 us (41%)
  matrix products  19.5 us (7%)
  other arithmetic  11.7 us (4%)
  between operations  4.79 us (2%)
  local copies, waits for them, and re-layouts  4.03 us (1%)
    ppermute x27, waiting for transfers between devices, passed_along(): return lax.ppermute(block, axis, route)  81.3 us
    ppermute x27, starting transfers between devices, passed_along(): return lax.ppermute(block, axis, route)  77.6 us
    ppermute x10, waiting for transfers between devices, swapped(): return lax.ppermute(block, axis, [(0, 1), (1, 0)])  13.8 us
    ppermute x8, starting transfers between devices, brought_home(): lax.ppermute(whole, ('ctx',) + HP, [(4 * c + h, 4 * TURNS[c][k] + c) for...  12.1 us
    ppermute x8, waiting for transfers between devices, brought_home(): lax.ppermute(whole, ('ctx',) + HP, [(4 * c + h, 4 * TURNS[c][k] + c) for...  9.37 us
    ppermute x4, starting transfers between devices, reduced(): lax.ppermute(half.astype(BF16), HP, route).astype(F32)  9.25 us
    ppermute x1, starting transfers between devices, transposed(): return lax.ppermute(block, ('ctx',) + HP, route)  8.02 us
    ppermute x1, waiting for transfers between devices, transposed(): return lax.ppermute(block, ('ctx',) + HP, route)  6.18 us
  transfers between devices with their start and end apart: 53, of which 26 were waited for; matrix products, arithmetic and copies ran while one was open for 9% of the time, Pallas kernels for 0%

profile of v7, /device:TPU:2, one launch (start us, length us, event | category | flops | bytes accessed | tf_op | source)
XLA Modules:
  0.0 267.1 jit_solution(4211152022870320407)
XLA Ops:
  1.5 5.5 %collective-permute-start.2 = (bf16[2,128,256]{2,1,0:T(8,128)(2,1)S(1)}, bf16[2,128,256]{2,1,0:T(8,128)(2,1)S(1)}, u32[]{:S(2)}, u32[]{:S(2)}) collective-permute-start(bf16[2,128,256]{2,1,0:T(8,128)(2,1)S(1)} %pad_maximum_fusion.4), channel_id=1, source_target_pairs={{0,12},{1,13},{2,14},{3,15},{16,28},{17,29},{18,30},{19,31}} | collective-permute-start | bytes 393224 | tf_op jit(solution)/shard_map/ppermute | solution.py:24
  7.0 1.3 collective-permute-start.1
  8.3 2.5 collective-permute-start
  13.8 1.7 collective-permute-done
  19.5 8.0 %collective-permute-start.3 = (bf16[128,1024]{1,0:T(8,128)(2,1)S(1)}, bf16[128,1024]{1,0:T(8,128)(2,1)S(1)}, u32[]{:S(2)}, u32[]{:S(2)}) collective-permute-start(bf16[128,1024]{1,0:T(8,128)(2,1)S(1)} %get-tuple-element.85), channel_id=1, source_target_pairs={{0,0},{1,4},{2,8},{3,12},{4,1},{5,5},{6,9},{7,13},{8,2},{9,6},{10,... | collective-permute-start | bytes 786440 | tf_op jit(solution)/shard_map/ppermute | solution.py:34
  28.7 3.6 %collective-permute-done.5 = f32[128]{0:T(128)S(1)} collective-permute-done((f32[128]{0:T(128)S(1)}, f32[128]{0:T(128)S(1)}, u32[]{:S(2)}, u32[]{:S(2)}) %collective-permute-start.5) | collective-permute-done | bytes 544 | tf_op jit(solution)/shard_map/ppermute | solution.py:28
  32.3 6.2 %collective-permute-done.3 = bf16[128,1024]{1,0:T(8,128)(2,1)S(1)} collective-permute-done((bf16[128,1024]{1,0:T(8,128)(2,1)S(1)}, bf16[128,1024]{1,0:T(8,128)(2,1)S(1)}, u32[]{:S(2)}, u32[]{:S(2)}) %collective-permute-start.3) | collective-permute-done | bytes 262176 | tf_op jit(solution)/shard_map/ppermute | solution.py:34
  38.5 6.4 %collective-permute-done.6 = bf16[128,1024]{1,0:T(8,128)(2,1)S(1)} collective-permute-done((bf16[128,1024]{1,0:T(8,128)(2,1)S(1)}, bf16[128,1024]{1,0:T(8,128)(2,1)S(1)}, u32[]{:S(2)}, u32[]{:S(2)}) %collective-permute-start.6) | collective-permute-done | bytes 262176 | tf_op jit(solution)/shard_map/ppermute | solution.py:28
  49.4 2.1 convolution_convert_fusion.1
  51.6 2.5 collective-permute-start.8
  55.4 2.1 convolution_convert_fusion
  57.6 1.3 collective-permute-start.13
  58.9 5.2 %collective-permute-start.12 = (bf16[128,1792]{1,0:T(8,128)(2,1)S(1)}, bf16[128,1792]{1,0:T(8,128)(2,1)S(1)}, u32[]{:S(2)}, u32[]{:S(2)}) collective-permute-start(bf16[128,1792]{1,0:T(8,128)(2,1)S(1)} %get-tuple-element.44), channel_id=1, source_target_pairs={{0,4},{4,8},{8,12},{1,5},{5,9},{9,13},{2,6},{6,10},{10,14},{3,7},{... | collective-permute-start | bytes 1376264 | tf_op jit(solution)/shard_map/ppermute | solution.py:24
  64.1 5.3 %collective-permute-done.9 = bf16[128,1792]{1,0:T(8,128)(2,1)S(1)} collective-permute-done((bf16[128,1792]{1,0:T(8,128)(2,1)S(1)}, bf16[128,1792]{1,0:T(8,128)(2,1)S(1)}, u32[]{:S(2)}, u32[]{:S(2)}) %collective-permute-start.9) | collective-permute-done | bytes 458784 | tf_op jit(solution)/shard_map/ppermute | solution.py:24
  70.9 4.6 %collective-permute-start.10 = (bf16[128,1792]{1,0:T(8,128)(2,1)S(1)}, bf16[128,1792]{1,0:T(8,128)(2,1)S(1)}, u32[]{:S(2)}, u32[]{:S(2)}) collective-permute-start(bf16[128,1792]{1,0:T(8,128)(2,1)S(1)} %get-tuple-element.47), channel_id=1, source_target_pairs={{0,4},{4,8},{8,12},{1,5},{5,9},{9,13},{2,6},{6,10},{10,14},{3,7},{... | collective-permute-start | bytes 1376264 | tf_op jit(solution)/shard_map/ppermute | solution.py:24
  75.5 3.7 %collective-permute-done.13 = bf16[128,1792]{1,0:T(8,128)(2,1)S(1)} collective-permute-done((bf16[128,1792]{1,0:T(8,128)(2,1)S(1)}, bf16[128,1792]{1,0:T(8,128)(2,1)S(1)}, u32[]{:S(2)}, u32[]{:S(2)}) %collective-permute-start.13) | collective-permute-done | bytes 458784 | tf_op jit(solution)/shard_map/ppermute | solution.py:24
  80.7 4.6 %collective-permute-start.16 = (bf16[128,1792]{1,0:T(8,128)(2,1)S(1)}, bf16[128,1792]{1,0:T(8,128)(2,1)S(1)}, u32[]{:S(2)}, u32[]{:S(2)}) collective-permute-start(bf16[128,1792]{1,0:T(8,128)(2,1)S(1)} %get-tuple-element.52), channel_id=1, source_target_pairs={{0,4},{4,8},{8,12},{1,5},{5,9},{9,13},{2,6},{6,10},{10,14},{3,7},{... | collective-permute-start | bytes 1376264 | tf_op jit(solution)/shard_map/ppermute | solution.py:24
  85.3 3.7 %collective-permute-done.11 = bf16[128,1792]{1,0:T(8,128)(2,1)S(1)} collective-permute-done((bf16[128,1792]{1,0:T(8,128)(2,1)S(1)}, bf16[128,1792]{1,0:T(8,128)(2,1)S(1)}, u32[]{:S(2)}, u32[]{:S(2)}) %collective-permute-start.11) | collective-permute-done | bytes 458784 | tf_op jit(solution)/shard_map/ppermute | solution.py:24
  90.6 4.6 %collective-permute-start.14 = (bf16[128,1792]{1,0:T(8,128)(2,1)S(1)}, bf16[128,1792]{1,0:T(8,128)(2,1)S(1)}, u32[]{:S(2)}, u32[]{:S(2)}) collective-permute-start(bf16[128,1792]{1,0:T(8,128)(2,1)S(1)} %get-tuple-element.55), channel_id=1, source_target_pairs={{0,4},{4,8},{8,12},{1,5},{5,9},{9,13},{2,6},{6,10},{10,14},{3,7},{... | collective-permute-start | bytes 1376264 | tf_op jit(solution)/shard_map/ppermute | solution.py:24
  95.2 3.7 %collective-permute-done.17 = bf16[128,1792]{1,0:T(8,128)(2,1)S(1)} collective-permute-done((bf16[128,1792]{1,0:T(8,128)(2,1)S(1)}, bf16[128,1792]{1,0:T(8,128)(2,1)S(1)}, u32[]{:S(2)}, u32[]{:S(2)}) %collective-permute-start.17) | collective-permute-done | bytes 458784 | tf_op jit(solution)/shard_map/ppermute | solution.py:24
  99.1 2.8 %collective-permute-start.18 = (bf16[128,1792]{1,0:T(8,128)(2,1)S(1)}, bf16[128,1792]{1,0:T(8,128)(2,1)S(1)}, u32[]{:S(2)}, u32[]{:S(2)}) collective-permute-start(bf16[128,1792]{1,0:T(8,128)(2,1)S(1)} %get-tuple-element.61), channel_id=1, source_target_pairs={{0,4},{4,8},{8,12},{1,5},{5,9},{9,13},{2,6},{6,10},{10,14},{3,7},{... | collective-permute-start | bytes 1376264 | tf_op jit(solution)/shard_map/ppermute | solution.py:24
  101.9 1.3 collective-permute-start.19
  103.2 5.5 %collective-permute-done.15 = bf16[128,1792]{1,0:T(8,128)(2,1)S(1)} collective-permute-done((bf16[128,1792]{1,0:T(8,128)(2,1)S(1)}, bf16[128,1792]{1,0:T(8,128)(2,1)S(1)}, u32[]{:S(2)}, u32[]{:S(2)}) %collective-permute-start.15) | collective-permute-done | bytes 458784 | tf_op jit(solution)/shard_map/ppermute | solution.py:24
  109.0 4.7 %collective-permute-done.18 = bf16[128,1792]{1,0:T(8,128)(2,1)S(1)} collective-permute-done((bf16[128,1792]{1,0:T(8,128)(2,1)S(1)}, bf16[128,1792]{1,0:T(8,128)(2,1)S(1)}, u32[]{:S(2)}, u32[]{:S(2)}) %collective-permute-start.18) | collective-permute-done | bytes 458784 | tf_op jit(solution)/shard_map/ppermute | solution.py:24
  113.6 4.1 %collective-permute-done.19 = bf16[128,1792]{1,0:T(8,128)(2,1)S(1)} collective-permute-done((bf16[128,1792]{1,0:T(8,128)(2,1)S(1)}, bf16[128,1792]{1,0:T(8,128)(2,1)S(1)}, u32[]{:S(2)}, u32[]{:S(2)}) %collective-permute-start.19) | collective-permute-done | bytes 458784 | tf_op jit(solution)/shard_map/ppermute | solution.py:24
  119.4 4.8 %collective-permute-start.24 = (bf16[128,1792]{1,0:T(8,128)(2,1)S(1)}, bf16[128,1792]{1,0:T(8,128)(2,1)S(1)}, u32[]{:S(2)}, u32[]{:S(2)}) collective-permute-start(bf16[128,1792]{1,0:T(8,128)(2,1)S(1)} %get-tuple-element.63), channel_id=1, source_target_pairs={{0,4},{4,8},{8,12},{1,5},{5,9},{9,13},{2,6},{6,10},{10,14},{3,7},{... | collective-permute-start | bytes 1376264 | tf_op jit(solution)/shard_map/ppermute | solution.py:24
  127.9 4.6 %collective-permute-start.26 = (bf16[128,3584]{1,0:T(8,128)(2,1)S(1)}, bf16[128,3584]{1,0:T(8,128)(2,1)S(1)}, u32[]{:S(2)}, u32[]{:S(2)}) collective-permute-start(bf16[128,3584]{1,0:T(8,128)(2,1)S(1)} %pad_maximum_fusion.1), channel_id=1, source_target_pairs={{0,4},{4,8},{8,12},{1,5},{5,9},{9,13},{2,6},{6,10},{10,14},{3,7},{... | collective-permute-start | bytes 2752520 | tf_op jit(solution)/shard_map/ppermute | solution.py:24
  135.7 1.3 select_convert_fusion.3
  137.0 1.8 collective-permute-done.45
  139.5 11.9 %collective-permute-done.25 = bf16[128,3584]{1,0:T(8,128)(2,1)S(1)} collective-permute-done((bf16[128,3584]{1,0:T(8,128)(2,1)S(1)}, bf16[128,3584]{1,0:T(8,128)(2,1)S(1)}, u32[]{:S(2)}, u32[]{:S(2)}) %collective-permute-start.25) | collective-permute-done | bytes 917536 | tf_op jit(solution)/shard_map/ppermute | solution.py:24
  154.0 1.3 select_convert_fusion.2
  156.7 5.1 %collective-permute-start.33 = (bf16[128,3584]{1,0:T(8,128)(2,1)S(1)}, bf16[128,3584]{1,0:T(8,128)(2,1)S(1)}, u32[]{:S(2)}, u32[]{:S(2)}) collective-permute-start(bf16[128,3584]{1,0:T(8,128)(2,1)S(1)} %collective-permute-done.26), channel_id=1, source_target_pairs={{0,4},{4,8},{8,12},{1,5},{5,9},{9,13},{2,6},{6,10},{10,14},{3,7},{... | collective-permute-start | bytes 2752520 | tf_op jit(solution)/shard_map/ppermute | solution.py:24
  161.9 2.2 collective-permute-start.21
  165.4 4.6 %collective-permute-start.32 = (bf16[128,1792]{1,0:T(8,128)(2,1)S(1)}, bf16[128,1792]{1,0:T(8,128)(2,1)S(1)}, u32[]{:S(2)}, u32[]{:S(2)}) collective-permute-start(bf16[128,1792]{1,0:T(8,128)(2,1)S(1)} %collective-permute-done.24), channel_id=1, source_target_pairs={{0,4},{4,8},{8,12},{1,5},{5,9},{9,13},{2,6},{6,10},{10,14},{3,7},{... | collective-permute-start | bytes 1376264 | tf_op jit(solution)/shard_map/ppermute | solution.py:24
  171.6 19.1 %collective-permute-done.30 = bf16[128,1792]{1,0:T(8,128)(2,1)S(1)} collective-permute-done((bf16[128,1792]{1,0:T(8,128)(2,1)S(1)}, bf16[128,1792]{1,0:T(8,128)(2,1)S(1)}, u32[]{:S(2)}, u32[]{:S(2)}) %collective-permute-start.30) | collective-permute-done | bytes 458784 | tf_op jit(solution)/shard_map/ppermute | solution.py:24
  193.1 5.0 %collective-permute-start.39 = (bf16[128,1792]{1,0:T(8,128)(2,1)S(1)}, bf16[128,1792]{1,0:T(8,128)(2,1)S(1)}, u32[]{:S(2)}, u32[]{:S(2)}) collective-permute-start(bf16[128,1792]{1,0:T(8,128)(2,1)S(1)} %collective-permute-done.32), channel_id=1, source_target_pairs={{0,4},{4,8},{8,12},{1,5},{5,9},{9,13},{2,6},{6,10},{10,14},{3,7},{... | collective-permute-start | bytes 1376264 | tf_op jit(solution)/shard_map/ppermute | solution.py:24
  199.8 4.6 %collective-permute-start.40 = (bf16[128,3584]{1,0:T(8,128)(2,1)S(1)}, bf16[128,3584]{1,0:T(8,128)(2,1)S(1)}, u32[]{:S(2)}, u32[]{:S(2)}) collective-permute-start(bf16[128,3584]{1,0:T(8,128)(2,1)S(1)} %collective-permute-done.33), channel_id=1, source_target_pairs={{0,4},{4,8},{8,12},{1,5},{5,9},{9,13},{2,6},{6,10},{10,14},{3,7},{... | collective-permute-start | bytes 2752520 | tf_op jit(solution)/shard_map/ppermute | solution.py:24
  205.1 1.3 fusion.36
  206.4 1.3 select_convert_fusion.1
  209.0 4.1 %collective-permute-start.50 = (bf16[128,1024]{1,0:T(8,128)(2,1)S(1)}, bf16[128,1024]{1,0:T(8,128)(2,1)S(1)}, u32[]{:S(2)}, u32[]{:S(2)}) collective-permute-start(bf16[128,1024]{1,0:T(8,128)(2,1)S(1)} %add_convert_fusion.2), channel_id=1, source_target_pairs={{2,4},{6,9},{10,6},{14,11},{18,20},{22,25},{26,22},{30,27}} | collective-permute-start | bytes 786440 | tf_op jit(solution)/shard_map/ppermute | solution.py:191
  213.1 13.8 %collective-permute-done.38 = bf16[128,3584]{1,0:T(8,128)(2,1)S(1)} collective-permute-done((bf16[128,3584]{1,0:T(8,128)(2,1)S(1)}, bf16[128,3584]{1,0:T(8,128)(2,1)S(1)}, u32[]{:S(2)}, u32[]{:S(2)}) %collective-permute-start.38) | collective-permute-done | bytes 917536 | tf_op jit(solution)/shard_map/ppermute | solution.py:24
  228.3 1.3 fusion.32
  230.3 1.3 select_convert_fusion
  233.3 4.5 %collective-permute-start.42 = (bf16[128,1024]{1,0:T(8,128)(2,1)S(1)}, bf16[128,1024]{1,0:T(8,128)(2,1)S(1)}, u32[]{:S(2)}, u32[]{:S(2)}) collective-permute-start(bf16[128,1024]{1,0:T(8,128)(2,1)S(1)} %fusion.52), channel_id=1, source_target_pairs={{1,3},{2,0},{5,7},{6,4},{9,11},{10,8},{13,15},{14,12},{17,19},{18,... | collective-permute-start | bytes 786440 | tf_op jit(solution)/shard_map/ppermute | solution.py:187
  237.8 4.1 %collective-permute-done.35 = bf16[128,1024]{1,0:T(8,128)(2,1)S(1)} collective-permute-done((bf16[128,1024]{1,0:T(8,128)(2,1)S(1)}, bf16[128,1024]{1,0:T(8,128)(2,1)S(1)}, u32[]{:S(2)}, u32[]{:S(2)}) %collective-permute-start.35) | collective-permute-done | bytes 262176 | tf_op jit(solution)/shard_map/ppermute | solution.py:187
  242.1 3.3 %collective-permute-start.48 = (f32[128]{0:T(128)S(1)}, f32[128]{0:T(128)S(1)}, u32[]{:S(2)}, u32[]{:S(2)}) collective-permute-start(f32[128]{0:T(128)S(1)} %get-tuple-element.76), channel_id=1, source_target_pairs={{0,12},{4,8},{8,4},{12,0},{1,13},{5,9},{9,5},{13,1},{2,14},{6,10},... | collective-permute-start | bytes 1544 | tf_op jit(solution)/shard_map/ppermute | solution.py:220
  248.7 3.3 %collective-permute-start.36 = (bf16[128,1024]{1,0:T(8,128)(2,1)S(1)}, bf16[128,1024]{1,0:T(8,128)(2,1)S(1)}, u32[]{:S(2)}, u32[]{:S(2)}) collective-permute-start(bf16[128,1024]{1,0:T(8,128)(2,1)S(1)} %add_convert_fusion.1), channel_id=1, source_target_pairs={{2,8},{6,13},{10,2},{14,7},{18,24},{22,29},{26,18},{30,23}} | collective-permute-start | bytes 786440 | tf_op jit(solution)/shard_map/ppermute | solution.py:191
  255.3 9.4 %collective-permute-done.51 = bf16[128,1024]{1,0:T(8,128)(2,1)S(1)} collective-permute-done((bf16[128,1024]{1,0:T(8,128)(2,1)S(1)}, bf16[128,1024]{1,0:T(8,128)(2,1)S(1)}, u32[]{:S(2)}, u32[]{:S(2)}) %collective-permute-start.51) | collective-permute-done | bytes 262176 | tf_op jit(solution)/shard_map/ppermute | solution.py:191
  (150 shorter events, 51.7 us)
Async XLA Ops:
  1.5 11.6 %collective-permute-start.2 = (bf16[2,128,256]{2,1,0:T(8,128)(2,1)S(1)}, bf16[2,128,256]{2,1,0:T(8,128)(2,1)S(1)}, u32[]{:S(2)}, u32[]{:S(2)}) collective-permute-start(bf16[2,128,256]{2,1,0:T(8,128)(2,1)S(1)} %pad_maximum_fusion.4), channel_id=1, source_target_pairs={{0,12},{1,13},{2,14},{3,15},{16,28},{17,29},{18,30},{19,31}} | collective-permute-start | bytes 393224 | tf_op jit(solution)/shard_map/ppermute | solution.py:24
  7.0 6.7 %collective-permute-start.1 = (bf16[2,128,256]{2,1,0:T(8,128)(2,1)S(1)}, bf16[2,128,256]{2,1,0:T(8,128)(2,1)S(1)}, u32[]{:S(2)}, u32[]{:S(2)}) collective-permute-start(bf16[2,128,256]{2,1,0:T(8,128)(2,1)S(1)} %pad_maximum_fusion.4), channel_id=1, source_target_pairs={{0,8},{4,12},{1,9},{5,13},{2,10},{6,14},{3,11},{7,15},{16,24},{20,... | collective-permute-start | bytes 393224 | tf_op jit(solution)/shard_map/ppermute | solution.py:24
  8.3 7.1 %collective-permute-start = (bf16[2,128,256]{2,1,0:T(8,128)(2,1)S(1)}, bf16[2,128,256]{2,1,0:T(8,128)(2,1)S(1)}, u32[]{:S(2)}, u32[]{:S(2)}) collective-permute-start(bf16[2,128,256]{2,1,0:T(8,128)(2,1)S(1)} %pad_maximum_fusion.4), channel_id=1, source_target_pairs={{0,4},{4,8},{8,12},{1,5},{5,9},{9,13},{2,6},{6,10},{10,14},{3,7},{... | collective-permute-start | bytes 393224 | tf_op jit(solution)/shard_map/ppermute | solution.py:24
  19.5 19.0 %collective-permute-start.3 = (bf16[128,1024]{1,0:T(8,128)(2,1)S(1)}, bf16[128,1024]{1,0:T(8,128)(2,1)S(1)}, u32[]{:S(2)}, u32[]{:S(2)}) collective-permute-start(bf16[128,1024]{1,0:T(8,128)(2,1)S(1)} %get-tuple-element.85), channel_id=1, source_target_pairs={{0,0},{1,4},{2,8},{3,12},{4,1},{5,5},{6,9},{7,13},{8,2},{9,6},{10,... | collective-permute-start | bytes 786440 | tf_op jit(solution)/shard_map/ppermute | solution.py:34
  38.5 6.4 %collective-permute-start.6 = (bf16[128,1024]{1,0:T(8,128)(2,1)S(1)}, bf16[128,1024]{1,0:T(8,128)(2,1)S(1)}, u32[]{:S(2)}, u32[]{:S(2)}) collective-permute-start(bf16[128,1024]{1,0:T(8,128)(2,1)S(1)} %collective-permute-done.3), channel_id=1, source_target_pairs={{0,2},{2,0},{1,3},{3,1},{4,6},{6,4},{5,7},{7,5},{8,10},{10,8},{9,1... | collective-permute-start | bytes 786440 | tf_op jit(solution)/shard_map/ppermute | solution.py:28
  51.6 17.8 %collective-permute-start.8 = (bf16[128,1792]{1,0:T(8,128)(2,1)S(1)}, bf16[128,1792]{1,0:T(8,128)(2,1)S(1)}, u32[]{:S(2)}, u32[]{:S(2)}) collective-permute-start(bf16[128,1792]{1,0:T(8,128)(2,1)S(1)} %get-tuple-element.41), channel_id=1, source_target_pairs={{0,4},{4,8},{8,12},{1,5},{5,9},{9,13},{2,6},{6,10},{10,14},{3,7},{... | collective-permute-start | bytes 1376264 | tf_op jit(solution)/shard_map/ppermute | solution.py:24
  54.1 15.3 %collective-permute-start.9 = (bf16[128,1792]{1,0:T(8,128)(2,1)S(1)}, bf16[128,1792]{1,0:T(8,128)(2,1)S(1)}, u32[]{:S(2)}, u32[]{:S(2)}) collective-permute-start(bf16[128,1792]{1,0:T(8,128)(2,1)S(1)} %get-tuple-element.42), channel_id=1, source_target_pairs={{4,0},{8,4},{12,8},{5,1},{9,5},{13,9},{6,2},{10,6},{14,10},{7,3},{... | collective-permute-start | bytes 1376264 | tf_op jit(solution)/shard_map/ppermute | solution.py:24
  57.6 21.6 %collective-permute-start.13 = (bf16[128,1792]{1,0:T(8,128)(2,1)S(1)}, bf16[128,1792]{1,0:T(8,128)(2,1)S(1)}, u32[]{:S(2)}, u32[]{:S(2)}) collective-permute-start(bf16[128,1792]{1,0:T(8,128)(2,1)S(1)} %get-tuple-element.49), channel_id=1, source_target_pairs={{4,0},{8,4},{12,8},{5,1},{9,5},{13,9},{6,2},{10,6},{14,10},{7,3},{... | collective-permute-start | bytes 1376264 | tf_op jit(solution)/shard_map/ppermute | solution.py:24
  58.9 20.3 %collective-permute-start.12 = (bf16[128,1792]{1,0:T(8,128)(2,1)S(1)}, bf16[128,1792]{1,0:T(8,128)(2,1)S(1)}, u32[]{:S(2)}, u32[]{:S(2)}) collective-permute-start(bf16[128,1792]{1,0:T(8,128)(2,1)S(1)} %get-tuple-element.44), channel_id=1, source_target_pairs={{0,4},{4,8},{8,12},{1,5},{5,9},{9,13},{2,6},{6,10},{10,14},{3,7},{... | collective-permute-start | bytes 1376264 | tf_op jit(solution)/shard_map/ppermute | solution.py:24
  69.6 19.4 %collective-permute-start.11 = (bf16[128,1792]{1,0:T(8,128)(2,1)S(1)}, bf16[128,1792]{1,0:T(8,128)(2,1)S(1)}, u32[]{:S(2)}, u32[]{:S(2)}) collective-permute-start(bf16[128,1792]{1,0:T(8,128)(2,1)S(1)} %get-tuple-element.48), channel_id=1, source_target_pairs={{4,0},{8,4},{12,8},{5,1},{9,5},{13,9},{6,2},{10,6},{14,10},{7,3},{... | collective-permute-start | bytes 1376264 | tf_op jit(solution)/shard_map/ppermute | solution.py:24
  70.9 18.1 %collective-permute-start.10 = (bf16[128,1792]{1,0:T(8,128)(2,1)S(1)}, bf16[128,1792]{1,0:T(8,128)(2,1)S(1)}, u32[]{:S(2)}, u32[]{:S(2)}) collective-permute-start(bf16[128,1792]{1,0:T(8,128)(2,1)S(1)} %get-tuple-element.47), channel_id=1, source_target_pairs={{0,4},{4,8},{8,12},{1,5},{5,9},{9,13},{2,6},{6,10},{10,14},{3,7},{... | collective-permute-start | bytes 1376264 | tf_op jit(solution)/shard_map/ppermute | solution.py:24
  79.4 19.4 %collective-permute-start.17 = (bf16[128,1792]{1,0:T(8,128)(2,1)S(1)}, bf16[128,1792]{1,0:T(8,128)(2,1)S(1)}, u32[]{:S(2)}, u32[]{:S(2)}) collective-permute-start(bf16[128,1792]{1,0:T(8,128)(2,1)S(1)} %get-tuple-element.58), channel_id=1, source_target_pairs={{4,0},{8,4},{12,8},{5,1},{9,5},{13,9},{6,2},{10,6},{14,10},{7,3},{... | collective-permute-start | bytes 1376264 | tf_op jit(solution)/shard_map/ppermute | solution.py:24
  80.7 18.1 %collective-permute-start.16 = (bf16[128,1792]{1,0:T(8,128)(2,1)S(1)}, bf16[128,1792]{1,0:T(8,128)(2,1)S(1)}, u32[]{:S(2)}, u32[]{:S(2)}) collective-permute-start(bf16[128,1792]{1,0:T(8,128)(2,1)S(1)} %get-tuple-element.52), channel_id=1, source_target_pairs={{0,4},{4,8},{8,12},{1,5},{5,9},{9,13},{2,6},{6,10},{10,14},{3,7},{... | collective-permute-start | bytes 1376264 | tf_op jit(solution)/shard_map/ppermute | solution.py:24
  89.3 19.4 %collective-permute-start.15 = (bf16[128,1792]{1,0:T(8,128)(2,1)S(1)}, bf16[128,1792]{1,0:T(8,128)(2,1)S(1)}, u32[]{:S(2)}, u32[]{:S(2)}) collective-permute-start(bf16[128,1792]{1,0:T(8,128)(2,1)S(1)} %get-tuple-element.56), channel_id=1, source_target_pairs={{4,0},{8,4},{12,8},{5,1},{9,5},{13,9},{6,2},{10,6},{14,10},{7,3},{... | collective-permute-start | bytes 1376264 | tf_op jit(solution)/shard_map/ppermute | solution.py:24
  90.6 18.1 %collective-permute-start.14 = (bf16[128,1792]{1,0:T(8,128)(2,1)S(1)}, bf16[128,1792]{1,0:T(8,128)(2,1)S(1)}, u32[]{:S(2)}, u32[]{:S(2)}) collective-permute-start(bf16[128,1792]{1,0:T(8,128)(2,1)S(1)} %get-tuple-element.55), channel_id=1, source_target_pairs={{0,4},{4,8},{8,12},{1,5},{5,9},{9,13},{2,6},{6,10},{10,14},{3,7},{... | collective-permute-start | bytes 1376264 | tf_op jit(solution)/shard_map/ppermute | solution.py:24
  99.1 14.5 %collective-permute-start.18 = (bf16[128,1792]{1,0:T(8,128)(2,1)S(1)}, bf16[128,1792]{1,0:T(8,128)(2,1)S(1)}, u32[]{:S(2)}, u32[]{:S(2)}) collective-permute-start(bf16[128,1792]{1,0:T(8,128)(2,1)S(1)} %get-tuple-element.61), channel_id=1, source_target_pairs={{0,4},{4,8},{8,12},{1,5},{5,9},{9,13},{2,6},{6,10},{10,14},{3,7},{... | collective-permute-start | bytes 1376264 | tf_op jit(solution)/shard_map/ppermute | solution.py:24
  101.9 15.9 %collective-permute-start.19 = (bf16[128,1792]{1,0:T(8,128)(2,1)S(1)}, bf16[128,1792]{1,0:T(8,128)(2,1)S(1)}, u32[]{:S(2)}, u32[]{:S(2)}) collective-permute-start(bf16[128,1792]{1,0:T(8,128)(2,1)S(1)} %get-tuple-element.62), channel_id=1, source_target_pairs={{4,0},{8,4},{12,8},{5,1},{9,5},{13,9},{6,2},{10,6},{14,10},{7,3},{... | collective-permute-start | bytes 1376264 | tf_op jit(solution)/shard_map/ppermute | solution.py:24
  118.1 20.7 %collective-permute-start.23 = (bf16[128,1792]{1,0:T(8,128)(2,1)S(1)}, bf16[128,1792]{1,0:T(8,128)(2,1)S(1)}, u32[]{:S(2)}, u32[]{:S(2)}) collective-permute-start(bf16[128,1792]{1,0:T(8,128)(2,1)S(1)} %get-tuple-element.63), channel_id=1, source_target_pairs={{4,0},{8,4},{12,8},{5,1},{9,5},{13,9},{6,2},{10,6},{14,10},{7,3},{... | collective-permute-start | bytes 1376264 | tf_op jit(solution)/shard_map/ppermute | solution.py:24
  119.4 19.4 %collective-permute-start.24 = (bf16[128,1792]{1,0:T(8,128)(2,1)S(1)}, bf16[128,1792]{1,0:T(8,128)(2,1)S(1)}, u32[]{:S(2)}, u32[]{:S(2)}) collective-permute-start(bf16[128,1792]{1,0:T(8,128)(2,1)S(1)} %get-tuple-element.63), channel_id=1, source_target_pairs={{0,4},{4,8},{8,12},{1,5},{5,9},{9,13},{2,6},{6,10},{10,14},{3,7},{... | collective-permute-start | bytes 1376264 | tf_op jit(solution)/shard_map/ppermute | solution.py:24
  126.6 24.8 %collective-permute-start.25 = (bf16[128,3584]{1,0:T(8,128)(2,1)S(1)}, bf16[128,3584]{1,0:T(8,128)(2,1)S(1)}, u32[]{:S(2)}, u32[]{:S(2)}) collective-permute-start(bf16[128,3584]{1,0:T(8,128)(2,1)S(1)} %pad_maximum_fusion.1), channel_id=1, source_target_pairs={{4,0},{8,4},{12,8},{5,1},{9,5},{13,9},{6,2},{10,6},{14,10},{7,3},{... | collective-permute-start | bytes 2752520 | tf_op jit(solution)/shard_map/ppermute | solution.py:24
  127.9 24.7 %collective-permute-start.26 = (bf16[128,3584]{1,0:T(8,128)(2,1)S(1)}, bf16[128,3584]{1,0:T(8,128)(2,1)S(1)}, u32[]{:S(2)}, u32[]{:S(2)}) collective-permute-start(bf16[128,3584]{1,0:T(8,128)(2,1)S(1)} %pad_maximum_fusion.1), channel_id=1, source_target_pairs={{0,4},{4,8},{8,12},{1,5},{5,9},{9,13},{2,6},{6,10},{10,14},{3,7},{... | collective-permute-start | bytes 2752520 | tf_op jit(solution)/shard_map/ppermute | solution.py:24
  135.2 3.6 %collective-permute-start.45 = (f32[256]{0:T(256)S(1)}, f32[256]{0:T(256)S(1)}, u32[]{:S(2)}, u32[]{:S(2)}) collective-permute-start(f32[256]{0:T(256)S(1)} %fusion.101), channel_id=1, source_target_pairs={{0,2},{2,0},{1,3},{3,1},{4,6},{6,4},{5,7},{7,5},{8,10},{10,8},{9,1... | collective-permute-start | bytes 3080 | tf_op jit(solution)/shard_map/ppermute | solution.py:28
  138.8 23.0 %collective-permute-start.20 = (bf16[128,1024]{1,0:T(8,128)(2,1)S(1)}, bf16[128,1024]{1,0:T(8,128)(2,1)S(1)}, u32[]{:S(2)}, u32[]{:S(2)}) collective-permute-start(bf16[128,1024]{1,0:T(8,128)(2,1)S(1)} %get-tuple-element.121), channel_id=1, source_target_pairs={{0,1},{1,0},{2,3},{3,2},{4,5},{5,4},{6,7},{7,6},{8,9},{9,8},{10,11... | collective-permute-start | bytes 786440 | tf_op jit(solution)/shard_map/ppermute | solution.py:28
  155.3 10.1 %collective-permute-start.27 = (bf16[128,1024]{1,0:T(8,128)(2,1)S(1)}, bf16[128,1024]{1,0:T(8,128)(2,1)S(1)}, u32[]{:S(2)}, u32[]{:S(2)}) collective-permute-start(bf16[128,1024]{1,0:T(8,128)(2,1)S(1)} %get-tuple-element.119), channel_id=1, source_target_pairs={{0,1},{1,0},{2,3},{3,2},{4,5},{5,4},{6,7},{7,6},{8,9},{9,8},{10,11... | collective-permute-start | bytes 786440 | tf_op jit(solution)/shard_map/ppermute | solution.py:28
  155.4 42.9 %collective-permute-start.31 = (bf16[128,3584]{1,0:T(8,128)(2,1)S(1)}, bf16[128,3584]{1,0:T(8,128)(2,1)S(1)}, u32[]{:S(2)}, u32[]{:S(2)}) collective-permute-start(bf16[128,3584]{1,0:T(8,128)(2,1)S(1)} %collective-permute-done.25), channel_id=1, source_target_pairs={{4,0},{8,4},{12,8},{5,1},{9,5},{13,9},{6,2},{10,6},{14,10},{7,3},{... | collective-permute-start | bytes 2752520 | tf_op jit(solution)/shard_map/ppermute | solution.py:24
  156.7 41.6 %collective-permute-start.33 = (bf16[128,3584]{1,0:T(8,128)(2,1)S(1)}, bf16[128,3584]{1,0:T(8,128)(2,1)S(1)}, u32[]{:S(2)}, u32[]{:S(2)}) collective-permute-start(bf16[128,3584]{1,0:T(8,128)(2,1)S(1)} %collective-permute-done.26), channel_id=1, source_target_pairs={{0,4},{4,8},{8,12},{1,5},{5,9},{9,13},{2,6},{6,10},{10,14},{3,7},{... | collective-permute-start | bytes 2752520 | tf_op jit(solution)/shard_map/ppermute | solution.py:24
  161.9 8.2 %collective-permute-start.21 = (bf16[128,1024]{1,0:T(8,128)(2,1)S(1)}, bf16[128,1024]{1,0:T(8,128)(2,1)S(1)}, u32[]{:S(2)}, u32[]{:S(2)}) collective-permute-start(bf16[128,1024]{1,0:T(8,128)(2,1)S(1)} %fusion.49), channel_id=1, source_target_pairs={{2,0},{1,3},{6,4},{5,7},{10,8},{9,11},{14,12},{13,15},{18,16},{17,... | collective-permute-start | bytes 786440 | tf_op jit(solution)/shard_map/ppermute | solution.py:187
  164.1 26.5 %collective-permute-start.30 = (bf16[128,1792]{1,0:T(8,128)(2,1)S(1)}, bf16[128,1792]{1,0:T(8,128)(2,1)S(1)}, u32[]{:S(2)}, u32[]{:S(2)}) collective-permute-start(bf16[128,1792]{1,0:T(8,128)(2,1)S(1)} %collective-permute-done.23), channel_id=1, source_target_pairs={{4,0},{8,4},{12,8},{5,1},{9,5},{13,9},{6,2},{10,6},{14,10},{7,3},{... | collective-permute-start | bytes 1376264 | tf_op jit(solution)/shard_map/ppermute | solution.py:24
  165.4 26.4 %collective-permute-start.32 = (bf16[128,1792]{1,0:T(8,128)(2,1)S(1)}, bf16[128,1792]{1,0:T(8,128)(2,1)S(1)}, u32[]{:S(2)}, u32[]{:S(2)}) collective-permute-start(bf16[128,1792]{1,0:T(8,128)(2,1)S(1)} %collective-permute-done.24), channel_id=1, source_target_pairs={{0,4},{4,8},{8,12},{1,5},{5,9},{9,13},{2,6},{6,10},{10,14},{3,7},{... | collective-permute-start | bytes 1376264 | tf_op jit(solution)/shard_map/ppermute | solution.py:24
  170.1 23.0 %collective-permute-start.28 = (bf16[128,1024]{1,0:T(8,128)(2,1)S(1)}, bf16[128,1024]{1,0:T(8,128)(2,1)S(1)}, u32[]{:S(2)}, u32[]{:S(2)}) collective-permute-start(bf16[128,1024]{1,0:T(8,128)(2,1)S(1)} %fusion.50), channel_id=1, source_target_pairs={{3,1},{0,2},{7,5},{4,6},{11,9},{8,10},{15,13},{12,14},{19,17},{16,... | collective-permute-start | bytes 786440 | tf_op jit(solution)/shard_map/ppermute | solution.py:187
  190.6 54.7 %collective-permute-start.49 = (bf16[128,1024]{1,0:T(8,128)(2,1)S(1)}, bf16[128,1024]{1,0:T(8,128)(2,1)S(1)}, u32[]{:S(2)}, u32[]{:S(2)}) collective-permute-start(bf16[128,1024]{1,0:T(8,128)(2,1)S(1)} %add_convert_fusion.3), channel_id=1, source_target_pairs={{3,0},{7,5},{11,10},{15,15},{19,16},{23,21},{27,26},{31,31}} | collective-permute-start | bytes 786440 | tf_op jit(solution)/shard_map/ppermute | solution.py:191
  191.8 15.9 %collective-permute-start.37 = (bf16[128,1792]{1,0:T(8,128)(2,1)S(1)}, bf16[128,1792]{1,0:T(8,128)(2,1)S(1)}, u32[]{:S(2)}, u32[]{:S(2)}) collective-permute-start(bf16[128,1792]{1,0:T(8,128)(2,1)S(1)} %collective-permute-done.30), channel_id=1, source_target_pairs={{4,0},{8,4},{12,8},{5,1},{9,5},{13,9},{6,2},{10,6},{14,10},{7,3},{... | collective-permute-start | bytes 1376264 | tf_op jit(solution)/shard_map/ppermute | solution.py:24
  193.1 15.9 %collective-permute-start.39 = (bf16[128,1792]{1,0:T(8,128)(2,1)S(1)}, bf16[128,1792]{1,0:T(8,128)(2,1)S(1)}, u32[]{:S(2)}, u32[]{:S(2)}) collective-permute-start(bf16[128,1792]{1,0:T(8,128)(2,1)S(1)} %collective-permute-done.32), channel_id=1, source_target_pairs={{0,4},{4,8},{8,12},{1,5},{5,9},{9,13},{2,6},{6,10},{10,14},{3,7},{... | collective-permute-start | bytes 1376264 | tf_op jit(solution)/shard_map/ppermute | solution.py:24
  198.5 28.4 %collective-permute-start.38 = (bf16[128,3584]{1,0:T(8,128)(2,1)S(1)}, bf16[128,3584]{1,0:T(8,128)(2,1)S(1)}, u32[]{:S(2)}, u32[]{:S(2)}) collective-permute-start(bf16[128,3584]{1,0:T(8,128)(2,1)S(1)} %collective-permute-done.31), channel_id=1, source_target_pairs={{4,0},{8,4},{12,8},{5,1},{9,5},{13,9},{6,2},{10,6},{14,10},{7,3},{... | collective-permute-start | bytes 2752520 | tf_op jit(solution)/shard_map/ppermute | solution.py:24
  199.8 28.3 %collective-permute-start.40 = (bf16[128,3584]{1,0:T(8,128)(2,1)S(1)}, bf16[128,3584]{1,0:T(8,128)(2,1)S(1)}, u32[]{:S(2)}, u32[]{:S(2)}) collective-permute-start(bf16[128,3584]{1,0:T(8,128)(2,1)S(1)} %collective-permute-done.33), channel_id=1, source_target_pairs={{0,4},{4,8},{8,12},{1,5},{5,9},{9,13},{2,6},{6,10},{10,14},{3,7},{... | collective-permute-start | bytes 2752520 | tf_op jit(solution)/shard_map/ppermute | solution.py:24
  207.7 39.0 %collective-permute-start.22 = (bf16[128,1024]{1,0:T(8,128)(2,1)S(1)}, bf16[128,1024]{1,0:T(8,128)(2,1)S(1)}, u32[]{:S(2)}, u32[]{:S(2)}) collective-permute-start(bf16[128,1024]{1,0:T(8,128)(2,1)S(1)} %add_convert_fusion.3), channel_id=1, source_target_pairs={{0,0},{4,5},{8,10},{12,15},{16,16},{20,21},{24,26},{28,31}} | collective-permute-start | bytes 786440 | tf_op jit(solution)/shard_map/ppermute | solution.py:191
  209.0 38.3 %collective-permute-start.50 = (bf16[128,1024]{1,0:T(8,128)(2,1)S(1)}, bf16[128,1024]{1,0:T(8,128)(2,1)S(1)}, u32[]{:S(2)}, u32[]{:S(2)}) collective-permute-start(bf16[128,1024]{1,0:T(8,128)(2,1)S(1)} %add_convert_fusion.2), channel_id=1, source_target_pairs={{2,4},{6,9},{10,6},{14,11},{18,20},{22,25},{26,22},{30,27}} | collective-permute-start | bytes 786440 | tf_op jit(solution)/shard_map/ppermute | solution.py:191
  226.9 4.8 %collective-permute-start.34 = (bf16[128,1024]{1,0:T(8,128)(2,1)S(1)}, bf16[128,1024]{1,0:T(8,128)(2,1)S(1)}, u32[]{:S(2)}, u32[]{:S(2)}) collective-permute-start(bf16[128,1024]{1,0:T(8,128)(2,1)S(1)} %get-tuple-element.117), channel_id=1, source_target_pairs={{0,1},{1,0},{2,3},{3,2},{4,5},{5,4},{6,7},{7,6},{8,9},{9,8},{10,11... | collective-permute-start | bytes 786440 | tf_op jit(solution)/shard_map/ppermute | solution.py:28
  231.8 10.1 %collective-permute-start.35 = (bf16[128,1024]{1,0:T(8,128)(2,1)S(1)}, bf16[128,1024]{1,0:T(8,128)(2,1)S(1)}, u32[]{:S(2)}, u32[]{:S(2)}) collective-permute-start(bf16[128,1024]{1,0:T(8,128)(2,1)S(1)} %fusion.51), channel_id=1, source_target_pairs={{0,2},{3,1},{4,6},{7,5},{8,10},{11,9},{12,14},{15,13},{16,18},{19,... | collective-permute-start | bytes 786440 | tf_op jit(solution)/shard_map/ppermute | solution.py:187
  233.3 12.8 %collective-permute-start.42 = (bf16[128,1024]{1,0:T(8,128)(2,1)S(1)}, bf16[128,1024]{1,0:T(8,128)(2,1)S(1)}, u32[]{:S(2)}, u32[]{:S(2)}) collective-permute-start(bf16[128,1024]{1,0:T(8,128)(2,1)S(1)} %fusion.52), channel_id=1, source_target_pairs={{1,3},{2,0},{5,7},{6,4},{9,11},{10,8},{13,15},{14,12},{17,19},{18,... | collective-permute-start | bytes 786440 | tf_op jit(solution)/shard_map/ppermute | solution.py:187
  242.1 6.6 %collective-permute-start.48 = (f32[128]{0:T(128)S(1)}, f32[128]{0:T(128)S(1)}, u32[]{:S(2)}, u32[]{:S(2)}) collective-permute-start(f32[128]{0:T(128)S(1)} %get-tuple-element.76), channel_id=1, source_target_pairs={{0,12},{4,8},{8,4},{12,0},{1,13},{5,9},{9,5},{13,1},{2,14},{6,10},... | collective-permute-start | bytes 1544 | tf_op jit(solution)/shard_map/ppermute | solution.py:220
  245.4 6.6 %collective-permute-start.47 = (f32[128]{0:T(128)S(1)}, f32[128]{0:T(128)S(1)}, u32[]{:S(2)}, u32[]{:S(2)}) collective-permute-start(f32[128]{0:T(128)S(1)} %get-tuple-element.76), channel_id=1, source_target_pairs={{0,8},{4,12},{8,0},{12,4},{1,9},{5,13},{9,1},{13,5},{2,10},{6,14},... | collective-permute-start | bytes 1544 | tf_op jit(solution)/shard_map/ppermute | solution.py:220
  246.1 6.6 %collective-permute-start.46 = (f32[128]{0:T(128)S(1)}, f32[128]{0:T(128)S(1)}, u32[]{:S(2)}, u32[]{:S(2)}) collective-permute-start(f32[128]{0:T(128)S(1)} %get-tuple-element.76), channel_id=1, source_target_pairs={{0,4},{4,0},{8,12},{12,8},{1,5},{5,1},{9,13},{13,9},{2,6},{6,2},{1... | collective-permute-start | bytes 1544 | tf_op jit(solution)/shard_map/ppermute | solution.py:220
  246.7 8.7 %collective-permute-start.29 = (bf16[128,1024]{1,0:T(8,128)(2,1)S(1)}, bf16[128,1024]{1,0:T(8,128)(2,1)S(1)}, u32[]{:S(2)}, u32[]{:S(2)}) collective-permute-start(bf16[128,1024]{1,0:T(8,128)(2,1)S(1)} %add_convert_fusion.2), channel_id=1, source_target_pairs={{1,4},{5,9},{9,6},{13,11},{17,20},{21,25},{25,22},{29,27}} | collective-permute-start | bytes 786440 | tf_op jit(solution)/shard_map/ppermute | solution.py:191
  247.4 17.3 %collective-permute-start.51 = (bf16[128,1024]{1,0:T(8,128)(2,1)S(1)}, bf16[128,1024]{1,0:T(8,128)(2,1)S(1)}, u32[]{:S(2)}, u32[]{:S(2)}) collective-permute-start(bf16[128,1024]{1,0:T(8,128)(2,1)S(1)} %add_convert_fusion.1), channel_id=1, source_target_pairs={{1,8},{5,13},{9,2},{13,7},{17,24},{21,29},{25,18},{29,23}} | collective-permute-start | bytes 786440 | tf_op jit(solution)/shard_map/ppermute | solution.py:191
  248.7 16.0 %collective-permute-start.36 = (bf16[128,1024]{1,0:T(8,128)(2,1)S(1)}, bf16[128,1024]{1,0:T(8,128)(2,1)S(1)}, u32[]{:S(2)}, u32[]{:S(2)}) collective-permute-start(bf16[128,1024]{1,0:T(8,128)(2,1)S(1)} %add_convert_fusion.1), channel_id=1, source_target_pairs={{2,8},{6,13},{10,2},{14,7},{18,24},{22,29},{26,18},{30,23}} | collective-permute-start | bytes 786440 | tf_op jit(solution)/shard_map/ppermute | solution.py:191
  252.0 12.7 %collective-permute-start.52 = (bf16[128,1024]{1,0:T(8,128)(2,1)S(1)}, bf16[128,1024]{1,0:T(8,128)(2,1)S(1)}, u32[]{:S(2)}, u32[]{:S(2)}) collective-permute-start(bf16[128,1024]{1,0:T(8,128)(2,1)S(1)} %add_convert_fusion), channel_id=1, source_target_pairs={{0,12},{4,1},{8,14},{12,3},{16,28},{20,17},{24,30},{28,19}} | collective-permute-start | bytes 786440 | tf_op jit(solution)/shard_map/ppermute | solution.py:191
  252.7 12.0 %collective-permute-start.43 = (bf16[128,1024]{1,0:T(8,128)(2,1)S(1)}, bf16[128,1024]{1,0:T(8,128)(2,1)S(1)}, u32[]{:S(2)}, u32[]{:S(2)}) collective-permute-start(bf16[128,1024]{1,0:T(8,128)(2,1)S(1)} %add_convert_fusion), channel_id=1, source_target_pairs={{3,12},{7,1},{11,14},{15,3},{19,28},{23,17},{27,30},{31,19}} | collective-permute-start | bytes 786440 | tf_op jit(solution)/shard_map/ppermute | solution.py:191
  (12 other events, 107.4 us)

commit v8 on v7

--- a/solution.py
+++ b/solution.py
@@ -3,7 +3,9 @@
 import jax
 import jax.numpy as jnp
 from jax import lax
+from jax.experimental import pallas as pl
 from jax.experimental.layout import Layout, with_layout_constraint
+from jax.experimental.pallas import tpu as pltpu
 from jax.sharding import PartitionSpec as P
 
 
@@ -34,47 +36,51 @@
     return lax.ppermute(block, ("ctx",) + HP, route)
 
 
-def attend_heads(query_part, key_rows, value_rows, allowed):
-    scores = jnp.einsum("thd,sd->hts", query_part, key_rows, preferred_element_type=F32) * (
-        1.0 / math.sqrt(HEAD_DIM)
-    )
-    masked = jnp.where(allowed[None], scores, -jnp.inf)
-    highest = jnp.max(masked, axis=-1, keepdims=True)
-    weights = jnp.exp(masked - highest)
-    normalized = (weights / jnp.sum(weights, axis=-1, keepdims=True)).astype(BF16)
-    return jnp.einsum("hts,sd->thd", normalized, value_rows, preferred_element_type=F32)
-
-
-def attention(student_query, teacher_keys, teacher_values, band_span):
+def attention_kernel(ctx_ref, query_ref, span_ref, resid_ref, *refs):
+    *pair_refs, out_ref = refs
+    rows = query_ref.shape[0]
+    kv_local = pair_refs[0].shape[2] // HEAD_DIM
+    group_size = HEADS // KV_HEADS
+    ctx = ctx_ref[0]
+    shape = (rows, rows)
+    offset = lax.broadcasted_iota(jnp.int32, shape, 0) - lax.broadcasted_iota(jnp.int32, shape, 1)
+    span = span_ref[...]
+    allowed = []
+    for back in range(len(pair_refs)):
+        distance = offset + back * rows
+        reach = jnp.where(ctx >= back, span, 0)
+        allowed.append((distance >= 0) & (distance < reach))
+    allowed = jnp.concatenate([jnp.where(v, 0.0, -jnp.inf) for v in allowed], axis=1)
+    for kv_head in range(kv_local):
+        cols = slice(kv_head * HEAD_DIM, (kv_head + 1) * HEAD_DIM)
+        keys = jnp.concatenate([r[0, :, cols] for r in pair_refs], axis=0)
+        values = jnp.concatenate([r[1, :, cols] for r in pair_refs], axis=0)
+        for g in range(group_size):
+            first = (kv_head * group_size + g) * HEAD_DIM
+            head = slice(first, first + HEAD_DIM)
+            scores = lax.dot_general(
+                query_ref[:, head], keys, (((1,), (1,)), ((), ())), preferred_element_type=F32
+            )
+            masked = scores * (1.0 / math.sqrt(HEAD_DIM)) + allowed
+            weights = jnp.exp(masked - jnp.max(masked, axis=1, keepdims=True))
+            normalized = weights * (1.0 / jnp.sum(weights, axis=1, keepdims=True))
+            mixed = jnp.dot(normalized.astype(BF16), values, preferred_element_type=F32)
+            out_ref[:, head] = (resid_ref[:, head].astype(F32) + mixed).astype(BF16)
+
+
+def attended_residual(student_query, teacher_keys, teacher_values, band_span, residual_in):
     rows = student_query.shape[0]
-    kv_local = teacher_keys.shape[1] // HEAD_DIM
-    group_size = HEADS // KV_HEADS
-    ctx_index = lax.axis_index("ctx")
     paired = jnp.stack([teacher_keys, teacher_values])
     back = min(-(-WINDOW // rows), lax.axis_size("ctx") - 1)
     blocks = [paired] + [passed_along(paired, "ctx", d) for d in range(1, back + 1)]
-    round_ids = jnp.arange(back + 1, dtype=jnp.int32)
-    key_pos = (
-        (ctx_index - round_ids)[:, None] * rows + jnp.arange(rows, dtype=jnp.int32)[None, :]
-    ).reshape(-1)
-    query_pos = ctx_index * rows + jnp.arange(rows, dtype=jnp.int32)
-    distance = query_pos[:, None] - key_pos[None, :]
-    allowed = (distance >= 0) & (distance < band_span[:, None]) & (key_pos[None, :] >= 0)
-    all_blocks = jnp.concatenate(blocks, axis=1)
-    outputs = []
-    for kv_head in range(kv_local):
-        cols = slice(kv_head * HEAD_DIM, (kv_head + 1) * HEAD_DIM)
-        first = kv_head * group_size * HEAD_DIM
-        query_part = student_query[:, first : first + group_size * HEAD_DIM]
-        outputs.append(
-            attend_heads(
-                query_part.reshape(rows, group_size, HEAD_DIM),
-                all_blocks[0][:, cols],
-                all_blocks[1][:, cols],
-                allowed,
-            ).reshape(rows, group_size * HEAD_DIM)
-        )
-    return jnp.concatenate(outputs, axis=1)
+    whole = pl.BlockSpec(memory_space=pltpu.VMEM)
+    return pl.pallas_call(
+        attention_kernel,
+        out_shape=jax.ShapeDtypeStruct(residual_in.shape, BF16),
+        in_specs=[pl.BlockSpec(memory_space=pltpu.SMEM)] + [whole] * (3 + len(blocks)),
+        out_specs=whole,
+        name="attention",
+    )(lax.axis_index("ctx")[None], student_query, band_span[:, None], residual_in, *blocks)
 
 
 def row_major(block):
@@ -143,23 +149,29 @@
     both = swapped(jnp.stack([tile, across]), "pair")
     gain = lax.dynamic_slice_in_dim(norm_gain, z * d_ctx, d_ctx, 0)
     resid = jnp.stack([tile, both[0], across, both[1]]).astype(F32)
-    scaled = (resid * gain).astype(BF16).reshape(4 * rows, d_ctx)
-
-    def projected(w):
-        return jnp.dot(scaled, w, preferred_element_type=F32).astype(BF16).reshape(4, rows, ff)
-
-    parts = [projected(w_gate)]
+    scaled = (resid * gain).astype(BF16)
+    scaled = scaled.reshape(4, rows, d_ctx)
+
+    def projected(blocks, w):
+        return jnp.dot(blocks, w, preferred_element_type=F32).astype(BF16)
+
+    farthest = picked(scaled, jnp.where(low, 3, 0) ^ hp)
     came = [None, None]
     for s in range(3):
-        for i in range(2):
-            if s == 0 and i == 1:
-                scaled, _ = lax.optimization_barrier((scaled, right))
-                parts.append(projected(w_up))
-            if s > 0:
+        for i, w in enumerate((w_gate, w_up)):
+            if s == 0:
+                if i == 1:
+                    farthest, scaled, _ = lax.optimization_barrier((farthest, scaled, right))
+                right = left = projected(farthest, w)
+            else:
+                if (s, i) == (1, 0):
+                    scaled, _ = lax.optimization_barrier((scaled, right))
+                    blocks = scaled.reshape(4 * rows, d_ctx)
+                    parts = [projected(blocks, v).reshape(4, rows, ff) for v in (w_gate, w_up)]
+                    came[0], parts[1] = lax.optimization_barrier((came[0], parts[1]))
                 came[i], _ = lax.optimization_barrier((came[i], right))
-            right = picked(parts[i], jnp.clip(3 - s + z, 0, 3) ^ hp)
-            left = picked(parts[i], jnp.clip(s - 3 + z, 0, 3) ^ hp)
-            if s > 0:
+                right = picked(parts[i], jnp.clip(3 - s + z, 0, 3) ^ hp)
+                left = picked(parts[i], jnp.clip(s - 3 + z, 0, 3) ^ hp)
                 right = (right.astype(F32) + came[i][0].astype(F32)).astype(BF16)
                 left = (left.astype(F32) + came[i][1].astype(F32)).astype(BF16)
             right, left = lax.optimization_barrier((right, left))
@@ -280,8 +292,7 @@
     teacher_feats,
     keep_tiles,
 ):
-    attended = attention(student_query, teacher_keys, teacher_values, band_span)
-    residual = (residual_in.astype(F32) + attended).astype(BF16)
+    residual = attended_residual(student_query, teacher_keys, teacher_values, band_span, residual_in)
     sizes = tuple(lax.axis_size(a) for a in ("ctx", "head", "pair"))
     weights = (w_gate, w_up, w_down)
     if sizes == (4, 2, 2):

time: 270 us -> 279 us (1.033)
  Pallas kernels: 0 us -> 4.88 us
  starting transfers between devices: 112 us -> 116 us
  waiting for transfers between devices: 115 us -> 118 us
    ppermute x10, starting transfers between devices: 0.73 us -> 6.39 us  [swapped(): return lax.ppermute(block, axis, [(0, 1), (1, 0)])]
    pallas_call x0 -> x1, Pallas kernels: none -> 4.88 us  [attended_residual(): pl.pallas_call(attention_kernel, out_shape=jax.ShapeDtypeStruct(residual_...]
    ppermute x27, starting transfers between devices: 77.6 us -> 72.9 us  [passed_along(): return lax.ppermute(block, axis, route)]
    ppermute x27, waiting for transfers between devices: 81.3 us -> 85.9 us  [passed_along(): return lax.ppermute(block, axis, route)]
  transfers between devices with their start and end apart: 53 -> 53, of which waited for: 26 -> 21; matrix products, arithmetic and copies ran while one was open for 9% -> 10% of each run, Pallas kernels for 0% -> 0%
where the time goes in v8:
time: 279 us; the launch traced here: 277 us
  waiting for transfers between devices  118 us (42%)
  starting transfers between devices  116 us (42%)
  matrix products  18.5 us (7%)
  other arithmetic  10.4 us (4%)
  Pallas kernels  4.88 us (2%)
  between operations  4.83 us (2%)
  local copies, waits for them, and re-layouts  4.72 us (2%)
    ppermute x27, waiting for transfers between devices, passed_along(): return lax.ppermute(block, axis, route)  85.9 us
    ppermute x27, starting transfers between devices, passed_along(): return lax.ppermute(block, axis, route)  72.9 us
    ppermute x8, starting transfers between devices, brought_home(): lax.ppermute(whole, ('ctx',) + HP, [(4 * c + h, 4 * TURNS[c][k] + c) for...  13.2 us
    ppermute x10, waiting for transfers between devices, swapped(): return lax.ppermute(block, axis, [(0, 1), (1, 0)])  11.8 us
    ppermute x4, starting transfers between devices, reduced(): lax.ppermute(half.astype(BF16), HP, route).astype(F32)  11.2 us
    ppermute x8, waiting for transfers between devices, brought_home(): lax.ppermute(whole, ('ctx',) + HP, [(4 * c + h, 4 * TURNS[c][k] + c) for...  10.2 us
    ppermute x1, starting transfers between devices, transposed(): return lax.ppermute(block, ('ctx',) + HP, route)  8.02 us
    ppermute x10, starting transfers between devices, swapped(): return lax.ppermute(block, axis, [(0, 1), (1, 0)])  6.39 us
  transfers between devices with their start and end apart: 53, of which 21 were waited for; matrix products, arithmetic and copies ran while one was open for 10% of the time, Pallas kernels for 0%

profile of v8, /device:TPU:2, one launch (start us, length us, event | category | flops | bytes accessed | tf_op | source)
XLA Modules:
  0.0 277.1 jit_solution(5543368409214462446)
XLA Ops:
  1.6 5.5 %collective-permute-start.2 = (bf16[2,128,256]{2,1,0:T(8,128)(2,1)S(1)}, bf16[2,128,256]{2,1,0:T(8,128)(2,1)S(1)}, u32[]{:S(2)}, u32[]{:S(2)}) collective-permute-start(bf16[2,128,256]{2,1,0:T(8,128)(2,1)S(1)} %pad_maximum_fusion.2.refs_0_), channel_id=1, source_target_pairs={{0,12},{1,13},{2,14},{3,15},{16,28},{17,29},{18,30},{19,31}} | collective-permute-start | bytes 393224 | tf_op jit(solution)/shard_map/ppermute | solution.py:26
  7.1 1.3 collective-permute-start.1
  8.4 2.5 collective-permute-start
  10.9 1.4 copy.16.span_ref
  12.3 1.5 collective-permute-done.1.refs_2_
  13.8 1.7 collective-permute-done.refs_1_
  16.1 4.9 %attention.1 = bf16[128,1024]{1,0:T(8,128)(2,1)} custom-call(s32[1]{0:T(128)} %bitcast.ctx_ref, bf16[128,1024]{1,0:T(8,128)(2,1)} %query_ref.1, s32[128,1]{1,0:T(8,128)} %copy.16.span_ref, bf16[128,1024]{1,0:T(8,128)(2,1)} %resid_ref.1, bf16[2,128,256]{2,1,0:T(8,128)(2,1)} %copy-done.4, bf16[2,128,256]{2,1,0:T(8,128)(2,1)} %copy-done.8, ...), custom_call_target="tpu_custom_call" | custom-call | tf_op jit(solution)/shard_map/attention/pallas_call | solution.py:77
  21.0 8.0 %collective-permute-start.3 = (bf16[128,1024]{1,0:T(8,128)(2,1)}, bf16[128,1024]{1,0:T(8,128)(2,1)S(1)}, u32[]{:S(2)}, u32[]{:S(2)}) collective-permute-start(bf16[128,1024]{1,0:T(8,128)(2,1)} %attention.1), channel_id=1, source_target_pairs={{0,0},{1,4},{2,8},{3,12},{4,1},{5,5},{6,9},{7,13},{8,2},{9,6},{10,... | collective-permute-start | bytes 786440 | tf_op jit(solution)/shard_map/ppermute | solution.py:36
  31.4 3.6 %collective-permute-done.5 = f32[128]{0:T(128)S(1)} collective-permute-done((f32[128]{0:T(128)S(1)}, f32[128]{0:T(128)S(1)}, u32[]{:S(2)}, u32[]{:S(2)}) %collective-permute-start.5) | collective-permute-done | bytes 544 | tf_op jit(solution)/shard_map/ppermute | solution.py:30
  34.9 5.4 %collective-permute-done.3 = bf16[128,1024]{1,0:T(8,128)(2,1)S(1)} collective-permute-done((bf16[128,1024]{1,0:T(8,128)(2,1)}, bf16[128,1024]{1,0:T(8,128)(2,1)S(1)}, u32[]{:S(2)}, u32[]{:S(2)}) %collective-permute-start.3) | collective-permute-done | bytes 262176 | tf_op jit(solution)/shard_map/ppermute | solution.py:36
  40.3 6.4 %collective-permute-done.6 = bf16[128,1024]{1,0:T(8,128)(2,1)S(1)} collective-permute-done((bf16[128,1024]{1,0:T(8,128)(2,1)S(1)}, bf16[128,1024]{1,0:T(8,128)(2,1)S(1)}, u32[]{:S(2)}, u32[]{:S(2)}) %collective-permute-start.6) | collective-permute-done | bytes 262176 | tf_op jit(solution)/shard_map/ppermute | solution.py:30
  49.6 1.6 copy-done.1
  51.9 2.5 collective-permute-start.8
  55.1 2.7 collective-permute-start.12
  60.4 2.1 convolution_convert_fusion
  62.5 2.1 convolution_convert_fusion.1
  64.6 16.9 %collective-permute-done.9 = bf16[128,1792]{1,0:T(8,128)(2,1)S(1)} collective-permute-done((bf16[128,1792]{1,0:T(8,128)(2,1)S(1)}, bf16[128,1792]{1,0:T(8,128)(2,1)S(1)}, u32[]{:S(2)}, u32[]{:S(2)}) %collective-permute-start.9) | collective-permute-done | bytes 458784 | tf_op jit(solution)/shard_map/ppermute | solution.py:26
  81.7 2.2 collective-permute-start.10
  86.7 5.2 %collective-permute-start.16 = (bf16[128,1792]{1,0:T(8,128)(2,1)S(1)}, bf16[128,1792]{1,0:T(8,128)(2,1)S(1)}, u32[]{:S(2)}, u32[]{:S(2)}) collective-permute-start(bf16[128,1792]{1,0:T(8,128)(2,1)S(1)} %get-tuple-element.62), channel_id=1, source_target_pairs={{0,4},{4,8},{8,12},{1,5},{5,9},{9,13},{2,6},{6,10},{10,14},{3,7},{... | collective-permute-start | bytes 1376264 | tf_op jit(solution)/shard_map/ppermute | solution.py:26
  92.0 7.2 %collective-permute-done.11 = bf16[128,1792]{1,0:T(8,128)(2,1)S(1)} collective-permute-done((bf16[128,1792]{1,0:T(8,128)(2,1)S(1)}, bf16[128,1792]{1,0:T(8,128)(2,1)S(1)}, u32[]{:S(2)}, u32[]{:S(2)}) %collective-permute-start.11) | collective-permute-done | bytes 458784 | tf_op jit(solution)/shard_map/ppermute | solution.py:26
  99.4 2.2 collective-permute-start.14
  101.6 5.0 %collective-permute-done.17 = bf16[128,1792]{1,0:T(8,128)(2,1)S(1)} collective-permute-done((bf16[128,1792]{1,0:T(8,128)(2,1)S(1)}, bf16[128,1792]{1,0:T(8,128)(2,1)S(1)}, u32[]{:S(2)}, u32[]{:S(2)}) %collective-permute-start.17) | collective-permute-done | bytes 458784 | tf_op jit(solution)/shard_map/ppermute | solution.py:26
  108.2 4.7 %collective-permute-start.18 = (bf16[128,1792]{1,0:T(8,128)(2,1)S(1)}, bf16[128,1792]{1,0:T(8,128)(2,1)S(1)}, u32[]{:S(2)}, u32[]{:S(2)}) collective-permute-start(bf16[128,1792]{1,0:T(8,128)(2,1)S(1)} %get-tuple-element.71), channel_id=1, source_target_pairs={{0,4},{4,8},{8,12},{1,5},{5,9},{9,13},{2,6},{6,10},{10,14},{3,7},{... | collective-permute-start | bytes 1376264 | tf_op jit(solution)/shard_map/ppermute | solution.py:26
  114.3 7.7 %collective-permute-done.15 = bf16[128,1792]{1,0:T(8,128)(2,1)S(1)} collective-permute-done((bf16[128,1792]{1,0:T(8,128)(2,1)S(1)}, bf16[128,1792]{1,0:T(8,128)(2,1)S(1)}, u32[]{:S(2)}, u32[]{:S(2)}) %collective-permute-start.15) | collective-permute-done | bytes 458784 | tf_op jit(solution)/shard_map/ppermute | solution.py:26
  122.3 6.4 %collective-permute-done.19 = bf16[128,1792]{1,0:T(8,128)(2,1)S(1)} collective-permute-done((bf16[128,1792]{1,0:T(8,128)(2,1)S(1)}, bf16[128,1792]{1,0:T(8,128)(2,1)S(1)}, u32[]{:S(2)}, u32[]{:S(2)}) %collective-permute-start.19) | collective-permute-done | bytes 458784 | tf_op jit(solution)/shard_map/ppermute | solution.py:26
  130.2 4.8 %collective-permute-start.24 = (bf16[128,1792]{1,0:T(8,128)(2,1)S(1)}, bf16[128,1792]{1,0:T(8,128)(2,1)S(1)}, u32[]{:S(2)}, u32[]{:S(2)}) collective-permute-start(bf16[128,1792]{1,0:T(8,128)(2,1)S(1)} %get-tuple-element.73), channel_id=1, source_target_pairs={{0,4},{4,8},{8,12},{1,5},{5,9},{9,13},{2,6},{6,10},{10,14},{3,7},{... | collective-permute-start | bytes 1376264 | tf_op jit(solution)/shard_map/ppermute | solution.py:26
  138.8 4.6 %collective-permute-start.26 = (bf16[128,3584]{1,0:T(8,128)(2,1)S(1)}, bf16[128,3584]{1,0:T(8,128)(2,1)S(1)}, u32[]{:S(2)}, u32[]{:S(2)}) collective-permute-start(bf16[128,3584]{1,0:T(8,128)(2,1)S(1)} %pad_maximum_fusion), channel_id=1, source_target_pairs={{0,4},{4,8},{8,12},{1,5},{5,9},{9,13},{2,6},{6,10},{10,14},{3,7},{... | collective-permute-start | bytes 2752520 | tf_op jit(solution)/shard_map/ppermute | solution.py:26
  146.0 2.1 collective-permute-start.45
  148.1 1.3 select_convert_fusion.3
  150.4 9.4 %collective-permute-done.25 = bf16[128,3584]{1,0:T(8,128)(2,1)S(1)} collective-permute-done((bf16[128,3584]{1,0:T(8,128)(2,1)S(1)}, bf16[128,3584]{1,0:T(8,128)(2,1)S(1)}, u32[]{:S(2)}, u32[]{:S(2)}) %collective-permute-start.25) | collective-permute-done | bytes 917536 | tf_op jit(solution)/shard_map/ppermute | solution.py:26
  162.4 1.3 select_convert_fusion.2
  165.1 5.1 %collective-permute-start.33 = (bf16[128,3584]{1,0:T(8,128)(2,1)S(1)}, bf16[128,3584]{1,0:T(8,128)(2,1)S(1)}, u32[]{:S(2)}, u32[]{:S(2)}) collective-permute-start(bf16[128,3584]{1,0:T(8,128)(2,1)S(1)} %collective-permute-done.26), channel_id=1, source_target_pairs={{0,4},{4,8},{8,12},{1,5},{5,9},{9,13},{2,6},{6,10},{10,14},{3,7},{... | collective-permute-start | bytes 2752520 | tf_op jit(solution)/shard_map/ppermute | solution.py:26
  170.3 4.0 %collective-permute-start.21 = (bf16[128,1024]{1,0:T(8,128)(2,1)S(1)}, bf16[128,1024]{1,0:T(8,128)(2,1)S(1)}, u32[]{:S(2)}, u32[]{:S(2)}) collective-permute-start(bf16[128,1024]{1,0:T(8,128)(2,1)S(1)} %fusion.33), channel_id=1, source_target_pairs={{2,0},{1,3},{6,4},{5,7},{10,8},{9,11},{14,12},{13,15},{18,16},{17,... | collective-permute-start | bytes 786440 | tf_op jit(solution)/shard_map/ppermute | solution.py:199
  175.6 4.6 %collective-permute-start.32 = (bf16[128,1792]{1,0:T(8,128)(2,1)S(1)}, bf16[128,1792]{1,0:T(8,128)(2,1)S(1)}, u32[]{:S(2)}, u32[]{:S(2)}) collective-permute-start(bf16[128,1792]{1,0:T(8,128)(2,1)S(1)} %collective-permute-done.24), channel_id=1, source_target_pairs={{0,4},{4,8},{8,12},{1,5},{5,9},{9,13},{2,6},{6,10},{10,14},{3,7},{... | collective-permute-start | bytes 1376264 | tf_op jit(solution)/shard_map/ppermute | solution.py:26
  181.8 17.2 %collective-permute-done.30 = bf16[128,1792]{1,0:T(8,128)(2,1)S(1)} collective-permute-done((bf16[128,1792]{1,0:T(8,128)(2,1)S(1)}, bf16[128,1792]{1,0:T(8,128)(2,1)S(1)}, u32[]{:S(2)}, u32[]{:S(2)}) %collective-permute-start.30) | collective-permute-done | bytes 458784 | tf_op jit(solution)/shard_map/ppermute | solution.py:26
  201.5 5.0 %collective-permute-start.39 = (bf16[128,1792]{1,0:T(8,128)(2,1)S(1)}, bf16[128,1792]{1,0:T(8,128)(2,1)S(1)}, u32[]{:S(2)}, u32[]{:S(2)}) collective-permute-start(bf16[128,1792]{1,0:T(8,128)(2,1)S(1)} %collective-permute-done.32), channel_id=1, source_target_pairs={{0,4},{4,8},{8,12},{1,5},{5,9},{9,13},{2,6},{6,10},{10,14},{3,7},{... | collective-permute-start | bytes 1376264 | tf_op jit(solution)/shard_map/ppermute | solution.py:26
  208.1 4.6 %collective-permute-start.40 = (bf16[128,3584]{1,0:T(8,128)(2,1)S(1)}, bf16[128,3584]{1,0:T(8,128)(2,1)S(1)}, u32[]{:S(2)}, u32[]{:S(2)}) collective-permute-start(bf16[128,3584]{1,0:T(8,128)(2,1)S(1)} %collective-permute-done.33), channel_id=1, source_target_pairs={{0,4},{4,8},{8,12},{1,5},{5,9},{9,13},{2,6},{6,10},{10,14},{3,7},{... | collective-permute-start | bytes 2752520 | tf_op jit(solution)/shard_map/ppermute | solution.py:26
  214.7 1.3 select_convert_fusion.1
  216.7 6.6 %collective-permute-start.50 = (bf16[128,1024]{1,0:T(8,128)(2,1)S(1)}, bf16[128,1024]{1,0:T(8,128)(2,1)S(1)}, u32[]{:S(2)}, u32[]{:S(2)}) collective-permute-start(bf16[128,1024]{1,0:T(8,128)(2,1)S(1)} %add_convert_fusion.2), channel_id=1, source_target_pairs={{2,4},{6,9},{10,6},{14,11},{18,20},{22,25},{26,22},{30,27}} | collective-permute-start | bytes 786440 | tf_op jit(solution)/shard_map/ppermute | solution.py:203
  223.3 10.7 %collective-permute-done.38 = bf16[128,3584]{1,0:T(8,128)(2,1)S(1)} collective-permute-done((bf16[128,3584]{1,0:T(8,128)(2,1)S(1)}, bf16[128,3584]{1,0:T(8,128)(2,1)S(1)}, u32[]{:S(2)}, u32[]{:S(2)}) %collective-permute-start.38) | collective-permute-done | bytes 917536 | tf_op jit(solution)/shard_map/ppermute | solution.py:26
  234.0 1.4 collective-permute-start.34
  237.9 1.3 select_convert_fusion
  239.3 2.7 collective-permute-start.41
  243.5 4.6 %collective-permute-start.42 = (bf16[128,1024]{1,0:T(8,128)(2,1)S(1)}, bf16[128,1024]{1,0:T(8,128)(2,1)S(1)}, u32[]{:S(2)}, u32[]{:S(2)}) collective-permute-start(bf16[128,1024]{1,0:T(8,128)(2,1)S(1)} %fusion.36), channel_id=1, source_target_pairs={{1,3},{2,0},{5,7},{6,4},{9,11},{10,8},{13,15},{14,12},{17,19},{18,... | collective-permute-start | bytes 786440 | tf_op jit(solution)/shard_map/ppermute | solution.py:199
  248.1 4.4 %collective-permute-done.35 = bf16[128,1024]{1,0:T(8,128)(2,1)S(1)} collective-permute-done((bf16[128,1024]{1,0:T(8,128)(2,1)S(1)}, bf16[128,1024]{1,0:T(8,128)(2,1)S(1)}, u32[]{:S(2)}, u32[]{:S(2)}) %collective-permute-start.35) | collective-permute-done | bytes 262176 | tf_op jit(solution)/shard_map/ppermute | solution.py:199
  253.2 2.9 %collective-permute-start.47 = (f32[128]{0:T(128)S(1)}, f32[128]{0:T(128)S(1)}, u32[]{:S(2)}, u32[]{:S(2)}) collective-permute-start(f32[128]{0:T(128)S(1)} %get-tuple-element.86), channel_id=1, source_target_pairs={{0,8},{4,12},{8,0},{12,4},{1,9},{5,13},{9,1},{13,5},{2,10},{6,14},... | collective-permute-start | bytes 1544 | tf_op jit(solution)/shard_map/ppermute | solution.py:232
  259.2 1.9 collective-permute-start.36
  264.5 10.2 %collective-permute-done.51 = bf16[128,1024]{1,0:T(8,128)(2,1)S(1)} collective-permute-done((bf16[128,1024]{1,0:T(8,128)(2,1)S(1)}, bf16[128,1024]{1,0:T(8,128)(2,1)S(1)}, u32[]{:S(2)}, u32[]{:S(2)}) %collective-permute-start.51) | collective-permute-done | bytes 262176 | tf_op jit(solution)/shard_map/ppermute | solution.py:203
  (142 shorter events, 49.8 us)
Async XLA Ops:
  1.6 10.7 %collective-permute-start.2 = (bf16[2,128,256]{2,1,0:T(8,128)(2,1)S(1)}, bf16[2,128,256]{2,1,0:T(8,128)(2,1)S(1)}, u32[]{:S(2)}, u32[]{:S(2)}) collective-permute-start(bf16[2,128,256]{2,1,0:T(8,128)(2,1)S(1)} %pad_maximum_fusion.2.refs_0_), channel_id=1, source_target_pairs={{0,12},{1,13},{2,14},{3,15},{16,28},{17,29},{18,30},{19,31}} | collective-permute-start | bytes 393224 | tf_op jit(solution)/shard_map/ppermute | solution.py:26
  7.1 6.7 %collective-permute-start.1 = (bf16[2,128,256]{2,1,0:T(8,128)(2,1)S(1)}, bf16[2,128,256]{2,1,0:T(8,128)(2,1)S(1)}, u32[]{:S(2)}, u32[]{:S(2)}) collective-permute-start(bf16[2,128,256]{2,1,0:T(8,128)(2,1)S(1)} %pad_maximum_fusion.2.refs_0_), channel_id=1, source_target_pairs={{0,8},{4,12},{1,9},{5,13},{2,10},{6,14},{3,11},{7,15},{16,24},{20,... | collective-permute-start | bytes 393224 | tf_op jit(solution)/shard_map/ppermute | solution.py:26
  8.4 7.1 %collective-permute-start = (bf16[2,128,256]{2,1,0:T(8,128)(2,1)S(1)}, bf16[2,128,256]{2,1,0:T(8,128)(2,1)S(1)}, u32[]{:S(2)}, u32[]{:S(2)}) collective-permute-start(bf16[2,128,256]{2,1,0:T(8,128)(2,1)S(1)} %pad_maximum_fusion.2.refs_0_), channel_id=1, source_target_pairs={{0,4},{4,8},{8,12},{1,5},{5,9},{9,13},{2,6},{6,10},{10,14},{3,7},{... | collective-permute-start | bytes 393224 | tf_op jit(solution)/shard_map/ppermute | solution.py:26
  21.0 19.3 %collective-permute-start.3 = (bf16[128,1024]{1,0:T(8,128)(2,1)}, bf16[128,1024]{1,0:T(8,128)(2,1)S(1)}, u32[]{:S(2)}, u32[]{:S(2)}) collective-permute-start(bf16[128,1024]{1,0:T(8,128)(2,1)} %attention.1), channel_id=1, source_target_pairs={{0,0},{1,4},{2,8},{3,12},{4,1},{5,5},{6,9},{7,13},{8,2},{9,6},{10,... | collective-permute-start | bytes 786440 | tf_op jit(solution)/shard_map/ppermute | solution.py:36
  40.3 6.4 %collective-permute-start.6 = (bf16[128,1024]{1,0:T(8,128)(2,1)S(1)}, bf16[128,1024]{1,0:T(8,128)(2,1)S(1)}, u32[]{:S(2)}, u32[]{:S(2)}) collective-permute-start(bf16[128,1024]{1,0:T(8,128)(2,1)S(1)} %collective-permute-done.3), channel_id=1, source_target_pairs={{0,2},{2,0},{1,3},{3,1},{4,6},{6,4},{5,7},{7,5},{8,10},{10,8},{9,1... | collective-permute-start | bytes 786440 | tf_op jit(solution)/shard_map/ppermute | solution.py:30
  51.9 29.5 %collective-permute-start.8 = (bf16[128,1792]{1,0:T(8,128)(2,1)S(1)}, bf16[128,1792]{1,0:T(8,128)(2,1)S(1)}, u32[]{:S(2)}, u32[]{:S(2)}) collective-permute-start(bf16[128,1792]{1,0:T(8,128)(2,1)S(1)} %convolution_convert_fusion.3), channel_id=1, source_target_pairs={{0,4},{4,8},{8,12},{1,5},{5,9},{9,13},{2,6},{6,10},{10,14},{3,7},{... | collective-permute-start | bytes 1376264 | tf_op jit(solution)/shard_map/ppermute | solution.py:26
  55.1 28.8 %collective-permute-start.12 = (bf16[128,1792]{1,0:T(8,128)(2,1)S(1)}, bf16[128,1792]{1,0:T(8,128)(2,1)S(1)}, u32[]{:S(2)}, u32[]{:S(2)}) collective-permute-start(bf16[128,1792]{1,0:T(8,128)(2,1)S(1)} %convolution_convert_fusion.2), channel_id=1, source_target_pairs={{0,4},{4,8},{8,12},{1,5},{5,9},{9,13},{2,6},{6,10},{10,14},{3,7},{... | collective-permute-start | bytes 1376264 | tf_op jit(solution)/shard_map/ppermute | solution.py:26
  57.8 26.1 %collective-permute-start.13 = (bf16[128,1792]{1,0:T(8,128)(2,1)S(1)}, bf16[128,1792]{1,0:T(8,128)(2,1)S(1)}, u32[]{:S(2)}, u32[]{:S(2)}) collective-permute-start(bf16[128,1792]{1,0:T(8,128)(2,1)S(1)} %convolution_convert_fusion.2), channel_id=1, source_target_pairs={{4,0},{8,4},{12,8},{5,1},{9,5},{13,9},{6,2},{10,6},{14,10},{7,3},{... | collective-permute-start | bytes 1376264 | tf_op jit(solution)/shard_map/ppermute | solution.py:26
  59.1 22.4 %collective-permute-start.9 = (bf16[128,1792]{1,0:T(8,128)(2,1)S(1)}, bf16[128,1792]{1,0:T(8,128)(2,1)S(1)}, u32[]{:S(2)}, u32[]{:S(2)}) collective-permute-start(bf16[128,1792]{1,0:T(8,128)(2,1)S(1)} %convolution_convert_fusion.3), channel_id=1, source_target_pairs={{4,0},{8,4},{12,8},{5,1},{9,5},{13,9},{6,2},{10,6},{14,10},{7,3},{... | collective-permute-start | bytes 1376264 | tf_op jit(solution)/shard_map/ppermute | solution.py:26
  81.7 17.5 %collective-permute-start.10 = (bf16[128,1792]{1,0:T(8,128)(2,1)S(1)}, bf16[128,1792]{1,0:T(8,128)(2,1)S(1)}, u32[]{:S(2)}, u32[]{:S(2)}) collective-permute-start(bf16[128,1792]{1,0:T(8,128)(2,1)S(1)} %get-tuple-element.56), channel_id=1, source_target_pairs={{0,4},{4,8},{8,12},{1,5},{5,9},{9,13},{2,6},{6,10},{10,14},{3,7},{... | collective-permute-start | bytes 1376264 | tf_op jit(solution)/shard_map/ppermute | solution.py:26
  83.9 15.3 %collective-permute-start.11 = (bf16[128,1792]{1,0:T(8,128)(2,1)S(1)}, bf16[128,1792]{1,0:T(8,128)(2,1)S(1)}, u32[]{:S(2)}, u32[]{:S(2)}) collective-permute-start(bf16[128,1792]{1,0:T(8,128)(2,1)S(1)} %get-tuple-element.57), channel_id=1, source_target_pairs={{4,0},{8,4},{12,8},{5,1},{9,5},{13,9},{6,2},{10,6},{14,10},{7,3},{... | collective-permute-start | bytes 1376264 | tf_op jit(solution)/shard_map/ppermute | solution.py:26
  85.4 21.2 %collective-permute-start.17 = (bf16[128,1792]{1,0:T(8,128)(2,1)S(1)}, bf16[128,1792]{1,0:T(8,128)(2,1)S(1)}, u32[]{:S(2)}, u32[]{:S(2)}) collective-permute-start(bf16[128,1792]{1,0:T(8,128)(2,1)S(1)} %get-tuple-element.68), channel_id=1, source_target_pairs={{4,0},{8,4},{12,8},{5,1},{9,5},{13,9},{6,2},{10,6},{14,10},{7,3},{... | collective-permute-start | bytes 1376264 | tf_op jit(solution)/shard_map/ppermute | solution.py:26
  86.7 19.9 %collective-permute-start.16 = (bf16[128,1792]{1,0:T(8,128)(2,1)S(1)}, bf16[128,1792]{1,0:T(8,128)(2,1)S(1)}, u32[]{:S(2)}, u32[]{:S(2)}) collective-permute-start(bf16[128,1792]{1,0:T(8,128)(2,1)S(1)} %get-tuple-element.62), channel_id=1, source_target_pairs={{0,4},{4,8},{8,12},{1,5},{5,9},{9,13},{2,6},{6,10},{10,14},{3,7},{... | collective-permute-start | bytes 1376264 | tf_op jit(solution)/shard_map/ppermute | solution.py:26
  99.4 22.5 %collective-permute-start.14 = (bf16[128,1792]{1,0:T(8,128)(2,1)S(1)}, bf16[128,1792]{1,0:T(8,128)(2,1)S(1)}, u32[]{:S(2)}, u32[]{:S(2)}) collective-permute-start(bf16[128,1792]{1,0:T(8,128)(2,1)S(1)} %get-tuple-element.65), channel_id=1, source_target_pairs={{0,4},{4,8},{8,12},{1,5},{5,9},{9,13},{2,6},{6,10},{10,14},{3,7},{... | collective-permute-start | bytes 1376264 | tf_op jit(solution)/shard_map/ppermute | solution.py:26
  106.7 15.3 %collective-permute-start.15 = (bf16[128,1792]{1,0:T(8,128)(2,1)S(1)}, bf16[128,1792]{1,0:T(8,128)(2,1)S(1)}, u32[]{:S(2)}, u32[]{:S(2)}) collective-permute-start(bf16[128,1792]{1,0:T(8,128)(2,1)S(1)} %get-tuple-element.66), channel_id=1, source_target_pairs={{4,0},{8,4},{12,8},{5,1},{9,5},{13,9},{6,2},{10,6},{14,10},{7,3},{... | collective-permute-start | bytes 1376264 | tf_op jit(solution)/shard_map/ppermute | solution.py:26
  108.2 14.0 %collective-permute-start.18 = (bf16[128,1792]{1,0:T(8,128)(2,1)S(1)}, bf16[128,1792]{1,0:T(8,128)(2,1)S(1)}, u32[]{:S(2)}, u32[]{:S(2)}) collective-permute-start(bf16[128,1792]{1,0:T(8,128)(2,1)S(1)} %get-tuple-element.71), channel_id=1, source_target_pairs={{0,4},{4,8},{8,12},{1,5},{5,9},{9,13},{2,6},{6,10},{10,14},{3,7},{... | collective-permute-start | bytes 1376264 | tf_op jit(solution)/shard_map/ppermute | solution.py:26
  113.0 15.6 %collective-permute-start.19 = (bf16[128,1792]{1,0:T(8,128)(2,1)S(1)}, bf16[128,1792]{1,0:T(8,128)(2,1)S(1)}, u32[]{:S(2)}, u32[]{:S(2)}) collective-permute-start(bf16[128,1792]{1,0:T(8,128)(2,1)S(1)} %get-tuple-element.72), channel_id=1, source_target_pairs={{4,0},{8,4},{12,8},{5,1},{9,5},{13,9},{6,2},{10,6},{14,10},{7,3},{... | collective-permute-start | bytes 1376264 | tf_op jit(solution)/shard_map/ppermute | solution.py:26
  128.9 20.8 %collective-permute-start.23 = (bf16[128,1792]{1,0:T(8,128)(2,1)S(1)}, bf16[128,1792]{1,0:T(8,128)(2,1)S(1)}, u32[]{:S(2)}, u32[]{:S(2)}) collective-permute-start(bf16[128,1792]{1,0:T(8,128)(2,1)S(1)} %get-tuple-element.73), channel_id=1, source_target_pairs={{4,0},{8,4},{12,8},{5,1},{9,5},{13,9},{6,2},{10,6},{14,10},{7,3},{... | collective-permute-start | bytes 1376264 | tf_op jit(solution)/shard_map/ppermute | solution.py:26
  130.2 19.5 %collective-permute-start.24 = (bf16[128,1792]{1,0:T(8,128)(2,1)S(1)}, bf16[128,1792]{1,0:T(8,128)(2,1)S(1)}, u32[]{:S(2)}, u32[]{:S(2)}) collective-permute-start(bf16[128,1792]{1,0:T(8,128)(2,1)S(1)} %get-tuple-element.73), channel_id=1, source_target_pairs={{0,4},{4,8},{8,12},{1,5},{5,9},{9,13},{2,6},{6,10},{10,14},{3,7},{... | collective-permute-start | bytes 1376264 | tf_op jit(solution)/shard_map/ppermute | solution.py:26
  137.5 22.4 %collective-permute-start.25 = (bf16[128,3584]{1,0:T(8,128)(2,1)S(1)}, bf16[128,3584]{1,0:T(8,128)(2,1)S(1)}, u32[]{:S(2)}, u32[]{:S(2)}) collective-permute-start(bf16[128,3584]{1,0:T(8,128)(2,1)S(1)} %pad_maximum_fusion), channel_id=1, source_target_pairs={{4,0},{8,4},{12,8},{5,1},{9,5},{13,9},{6,2},{10,6},{14,10},{7,3},{... | collective-permute-start | bytes 2752520 | tf_op jit(solution)/shard_map/ppermute | solution.py:26
  138.8 22.2 %collective-permute-start.26 = (bf16[128,3584]{1,0:T(8,128)(2,1)S(1)}, bf16[128,3584]{1,0:T(8,128)(2,1)S(1)}, u32[]{:S(2)}, u32[]{:S(2)}) collective-permute-start(bf16[128,3584]{1,0:T(8,128)(2,1)S(1)} %pad_maximum_fusion), channel_id=1, source_target_pairs={{0,4},{4,8},{8,12},{1,5},{5,9},{9,13},{2,6},{6,10},{10,14},{3,7},{... | collective-permute-start | bytes 2752520 | tf_op jit(solution)/shard_map/ppermute | solution.py:26
  149.6 20.5 %collective-permute-start.20 = (bf16[128,1024]{1,0:T(8,128)(2,1)S(1)}, bf16[128,1024]{1,0:T(8,128)(2,1)S(1)}, u32[]{:S(2)}, u32[]{:S(2)}) collective-permute-start(bf16[128,1024]{1,0:T(8,128)(2,1)S(1)} %get-tuple-element.121), channel_id=1, source_target_pairs={{0,1},{1,0},{2,3},{3,2},{4,5},{5,4},{6,7},{7,6},{8,9},{9,8},{10,11... | collective-permute-start | bytes 786440 | tf_op jit(solution)/shard_map/ppermute | solution.py:30
  163.7 11.9 %collective-permute-start.27 = (bf16[128,1024]{1,0:T(8,128)(2,1)S(1)}, bf16[128,1024]{1,0:T(8,128)(2,1)S(1)}, u32[]{:S(2)}, u32[]{:S(2)}) collective-permute-start(bf16[128,1024]{1,0:T(8,128)(2,1)S(1)} %get-tuple-element.119), channel_id=1, source_target_pairs={{0,1},{1,0},{2,3},{3,2},{4,5},{5,4},{6,7},{7,6},{8,9},{9,8},{10,11... | collective-permute-start | bytes 786440 | tf_op jit(solution)/shard_map/ppermute | solution.py:30
  163.8 42.9 %collective-permute-start.31 = (bf16[128,3584]{1,0:T(8,128)(2,1)S(1)}, bf16[128,3584]{1,0:T(8,128)(2,1)S(1)}, u32[]{:S(2)}, u32[]{:S(2)}) collective-permute-start(bf16[128,3584]{1,0:T(8,128)(2,1)S(1)} %collective-permute-done.25), channel_id=1, source_target_pairs={{4,0},{8,4},{12,8},{5,1},{9,5},{13,9},{6,2},{10,6},{14,10},{7,3},{... | collective-permute-start | bytes 2752520 | tf_op jit(solution)/shard_map/ppermute | solution.py:26
  165.1 41.6 %collective-permute-start.33 = (bf16[128,3584]{1,0:T(8,128)(2,1)S(1)}, bf16[128,3584]{1,0:T(8,128)(2,1)S(1)}, u32[]{:S(2)}, u32[]{:S(2)}) collective-permute-start(bf16[128,3584]{1,0:T(8,128)(2,1)S(1)} %collective-permute-done.26), channel_id=1, source_target_pairs={{0,4},{4,8},{8,12},{1,5},{5,9},{9,13},{2,6},{6,10},{10,14},{3,7},{... | collective-permute-start | bytes 2752520 | tf_op jit(solution)/shard_map/ppermute | solution.py:26
  170.3 10.0 %collective-permute-start.21 = (bf16[128,1024]{1,0:T(8,128)(2,1)S(1)}, bf16[128,1024]{1,0:T(8,128)(2,1)S(1)}, u32[]{:S(2)}, u32[]{:S(2)}) collective-permute-start(bf16[128,1024]{1,0:T(8,128)(2,1)S(1)} %fusion.33), channel_id=1, source_target_pairs={{2,0},{1,3},{6,4},{5,7},{10,8},{9,11},{14,12},{13,15},{18,16},{17,... | collective-permute-start | bytes 786440 | tf_op jit(solution)/shard_map/ppermute | solution.py:199
  174.3 24.7 %collective-permute-start.30 = (bf16[128,1792]{1,0:T(8,128)(2,1)S(1)}, bf16[128,1792]{1,0:T(8,128)(2,1)S(1)}, u32[]{:S(2)}, u32[]{:S(2)}) collective-permute-start(bf16[128,1792]{1,0:T(8,128)(2,1)S(1)} %collective-permute-done.23), channel_id=1, source_target_pairs={{4,0},{8,4},{12,8},{5,1},{9,5},{13,9},{6,2},{10,6},{14,10},{7,3},{... | collective-permute-start | bytes 1376264 | tf_op jit(solution)/shard_map/ppermute | solution.py:26
  175.6 24.6 %collective-permute-start.32 = (bf16[128,1792]{1,0:T(8,128)(2,1)S(1)}, bf16[128,1792]{1,0:T(8,128)(2,1)S(1)}, u32[]{:S(2)}, u32[]{:S(2)}) collective-permute-start(bf16[128,1792]{1,0:T(8,128)(2,1)S(1)} %collective-permute-done.24), channel_id=1, source_target_pairs={{0,4},{4,8},{8,12},{1,5},{5,9},{9,13},{2,6},{6,10},{10,14},{3,7},{... | collective-permute-start | bytes 1376264 | tf_op jit(solution)/shard_map/ppermute | solution.py:26
  180.3 21.2 %collective-permute-start.28 = (bf16[128,1024]{1,0:T(8,128)(2,1)S(1)}, bf16[128,1024]{1,0:T(8,128)(2,1)S(1)}, u32[]{:S(2)}, u32[]{:S(2)}) collective-permute-start(bf16[128,1024]{1,0:T(8,128)(2,1)S(1)} %fusion.34), channel_id=1, source_target_pairs={{3,1},{0,2},{7,5},{4,6},{11,9},{8,10},{15,13},{12,14},{19,17},{16,... | collective-permute-start | bytes 786440 | tf_op jit(solution)/shard_map/ppermute | solution.py:199
  199.0 54.2 %collective-permute-start.49 = (bf16[128,1024]{1,0:T(8,128)(2,1)S(1)}, bf16[128,1024]{1,0:T(8,128)(2,1)S(1)}, u32[]{:S(2)}, u32[]{:S(2)}) collective-permute-start(bf16[128,1024]{1,0:T(8,128)(2,1)S(1)} %add_convert_fusion.3), channel_id=1, source_target_pairs={{3,0},{7,5},{11,10},{15,15},{19,16},{23,21},{27,26},{31,31}} | collective-permute-start | bytes 786440 | tf_op jit(solution)/shard_map/ppermute | solution.py:203
  200.2 15.9 %collective-permute-start.37 = (bf16[128,1792]{1,0:T(8,128)(2,1)S(1)}, bf16[128,1792]{1,0:T(8,128)(2,1)S(1)}, u32[]{:S(2)}, u32[]{:S(2)}) collective-permute-start(bf16[128,1792]{1,0:T(8,128)(2,1)S(1)} %collective-permute-done.30), channel_id=1, source_target_pairs={{4,0},{8,4},{12,8},{5,1},{9,5},{13,9},{6,2},{10,6},{14,10},{7,3},{... | collective-permute-start | bytes 1376264 | tf_op jit(solution)/shard_map/ppermute | solution.py:26
  201.5 15.2 %collective-permute-start.39 = (bf16[128,1792]{1,0:T(8,128)(2,1)S(1)}, bf16[128,1792]{1,0:T(8,128)(2,1)S(1)}, u32[]{:S(2)}, u32[]{:S(2)}) collective-permute-start(bf16[128,1792]{1,0:T(8,128)(2,1)S(1)} %collective-permute-done.32), channel_id=1, source_target_pairs={{0,4},{4,8},{8,12},{1,5},{5,9},{9,13},{2,6},{6,10},{10,14},{3,7},{... | collective-permute-start | bytes 1376264 | tf_op jit(solution)/shard_map/ppermute | solution.py:26
  206.8 27.2 %collective-permute-start.38 = (bf16[128,3584]{1,0:T(8,128)(2,1)S(1)}, bf16[128,3584]{1,0:T(8,128)(2,1)S(1)}, u32[]{:S(2)}, u32[]{:S(2)}) collective-permute-start(bf16[128,3584]{1,0:T(8,128)(2,1)S(1)} %collective-permute-done.31), channel_id=1, source_target_pairs={{4,0},{8,4},{12,8},{5,1},{9,5},{13,9},{6,2},{10,6},{14,10},{7,3},{... | collective-permute-start | bytes 2752520 | tf_op jit(solution)/shard_map/ppermute | solution.py:26
  208.1 27.6 %collective-permute-start.40 = (bf16[128,3584]{1,0:T(8,128)(2,1)S(1)}, bf16[128,3584]{1,0:T(8,128)(2,1)S(1)}, u32[]{:S(2)}, u32[]{:S(2)}) collective-permute-start(bf16[128,3584]{1,0:T(8,128)(2,1)S(1)} %collective-permute-done.33), channel_id=1, source_target_pairs={{0,4},{4,8},{8,12},{1,5},{5,9},{9,13},{2,6},{6,10},{10,14},{3,7},{... | collective-permute-start | bytes 2752520 | tf_op jit(solution)/shard_map/ppermute | solution.py:26
  216.0 41.2 %collective-permute-start.22 = (bf16[128,1024]{1,0:T(8,128)(2,1)S(1)}, bf16[128,1024]{1,0:T(8,128)(2,1)S(1)}, u32[]{:S(2)}, u32[]{:S(2)}) collective-permute-start(bf16[128,1024]{1,0:T(8,128)(2,1)S(1)} %add_convert_fusion.3), channel_id=1, source_target_pairs={{0,0},{4,5},{8,10},{12,15},{16,16},{20,21},{24,26},{28,31}} | collective-permute-start | bytes 786440 | tf_op jit(solution)/shard_map/ppermute | solution.py:203
  216.7 41.2 %collective-permute-start.50 = (bf16[128,1024]{1,0:T(8,128)(2,1)S(1)}, bf16[128,1024]{1,0:T(8,128)(2,1)S(1)}, u32[]{:S(2)}, u32[]{:S(2)}) collective-permute-start(bf16[128,1024]{1,0:T(8,128)(2,1)S(1)} %add_convert_fusion.2), channel_id=1, source_target_pairs={{2,4},{6,9},{10,6},{14,11},{18,20},{22,25},{26,22},{30,27}} | collective-permute-start | bytes 786440 | tf_op jit(solution)/shard_map/ppermute | solution.py:203
  234.0 8.0 %collective-permute-start.34 = (bf16[128,1024]{1,0:T(8,128)(2,1)S(1)}, bf16[128,1024]{1,0:T(8,128)(2,1)S(1)}, u32[]{:S(2)}, u32[]{:S(2)}) collective-permute-start(bf16[128,1024]{1,0:T(8,128)(2,1)S(1)} %get-tuple-element.117), channel_id=1, source_target_pairs={{0,1},{1,0},{2,3},{3,2},{4,5},{5,4},{6,7},{7,6},{8,9},{9,8},{10,11... | collective-permute-start | bytes 786440 | tf_op jit(solution)/shard_map/ppermute | solution.py:30
  239.3 4.1 %collective-permute-start.41 = (bf16[128,1024]{1,0:T(8,128)(2,1)S(1)}, bf16[128,1024]{1,0:T(8,128)(2,1)S(1)}, u32[]{:S(2)}, u32[]{:S(2)}) collective-permute-start(bf16[128,1024]{1,0:T(8,128)(2,1)S(1)} %get-tuple-element.115), channel_id=1, source_target_pairs={{0,1},{1,0},{2,3},{3,2},{4,5},{5,4},{6,7},{7,6},{8,9},{9,8},{10,11... | collective-permute-start | bytes 786440 | tf_op jit(solution)/shard_map/ppermute | solution.py:30
  242.1 10.4 %collective-permute-start.35 = (bf16[128,1024]{1,0:T(8,128)(2,1)S(1)}, bf16[128,1024]{1,0:T(8,128)(2,1)S(1)}, u32[]{:S(2)}, u32[]{:S(2)}) collective-permute-start(bf16[128,1024]{1,0:T(8,128)(2,1)S(1)} %fusion.35), channel_id=1, source_target_pairs={{0,2},{3,1},{4,6},{7,5},{8,10},{11,9},{12,14},{15,13},{16,18},{19,... | collective-permute-start | bytes 786440 | tf_op jit(solution)/shard_map/ppermute | solution.py:199
  243.5 12.5 %collective-permute-start.42 = (bf16[128,1024]{1,0:T(8,128)(2,1)S(1)}, bf16[128,1024]{1,0:T(8,128)(2,1)S(1)}, u32[]{:S(2)}, u32[]{:S(2)}) collective-permute-start(bf16[128,1024]{1,0:T(8,128)(2,1)S(1)} %fusion.36), channel_id=1, source_target_pairs={{1,3},{2,0},{5,7},{6,4},{9,11},{10,8},{13,15},{14,12},{17,19},{18,... | collective-permute-start | bytes 786440 | tf_op jit(solution)/shard_map/ppermute | solution.py:199
  252.6 6.6 %collective-permute-start.48 = (f32[128]{0:T(128)S(1)}, f32[128]{0:T(128)S(1)}, u32[]{:S(2)}, u32[]{:S(2)}) collective-permute-start(f32[128]{0:T(128)S(1)} %get-tuple-element.86), channel_id=1, source_target_pairs={{0,12},{4,8},{8,4},{12,0},{1,13},{5,9},{9,5},{13,1},{2,14},{6,10},... | collective-permute-start | bytes 1544 | tf_op jit(solution)/shard_map/ppermute | solution.py:232
  253.2 8.0 %collective-permute-start.47 = (f32[128]{0:T(128)S(1)}, f32[128]{0:T(128)S(1)}, u32[]{:S(2)}, u32[]{:S(2)}) collective-permute-start(f32[128]{0:T(128)S(1)} %get-tuple-element.86), channel_id=1, source_target_pairs={{0,8},{4,12},{8,0},{12,4},{1,9},{5,13},{9,1},{13,5},{2,10},{6,14},... | collective-permute-start | bytes 1544 | tf_op jit(solution)/shard_map/ppermute | solution.py:232
  256.0 5.8 %collective-permute-start.46 = (f32[128]{0:T(128)S(1)}, f32[128]{0:T(128)S(1)}, u32[]{:S(2)}, u32[]{:S(2)}) collective-permute-start(f32[128]{0:T(128)S(1)} %get-tuple-element.86), channel_id=1, source_target_pairs={{0,4},{4,0},{8,12},{12,8},{1,5},{5,1},{9,13},{13,9},{2,6},{6,2},{1... | collective-permute-start | bytes 1544 | tf_op jit(solution)/shard_map/ppermute | solution.py:232
  257.2 7.3 %collective-permute-start.29 = (bf16[128,1024]{1,0:T(8,128)(2,1)S(1)}, bf16[128,1024]{1,0:T(8,128)(2,1)S(1)}, u32[]{:S(2)}, u32[]{:S(2)}) collective-permute-start(bf16[128,1024]{1,0:T(8,128)(2,1)S(1)} %add_convert_fusion.2), channel_id=1, source_target_pairs={{1,4},{5,9},{9,6},{13,11},{17,20},{21,25},{25,22},{29,27}} | collective-permute-start | bytes 786440 | tf_op jit(solution)/shard_map/ppermute | solution.py:203
  257.9 16.8 %collective-permute-start.51 = (bf16[128,1024]{1,0:T(8,128)(2,1)S(1)}, bf16[128,1024]{1,0:T(8,128)(2,1)S(1)}, u32[]{:S(2)}, u32[]{:S(2)}) collective-permute-start(bf16[128,1024]{1,0:T(8,128)(2,1)S(1)} %add_convert_fusion.1), channel_id=1, source_target_pairs={{1,8},{5,13},{9,2},{13,7},{17,24},{21,29},{25,18},{29,23}} | collective-permute-start | bytes 786440 | tf_op jit(solution)/shard_map/ppermute | solution.py:203
  259.2 15.4 %collective-permute-start.36 = (bf16[128,1024]{1,0:T(8,128)(2,1)S(1)}, bf16[128,1024]{1,0:T(8,128)(2,1)S(1)}, u32[]{:S(2)}, u32[]{:S(2)}) collective-permute-start(bf16[128,1024]{1,0:T(8,128)(2,1)S(1)} %add_convert_fusion.1), channel_id=1, source_target_pairs={{2,8},{6,13},{10,2},{14,7},{18,24},{22,29},{26,18},{30,23}} | collective-permute-start | bytes 786440 | tf_op jit(solution)/shard_map/ppermute | solution.py:203
  261.2 13.5 %collective-permute-start.52 = (bf16[128,1024]{1,0:T(8,128)(2,1)S(1)}, bf16[128,1024]{1,0:T(8,128)(2,1)S(1)}, u32[]{:S(2)}, u32[]{:S(2)}) collective-permute-start(bf16[128,1024]{1,0:T(8,128)(2,1)S(1)} %add_convert_fusion), channel_id=1, source_target_pairs={{0,12},{4,1},{8,14},{12,3},{16,28},{20,17},{24,30},{28,19}} | collective-permute-start | bytes 786440 | tf_op jit(solution)/shard_map/ppermute | solution.py:203
  261.9 12.8 %collective-permute-start.43 = (bf16[128,1024]{1,0:T(8,128)(2,1)S(1)}, bf16[128,1024]{1,0:T(8,128)(2,1)S(1)}, u32[]{:S(2)}, u32[]{:S(2)}) collective-permute-start(bf16[128,1024]{1,0:T(8,128)(2,1)S(1)} %add_convert_fusion), channel_id=1, source_target_pairs={{3,12},{7,1},{11,14},{15,3},{19,28},{23,17},{27,30},{31,19}} | collective-permute-start | bytes 786440 | tf_op jit(solution)/shard_map/ppermute | solution.py:203
  (16 other events, 204.9 us)

commit v9 on v7

--- a/solution.py
+++ b/solution.py
@@ -111,15 +111,18 @@
     grad_gate = (grad_act * up_proj * 2.0 * lifted).astype(BF16)
     grad_up = (grad_act * squared).astype(BF16)
     inner = 3.0 * jnp.sum(grad_act * act, axis=1)
-    return hidden, grad_gate, grad_up, inner, jnp.sum(grad_act * differ)
-
-
-def products(hidden, grad_gate, grad_up, weights):
-    w_gate, w_up, w_down = weights
+    loss = jnp.sum(grad_act * differ)
+    return hidden, grad_gate, grad_up, inner, loss
+
+
+def down_product(hidden, weights):
+    return jnp.dot(hidden, weights[2], preferred_element_type=F32)
+
+
+def grad_product(grad_gate, grad_up, weights):
     contract = (((1,), (1,)), ((), ()))
-    down = jnp.dot(hidden, w_down, preferred_element_type=F32)
-    grad = lax.dot_general(grad_gate, w_gate, contract, preferred_element_type=F32)
-    return down, grad + lax.dot_general(grad_up, w_up, contract, preferred_element_type=F32)
+    grad = lax.dot_general(grad_gate, weights[0], contract, preferred_element_type=F32)
+    return grad + lax.dot_general(grad_up, weights[1], contract, preferred_element_type=F32)
 
 
 TURNS = ((0, 1, 2, 3), (1, 2, 3, 0), (2, 1, 0, 3), (3, 2, 1, 0))
@@ -156,7 +159,7 @@
                 scaled, _ = lax.optimization_barrier((scaled, right))
                 parts.append(projected(w_up))
             if s > 0:
-                came[i], _ = lax.optimization_barrier((came[i], right))
+                came[i], _ = lax.optimization_barrier((came[i], (left, right)))
             right = picked(parts[i], jnp.clip(3 - s + z, 0, 3) ^ hp)
             left = picked(parts[i], jnp.clip(s - 3 + z, 0, 3) ^ hp)
             if s > 0:
@@ -175,8 +178,9 @@
     streams = [hidden, jnp.concatenate([grad_gate, grad_up], axis=1)]
     right, left = [streams], [streams]
     for s in range(3):
-        right.append([shifted(v, 1) for v in right[s]])
-        left.append([shifted(v, -1) for v in left[s]])
+        sent = [shifted(right[s][0], 1)], [shifted(left[s][0], -1)]
+        right.append(sent[0] + [shifted(right[s][1], 1)])
+        left.append(sent[1] + [shifted(left[s][1], -1)])
     right, left = right[1:], left[1:]
 
     def reduced(k, down, grad):
@@ -192,29 +196,30 @@
             for h in (k, k ^ 3)
         ]
 
-    def turn(k, values):
-        both = values[1]
-        return reduced(k, *products(values[0], both[:, :ff], both[:, ff:], weights))
-
-    def chosen(a, b):
-        return [jnp.where(low, v, w) for v, w in zip(a, b)]
-
     count = jnp.sum(keep_tiles.astype(F32)) * TILE
     small = jnp.concatenate([inner, loss[None], count[None], jnp.zeros(126, F32)])
     small = summed_over_hp(small)
 
-    home, values = [], streams
     ends = (z == 0) | (z == 3)
+
+    def chosen(k, i, before):
+        if k == 0:
+            return streams[i]
+        arrived = (left[k - 1][i], right[k - 1][i])
+        if k > 1:
+            _, arrived = lax.optimization_barrier((before, arrived))
+        value = jnp.where(low, *arrived)
+        if k == 3:
+            value = jnp.where(ends, value, jnp.where(low, right[0][i], left[0][i]))
+        return value
+
+    home, values = [], [None, None]
     for k in range(4):
-        if k == 1:
-            values = chosen(left[0], right[0])
-        if k > 1:
-            _, arrived = lax.optimization_barrier((values, (left[k - 1], right[k - 1])))
-            values = chosen(*arrived)
-        if k == 3:
-            inward = chosen(right[0], left[0])
-            values = [jnp.where(ends, v, w) for v, w in zip(values, inward)]
-        sent, whole = turn(k, values)
+        values[0] = chosen(k, 0, values[0])
+        down = down_product(values[0], weights)
+        values[1] = chosen(k, 1, values[1])
+        grad = grad_product(values[1][:, :ff], values[1][:, ff:], weights)
+        sent, whole = reduced(k, down, grad)
         home.append(brought_home(k, whole))
     part, _ = lax.optimization_barrier((small[rows:], sent))
     totals = part + sum(lax.ppermute(part, "ctx", [(c, c ^ d) for c in range(4)]) for d in (1, 2, 3))
@@ -249,7 +254,7 @@
     ]
     keep_cols = marked[:, ff : ff + tiles]
     *values, inner, loss = elementwise(sums[0], sums[1], marked[:, :ff], keep_cols)
-    down, grad = products(*values, weights)
+    down, grad = down_product(values[0], weights), grad_product(*values[1:], weights)
     count = jnp.sum(keep_cols.astype(F32)) * TILE
     small = lax.psum(jnp.concatenate([inner, loss[None], count[None]]), HP)
     loss_value = (small[-2] / small[-1]).reshape(1)

time: 270 us -> 288 us (1.067)
  waiting for transfers between devices: 115 us -> 140 us
  starting transfers between devices: 112 us -> 103 us
    ppermute x27, waiting for transfers between devices: 81.3 us -> 106 us  [passed_along(): return lax.ppermute(block, axis, route)]
    ppermute x27, starting transfers between devices: 77.6 us -> 69.6 us  [passed_along(): return lax.ppermute(block, axis, route)]
    ppermute x4, waiting for transfers between devices: 4.15 us -> 10.1 us  [reduced(): lax.ppermute(half.astype(BF16), HP, route).astype(F32)]
    ppermute x10, starting transfers between devices: 0.73 us -> 4.95 us  [swapped(): return lax.ppermute(block, axis, [(0, 1), (1, 0)])]
    ppermute x1, starting transfers between devices: 8.02 us -> 3.87 us  [transposed(): return lax.ppermute(block, ('ctx',) + HP, route)]
  transfers between devices with their start and end apart: 53 -> 53, of which waited for: 26 -> 30; matrix products, arithmetic and copies ran while one was open for 9% -> 8% of each run, Pallas kernels for 0% -> 0%
where the time goes in v9:
time: 288 us; the launch traced here: 283 us
  waiting for transfers between devices  140 us (49%)
  starting transfers between devices  103 us (36%)
  matrix products  19.6 us (7%)
  other arithmetic  11.9 us (4%)
  between operations  4.75 us (2%)
  local copies, waits for them, and re-layouts  4.03 us (1%)
    ppermute x27, waiting for transfers between devices, passed_along(): return lax.ppermute(block, axis, route)  106 us
    ppermute x27, starting transfers between devices, passed_along(): return lax.ppermute(block, axis, route)  69.6 us
    ppermute x10, waiting for transfers between devices, swapped(): return lax.ppermute(block, axis, [(0, 1), (1, 0)])  11.3 us
    ppermute x4, starting transfers between devices, reduced(): lax.ppermute(half.astype(BF16), HP, route).astype(F32)  10.7 us
    ppermute x4, waiting for transfers between devices, reduced(): lax.ppermute(half.astype(BF16), HP, route).astype(F32)  10.1 us
    ppermute x8, starting transfers between devices, brought_home(): lax.ppermute(whole, ('ctx',) + HP, [(4 * c + h, 4 * TURNS[c][k] + c) for...  9.25 us
    ppermute x8, waiting for transfers between devices, brought_home(): lax.ppermute(whole, ('ctx',) + HP, [(4 * c + h, 4 * TURNS[c][k] + c) for...  7.77 us
  transfers between devices with their start and end apart: 53, of which 30 were waited for; matrix products, arithmetic and copies ran while one was open for 8% of the time, Pallas kernels for 0%

profile of v9, /device:TPU:2, one launch (start us, length us, event | category | flops | bytes accessed | tf_op | source)
XLA Modules:
  0.0 283.2 jit_solution(1342876020522607606)
XLA Ops:
  1.5 3.5 %collective-permute-start = (bf16[2,128,256]{2,1,0:T(8,128)(2,1)S(1)}, bf16[2,128,256]{2,1,0:T(8,128)(2,1)S(1)}, u32[]{:S(2)}, u32[]{:S(2)}) collective-permute-start(bf16[2,128,256]{2,1,0:T(8,128)(2,1)S(1)} %pad_maximum_fusion.4), channel_id=1, source_target_pairs={{0,4},{4,8},{8,12},{1,5},{5,9},{9,13},{2,6},{6,10},{10,14},{3,7},{... | collective-permute-start | bytes 393224 | tf_op jit(solution)/shard_map/ppermute | solution.py:24
  5.0 4.5 %collective-permute-start.1 = (bf16[2,128,256]{2,1,0:T(8,128)(2,1)S(1)}, bf16[2,128,256]{2,1,0:T(8,128)(2,1)S(1)}, u32[]{:S(2)}, u32[]{:S(2)}) collective-permute-start(bf16[2,128,256]{2,1,0:T(8,128)(2,1)S(1)} %pad_maximum_fusion.4), channel_id=1, source_target_pairs={{0,8},{4,12},{1,9},{5,13},{2,10},{6,14},{3,11},{7,15},{16,24},{20,... | collective-permute-start | bytes 393224 | tf_op jit(solution)/shard_map/ppermute | solution.py:24
  13.4 1.4 collective-permute-done.2
  18.8 3.9 %collective-permute-start.3 = (bf16[128,1024]{1,0:T(8,128)(2,1)S(1)}, bf16[128,1024]{1,0:T(8,128)(2,1)S(1)}, u32[]{:S(2)}, u32[]{:S(2)}) collective-permute-start(bf16[128,1024]{1,0:T(8,128)(2,1)S(1)} %get-tuple-element.85), channel_id=1, source_target_pairs={{0,0},{1,4},{2,8},{3,12},{4,1},{5,5},{6,9},{7,13},{8,2},{9,6},{10,... | collective-permute-start | bytes 786440 | tf_op jit(solution)/shard_map/ppermute | solution.py:34
  22.7 3.9 %collective-permute-start.4 = (f32[128]{0:T(128)S(1)}, f32[128]{0:T(128)S(1)}, u32[]{:S(2)}, u32[]{:S(2)}) collective-permute-start(f32[128]{0:T(128)S(1)} %get-tuple-element.84), channel_id=1, source_target_pairs={{0,1},{1,0},{2,3},{3,2},{4,5},{5,4},{6,7},{7,6},{8,9},{9,8},{10,11... | collective-permute-start | bytes 1544 | tf_op jit(solution)/shard_map/ppermute | solution.py:28
  27.5 3.6 %collective-permute-done.5 = f32[128]{0:T(128)S(1)} collective-permute-done((f32[128]{0:T(128)S(1)}, f32[128]{0:T(128)S(1)}, u32[]{:S(2)}, u32[]{:S(2)}) %collective-permute-start.5) | collective-permute-done | bytes 544 | tf_op jit(solution)/shard_map/ppermute | solution.py:28
  31.0 5.5 %collective-permute-done.3 = bf16[128,1024]{1,0:T(8,128)(2,1)S(1)} collective-permute-done((bf16[128,1024]{1,0:T(8,128)(2,1)S(1)}, bf16[128,1024]{1,0:T(8,128)(2,1)S(1)}, u32[]{:S(2)}, u32[]{:S(2)}) %collective-permute-start.3) | collective-permute-done | bytes 262176 | tf_op jit(solution)/shard_map/ppermute | solution.py:34
  36.5 6.4 %collective-permute-done.6 = bf16[128,1024]{1,0:T(8,128)(2,1)S(1)} collective-permute-done((bf16[128,1024]{1,0:T(8,128)(2,1)S(1)}, bf16[128,1024]{1,0:T(8,128)(2,1)S(1)}, u32[]{:S(2)}, u32[]{:S(2)}) %collective-permute-start.6) | collective-permute-done | bytes 262176 | tf_op jit(solution)/shard_map/ppermute | solution.py:28
  47.5 2.1 convolution_convert_fusion.1
  49.6 3.4 %collective-permute-start.8 = (bf16[128,1792]{1,0:T(8,128)(2,1)S(1)}, bf16[128,1792]{1,0:T(8,128)(2,1)S(1)}, u32[]{:S(2)}, u32[]{:S(2)}) collective-permute-start(bf16[128,1792]{1,0:T(8,128)(2,1)S(1)} %get-tuple-element.41), channel_id=1, source_target_pairs={{0,4},{4,8},{8,12},{1,5},{5,9},{9,13},{2,6},{6,10},{10,14},{3,7},{... | collective-permute-start | bytes 1376264 | tf_op jit(solution)/shard_map/ppermute | solution.py:24
  54.4 2.1 convolution_convert_fusion
  56.5 4.6 %collective-permute-start.12 = (bf16[128,1792]{1,0:T(8,128)(2,1)S(1)}, bf16[128,1792]{1,0:T(8,128)(2,1)S(1)}, u32[]{:S(2)}, u32[]{:S(2)}) collective-permute-start(bf16[128,1792]{1,0:T(8,128)(2,1)S(1)} %get-tuple-element.45), channel_id=1, source_target_pairs={{0,4},{4,8},{8,12},{1,5},{5,9},{9,13},{2,6},{6,10},{10,14},{3,7},{... | collective-permute-start | bytes 1376264 | tf_op jit(solution)/shard_map/ppermute | solution.py:24
  62.4 1.5 collective-permute-done.8
  63.9 4.4 %collective-permute-done.9 = bf16[128,1792]{1,0:T(8,128)(2,1)S(1)} collective-permute-done((bf16[128,1792]{1,0:T(8,128)(2,1)S(1)}, bf16[128,1792]{1,0:T(8,128)(2,1)S(1)}, u32[]{:S(2)}, u32[]{:S(2)}) %collective-permute-start.9) | collective-permute-done | bytes 458784 | tf_op jit(solution)/shard_map/ppermute | solution.py:24
  68.6 2.0 collective-permute-start.10
  71.9 1.8 collective-permute-done.12
  73.7 4.4 %collective-permute-done.13 = bf16[128,1792]{1,0:T(8,128)(2,1)S(1)} collective-permute-done((bf16[128,1792]{1,0:T(8,128)(2,1)S(1)}, bf16[128,1792]{1,0:T(8,128)(2,1)S(1)}, u32[]{:S(2)}, u32[]{:S(2)}) %collective-permute-start.13) | collective-permute-done | bytes 458784 | tf_op jit(solution)/shard_map/ppermute | solution.py:24
  78.4 2.0 collective-permute-start.16
  81.7 1.9 collective-permute-done.10
  83.6 4.4 %collective-permute-done.11 = bf16[128,1792]{1,0:T(8,128)(2,1)S(1)} collective-permute-done((bf16[128,1792]{1,0:T(8,128)(2,1)S(1)}, bf16[128,1792]{1,0:T(8,128)(2,1)S(1)}, u32[]{:S(2)}, u32[]{:S(2)}) %collective-permute-start.11) | collective-permute-done | bytes 458784 | tf_op jit(solution)/shard_map/ppermute | solution.py:24
  88.2 2.0 collective-permute-start.14
  91.6 1.8 collective-permute-done.16
  93.4 4.4 %collective-permute-done.17 = bf16[128,1792]{1,0:T(8,128)(2,1)S(1)} collective-permute-done((bf16[128,1792]{1,0:T(8,128)(2,1)S(1)}, bf16[128,1792]{1,0:T(8,128)(2,1)S(1)}, u32[]{:S(2)}, u32[]{:S(2)}) %collective-permute-start.17) | collective-permute-done | bytes 458784 | tf_op jit(solution)/shard_map/ppermute | solution.py:24
  98.1 2.1 collective-permute-start.18
  100.2 1.5 collective-permute-start.19
  101.7 1.5 collective-permute-done.14
  103.2 4.4 %collective-permute-done.15 = bf16[128,1792]{1,0:T(8,128)(2,1)S(1)} collective-permute-done((bf16[128,1792]{1,0:T(8,128)(2,1)S(1)}, bf16[128,1792]{1,0:T(8,128)(2,1)S(1)}, u32[]{:S(2)}, u32[]{:S(2)}) %collective-permute-start.15) | collective-permute-done | bytes 458784 | tf_op jit(solution)/shard_map/ppermute | solution.py:24
  107.9 4.7 %collective-permute-done.18 = bf16[128,1792]{1,0:T(8,128)(2,1)S(1)} collective-permute-done((bf16[128,1792]{1,0:T(8,128)(2,1)S(1)}, bf16[128,1792]{1,0:T(8,128)(2,1)S(1)}, u32[]{:S(2)}, u32[]{:S(2)}) %collective-permute-start.18) | collective-permute-done | bytes 458784 | tf_op jit(solution)/shard_map/ppermute | solution.py:24
  112.6 4.1 %collective-permute-done.19 = bf16[128,1792]{1,0:T(8,128)(2,1)S(1)} collective-permute-done((bf16[128,1792]{1,0:T(8,128)(2,1)S(1)}, bf16[128,1792]{1,0:T(8,128)(2,1)S(1)}, u32[]{:S(2)}, u32[]{:S(2)}) %collective-permute-start.19) | collective-permute-done | bytes 458784 | tf_op jit(solution)/shard_map/ppermute | solution.py:24
  125.3 4.6 %collective-permute-start.26 = (bf16[128,3584]{1,0:T(8,128)(2,1)S(1)}, bf16[128,3584]{1,0:T(8,128)(2,1)S(1)}, u32[]{:S(2)}, u32[]{:S(2)}) collective-permute-start(bf16[128,3584]{1,0:T(8,128)(2,1)S(1)} %pad_maximum_fusion.1), channel_id=1, source_target_pairs={{0,4},{4,8},{8,12},{1,5},{5,9},{9,13},{2,6},{6,10},{10,14},{3,7},{... | collective-permute-start | bytes 2752520 | tf_op jit(solution)/shard_map/ppermute | solution.py:24
  131.2 4.6 %collective-permute-start.24 = (bf16[128,1792]{1,0:T(8,128)(2,1)S(1)}, bf16[128,1792]{1,0:T(8,128)(2,1)S(1)}, u32[]{:S(2)}, u32[]{:S(2)}) collective-permute-start(bf16[128,1792]{1,0:T(8,128)(2,1)S(1)} %get-tuple-element.63), channel_id=1, source_target_pairs={{0,4},{4,8},{8,12},{1,5},{5,9},{9,13},{2,6},{6,10},{10,14},{3,7},{... | collective-permute-start | bytes 1376264 | tf_op jit(solution)/shard_map/ppermute | solution.py:24
  136.0 3.7 %collective-permute-start.21 = (bf16[128,1024]{1,0:T(8,128)(2,1)S(1)}, bf16[128,1024]{1,0:T(8,128)(2,1)S(1)}, u32[]{:S(2)}, u32[]{:S(2)}) collective-permute-start(bf16[128,1024]{1,0:T(8,128)(2,1)S(1)} %fusion.49), channel_id=1, source_target_pairs={{2,0},{1,3},{6,4},{5,7},{10,8},{9,11},{14,12},{13,15},{18,16},{17,... | collective-permute-start | bytes 786440 | tf_op jit(solution)/shard_map/ppermute | solution.py:191
  139.6 18.1 %collective-permute-done.23 = bf16[128,1792]{1,0:T(8,128)(2,1)S(1)} collective-permute-done((bf16[128,1792]{1,0:T(8,128)(2,1)S(1)}, bf16[128,1792]{1,0:T(8,128)(2,1)S(1)}, u32[]{:S(2)}, u32[]{:S(2)}) %collective-permute-start.23) | collective-permute-done | bytes 458784 | tf_op jit(solution)/shard_map/ppermute | solution.py:24
  159.0 4.6 %collective-permute-start.31 = (bf16[128,1792]{1,0:T(8,128)(2,1)S(1)}, bf16[128,1792]{1,0:T(8,128)(2,1)S(1)}, u32[]{:S(2)}, u32[]{:S(2)}) collective-permute-start(bf16[128,1792]{1,0:T(8,128)(2,1)S(1)} %collective-permute-done.24), channel_id=1, source_target_pairs={{0,4},{4,8},{8,12},{1,5},{5,9},{9,13},{2,6},{6,10},{10,14},{3,7},{... | collective-permute-start | bytes 1376264 | tf_op jit(solution)/shard_map/ppermute | solution.py:24
  165.2 5.8 %collective-permute-done.30 = bf16[128,1792]{1,0:T(8,128)(2,1)S(1)} collective-permute-done((bf16[128,1792]{1,0:T(8,128)(2,1)S(1)}, bf16[128,1792]{1,0:T(8,128)(2,1)S(1)}, u32[]{:S(2)}, u32[]{:S(2)}) %collective-permute-start.30) | collective-permute-done | bytes 458784 | tf_op jit(solution)/shard_map/ppermute | solution.py:24
  177.6 5.7 %collective-permute-start.38 = (bf16[128,1792]{1,0:T(8,128)(2,1)S(1)}, bf16[128,1792]{1,0:T(8,128)(2,1)S(1)}, u32[]{:S(2)}, u32[]{:S(2)}) collective-permute-start(bf16[128,1792]{1,0:T(8,128)(2,1)S(1)} %collective-permute-done.31), channel_id=1, source_target_pairs={{0,4},{4,8},{8,12},{1,5},{5,9},{9,13},{2,6},{6,10},{10,14},{3,7},{... | collective-permute-start | bytes 1376264 | tf_op jit(solution)/shard_map/ppermute | solution.py:24
  183.9 4.0 %collective-permute-start.33 = (bf16[128,3584]{1,0:T(8,128)(2,1)S(1)}, bf16[128,3584]{1,0:T(8,128)(2,1)S(1)}, u32[]{:S(2)}, u32[]{:S(2)}) collective-permute-start(bf16[128,3584]{1,0:T(8,128)(2,1)S(1)} %collective-permute-done.26), channel_id=1, source_target_pairs={{0,4},{4,8},{8,12},{1,5},{5,9},{9,13},{2,6},{6,10},{10,14},{3,7},{... | collective-permute-start | bytes 2752520 | tf_op jit(solution)/shard_map/ppermute | solution.py:24
  188.0 22.2 %collective-permute-done.37 = bf16[128,1792]{1,0:T(8,128)(2,1)S(1)} collective-permute-done((bf16[128,1792]{1,0:T(8,128)(2,1)S(1)}, bf16[128,1792]{1,0:T(8,128)(2,1)S(1)}, u32[]{:S(2)}, u32[]{:S(2)}) %collective-permute-start.37) | collective-permute-done | bytes 458784 | tf_op jit(solution)/shard_map/ppermute | solution.py:24
  212.9 6.2 %collective-permute-done.28 = bf16[128,1024]{1,0:T(8,128)(2,1)S(1)} collective-permute-done((bf16[128,1024]{1,0:T(8,128)(2,1)S(1)}, bf16[128,1024]{1,0:T(8,128)(2,1)S(1)}, u32[]{:S(2)}, u32[]{:S(2)}) %collective-permute-start.28) | collective-permute-done | bytes 262176 | tf_op jit(solution)/shard_map/ppermute | solution.py:191
  221.3 5.2 %collective-permute-start.40 = (bf16[128,3584]{1,0:T(8,128)(2,1)S(1)}, bf16[128,3584]{1,0:T(8,128)(2,1)S(1)}, u32[]{:S(2)}, u32[]{:S(2)}) collective-permute-start(bf16[128,3584]{1,0:T(8,128)(2,1)S(1)} %collective-permute-done.33), channel_id=1, source_target_pairs={{0,4},{4,8},{8,12},{1,5},{5,9},{9,13},{2,6},{6,10},{10,14},{3,7},{... | collective-permute-start | bytes 2752520 | tf_op jit(solution)/shard_map/ppermute | solution.py:24
  229.2 15.9 %collective-permute-done.39 = bf16[128,3584]{1,0:T(8,128)(2,1)S(1)} collective-permute-done((bf16[128,3584]{1,0:T(8,128)(2,1)S(1)}, bf16[128,3584]{1,0:T(8,128)(2,1)S(1)}, u32[]{:S(2)}, u32[]{:S(2)}) %collective-permute-start.39) | collective-permute-done | bytes 917536 | tf_op jit(solution)/shard_map/ppermute | solution.py:24
  250.7 4.5 %collective-permute-start.42 = (bf16[128,1024]{1,0:T(8,128)(2,1)S(1)}, bf16[128,1024]{1,0:T(8,128)(2,1)S(1)}, u32[]{:S(2)}, u32[]{:S(2)}) collective-permute-start(bf16[128,1024]{1,0:T(8,128)(2,1)S(1)} %fusion.52), channel_id=1, source_target_pairs={{1,3},{2,0},{5,7},{6,4},{9,11},{10,8},{13,15},{14,12},{17,19},{18,... | collective-permute-start | bytes 786440 | tf_op jit(solution)/shard_map/ppermute | solution.py:191
  255.2 3.9 %collective-permute-done.35 = bf16[128,1024]{1,0:T(8,128)(2,1)S(1)} collective-permute-done((bf16[128,1024]{1,0:T(8,128)(2,1)S(1)}, bf16[128,1024]{1,0:T(8,128)(2,1)S(1)}, u32[]{:S(2)}, u32[]{:S(2)}) %collective-permute-start.35) | collective-permute-done | bytes 262176 | tf_op jit(solution)/shard_map/ppermute | solution.py:191
  259.2 1.5 collective-permute-start.46
  261.5 2.1 collective-permute-start.48
  263.8 2.7 collective-permute-start.50
  266.5 1.9 collective-permute-start.36
  273.1 7.5 %collective-permute-done.36 = bf16[128,1024]{1,0:T(8,128)(2,1)S(1)} collective-permute-done((bf16[128,1024]{1,0:T(8,128)(2,1)S(1)}, bf16[128,1024]{1,0:T(8,128)(2,1)S(1)}, u32[]{:S(2)}, u32[]{:S(2)}) %collective-permute-start.36) | collective-permute-done | bytes 262176 | tf_op jit(solution)/shard_map/ppermute | solution.py:195
  (150 shorter events, 60.1 us)
Async XLA Ops:
  1.5 11.6 %collective-permute-start = (bf16[2,128,256]{2,1,0:T(8,128)(2,1)S(1)}, bf16[2,128,256]{2,1,0:T(8,128)(2,1)S(1)}, u32[]{:S(2)}, u32[]{:S(2)}) collective-permute-start(bf16[2,128,256]{2,1,0:T(8,128)(2,1)S(1)} %pad_maximum_fusion.4), channel_id=1, source_target_pairs={{0,4},{4,8},{8,12},{1,5},{5,9},{9,13},{2,6},{6,10},{10,14},{3,7},{... | collective-permute-start | bytes 393224 | tf_op jit(solution)/shard_map/ppermute | solution.py:24
  5.0 8.4 %collective-permute-start.1 = (bf16[2,128,256]{2,1,0:T(8,128)(2,1)S(1)}, bf16[2,128,256]{2,1,0:T(8,128)(2,1)S(1)}, u32[]{:S(2)}, u32[]{:S(2)}) collective-permute-start(bf16[2,128,256]{2,1,0:T(8,128)(2,1)S(1)} %pad_maximum_fusion.4), channel_id=1, source_target_pairs={{0,8},{4,12},{1,9},{5,13},{2,10},{6,14},{3,11},{7,15},{16,24},{20,... | collective-permute-start | bytes 393224 | tf_op jit(solution)/shard_map/ppermute | solution.py:24
  9.5 5.3 %collective-permute-start.2 = (bf16[2,128,256]{2,1,0:T(8,128)(2,1)S(1)}, bf16[2,128,256]{2,1,0:T(8,128)(2,1)S(1)}, u32[]{:S(2)}, u32[]{:S(2)}) collective-permute-start(bf16[2,128,256]{2,1,0:T(8,128)(2,1)S(1)} %pad_maximum_fusion.4), channel_id=1, source_target_pairs={{0,12},{1,13},{2,14},{3,15},{16,28},{17,29},{18,30},{19,31}} | collective-permute-start | bytes 393224 | tf_op jit(solution)/shard_map/ppermute | solution.py:24
  18.8 17.7 %collective-permute-start.3 = (bf16[128,1024]{1,0:T(8,128)(2,1)S(1)}, bf16[128,1024]{1,0:T(8,128)(2,1)S(1)}, u32[]{:S(2)}, u32[]{:S(2)}) collective-permute-start(bf16[128,1024]{1,0:T(8,128)(2,1)S(1)} %get-tuple-element.85), channel_id=1, source_target_pairs={{0,0},{1,4},{2,8},{3,12},{4,1},{5,5},{6,9},{7,13},{8,2},{9,6},{10,... | collective-permute-start | bytes 786440 | tf_op jit(solution)/shard_map/ppermute | solution.py:34
  22.7 4.8 %collective-permute-start.4 = (f32[128]{0:T(128)S(1)}, f32[128]{0:T(128)S(1)}, u32[]{:S(2)}, u32[]{:S(2)}) collective-permute-start(f32[128]{0:T(128)S(1)} %get-tuple-element.84), channel_id=1, source_target_pairs={{0,1},{1,0},{2,3},{3,2},{4,5},{5,4},{6,7},{7,6},{8,9},{9,8},{10,11... | collective-permute-start | bytes 1544 | tf_op jit(solution)/shard_map/ppermute | solution.py:28
  36.5 6.4 %collective-permute-start.6 = (bf16[128,1024]{1,0:T(8,128)(2,1)S(1)}, bf16[128,1024]{1,0:T(8,128)(2,1)S(1)}, u32[]{:S(2)}, u32[]{:S(2)}) collective-permute-start(bf16[128,1024]{1,0:T(8,128)(2,1)S(1)} %collective-permute-done.3), channel_id=1, source_target_pairs={{0,2},{2,0},{1,3},{3,1},{4,6},{6,4},{5,7},{7,5},{8,10},{10,8},{9,1... | collective-permute-start | bytes 786440 | tf_op jit(solution)/shard_map/ppermute | solution.py:28
  49.6 14.3 %collective-permute-start.8 = (bf16[128,1792]{1,0:T(8,128)(2,1)S(1)}, bf16[128,1792]{1,0:T(8,128)(2,1)S(1)}, u32[]{:S(2)}, u32[]{:S(2)}) collective-permute-start(bf16[128,1792]{1,0:T(8,128)(2,1)S(1)} %get-tuple-element.41), channel_id=1, source_target_pairs={{0,4},{4,8},{8,12},{1,5},{5,9},{9,13},{2,6},{6,10},{10,14},{3,7},{... | collective-permute-start | bytes 1376264 | tf_op jit(solution)/shard_map/ppermute | solution.py:24
  53.0 15.3 %collective-permute-start.9 = (bf16[128,1792]{1,0:T(8,128)(2,1)S(1)}, bf16[128,1792]{1,0:T(8,128)(2,1)S(1)}, u32[]{:S(2)}, u32[]{:S(2)}) collective-permute-start(bf16[128,1792]{1,0:T(8,128)(2,1)S(1)} %get-tuple-element.42), channel_id=1, source_target_pairs={{4,0},{8,4},{12,8},{5,1},{9,5},{13,9},{6,2},{10,6},{14,10},{7,3},{... | collective-permute-start | bytes 1376264 | tf_op jit(solution)/shard_map/ppermute | solution.py:24
  56.5 17.2 %collective-permute-start.12 = (bf16[128,1792]{1,0:T(8,128)(2,1)S(1)}, bf16[128,1792]{1,0:T(8,128)(2,1)S(1)}, u32[]{:S(2)}, u32[]{:S(2)}) collective-permute-start(bf16[128,1792]{1,0:T(8,128)(2,1)S(1)} %get-tuple-element.45), channel_id=1, source_target_pairs={{0,4},{4,8},{8,12},{1,5},{5,9},{9,13},{2,6},{6,10},{10,14},{3,7},{... | collective-permute-start | bytes 1376264 | tf_op jit(solution)/shard_map/ppermute | solution.py:24
  61.1 17.1 %collective-permute-start.13 = (bf16[128,1792]{1,0:T(8,128)(2,1)S(1)}, bf16[128,1792]{1,0:T(8,128)(2,1)S(1)}, u32[]{:S(2)}, u32[]{:S(2)}) collective-permute-start(bf16[128,1792]{1,0:T(8,128)(2,1)S(1)} %get-tuple-element.44), channel_id=1, source_target_pairs={{4,0},{8,4},{12,8},{5,1},{9,5},{13,9},{6,2},{10,6},{14,10},{7,3},{... | collective-permute-start | bytes 1376264 | tf_op jit(solution)/shard_map/ppermute | solution.py:24
  68.6 15.0 %collective-permute-start.10 = (bf16[128,1792]{1,0:T(8,128)(2,1)S(1)}, bf16[128,1792]{1,0:T(8,128)(2,1)S(1)}, u32[]{:S(2)}, u32[]{:S(2)}) collective-permute-start(bf16[128,1792]{1,0:T(8,128)(2,1)S(1)} %get-tuple-element.48), channel_id=1, source_target_pairs={{0,4},{4,8},{8,12},{1,5},{5,9},{9,13},{2,6},{6,10},{10,14},{3,7},{... | collective-permute-start | bytes 1376264 | tf_op jit(solution)/shard_map/ppermute | solution.py:24
  70.6 17.4 %collective-permute-start.11 = (bf16[128,1792]{1,0:T(8,128)(2,1)S(1)}, bf16[128,1792]{1,0:T(8,128)(2,1)S(1)}, u32[]{:S(2)}, u32[]{:S(2)}) collective-permute-start(bf16[128,1792]{1,0:T(8,128)(2,1)S(1)} %get-tuple-element.49), channel_id=1, source_target_pairs={{4,0},{8,4},{12,8},{5,1},{9,5},{13,9},{6,2},{10,6},{14,10},{7,3},{... | collective-permute-start | bytes 1376264 | tf_op jit(solution)/shard_map/ppermute | solution.py:24
  78.4 15.0 %collective-permute-start.16 = (bf16[128,1792]{1,0:T(8,128)(2,1)S(1)}, bf16[128,1792]{1,0:T(8,128)(2,1)S(1)}, u32[]{:S(2)}, u32[]{:S(2)}) collective-permute-start(bf16[128,1792]{1,0:T(8,128)(2,1)S(1)} %get-tuple-element.53), channel_id=1, source_target_pairs={{0,4},{4,8},{8,12},{1,5},{5,9},{9,13},{2,6},{6,10},{10,14},{3,7},{... | collective-permute-start | bytes 1376264 | tf_op jit(solution)/shard_map/ppermute | solution.py:24
  80.4 17.4 %collective-permute-start.17 = (bf16[128,1792]{1,0:T(8,128)(2,1)S(1)}, bf16[128,1792]{1,0:T(8,128)(2,1)S(1)}, u32[]{:S(2)}, u32[]{:S(2)}) collective-permute-start(bf16[128,1792]{1,0:T(8,128)(2,1)S(1)} %get-tuple-element.52), channel_id=1, source_target_pairs={{4,0},{8,4},{12,8},{5,1},{9,5},{13,9},{6,2},{10,6},{14,10},{7,3},{... | collective-permute-start | bytes 1376264 | tf_op jit(solution)/shard_map/ppermute | solution.py:24
  88.2 15.0 %collective-permute-start.14 = (bf16[128,1792]{1,0:T(8,128)(2,1)S(1)}, bf16[128,1792]{1,0:T(8,128)(2,1)S(1)}, u32[]{:S(2)}, u32[]{:S(2)}) collective-permute-start(bf16[128,1792]{1,0:T(8,128)(2,1)S(1)} %get-tuple-element.56), channel_id=1, source_target_pairs={{0,4},{4,8},{8,12},{1,5},{5,9},{9,13},{2,6},{6,10},{10,14},{3,7},{... | collective-permute-start | bytes 1376264 | tf_op jit(solution)/shard_map/ppermute | solution.py:24
  90.3 17.4 %collective-permute-start.15 = (bf16[128,1792]{1,0:T(8,128)(2,1)S(1)}, bf16[128,1792]{1,0:T(8,128)(2,1)S(1)}, u32[]{:S(2)}, u32[]{:S(2)}) collective-permute-start(bf16[128,1792]{1,0:T(8,128)(2,1)S(1)} %get-tuple-element.57), channel_id=1, source_target_pairs={{4,0},{8,4},{12,8},{5,1},{9,5},{13,9},{6,2},{10,6},{14,10},{7,3},{... | collective-permute-start | bytes 1376264 | tf_op jit(solution)/shard_map/ppermute | solution.py:24
  98.1 14.5 %collective-permute-start.18 = (bf16[128,1792]{1,0:T(8,128)(2,1)S(1)}, bf16[128,1792]{1,0:T(8,128)(2,1)S(1)}, u32[]{:S(2)}, u32[]{:S(2)}) collective-permute-start(bf16[128,1792]{1,0:T(8,128)(2,1)S(1)} %get-tuple-element.61), channel_id=1, source_target_pairs={{0,4},{4,8},{8,12},{1,5},{5,9},{9,13},{2,6},{6,10},{10,14},{3,7},{... | collective-permute-start | bytes 1376264 | tf_op jit(solution)/shard_map/ppermute | solution.py:24
  100.2 16.5 %collective-permute-start.19 = (bf16[128,1792]{1,0:T(8,128)(2,1)S(1)}, bf16[128,1792]{1,0:T(8,128)(2,1)S(1)}, u32[]{:S(2)}, u32[]{:S(2)}) collective-permute-start(bf16[128,1792]{1,0:T(8,128)(2,1)S(1)} %get-tuple-element.62), channel_id=1, source_target_pairs={{4,0},{8,4},{12,8},{5,1},{9,5},{13,9},{6,2},{10,6},{14,10},{7,3},{... | collective-permute-start | bytes 1376264 | tf_op jit(solution)/shard_map/ppermute | solution.py:24
  122.3 13.5 %collective-permute-start.20 = (bf16[128,1024]{1,0:T(8,128)(2,1)S(1)}, bf16[128,1024]{1,0:T(8,128)(2,1)S(1)}, u32[]{:S(2)}, u32[]{:S(2)}) collective-permute-start(bf16[128,1024]{1,0:T(8,128)(2,1)S(1)} %get-tuple-element.121), channel_id=1, source_target_pairs={{0,1},{1,0},{2,3},{3,2},{4,5},{5,4},{6,7},{7,6},{8,9},{9,8},{10,11... | collective-permute-start | bytes 786440 | tf_op jit(solution)/shard_map/ppermute | solution.py:28
  123.6 7.6 %collective-permute-start.45 = (f32[256]{0:T(256)S(1)}, f32[256]{0:T(256)S(1)}, u32[]{:S(2)}, u32[]{:S(2)}) collective-permute-start(f32[256]{0:T(256)S(1)} %fusion.101), channel_id=1, source_target_pairs={{0,2},{2,0},{1,3},{3,1},{4,6},{6,4},{5,7},{7,5},{8,10},{10,8},{9,1... | collective-permute-start | bytes 3080 | tf_op jit(solution)/shard_map/ppermute | solution.py:28
  124.0 48.1 %collective-permute-start.25 = (bf16[128,3584]{1,0:T(8,128)(2,1)S(1)}, bf16[128,3584]{1,0:T(8,128)(2,1)S(1)}, u32[]{:S(2)}, u32[]{:S(2)}) collective-permute-start(bf16[128,3584]{1,0:T(8,128)(2,1)S(1)} %pad_maximum_fusion.1), channel_id=1, source_target_pairs={{4,0},{8,4},{12,8},{5,1},{9,5},{13,9},{6,2},{10,6},{14,10},{7,3},{... | collective-permute-start | bytes 2752520 | tf_op jit(solution)/shard_map/ppermute | solution.py:24
  125.3 46.8 %collective-permute-start.26 = (bf16[128,3584]{1,0:T(8,128)(2,1)S(1)}, bf16[128,3584]{1,0:T(8,128)(2,1)S(1)}, u32[]{:S(2)}, u32[]{:S(2)}) collective-permute-start(bf16[128,3584]{1,0:T(8,128)(2,1)S(1)} %pad_maximum_fusion.1), channel_id=1, source_target_pairs={{0,4},{4,8},{8,12},{1,5},{5,9},{9,13},{2,6},{6,10},{10,14},{3,7},{... | collective-permute-start | bytes 2752520 | tf_op jit(solution)/shard_map/ppermute | solution.py:24
  129.9 27.8 %collective-permute-start.23 = (bf16[128,1792]{1,0:T(8,128)(2,1)S(1)}, bf16[128,1792]{1,0:T(8,128)(2,1)S(1)}, u32[]{:S(2)}, u32[]{:S(2)}) collective-permute-start(bf16[128,1792]{1,0:T(8,128)(2,1)S(1)} %get-tuple-element.63), channel_id=1, source_target_pairs={{4,0},{8,4},{12,8},{5,1},{9,5},{13,9},{6,2},{10,6},{14,10},{7,3},{... | collective-permute-start | bytes 1376264 | tf_op jit(solution)/shard_map/ppermute | solution.py:24
  131.2 27.8 %collective-permute-start.24 = (bf16[128,1792]{1,0:T(8,128)(2,1)S(1)}, bf16[128,1792]{1,0:T(8,128)(2,1)S(1)}, u32[]{:S(2)}, u32[]{:S(2)}) collective-permute-start(bf16[128,1792]{1,0:T(8,128)(2,1)S(1)} %get-tuple-element.63), channel_id=1, source_target_pairs={{0,4},{4,8},{8,12},{1,5},{5,9},{9,13},{2,6},{6,10},{10,14},{3,7},{... | collective-permute-start | bytes 1376264 | tf_op jit(solution)/shard_map/ppermute | solution.py:24
  136.0 28.4 %collective-permute-start.21 = (bf16[128,1024]{1,0:T(8,128)(2,1)S(1)}, bf16[128,1024]{1,0:T(8,128)(2,1)S(1)}, u32[]{:S(2)}, u32[]{:S(2)}) collective-permute-start(bf16[128,1024]{1,0:T(8,128)(2,1)S(1)} %fusion.49), channel_id=1, source_target_pairs={{2,0},{1,3},{6,4},{5,7},{10,8},{9,11},{14,12},{13,15},{18,16},{17,... | collective-permute-start | bytes 786440 | tf_op jit(solution)/shard_map/ppermute | solution.py:191
  157.7 13.2 %collective-permute-start.30 = (bf16[128,1792]{1,0:T(8,128)(2,1)S(1)}, bf16[128,1792]{1,0:T(8,128)(2,1)S(1)}, u32[]{:S(2)}, u32[]{:S(2)}) collective-permute-start(bf16[128,1792]{1,0:T(8,128)(2,1)S(1)} %collective-permute-done.23), channel_id=1, source_target_pairs={{4,0},{8,4},{12,8},{5,1},{9,5},{13,9},{6,2},{10,6},{14,10},{7,3},{... | collective-permute-start | bytes 1376264 | tf_op jit(solution)/shard_map/ppermute | solution.py:24
  159.0 13.1 %collective-permute-start.31 = (bf16[128,1792]{1,0:T(8,128)(2,1)S(1)}, bf16[128,1792]{1,0:T(8,128)(2,1)S(1)}, u32[]{:S(2)}, u32[]{:S(2)}) collective-permute-start(bf16[128,1792]{1,0:T(8,128)(2,1)S(1)} %collective-permute-done.24), channel_id=1, source_target_pairs={{0,4},{4,8},{8,12},{1,5},{5,9},{9,13},{2,6},{6,10},{10,14},{3,7},{... | collective-permute-start | bytes 1376264 | tf_op jit(solution)/shard_map/ppermute | solution.py:24
  164.5 96.2 %collective-permute-start.22 = (bf16[128,1024]{1,0:T(8,128)(2,1)S(1)}, bf16[128,1024]{1,0:T(8,128)(2,1)S(1)}, u32[]{:S(2)}, u32[]{:S(2)}) collective-permute-start(bf16[128,1024]{1,0:T(8,128)(2,1)S(1)} %add_convert_fusion.3), channel_id=1, source_target_pairs={{0,0},{4,5},{8,10},{12,15},{16,16},{20,21},{24,26},{28,31}} | collective-permute-start | bytes 786440 | tf_op jit(solution)/shard_map/ppermute | solution.py:195
  174.8 9.1 %collective-permute-start.27 = (bf16[128,1024]{1,0:T(8,128)(2,1)S(1)}, bf16[128,1024]{1,0:T(8,128)(2,1)S(1)}, u32[]{:S(2)}, u32[]{:S(2)}) collective-permute-start(bf16[128,1024]{1,0:T(8,128)(2,1)S(1)} %get-tuple-element.119), channel_id=1, source_target_pairs={{0,1},{1,0},{2,3},{3,2},{4,5},{5,4},{6,7},{7,6},{8,9},{9,8},{10,11... | collective-permute-start | bytes 786440 | tf_op jit(solution)/shard_map/ppermute | solution.py:28
  175.0 45.0 %collective-permute-start.32 = (bf16[128,3584]{1,0:T(8,128)(2,1)S(1)}, bf16[128,3584]{1,0:T(8,128)(2,1)S(1)}, u32[]{:S(2)}, u32[]{:S(2)}) collective-permute-start(bf16[128,3584]{1,0:T(8,128)(2,1)S(1)} %collective-permute-done.25), channel_id=1, source_target_pairs={{4,0},{8,4},{12,8},{5,1},{9,5},{13,9},{6,2},{10,6},{14,10},{7,3},{... | collective-permute-start | bytes 2752520 | tf_op jit(solution)/shard_map/ppermute | solution.py:24
  176.3 33.9 %collective-permute-start.37 = (bf16[128,1792]{1,0:T(8,128)(2,1)S(1)}, bf16[128,1792]{1,0:T(8,128)(2,1)S(1)}, u32[]{:S(2)}, u32[]{:S(2)}) collective-permute-start(bf16[128,1792]{1,0:T(8,128)(2,1)S(1)} %collective-permute-done.30), channel_id=1, source_target_pairs={{4,0},{8,4},{12,8},{5,1},{9,5},{13,9},{6,2},{10,6},{14,10},{7,3},{... | collective-permute-start | bytes 1376264 | tf_op jit(solution)/shard_map/ppermute | solution.py:24
  177.6 33.3 %collective-permute-start.38 = (bf16[128,1792]{1,0:T(8,128)(2,1)S(1)}, bf16[128,1792]{1,0:T(8,128)(2,1)S(1)}, u32[]{:S(2)}, u32[]{:S(2)}) collective-permute-start(bf16[128,1792]{1,0:T(8,128)(2,1)S(1)} %collective-permute-done.31), channel_id=1, source_target_pairs={{0,4},{4,8},{8,12},{1,5},{5,9},{9,13},{2,6},{6,10},{10,14},{3,7},{... | collective-permute-start | bytes 1376264 | tf_op jit(solution)/shard_map/ppermute | solution.py:24
  183.9 36.1 %collective-permute-start.33 = (bf16[128,3584]{1,0:T(8,128)(2,1)S(1)}, bf16[128,3584]{1,0:T(8,128)(2,1)S(1)}, u32[]{:S(2)}, u32[]{:S(2)}) collective-permute-start(bf16[128,3584]{1,0:T(8,128)(2,1)S(1)} %collective-permute-done.26), channel_id=1, source_target_pairs={{0,4},{4,8},{8,12},{1,5},{5,9},{9,13},{2,6},{6,10},{10,14},{3,7},{... | collective-permute-start | bytes 2752520 | tf_op jit(solution)/shard_map/ppermute | solution.py:24
  210.2 53.6 %collective-permute-start.49 = (bf16[128,1024]{1,0:T(8,128)(2,1)S(1)}, bf16[128,1024]{1,0:T(8,128)(2,1)S(1)}, u32[]{:S(2)}, u32[]{:S(2)}) collective-permute-start(bf16[128,1024]{1,0:T(8,128)(2,1)S(1)} %add_convert_fusion.3), channel_id=1, source_target_pairs={{3,0},{7,5},{11,10},{15,15},{19,16},{23,21},{27,26},{31,31}} | collective-permute-start | bytes 786440 | tf_op jit(solution)/shard_map/ppermute | solution.py:195
  210.9 8.3 %collective-permute-start.28 = (bf16[128,1024]{1,0:T(8,128)(2,1)S(1)}, bf16[128,1024]{1,0:T(8,128)(2,1)S(1)}, u32[]{:S(2)}, u32[]{:S(2)}) collective-permute-start(bf16[128,1024]{1,0:T(8,128)(2,1)S(1)} %fusion.50), channel_id=1, source_target_pairs={{3,1},{0,2},{7,5},{4,6},{11,9},{8,10},{15,13},{12,14},{19,17},{16,... | collective-permute-start | bytes 786440 | tf_op jit(solution)/shard_map/ppermute | solution.py:191
  219.3 47.2 %collective-permute-start.29 = (bf16[128,1024]{1,0:T(8,128)(2,1)S(1)}, bf16[128,1024]{1,0:T(8,128)(2,1)S(1)}, u32[]{:S(2)}, u32[]{:S(2)}) collective-permute-start(bf16[128,1024]{1,0:T(8,128)(2,1)S(1)} %add_convert_fusion.2), channel_id=1, source_target_pairs={{1,4},{5,9},{9,6},{13,11},{17,20},{21,25},{25,22},{29,27}} | collective-permute-start | bytes 786440 | tf_op jit(solution)/shard_map/ppermute | solution.py:195
  220.0 25.0 %collective-permute-start.39 = (bf16[128,3584]{1,0:T(8,128)(2,1)S(1)}, bf16[128,3584]{1,0:T(8,128)(2,1)S(1)}, u32[]{:S(2)}, u32[]{:S(2)}) collective-permute-start(bf16[128,3584]{1,0:T(8,128)(2,1)S(1)} %collective-permute-done.32), channel_id=1, source_target_pairs={{4,0},{8,4},{12,8},{5,1},{9,5},{13,9},{6,2},{10,6},{14,10},{7,3},{... | collective-permute-start | bytes 2752520 | tf_op jit(solution)/shard_map/ppermute | solution.py:24
  221.3 24.9 %collective-permute-start.40 = (bf16[128,3584]{1,0:T(8,128)(2,1)S(1)}, bf16[128,3584]{1,0:T(8,128)(2,1)S(1)}, u32[]{:S(2)}, u32[]{:S(2)}) collective-permute-start(bf16[128,3584]{1,0:T(8,128)(2,1)S(1)} %collective-permute-done.33), channel_id=1, source_target_pairs={{0,4},{4,8},{8,12},{1,5},{5,9},{9,13},{2,6},{6,10},{10,14},{3,7},{... | collective-permute-start | bytes 2752520 | tf_op jit(solution)/shard_map/ppermute | solution.py:24
  249.2 9.9 %collective-permute-start.35 = (bf16[128,1024]{1,0:T(8,128)(2,1)S(1)}, bf16[128,1024]{1,0:T(8,128)(2,1)S(1)}, u32[]{:S(2)}, u32[]{:S(2)}) collective-permute-start(bf16[128,1024]{1,0:T(8,128)(2,1)S(1)} %fusion.51), channel_id=1, source_target_pairs={{0,2},{3,1},{4,6},{7,5},{8,10},{11,9},{12,14},{15,13},{16,18},{19,... | collective-permute-start | bytes 786440 | tf_op jit(solution)/shard_map/ppermute | solution.py:191
  250.7 10.8 %collective-permute-start.42 = (bf16[128,1024]{1,0:T(8,128)(2,1)S(1)}, bf16[128,1024]{1,0:T(8,128)(2,1)S(1)}, u32[]{:S(2)}, u32[]{:S(2)}) collective-permute-start(bf16[128,1024]{1,0:T(8,128)(2,1)S(1)} %fusion.52), channel_id=1, source_target_pairs={{1,3},{2,0},{5,7},{6,4},{9,11},{10,8},{13,15},{14,12},{17,19},{18,... | collective-permute-start | bytes 786440 | tf_op jit(solution)/shard_map/ppermute | solution.py:191
  259.2 9.2 %collective-permute-start.46 = (f32[128]{0:T(128)S(1)}, f32[128]{0:T(128)S(1)}, u32[]{:S(2)}, u32[]{:S(2)}) collective-permute-start(f32[128]{0:T(128)S(1)} %get-tuple-element.76), channel_id=1, source_target_pairs={{0,4},{4,0},{8,12},{12,8},{1,5},{5,1},{9,13},{13,9},{2,6},{6,2},{1... | collective-permute-start | bytes 1544 | tf_op jit(solution)/shard_map/ppermute | solution.py:225
  260.7 9.0 %collective-permute-start.47 = (f32[128]{0:T(128)S(1)}, f32[128]{0:T(128)S(1)}, u32[]{:S(2)}, u32[]{:S(2)}) collective-permute-start(f32[128]{0:T(128)S(1)} %get-tuple-element.76), channel_id=1, source_target_pairs={{0,8},{4,12},{8,0},{12,4},{1,9},{5,13},{9,1},{13,5},{2,10},{6,14},... | collective-permute-start | bytes 1544 | tf_op jit(solution)/shard_map/ppermute | solution.py:225
  261.5 8.9 %collective-permute-start.48 = (f32[128]{0:T(128)S(1)}, f32[128]{0:T(128)S(1)}, u32[]{:S(2)}, u32[]{:S(2)}) collective-permute-start(f32[128]{0:T(128)S(1)} %get-tuple-element.76), channel_id=1, source_target_pairs={{0,12},{4,8},{8,4},{12,0},{1,13},{5,9},{9,5},{13,1},{2,14},{6,10},... | collective-permute-start | bytes 1544 | tf_op jit(solution)/shard_map/ppermute | solution.py:225
  263.8 9.2 %collective-permute-start.50 = (bf16[128,1024]{1,0:T(8,128)(2,1)S(1)}, bf16[128,1024]{1,0:T(8,128)(2,1)S(1)}, u32[]{:S(2)}, u32[]{:S(2)}) collective-permute-start(bf16[128,1024]{1,0:T(8,128)(2,1)S(1)} %add_convert_fusion.2), channel_id=1, source_target_pairs={{2,4},{6,9},{10,6},{14,11},{18,20},{22,25},{26,22},{30,27}} | collective-permute-start | bytes 786440 | tf_op jit(solution)/shard_map/ppermute | solution.py:195
  266.5 14.1 %collective-permute-start.36 = (bf16[128,1024]{1,0:T(8,128)(2,1)S(1)}, bf16[128,1024]{1,0:T(8,128)(2,1)S(1)}, u32[]{:S(2)}, u32[]{:S(2)}) collective-permute-start(bf16[128,1024]{1,0:T(8,128)(2,1)S(1)} %add_convert_fusion.1), channel_id=1, source_target_pairs={{2,8},{6,13},{10,2},{14,7},{18,24},{22,29},{26,18},{30,23}} | collective-permute-start | bytes 786440 | tf_op jit(solution)/shard_map/ppermute | solution.py:195
  268.4 12.4 %collective-permute-start.51 = (bf16[128,1024]{1,0:T(8,128)(2,1)S(1)}, bf16[128,1024]{1,0:T(8,128)(2,1)S(1)}, u32[]{:S(2)}, u32[]{:S(2)}) collective-permute-start(bf16[128,1024]{1,0:T(8,128)(2,1)S(1)} %add_convert_fusion.1), channel_id=1, source_target_pairs={{1,8},{5,13},{9,2},{13,7},{17,24},{21,29},{25,18},{29,23}} | collective-permute-start | bytes 786440 | tf_op jit(solution)/shard_map/ppermute | solution.py:195
  269.7 11.1 %collective-permute-start.43 = (bf16[128,1024]{1,0:T(8,128)(2,1)S(1)}, bf16[128,1024]{1,0:T(8,128)(2,1)S(1)}, u32[]{:S(2)}, u32[]{:S(2)}) collective-permute-start(bf16[128,1024]{1,0:T(8,128)(2,1)S(1)} %add_convert_fusion), channel_id=1, source_target_pairs={{3,12},{7,1},{11,14},{15,3},{19,28},{23,17},{27,30},{31,19}} | collective-permute-start | bytes 786440 | tf_op jit(solution)/shard_map/ppermute | solution.py:195
  270.4 10.4 %collective-permute-start.52 = (bf16[128,1024]{1,0:T(8,128)(2,1)S(1)}, bf16[128,1024]{1,0:T(8,128)(2,1)S(1)}, u32[]{:S(2)}, u32[]{:S(2)}) collective-permute-start(bf16[128,1024]{1,0:T(8,128)(2,1)S(1)} %add_convert_fusion), channel_id=1, source_target_pairs={{0,12},{4,1},{8,14},{12,3},{16,28},{20,17},{24,30},{28,19}} | collective-permute-start | bytes 786440 | tf_op jit(solution)/shard_map/ppermute | solution.py:195
  (12 other events, 99.2 us)

commit v10 on v9

--- a/solution.py
+++ b/solution.py
@@ -146,23 +146,29 @@
     both = swapped(jnp.stack([tile, across]), "pair")
     gain = lax.dynamic_slice_in_dim(norm_gain, z * d_ctx, d_ctx, 0)
     resid = jnp.stack([tile, both[0], across, both[1]]).astype(F32)
-    scaled = (resid * gain).astype(BF16).reshape(4 * rows, d_ctx)
-
-    def projected(w):
-        return jnp.dot(scaled, w, preferred_element_type=F32).astype(BF16).reshape(4, rows, ff)
-
-    parts = [projected(w_gate)]
+    scaled = (resid * gain).astype(BF16)
+    scaled = scaled.reshape(4, rows, d_ctx)
+
+    def projected(blocks, w):
+        return jnp.dot(blocks, w, preferred_element_type=F32).astype(BF16)
+
+    farthest = picked(scaled, jnp.where(low, 3, 0) ^ hp)
     came = [None, None]
     for s in range(3):
-        for i in range(2):
-            if s == 0 and i == 1:
-                scaled, _ = lax.optimization_barrier((scaled, right))
-                parts.append(projected(w_up))
-            if s > 0:
+        for i, w in enumerate((w_gate, w_up)):
+            if s == 0:
+                if i == 1:
+                    farthest, scaled, _ = lax.optimization_barrier((farthest, scaled, right))
+                right = left = projected(farthest, w)
+            else:
+                if (s, i) == (1, 0):
+                    scaled, _ = lax.optimization_barrier((scaled, right))
+                    blocks = scaled.reshape(4 * rows, d_ctx)
+                    parts = [projected(blocks, v).reshape(4, rows, ff) for v in (w_gate, w_up)]
+                    came[0], parts[1] = lax.optimization_barrier((came[0], parts[1]))
                 came[i], _ = lax.optimization_barrier((came[i], (left, right)))
-            right = picked(parts[i], jnp.clip(3 - s + z, 0, 3) ^ hp)
-            left = picked(parts[i], jnp.clip(s - 3 + z, 0, 3) ^ hp)
-            if s > 0:
+                right = picked(parts[i], jnp.clip(3 - s + z, 0, 3) ^ hp)
+                left = picked(parts[i], jnp.clip(s - 3 + z, 0, 3) ^ hp)
                 right = (right.astype(F32) + came[i][0].astype(F32)).astype(BF16)
                 left = (left.astype(F32) + came[i][1].astype(F32)).astype(BF16)
             right, left = lax.optimization_barrier((right, left))

time: 288 us -> 291 us (1.010)
  starting transfers between devices: 103 us -> 109 us
  waiting for transfers between devices: 140 us -> 136 us
    ppermute x27, starting transfers between devices: 69.6 us -> 74.7 us  [passed_along(): return lax.ppermute(block, axis, route)]
    ppermute x27, waiting for transfers between devices: 106 us -> 102 us  [passed_along(): return lax.ppermute(block, axis, route)]
  transfers between devices with their start and end apart: 53 -> 53, of which waited for: 30 -> 26; matrix products, arithmetic and copies ran while one was open for 8% -> 9% of each run, Pallas kernels for 0% -> 0%
where the time goes in v10:
time: 291 us; the launch traced here: 286 us
  waiting for transfers between devices  136 us (47%)
  starting transfers between devices  109 us (37%)
  matrix products  20.9 us (7%)
  other arithmetic  11.7 us (4%)
  between operations  4.79 us (2%)
  local copies, waits for them, and re-layouts  4.05 us (1%)
    ppermute x27, waiting for transfers between devices, passed_along(): return lax.ppermute(block, axis, route)  102 us
    ppermute x27, starting transfers between devices, passed_along(): return lax.ppermute(block, axis, route)  74.7 us
    ppermute x10, waiting for transfers between devices, swapped(): return lax.ppermute(block, axis, [(0, 1), (1, 0)])  11.3 us
    ppermute x4, starting transfers between devices, reduced(): lax.ppermute(half.astype(BF16), HP, route).astype(F32)  9.97 us
    ppermute x8, starting transfers between devices, brought_home(): lax.ppermute(whole, ('ctx',) + HP, [(4 * c + h, 4 * TURNS[c][k] + c) for...  9.91 us
    ppermute x4, waiting for transfers between devices, reduced(): lax.ppermute(half.astype(BF16), HP, route).astype(F32)  9.47 us
    ppermute x8, waiting for transfers between devices, brought_home(): lax.ppermute(whole, ('ctx',) + HP, [(4 * c + h, 4 * TURNS[c][k] + c) for...  7.77 us
  transfers between devices with their start and end apart: 53, of which 26 were waited for; matrix products, arithmetic and copies ran while one was open for 9% of the time, Pallas kernels for 0%

profile of v10, /device:TPU:2, one launch (start us, length us, event | category | flops | bytes accessed | tf_op | source)
XLA Modules:
  0.0 286.4 jit_solution(16190682740301751923)
XLA Ops:
  1.5 3.5 %collective-permute-start = (bf16[2,128,256]{2,1,0:T(8,128)(2,1)S(1)}, bf16[2,128,256]{2,1,0:T(8,128)(2,1)S(1)}, u32[]{:S(2)}, u32[]{:S(2)}) collective-permute-start(bf16[2,128,256]{2,1,0:T(8,128)(2,1)S(1)} %pad_maximum_fusion.3), channel_id=1, source_target_pairs={{0,4},{4,8},{8,12},{1,5},{5,9},{9,13},{2,6},{6,10},{10,14},{3,7},{... | collective-permute-start | bytes 393224 | tf_op jit(solution)/shard_map/ppermute | solution.py:24
  5.0 4.5 %collective-permute-start.1 = (bf16[2,128,256]{2,1,0:T(8,128)(2,1)S(1)}, bf16[2,128,256]{2,1,0:T(8,128)(2,1)S(1)}, u32[]{:S(2)}, u32[]{:S(2)}) collective-permute-start(bf16[2,128,256]{2,1,0:T(8,128)(2,1)S(1)} %pad_maximum_fusion.3), channel_id=1, source_target_pairs={{0,8},{4,12},{1,9},{5,13},{2,10},{6,14},{3,11},{7,15},{16,24},{20,... | collective-permute-start | bytes 393224 | tf_op jit(solution)/shard_map/ppermute | solution.py:24
  13.4 1.4 collective-permute-done.2
  18.8 3.9 %collective-permute-start.3 = (bf16[128,1024]{1,0:T(8,128)(2,1)S(1)}, bf16[128,1024]{1,0:T(8,128)(2,1)S(1)}, u32[]{:S(2)}, u32[]{:S(2)}) collective-permute-start(bf16[128,1024]{1,0:T(8,128)(2,1)S(1)} %get-tuple-element.95), channel_id=1, source_target_pairs={{0,0},{1,4},{2,8},{3,12},{4,1},{5,5},{6,9},{7,13},{8,2},{9,6},{10,... | collective-permute-start | bytes 786440 | tf_op jit(solution)/shard_map/ppermute | solution.py:34
  22.7 3.9 %collective-permute-start.4 = (f32[128]{0:T(128)S(1)}, f32[128]{0:T(128)S(1)}, u32[]{:S(2)}, u32[]{:S(2)}) collective-permute-start(f32[128]{0:T(128)S(1)} %get-tuple-element.94), channel_id=1, source_target_pairs={{0,1},{1,0},{2,3},{3,2},{4,5},{5,4},{6,7},{7,6},{8,9},{9,8},{10,11... | collective-permute-start | bytes 1544 | tf_op jit(solution)/shard_map/ppermute | solution.py:28
  27.5 3.6 %collective-permute-done.5 = f32[128]{0:T(128)S(1)} collective-permute-done((f32[128]{0:T(128)S(1)}, f32[128]{0:T(128)S(1)}, u32[]{:S(2)}, u32[]{:S(2)}) %collective-permute-start.5) | collective-permute-done | bytes 544 | tf_op jit(solution)/shard_map/ppermute | solution.py:28
  31.0 5.5 %collective-permute-done.3 = bf16[128,1024]{1,0:T(8,128)(2,1)S(1)} collective-permute-done((bf16[128,1024]{1,0:T(8,128)(2,1)S(1)}, bf16[128,1024]{1,0:T(8,128)(2,1)S(1)}, u32[]{:S(2)}, u32[]{:S(2)}) %collective-permute-start.3) | collective-permute-done | bytes 262176 | tf_op jit(solution)/shard_map/ppermute | solution.py:34
  36.5 6.4 %collective-permute-done.6 = bf16[128,1024]{1,0:T(8,128)(2,1)S(1)} collective-permute-done((bf16[128,1024]{1,0:T(8,128)(2,1)S(1)}, bf16[128,1024]{1,0:T(8,128)(2,1)S(1)}, u32[]{:S(2)}, u32[]{:S(2)}) %collective-permute-start.6) | collective-permute-done | bytes 262176 | tf_op jit(solution)/shard_map/ppermute | solution.py:28
  48.1 3.4 %collective-permute-start.8 = (bf16[128,1792]{1,0:T(8,128)(2,1)S(1)}, bf16[128,1792]{1,0:T(8,128)(2,1)S(1)}, u32[]{:S(2)}, u32[]{:S(2)}) collective-permute-start(bf16[128,1792]{1,0:T(8,128)(2,1)S(1)} %convolution_convert_fusion.3), channel_id=1, source_target_pairs={{0,4},{4,8},{8,12},{1,5},{5,9},{9,13},{2,6},{6,10},{10,14},{3,7},{... | collective-permute-start | bytes 1376264 | tf_op jit(solution)/shard_map/ppermute | solution.py:24
  52.2 1.9 collective-permute-start.12
  54.1 2.1 convolution_convert_fusion
  58.8 2.1 convolution_convert_fusion.1
  60.9 1.5 collective-permute-done.8
  62.4 9.2 %collective-permute-done.9 = bf16[128,1792]{1,0:T(8,128)(2,1)S(1)} collective-permute-done((bf16[128,1792]{1,0:T(8,128)(2,1)S(1)}, bf16[128,1792]{1,0:T(8,128)(2,1)S(1)}, u32[]{:S(2)}, u32[]{:S(2)}) %collective-permute-start.9) | collective-permute-done | bytes 458784 | tf_op jit(solution)/shard_map/ppermute | solution.py:24
  71.8 3.9 %collective-permute-start.10 = (bf16[128,1792]{1,0:T(8,128)(2,1)S(1)}, bf16[128,1792]{1,0:T(8,128)(2,1)S(1)}, u32[]{:S(2)}, u32[]{:S(2)}) collective-permute-start(bf16[128,1792]{1,0:T(8,128)(2,1)S(1)} %get-tuple-element.57), channel_id=1, source_target_pairs={{0,4},{4,8},{8,12},{1,5},{5,9},{9,13},{2,6},{6,10},{10,14},{3,7},{... | collective-permute-start | bytes 1376264 | tf_op jit(solution)/shard_map/ppermute | solution.py:24
  77.1 4.3 %collective-permute-done.13 = bf16[128,1792]{1,0:T(8,128)(2,1)S(1)} collective-permute-done((bf16[128,1792]{1,0:T(8,128)(2,1)S(1)}, bf16[128,1792]{1,0:T(8,128)(2,1)S(1)}, u32[]{:S(2)}, u32[]{:S(2)}) %collective-permute-start.13) | collective-permute-done | bytes 458784 | tf_op jit(solution)/shard_map/ppermute | solution.py:24
  81.7 3.9 %collective-permute-start.16 = (bf16[128,1792]{1,0:T(8,128)(2,1)S(1)}, bf16[128,1792]{1,0:T(8,128)(2,1)S(1)}, u32[]{:S(2)}, u32[]{:S(2)}) collective-permute-start(bf16[128,1792]{1,0:T(8,128)(2,1)S(1)} %get-tuple-element.63), channel_id=1, source_target_pairs={{0,4},{4,8},{8,12},{1,5},{5,9},{9,13},{2,6},{6,10},{10,14},{3,7},{... | collective-permute-start | bytes 1376264 | tf_op jit(solution)/shard_map/ppermute | solution.py:24
  86.9 4.3 %collective-permute-done.11 = bf16[128,1792]{1,0:T(8,128)(2,1)S(1)} collective-permute-done((bf16[128,1792]{1,0:T(8,128)(2,1)S(1)}, bf16[128,1792]{1,0:T(8,128)(2,1)S(1)}, u32[]{:S(2)}, u32[]{:S(2)}) %collective-permute-start.11) | collective-permute-done | bytes 458784 | tf_op jit(solution)/shard_map/ppermute | solution.py:24
  91.5 3.9 %collective-permute-start.14 = (bf16[128,1792]{1,0:T(8,128)(2,1)S(1)}, bf16[128,1792]{1,0:T(8,128)(2,1)S(1)}, u32[]{:S(2)}, u32[]{:S(2)}) collective-permute-start(bf16[128,1792]{1,0:T(8,128)(2,1)S(1)} %get-tuple-element.66), channel_id=1, source_target_pairs={{0,4},{4,8},{8,12},{1,5},{5,9},{9,13},{2,6},{6,10},{10,14},{3,7},{... | collective-permute-start | bytes 1376264 | tf_op jit(solution)/shard_map/ppermute | solution.py:24
  96.7 4.3 %collective-permute-done.17 = bf16[128,1792]{1,0:T(8,128)(2,1)S(1)} collective-permute-done((bf16[128,1792]{1,0:T(8,128)(2,1)S(1)}, bf16[128,1792]{1,0:T(8,128)(2,1)S(1)}, u32[]{:S(2)}, u32[]{:S(2)}) %collective-permute-start.17) | collective-permute-done | bytes 458784 | tf_op jit(solution)/shard_map/ppermute | solution.py:24
  101.3 4.1 %collective-permute-start.18 = (bf16[128,1792]{1,0:T(8,128)(2,1)S(1)}, bf16[128,1792]{1,0:T(8,128)(2,1)S(1)}, u32[]{:S(2)}, u32[]{:S(2)}) collective-permute-start(bf16[128,1792]{1,0:T(8,128)(2,1)S(1)} %get-tuple-element.71), channel_id=1, source_target_pairs={{0,4},{4,8},{8,12},{1,5},{5,9},{9,13},{2,6},{6,10},{10,14},{3,7},{... | collective-permute-start | bytes 1376264 | tf_op jit(solution)/shard_map/ppermute | solution.py:24
  105.4 1.5 collective-permute-start.19
  106.9 4.0 %collective-permute-done.15 = bf16[128,1792]{1,0:T(8,128)(2,1)S(1)} collective-permute-done((bf16[128,1792]{1,0:T(8,128)(2,1)S(1)}, bf16[128,1792]{1,0:T(8,128)(2,1)S(1)}, u32[]{:S(2)}, u32[]{:S(2)}) %collective-permute-start.15) | collective-permute-done | bytes 458784 | tf_op jit(solution)/shard_map/ppermute | solution.py:24
  112.4 7.5 %collective-permute-done.19 = bf16[128,1792]{1,0:T(8,128)(2,1)S(1)} collective-permute-done((bf16[128,1792]{1,0:T(8,128)(2,1)S(1)}, bf16[128,1792]{1,0:T(8,128)(2,1)S(1)}, u32[]{:S(2)}, u32[]{:S(2)}) %collective-permute-start.19) | collective-permute-done | bytes 458784 | tf_op jit(solution)/shard_map/ppermute | solution.py:24
  124.2 1.3 select_convert_fusion.3
  129.2 4.6 %collective-permute-start.26 = (bf16[128,3584]{1,0:T(8,128)(2,1)S(1)}, bf16[128,3584]{1,0:T(8,128)(2,1)S(1)}, u32[]{:S(2)}, u32[]{:S(2)}) collective-permute-start(bf16[128,3584]{1,0:T(8,128)(2,1)S(1)} %pad_maximum_fusion), channel_id=1, source_target_pairs={{0,4},{4,8},{8,12},{1,5},{5,9},{9,13},{2,6},{6,10},{10,14},{3,7},{... | collective-permute-start | bytes 2752520 | tf_op jit(solution)/shard_map/ppermute | solution.py:24
  135.1 4.6 %collective-permute-start.24 = (bf16[128,1792]{1,0:T(8,128)(2,1)S(1)}, bf16[128,1792]{1,0:T(8,128)(2,1)S(1)}, u32[]{:S(2)}, u32[]{:S(2)}) collective-permute-start(bf16[128,1792]{1,0:T(8,128)(2,1)S(1)} %get-tuple-element.73), channel_id=1, source_target_pairs={{0,4},{4,8},{8,12},{1,5},{5,9},{9,13},{2,6},{6,10},{10,14},{3,7},{... | collective-permute-start | bytes 1376264 | tf_op jit(solution)/shard_map/ppermute | solution.py:24
  139.9 2.9 %collective-permute-start.21 = (bf16[128,1024]{1,0:T(8,128)(2,1)S(1)}, bf16[128,1024]{1,0:T(8,128)(2,1)S(1)}, u32[]{:S(2)}, u32[]{:S(2)}) collective-permute-start(bf16[128,1024]{1,0:T(8,128)(2,1)S(1)} %fusion.48), channel_id=1, source_target_pairs={{2,0},{1,3},{6,4},{5,7},{10,8},{9,11},{14,12},{13,15},{18,16},{17,... | collective-permute-start | bytes 786440 | tf_op jit(solution)/shard_map/ppermute | solution.py:197
  142.8 18.8 %collective-permute-done.23 = bf16[128,1792]{1,0:T(8,128)(2,1)S(1)} collective-permute-done((bf16[128,1792]{1,0:T(8,128)(2,1)S(1)}, bf16[128,1792]{1,0:T(8,128)(2,1)S(1)}, u32[]{:S(2)}, u32[]{:S(2)}) %collective-permute-start.23) | collective-permute-done | bytes 458784 | tf_op jit(solution)/shard_map/ppermute | solution.py:24
  162.9 4.6 %collective-permute-start.31 = (bf16[128,1792]{1,0:T(8,128)(2,1)S(1)}, bf16[128,1792]{1,0:T(8,128)(2,1)S(1)}, u32[]{:S(2)}, u32[]{:S(2)}) collective-permute-start(bf16[128,1792]{1,0:T(8,128)(2,1)S(1)} %collective-permute-done.24), channel_id=1, source_target_pairs={{0,4},{4,8},{8,12},{1,5},{5,9},{9,13},{2,6},{6,10},{10,14},{3,7},{... | collective-permute-start | bytes 1376264 | tf_op jit(solution)/shard_map/ppermute | solution.py:24
  169.1 5.8 %collective-permute-done.30 = bf16[128,1792]{1,0:T(8,128)(2,1)S(1)} collective-permute-done((bf16[128,1792]{1,0:T(8,128)(2,1)S(1)}, bf16[128,1792]{1,0:T(8,128)(2,1)S(1)}, u32[]{:S(2)}, u32[]{:S(2)}) %collective-permute-start.30) | collective-permute-done | bytes 458784 | tf_op jit(solution)/shard_map/ppermute | solution.py:24
  177.4 1.3 select_convert_fusion.2
  181.5 5.7 %collective-permute-start.38 = (bf16[128,1792]{1,0:T(8,128)(2,1)S(1)}, bf16[128,1792]{1,0:T(8,128)(2,1)S(1)}, u32[]{:S(2)}, u32[]{:S(2)}) collective-permute-start(bf16[128,1792]{1,0:T(8,128)(2,1)S(1)} %collective-permute-done.31), channel_id=1, source_target_pairs={{0,4},{4,8},{8,12},{1,5},{5,9},{9,13},{2,6},{6,10},{10,14},{3,7},{... | collective-permute-start | bytes 1376264 | tf_op jit(solution)/shard_map/ppermute | solution.py:24
  187.8 3.9 %collective-permute-start.33 = (bf16[128,3584]{1,0:T(8,128)(2,1)S(1)}, bf16[128,3584]{1,0:T(8,128)(2,1)S(1)}, u32[]{:S(2)}, u32[]{:S(2)}) collective-permute-start(bf16[128,3584]{1,0:T(8,128)(2,1)S(1)} %collective-permute-done.26), channel_id=1, source_target_pairs={{0,4},{4,8},{8,12},{1,5},{5,9},{9,13},{2,6},{6,10},{10,14},{3,7},{... | collective-permute-start | bytes 2752520 | tf_op jit(solution)/shard_map/ppermute | solution.py:24
  191.9 22.2 %collective-permute-done.37 = bf16[128,1792]{1,0:T(8,128)(2,1)S(1)} collective-permute-done((bf16[128,1792]{1,0:T(8,128)(2,1)S(1)}, bf16[128,1792]{1,0:T(8,128)(2,1)S(1)}, u32[]{:S(2)}, u32[]{:S(2)}) %collective-permute-start.37) | collective-permute-done | bytes 458784 | tf_op jit(solution)/shard_map/ppermute | solution.py:24
  216.8 6.2 %collective-permute-done.28 = bf16[128,1024]{1,0:T(8,128)(2,1)S(1)} collective-permute-done((bf16[128,1024]{1,0:T(8,128)(2,1)S(1)}, bf16[128,1024]{1,0:T(8,128)(2,1)S(1)}, u32[]{:S(2)}, u32[]{:S(2)}) %collective-permute-start.28) | collective-permute-done | bytes 262176 | tf_op jit(solution)/shard_map/ppermute | solution.py:197
  225.2 5.2 %collective-permute-start.40 = (bf16[128,3584]{1,0:T(8,128)(2,1)S(1)}, bf16[128,3584]{1,0:T(8,128)(2,1)S(1)}, u32[]{:S(2)}, u32[]{:S(2)}) collective-permute-start(bf16[128,3584]{1,0:T(8,128)(2,1)S(1)} %collective-permute-done.33), channel_id=1, source_target_pairs={{0,4},{4,8},{8,12},{1,5},{5,9},{9,13},{2,6},{6,10},{10,14},{3,7},{... | collective-permute-start | bytes 2752520 | tf_op jit(solution)/shard_map/ppermute | solution.py:24
  231.8 1.3 select_convert_fusion.1
  233.1 15.1 %collective-permute-done.39 = bf16[128,3584]{1,0:T(8,128)(2,1)S(1)} collective-permute-done((bf16[128,3584]{1,0:T(8,128)(2,1)S(1)}, bf16[128,3584]{1,0:T(8,128)(2,1)S(1)}, u32[]{:S(2)}, u32[]{:S(2)}) %collective-permute-start.39) | collective-permute-done | bytes 917536 | tf_op jit(solution)/shard_map/ppermute | solution.py:24
  249.6 1.3 fusion.31
  250.9 1.3 select_convert_fusion
  253.9 4.5 %collective-permute-start.42 = (bf16[128,1024]{1,0:T(8,128)(2,1)S(1)}, bf16[128,1024]{1,0:T(8,128)(2,1)S(1)}, u32[]{:S(2)}, u32[]{:S(2)}) collective-permute-start(bf16[128,1024]{1,0:T(8,128)(2,1)S(1)} %fusion.51), channel_id=1, source_target_pairs={{1,3},{2,0},{5,7},{6,4},{9,11},{10,8},{13,15},{14,12},{17,19},{18,... | collective-permute-start | bytes 786440 | tf_op jit(solution)/shard_map/ppermute | solution.py:197
  258.4 3.2 %collective-permute-done.35 = bf16[128,1024]{1,0:T(8,128)(2,1)S(1)} collective-permute-done((bf16[128,1024]{1,0:T(8,128)(2,1)S(1)}, bf16[128,1024]{1,0:T(8,128)(2,1)S(1)}, u32[]{:S(2)}, u32[]{:S(2)}) %collective-permute-start.35) | collective-permute-done | bytes 262176 | tf_op jit(solution)/shard_map/ppermute | solution.py:197
  261.7 1.6 collective-permute-start.46
  264.0 2.2 collective-permute-start.48
  266.3 3.3 %collective-permute-start.50 = (bf16[128,1024]{1,0:T(8,128)(2,1)S(1)}, bf16[128,1024]{1,0:T(8,128)(2,1)S(1)}, u32[]{:S(2)}, u32[]{:S(2)}) collective-permute-start(bf16[128,1024]{1,0:T(8,128)(2,1)S(1)} %add_convert_fusion.2), channel_id=1, source_target_pairs={{2,4},{6,9},{10,6},{14,11},{18,20},{22,25},{26,22},{30,27}} | collective-permute-start | bytes 786440 | tf_op jit(solution)/shard_map/ppermute | solution.py:201
  269.7 1.9 collective-permute-start.36
  276.2 6.9 %collective-permute-done.36 = bf16[128,1024]{1,0:T(8,128)(2,1)S(1)} collective-permute-done((bf16[128,1024]{1,0:T(8,128)(2,1)S(1)}, bf16[128,1024]{1,0:T(8,128)(2,1)S(1)}, u32[]{:S(2)}, u32[]{:S(2)}) %collective-permute-start.36) | collective-permute-done | bytes 262176 | tf_op jit(solution)/shard_map/ppermute | solution.py:201
  (150 shorter events, 57.2 us)
Async XLA Ops:
  1.5 11.6 %collective-permute-start = (bf16[2,128,256]{2,1,0:T(8,128)(2,1)S(1)}, bf16[2,128,256]{2,1,0:T(8,128)(2,1)S(1)}, u32[]{:S(2)}, u32[]{:S(2)}) collective-permute-start(bf16[2,128,256]{2,1,0:T(8,128)(2,1)S(1)} %pad_maximum_fusion.3), channel_id=1, source_target_pairs={{0,4},{4,8},{8,12},{1,5},{5,9},{9,13},{2,6},{6,10},{10,14},{3,7},{... | collective-permute-start | bytes 393224 | tf_op jit(solution)/shard_map/ppermute | solution.py:24
  5.0 8.4 %collective-permute-start.1 = (bf16[2,128,256]{2,1,0:T(8,128)(2,1)S(1)}, bf16[2,128,256]{2,1,0:T(8,128)(2,1)S(1)}, u32[]{:S(2)}, u32[]{:S(2)}) collective-permute-start(bf16[2,128,256]{2,1,0:T(8,128)(2,1)S(1)} %pad_maximum_fusion.3), channel_id=1, source_target_pairs={{0,8},{4,12},{1,9},{5,13},{2,10},{6,14},{3,11},{7,15},{16,24},{20,... | collective-permute-start | bytes 393224 | tf_op jit(solution)/shard_map/ppermute | solution.py:24
  9.5 5.3 %collective-permute-start.2 = (bf16[2,128,256]{2,1,0:T(8,128)(2,1)S(1)}, bf16[2,128,256]{2,1,0:T(8,128)(2,1)S(1)}, u32[]{:S(2)}, u32[]{:S(2)}) collective-permute-start(bf16[2,128,256]{2,1,0:T(8,128)(2,1)S(1)} %pad_maximum_fusion.3), channel_id=1, source_target_pairs={{0,12},{1,13},{2,14},{3,15},{16,28},{17,29},{18,30},{19,31}} | collective-permute-start | bytes 393224 | tf_op jit(solution)/shard_map/ppermute | solution.py:24
  18.8 17.7 %collective-permute-start.3 = (bf16[128,1024]{1,0:T(8,128)(2,1)S(1)}, bf16[128,1024]{1,0:T(8,128)(2,1)S(1)}, u32[]{:S(2)}, u32[]{:S(2)}) collective-permute-start(bf16[128,1024]{1,0:T(8,128)(2,1)S(1)} %get-tuple-element.95), channel_id=1, source_target_pairs={{0,0},{1,4},{2,8},{3,12},{4,1},{5,5},{6,9},{7,13},{8,2},{9,6},{10,... | collective-permute-start | bytes 786440 | tf_op jit(solution)/shard_map/ppermute | solution.py:34
  22.7 4.8 %collective-permute-start.4 = (f32[128]{0:T(128)S(1)}, f32[128]{0:T(128)S(1)}, u32[]{:S(2)}, u32[]{:S(2)}) collective-permute-start(f32[128]{0:T(128)S(1)} %get-tuple-element.94), channel_id=1, source_target_pairs={{0,1},{1,0},{2,3},{3,2},{4,5},{5,4},{6,7},{7,6},{8,9},{9,8},{10,11... | collective-permute-start | bytes 1544 | tf_op jit(solution)/shard_map/ppermute | solution.py:28
  36.5 6.4 %collective-permute-start.6 = (bf16[128,1024]{1,0:T(8,128)(2,1)S(1)}, bf16[128,1024]{1,0:T(8,128)(2,1)S(1)}, u32[]{:S(2)}, u32[]{:S(2)}) collective-permute-start(bf16[128,1024]{1,0:T(8,128)(2,1)S(1)} %collective-permute-done.3), channel_id=1, source_target_pairs={{0,2},{2,0},{1,3},{3,1},{4,6},{6,4},{5,7},{7,5},{8,10},{10,8},{9,1... | collective-permute-start | bytes 786440 | tf_op jit(solution)/shard_map/ppermute | solution.py:28
  48.1 14.3 %collective-permute-start.8 = (bf16[128,1792]{1,0:T(8,128)(2,1)S(1)}, bf16[128,1792]{1,0:T(8,128)(2,1)S(1)}, u32[]{:S(2)}, u32[]{:S(2)}) collective-permute-start(bf16[128,1792]{1,0:T(8,128)(2,1)S(1)} %convolution_convert_fusion.3), channel_id=1, source_target_pairs={{0,4},{4,8},{8,12},{1,5},{5,9},{9,13},{2,6},{6,10},{10,14},{3,7},{... | collective-permute-start | bytes 1376264 | tf_op jit(solution)/shard_map/ppermute | solution.py:24
  52.2 24.9 %collective-permute-start.12 = (bf16[128,1792]{1,0:T(8,128)(2,1)S(1)}, bf16[128,1792]{1,0:T(8,128)(2,1)S(1)}, u32[]{:S(2)}, u32[]{:S(2)}) collective-permute-start(bf16[128,1792]{1,0:T(8,128)(2,1)S(1)} %convolution_convert_fusion.2), channel_id=1, source_target_pairs={{0,4},{4,8},{8,12},{1,5},{5,9},{9,13},{2,6},{6,10},{10,14},{3,7},{... | collective-permute-start | bytes 1376264 | tf_op jit(solution)/shard_map/ppermute | solution.py:24
  56.2 15.3 %collective-permute-start.9 = (bf16[128,1792]{1,0:T(8,128)(2,1)S(1)}, bf16[128,1792]{1,0:T(8,128)(2,1)S(1)}, u32[]{:S(2)}, u32[]{:S(2)}) collective-permute-start(bf16[128,1792]{1,0:T(8,128)(2,1)S(1)} %convolution_convert_fusion.3), channel_id=1, source_target_pairs={{4,0},{8,4},{12,8},{5,1},{9,5},{13,9},{6,2},{10,6},{14,10},{7,3},{... | collective-permute-start | bytes 1376264 | tf_op jit(solution)/shard_map/ppermute | solution.py:24
  57.5 23.9 %collective-permute-start.13 = (bf16[128,1792]{1,0:T(8,128)(2,1)S(1)}, bf16[128,1792]{1,0:T(8,128)(2,1)S(1)}, u32[]{:S(2)}, u32[]{:S(2)}) collective-permute-start(bf16[128,1792]{1,0:T(8,128)(2,1)S(1)} %convolution_convert_fusion.2), channel_id=1, source_target_pairs={{4,0},{8,4},{12,8},{5,1},{9,5},{13,9},{6,2},{10,6},{14,10},{7,3},{... | collective-permute-start | bytes 1376264 | tf_op jit(solution)/shard_map/ppermute | solution.py:24
  71.8 15.1 %collective-permute-start.10 = (bf16[128,1792]{1,0:T(8,128)(2,1)S(1)}, bf16[128,1792]{1,0:T(8,128)(2,1)S(1)}, u32[]{:S(2)}, u32[]{:S(2)}) collective-permute-start(bf16[128,1792]{1,0:T(8,128)(2,1)S(1)} %get-tuple-element.57), channel_id=1, source_target_pairs={{0,4},{4,8},{8,12},{1,5},{5,9},{9,13},{2,6},{6,10},{10,14},{3,7},{... | collective-permute-start | bytes 1376264 | tf_op jit(solution)/shard_map/ppermute | solution.py:24
  75.8 15.5 %collective-permute-start.11 = (bf16[128,1792]{1,0:T(8,128)(2,1)S(1)}, bf16[128,1792]{1,0:T(8,128)(2,1)S(1)}, u32[]{:S(2)}, u32[]{:S(2)}) collective-permute-start(bf16[128,1792]{1,0:T(8,128)(2,1)S(1)} %get-tuple-element.58), channel_id=1, source_target_pairs={{4,0},{8,4},{12,8},{5,1},{9,5},{13,9},{6,2},{10,6},{14,10},{7,3},{... | collective-permute-start | bytes 1376264 | tf_op jit(solution)/shard_map/ppermute | solution.py:24
  81.7 15.1 %collective-permute-start.16 = (bf16[128,1792]{1,0:T(8,128)(2,1)S(1)}, bf16[128,1792]{1,0:T(8,128)(2,1)S(1)}, u32[]{:S(2)}, u32[]{:S(2)}) collective-permute-start(bf16[128,1792]{1,0:T(8,128)(2,1)S(1)} %get-tuple-element.63), channel_id=1, source_target_pairs={{0,4},{4,8},{8,12},{1,5},{5,9},{9,13},{2,6},{6,10},{10,14},{3,7},{... | collective-permute-start | bytes 1376264 | tf_op jit(solution)/shard_map/ppermute | solution.py:24
  85.6 15.5 %collective-permute-start.17 = (bf16[128,1792]{1,0:T(8,128)(2,1)S(1)}, bf16[128,1792]{1,0:T(8,128)(2,1)S(1)}, u32[]{:S(2)}, u32[]{:S(2)}) collective-permute-start(bf16[128,1792]{1,0:T(8,128)(2,1)S(1)} %get-tuple-element.62), channel_id=1, source_target_pairs={{4,0},{8,4},{12,8},{5,1},{9,5},{13,9},{6,2},{10,6},{14,10},{7,3},{... | collective-permute-start | bytes 1376264 | tf_op jit(solution)/shard_map/ppermute | solution.py:24
  91.5 15.4 %collective-permute-start.14 = (bf16[128,1792]{1,0:T(8,128)(2,1)S(1)}, bf16[128,1792]{1,0:T(8,128)(2,1)S(1)}, u32[]{:S(2)}, u32[]{:S(2)}) collective-permute-start(bf16[128,1792]{1,0:T(8,128)(2,1)S(1)} %get-tuple-element.66), channel_id=1, source_target_pairs={{0,4},{4,8},{8,12},{1,5},{5,9},{9,13},{2,6},{6,10},{10,14},{3,7},{... | collective-permute-start | bytes 1376264 | tf_op jit(solution)/shard_map/ppermute | solution.py:24
  95.4 15.5 %collective-permute-start.15 = (bf16[128,1792]{1,0:T(8,128)(2,1)S(1)}, bf16[128,1792]{1,0:T(8,128)(2,1)S(1)}, u32[]{:S(2)}, u32[]{:S(2)}) collective-permute-start(bf16[128,1792]{1,0:T(8,128)(2,1)S(1)} %get-tuple-element.67), channel_id=1, source_target_pairs={{4,0},{8,4},{12,8},{5,1},{9,5},{13,9},{6,2},{10,6},{14,10},{7,3},{... | collective-permute-start | bytes 1376264 | tf_op jit(solution)/shard_map/ppermute | solution.py:24
  101.3 11.1 %collective-permute-start.18 = (bf16[128,1792]{1,0:T(8,128)(2,1)S(1)}, bf16[128,1792]{1,0:T(8,128)(2,1)S(1)}, u32[]{:S(2)}, u32[]{:S(2)}) collective-permute-start(bf16[128,1792]{1,0:T(8,128)(2,1)S(1)} %get-tuple-element.71), channel_id=1, source_target_pairs={{0,4},{4,8},{8,12},{1,5},{5,9},{9,13},{2,6},{6,10},{10,14},{3,7},{... | collective-permute-start | bytes 1376264 | tf_op jit(solution)/shard_map/ppermute | solution.py:24
  105.4 14.5 %collective-permute-start.19 = (bf16[128,1792]{1,0:T(8,128)(2,1)S(1)}, bf16[128,1792]{1,0:T(8,128)(2,1)S(1)}, u32[]{:S(2)}, u32[]{:S(2)}) collective-permute-start(bf16[128,1792]{1,0:T(8,128)(2,1)S(1)} %get-tuple-element.72), channel_id=1, source_target_pairs={{4,0},{8,4},{12,8},{5,1},{9,5},{13,9},{6,2},{10,6},{14,10},{7,3},{... | collective-permute-start | bytes 1376264 | tf_op jit(solution)/shard_map/ppermute | solution.py:24
  125.5 14.2 %collective-permute-start.20 = (bf16[128,1024]{1,0:T(8,128)(2,1)S(1)}, bf16[128,1024]{1,0:T(8,128)(2,1)S(1)}, u32[]{:S(2)}, u32[]{:S(2)}) collective-permute-start(bf16[128,1024]{1,0:T(8,128)(2,1)S(1)} %get-tuple-element.127), channel_id=1, source_target_pairs={{0,1},{1,0},{2,3},{3,2},{4,5},{5,4},{6,7},{7,6},{8,9},{9,8},{10,11... | collective-permute-start | bytes 786440 | tf_op jit(solution)/shard_map/ppermute | solution.py:28
  126.8 8.3 %collective-permute-start.45 = (f32[256]{0:T(256)S(1)}, f32[256]{0:T(256)S(1)}, u32[]{:S(2)}, u32[]{:S(2)}) collective-permute-start(f32[256]{0:T(256)S(1)} %fusion.104), channel_id=1, source_target_pairs={{0,2},{2,0},{1,3},{3,1},{4,6},{6,4},{5,7},{7,5},{8,10},{10,8},{9,1... | collective-permute-start | bytes 3080 | tf_op jit(solution)/shard_map/ppermute | solution.py:28
  127.9 48.1 %collective-permute-start.25 = (bf16[128,3584]{1,0:T(8,128)(2,1)S(1)}, bf16[128,3584]{1,0:T(8,128)(2,1)S(1)}, u32[]{:S(2)}, u32[]{:S(2)}) collective-permute-start(bf16[128,3584]{1,0:T(8,128)(2,1)S(1)} %pad_maximum_fusion), channel_id=1, source_target_pairs={{4,0},{8,4},{12,8},{5,1},{9,5},{13,9},{6,2},{10,6},{14,10},{7,3},{... | collective-permute-start | bytes 2752520 | tf_op jit(solution)/shard_map/ppermute | solution.py:24
  129.2 46.8 %collective-permute-start.26 = (bf16[128,3584]{1,0:T(8,128)(2,1)S(1)}, bf16[128,3584]{1,0:T(8,128)(2,1)S(1)}, u32[]{:S(2)}, u32[]{:S(2)}) collective-permute-start(bf16[128,3584]{1,0:T(8,128)(2,1)S(1)} %pad_maximum_fusion), channel_id=1, source_target_pairs={{0,4},{4,8},{8,12},{1,5},{5,9},{9,13},{2,6},{6,10},{10,14},{3,7},{... | collective-permute-start | bytes 2752520 | tf_op jit(solution)/shard_map/ppermute | solution.py:24
  133.8 27.8 %collective-permute-start.23 = (bf16[128,1792]{1,0:T(8,128)(2,1)S(1)}, bf16[128,1792]{1,0:T(8,128)(2,1)S(1)}, u32[]{:S(2)}, u32[]{:S(2)}) collective-permute-start(bf16[128,1792]{1,0:T(8,128)(2,1)S(1)} %get-tuple-element.73), channel_id=1, source_target_pairs={{4,0},{8,4},{12,8},{5,1},{9,5},{13,9},{6,2},{10,6},{14,10},{7,3},{... | collective-permute-start | bytes 1376264 | tf_op jit(solution)/shard_map/ppermute | solution.py:24
  135.1 27.8 %collective-permute-start.24 = (bf16[128,1792]{1,0:T(8,128)(2,1)S(1)}, bf16[128,1792]{1,0:T(8,128)(2,1)S(1)}, u32[]{:S(2)}, u32[]{:S(2)}) collective-permute-start(bf16[128,1792]{1,0:T(8,128)(2,1)S(1)} %get-tuple-element.73), channel_id=1, source_target_pairs={{0,4},{4,8},{8,12},{1,5},{5,9},{9,13},{2,6},{6,10},{10,14},{3,7},{... | collective-permute-start | bytes 1376264 | tf_op jit(solution)/shard_map/ppermute | solution.py:24
  139.9 28.4 %collective-permute-start.21 = (bf16[128,1024]{1,0:T(8,128)(2,1)S(1)}, bf16[128,1024]{1,0:T(8,128)(2,1)S(1)}, u32[]{:S(2)}, u32[]{:S(2)}) collective-permute-start(bf16[128,1024]{1,0:T(8,128)(2,1)S(1)} %fusion.48), channel_id=1, source_target_pairs={{2,0},{1,3},{6,4},{5,7},{10,8},{9,11},{14,12},{13,15},{18,16},{17,... | collective-permute-start | bytes 786440 | tf_op jit(solution)/shard_map/ppermute | solution.py:197
  161.6 13.2 %collective-permute-start.30 = (bf16[128,1792]{1,0:T(8,128)(2,1)S(1)}, bf16[128,1792]{1,0:T(8,128)(2,1)S(1)}, u32[]{:S(2)}, u32[]{:S(2)}) collective-permute-start(bf16[128,1792]{1,0:T(8,128)(2,1)S(1)} %collective-permute-done.23), channel_id=1, source_target_pairs={{4,0},{8,4},{12,8},{5,1},{9,5},{13,9},{6,2},{10,6},{14,10},{7,3},{... | collective-permute-start | bytes 1376264 | tf_op jit(solution)/shard_map/ppermute | solution.py:24
  162.9 13.1 %collective-permute-start.31 = (bf16[128,1792]{1,0:T(8,128)(2,1)S(1)}, bf16[128,1792]{1,0:T(8,128)(2,1)S(1)}, u32[]{:S(2)}, u32[]{:S(2)}) collective-permute-start(bf16[128,1792]{1,0:T(8,128)(2,1)S(1)} %collective-permute-done.24), channel_id=1, source_target_pairs={{0,4},{4,8},{8,12},{1,5},{5,9},{9,13},{2,6},{6,10},{10,14},{3,7},{... | collective-permute-start | bytes 1376264 | tf_op jit(solution)/shard_map/ppermute | solution.py:24
  168.4 94.9 %collective-permute-start.22 = (bf16[128,1024]{1,0:T(8,128)(2,1)S(1)}, bf16[128,1024]{1,0:T(8,128)(2,1)S(1)}, u32[]{:S(2)}, u32[]{:S(2)}) collective-permute-start(bf16[128,1024]{1,0:T(8,128)(2,1)S(1)} %add_convert_fusion.3), channel_id=1, source_target_pairs={{0,0},{4,5},{8,10},{12,15},{16,16},{20,21},{24,26},{28,31}} | collective-permute-start | bytes 786440 | tf_op jit(solution)/shard_map/ppermute | solution.py:201
  178.7 9.1 %collective-permute-start.27 = (bf16[128,1024]{1,0:T(8,128)(2,1)S(1)}, bf16[128,1024]{1,0:T(8,128)(2,1)S(1)}, u32[]{:S(2)}, u32[]{:S(2)}) collective-permute-start(bf16[128,1024]{1,0:T(8,128)(2,1)S(1)} %get-tuple-element.125), channel_id=1, source_target_pairs={{0,1},{1,0},{2,3},{3,2},{4,5},{5,4},{6,7},{7,6},{8,9},{9,8},{10,11... | collective-permute-start | bytes 786440 | tf_op jit(solution)/shard_map/ppermute | solution.py:28
  178.9 45.0 %collective-permute-start.32 = (bf16[128,3584]{1,0:T(8,128)(2,1)S(1)}, bf16[128,3584]{1,0:T(8,128)(2,1)S(1)}, u32[]{:S(2)}, u32[]{:S(2)}) collective-permute-start(bf16[128,3584]{1,0:T(8,128)(2,1)S(1)} %collective-permute-done.25), channel_id=1, source_target_pairs={{4,0},{8,4},{12,8},{5,1},{9,5},{13,9},{6,2},{10,6},{14,10},{7,3},{... | collective-permute-start | bytes 2752520 | tf_op jit(solution)/shard_map/ppermute | solution.py:24
  180.2 33.9 %collective-permute-start.37 = (bf16[128,1792]{1,0:T(8,128)(2,1)S(1)}, bf16[128,1792]{1,0:T(8,128)(2,1)S(1)}, u32[]{:S(2)}, u32[]{:S(2)}) collective-permute-start(bf16[128,1792]{1,0:T(8,128)(2,1)S(1)} %collective-permute-done.30), channel_id=1, source_target_pairs={{4,0},{8,4},{12,8},{5,1},{9,5},{13,9},{6,2},{10,6},{14,10},{7,3},{... | collective-permute-start | bytes 1376264 | tf_op jit(solution)/shard_map/ppermute | solution.py:24
  181.5 33.3 %collective-permute-start.38 = (bf16[128,1792]{1,0:T(8,128)(2,1)S(1)}, bf16[128,1792]{1,0:T(8,128)(2,1)S(1)}, u32[]{:S(2)}, u32[]{:S(2)}) collective-permute-start(bf16[128,1792]{1,0:T(8,128)(2,1)S(1)} %collective-permute-done.31), channel_id=1, source_target_pairs={{0,4},{4,8},{8,12},{1,5},{5,9},{9,13},{2,6},{6,10},{10,14},{3,7},{... | collective-permute-start | bytes 1376264 | tf_op jit(solution)/shard_map/ppermute | solution.py:24
  187.8 36.1 %collective-permute-start.33 = (bf16[128,3584]{1,0:T(8,128)(2,1)S(1)}, bf16[128,3584]{1,0:T(8,128)(2,1)S(1)}, u32[]{:S(2)}, u32[]{:S(2)}) collective-permute-start(bf16[128,3584]{1,0:T(8,128)(2,1)S(1)} %collective-permute-done.26), channel_id=1, source_target_pairs={{0,4},{4,8},{8,12},{1,5},{5,9},{9,13},{2,6},{6,10},{10,14},{3,7},{... | collective-permute-start | bytes 2752520 | tf_op jit(solution)/shard_map/ppermute | solution.py:24
  214.1 52.2 %collective-permute-start.49 = (bf16[128,1024]{1,0:T(8,128)(2,1)S(1)}, bf16[128,1024]{1,0:T(8,128)(2,1)S(1)}, u32[]{:S(2)}, u32[]{:S(2)}) collective-permute-start(bf16[128,1024]{1,0:T(8,128)(2,1)S(1)} %add_convert_fusion.3), channel_id=1, source_target_pairs={{3,0},{7,5},{11,10},{15,15},{19,16},{23,21},{27,26},{31,31}} | collective-permute-start | bytes 786440 | tf_op jit(solution)/shard_map/ppermute | solution.py:201
  214.8 8.3 %collective-permute-start.28 = (bf16[128,1024]{1,0:T(8,128)(2,1)S(1)}, bf16[128,1024]{1,0:T(8,128)(2,1)S(1)}, u32[]{:S(2)}, u32[]{:S(2)}) collective-permute-start(bf16[128,1024]{1,0:T(8,128)(2,1)S(1)} %fusion.49), channel_id=1, source_target_pairs={{3,1},{0,2},{7,5},{4,6},{11,9},{8,10},{15,13},{12,14},{19,17},{16,... | collective-permute-start | bytes 786440 | tf_op jit(solution)/shard_map/ppermute | solution.py:197
  223.2 46.5 %collective-permute-start.29 = (bf16[128,1024]{1,0:T(8,128)(2,1)S(1)}, bf16[128,1024]{1,0:T(8,128)(2,1)S(1)}, u32[]{:S(2)}, u32[]{:S(2)}) collective-permute-start(bf16[128,1024]{1,0:T(8,128)(2,1)S(1)} %add_convert_fusion.2), channel_id=1, source_target_pairs={{1,4},{5,9},{9,6},{13,11},{17,20},{21,25},{25,22},{29,27}} | collective-permute-start | bytes 786440 | tf_op jit(solution)/shard_map/ppermute | solution.py:201
  223.9 24.3 %collective-permute-start.39 = (bf16[128,3584]{1,0:T(8,128)(2,1)S(1)}, bf16[128,3584]{1,0:T(8,128)(2,1)S(1)}, u32[]{:S(2)}, u32[]{:S(2)}) collective-permute-start(bf16[128,3584]{1,0:T(8,128)(2,1)S(1)} %collective-permute-done.32), channel_id=1, source_target_pairs={{4,0},{8,4},{12,8},{5,1},{9,5},{13,9},{6,2},{10,6},{14,10},{7,3},{... | collective-permute-start | bytes 2752520 | tf_op jit(solution)/shard_map/ppermute | solution.py:24
  225.2 24.2 %collective-permute-start.40 = (bf16[128,3584]{1,0:T(8,128)(2,1)S(1)}, bf16[128,3584]{1,0:T(8,128)(2,1)S(1)}, u32[]{:S(2)}, u32[]{:S(2)}) collective-permute-start(bf16[128,3584]{1,0:T(8,128)(2,1)S(1)} %collective-permute-done.33), channel_id=1, source_target_pairs={{0,4},{4,8},{8,12},{1,5},{5,9},{9,13},{2,6},{6,10},{10,14},{3,7},{... | collective-permute-start | bytes 2752520 | tf_op jit(solution)/shard_map/ppermute | solution.py:24
  252.4 9.2 %collective-permute-start.35 = (bf16[128,1024]{1,0:T(8,128)(2,1)S(1)}, bf16[128,1024]{1,0:T(8,128)(2,1)S(1)}, u32[]{:S(2)}, u32[]{:S(2)}) collective-permute-start(bf16[128,1024]{1,0:T(8,128)(2,1)S(1)} %fusion.50), channel_id=1, source_target_pairs={{0,2},{3,1},{4,6},{7,5},{8,10},{11,9},{12,14},{15,13},{16,18},{19,... | collective-permute-start | bytes 786440 | tf_op jit(solution)/shard_map/ppermute | solution.py:197
  253.9 10.1 %collective-permute-start.42 = (bf16[128,1024]{1,0:T(8,128)(2,1)S(1)}, bf16[128,1024]{1,0:T(8,128)(2,1)S(1)}, u32[]{:S(2)}, u32[]{:S(2)}) collective-permute-start(bf16[128,1024]{1,0:T(8,128)(2,1)S(1)} %fusion.51), channel_id=1, source_target_pairs={{1,3},{2,0},{5,7},{6,4},{9,11},{10,8},{13,15},{14,12},{17,19},{18,... | collective-permute-start | bytes 786440 | tf_op jit(solution)/shard_map/ppermute | solution.py:197
  261.7 9.9 %collective-permute-start.46 = (f32[128]{0:T(128)S(1)}, f32[128]{0:T(128)S(1)}, u32[]{:S(2)}, u32[]{:S(2)}) collective-permute-start(f32[128]{0:T(128)S(1)} %get-tuple-element.86), channel_id=1, source_target_pairs={{0,4},{4,0},{8,12},{12,8},{1,5},{5,1},{9,13},{13,9},{2,6},{6,2},{1... | collective-permute-start | bytes 1544 | tf_op jit(solution)/shard_map/ppermute | solution.py:231
  263.3 9.6 %collective-permute-start.47 = (f32[128]{0:T(128)S(1)}, f32[128]{0:T(128)S(1)}, u32[]{:S(2)}, u32[]{:S(2)}) collective-permute-start(f32[128]{0:T(128)S(1)} %get-tuple-element.86), channel_id=1, source_target_pairs={{0,8},{4,12},{8,0},{12,4},{1,9},{5,13},{9,1},{13,5},{2,10},{6,14},... | collective-permute-start | bytes 1544 | tf_op jit(solution)/shard_map/ppermute | solution.py:231
  264.0 9.6 %collective-permute-start.48 = (f32[128]{0:T(128)S(1)}, f32[128]{0:T(128)S(1)}, u32[]{:S(2)}, u32[]{:S(2)}) collective-permute-start(f32[128]{0:T(128)S(1)} %get-tuple-element.86), channel_id=1, source_target_pairs={{0,12},{4,8},{8,4},{12,0},{1,13},{5,9},{9,5},{13,1},{2,14},{6,10},... | collective-permute-start | bytes 1544 | tf_op jit(solution)/shard_map/ppermute | solution.py:231
  266.3 9.9 %collective-permute-start.50 = (bf16[128,1024]{1,0:T(8,128)(2,1)S(1)}, bf16[128,1024]{1,0:T(8,128)(2,1)S(1)}, u32[]{:S(2)}, u32[]{:S(2)}) collective-permute-start(bf16[128,1024]{1,0:T(8,128)(2,1)S(1)} %add_convert_fusion.2), channel_id=1, source_target_pairs={{2,4},{6,9},{10,6},{14,11},{18,20},{22,25},{26,22},{30,27}} | collective-permute-start | bytes 786440 | tf_op jit(solution)/shard_map/ppermute | solution.py:201
  269.7 13.5 %collective-permute-start.36 = (bf16[128,1024]{1,0:T(8,128)(2,1)S(1)}, bf16[128,1024]{1,0:T(8,128)(2,1)S(1)}, u32[]{:S(2)}, u32[]{:S(2)}) collective-permute-start(bf16[128,1024]{1,0:T(8,128)(2,1)S(1)} %add_convert_fusion.1), channel_id=1, source_target_pairs={{2,8},{6,13},{10,2},{14,7},{18,24},{22,29},{26,18},{30,23}} | collective-permute-start | bytes 786440 | tf_op jit(solution)/shard_map/ppermute | solution.py:201
  271.6 12.4 %collective-permute-start.51 = (bf16[128,1024]{1,0:T(8,128)(2,1)S(1)}, bf16[128,1024]{1,0:T(8,128)(2,1)S(1)}, u32[]{:S(2)}, u32[]{:S(2)}) collective-permute-start(bf16[128,1024]{1,0:T(8,128)(2,1)S(1)} %add_convert_fusion.1), channel_id=1, source_target_pairs={{1,8},{5,13},{9,2},{13,7},{17,24},{21,29},{25,18},{29,23}} | collective-permute-start | bytes 786440 | tf_op jit(solution)/shard_map/ppermute | solution.py:201
  272.9 11.1 %collective-permute-start.43 = (bf16[128,1024]{1,0:T(8,128)(2,1)S(1)}, bf16[128,1024]{1,0:T(8,128)(2,1)S(1)}, u32[]{:S(2)}, u32[]{:S(2)}) collective-permute-start(bf16[128,1024]{1,0:T(8,128)(2,1)S(1)} %add_convert_fusion), channel_id=1, source_target_pairs={{3,12},{7,1},{11,14},{15,3},{19,28},{23,17},{27,30},{31,19}} | collective-permute-start | bytes 786440 | tf_op jit(solution)/shard_map/ppermute | solution.py:201
  273.6 10.4 %collective-permute-start.52 = (bf16[128,1024]{1,0:T(8,128)(2,1)S(1)}, bf16[128,1024]{1,0:T(8,128)(2,1)S(1)}, u32[]{:S(2)}, u32[]{:S(2)}) collective-permute-start(bf16[128,1024]{1,0:T(8,128)(2,1)S(1)} %add_convert_fusion), channel_id=1, source_target_pairs={{0,12},{4,1},{8,14},{12,3},{16,28},{20,17},{24,30},{28,19}} | collective-permute-start | bytes 786440 | tf_op jit(solution)/shard_map/ppermute | solution.py:201
  (12 other events, 97.9 us)
